TPU v7x, 256 devices: a whole 4x4x8 slice. The times are simulated.
256 devices in a mesh: expert: 8 (over y, core), dp: 32 (over x, z).
Axes of the slice: x: 4, y: 4, z: 8, core: 2. Of those that a mesh axis runs over, the one named last changes fastest.
Arguments:
- hidden: bfloat16 [8, 14336, 1024], P('expert', 'dp'), may hold values from -6 to 6
- weight_codes: int32 [8, 14336, 2048], P('expert', 'dp'), may hold values from -8 to 7
- group_scales: float32 [8, 448, 2048], P('expert', 'dp'), may hold values from 0.0006681531 to 0.0050111483
- expert_index: int32 [4096, 2], P('expert'), may hold values from 0 to 7, all different within a row
- gate_values: float32 [4096, 2], P('expert'), may hold values from 0.2 to 1
- output_grad: bfloat16 [4096, 2048], P('expert', 'dp'), may hold values from -6 to 6
Outputs:
- combined: bfloat16 [4096, 2048], P('expert', 'dp')
- gate_grad: float32 [4096, 2], P('expert')
- hidden_grad: bfloat16 [8, 14336, 1024], P('expert', 'dp')
- weight_grad: float32 [8, 14336, 2048], P('expert', 'dp')
- scale_grad: float32 [8, 448, 2048], P('expert', 'dp')
Inputs may be any that keep to these rules, and one draw needn't show every extreme that they name: `expert_index`: the 2 entries of a token name different experts.
All inputs are finite; a program needn't handle non-finite values.
Results may differ from a plain program's by a relative error of at most 0.0058.
Values may be sent and summed in bfloat16 or wider, within the bound.
No kernel may reach another device: no remote copies, remote signals or barrier semaphores. Data moves between devices by JAX's collectives and lax.ppermute only.
A program may use at most 128 MiB of HBM per device.

v0:
```python
import jax
import jax.numpy as jnp
from jax import lax
from jax.sharding import PartitionSpec as P

EXPERTS = 8
GROUP = 32


def dequantize(weight_codes, group_scales):
    experts_here, units_here, feature_width = weight_codes.shape
    grouped = weight_codes.astype(jnp.float32).reshape(
        experts_here, units_here // GROUP, GROUP, feature_width
    )
    return (
        (grouped * group_scales[:, :, None, :])
        .reshape(experts_here, units_here, feature_width)
        .astype(jnp.bfloat16)
    )


def choice_ranks(flat_experts):
    onehot = (flat_experts[:, None] == jnp.arange(EXPERTS, dtype=jnp.int32)[None, :]).astype(
        jnp.int32
    )
    return jnp.sum((jnp.cumsum(onehot, axis=0) - onehot) * onehot, axis=1)


def on_device(hidden, weight_codes, group_scales, expert_index, gate_values, output_grad):
    local_experts = hidden.shape[0]
    slot_total = hidden.shape[2]
    feature_width = weight_codes.shape[2]
    expert_groups = lax.axis_size("expert")
    data_ranks = lax.axis_size("dp")
    tokens_here, choices = expert_index.shape
    capacity = tokens_here * choices // EXPERTS
    column_count = feature_width // data_ranks
    weight_table = dequantize(weight_codes, group_scales)
    table_cols = weight_table
    partial_value = jnp.einsum(
        "efs,efd->des", hidden, table_cols, preferred_element_type=jnp.float32
    )
    summed = lax.psum(partial_value.reshape(feature_width, local_experts * slot_total), "dp")
    owned_rows = lax.dynamic_slice_in_dim(
        summed, lax.axis_index("dp") * column_count, column_count, 0
    )
    outgoing = owned_rows.astype(jnp.bfloat16).reshape(column_count, local_experts, slot_total)
    returned = lax.all_to_all(outgoing, "expert", split_axis=2, concat_axis=2, tiled=True)
    returned = returned.reshape(column_count, local_experts * slot_total)
    flat_experts = expert_index.reshape(-1)
    ranking = choice_ranks(flat_experts)
    kept_mask = ranking < capacity
    clipped = jnp.minimum(ranking, capacity - 1)
    group_of = flat_experts // local_experts
    within = flat_experts % local_experts
    columns = jnp.arange(EXPERTS * capacity, dtype=jnp.int32)
    place_index = (within * expert_groups + group_of) * capacity + clipped
    picker = ((place_index[:, None] == columns[None, :]) & kept_mask[:, None]).astype(jnp.bfloat16)
    gathered = jnp.einsum("ac,dc->ad", picker, returned, preferred_element_type=jnp.float32)
    gathered = gathered.reshape(tokens_here, choices, column_count)
    keep_float = kept_mask.reshape(tokens_here, choices).astype(jnp.float32)
    weighted = gate_values * keep_float
    grad_float = output_grad.astype(jnp.float32)
    combined = jnp.sum(weighted[:, :, None] * gathered, axis=1).astype(jnp.bfloat16)
    gate_partial = keep_float * jnp.sum(grad_float[:, None, :] * gathered, axis=2)
    gate_grad = lax.psum(gate_partial, "dp")
    values = (
        (weighted[:, :, None] * grad_float[:, None, :])
        .reshape(tokens_here * choices, column_count)
        .astype(jnp.bfloat16)
    )
    outbound = jnp.einsum("ac,ad->cd", picker, values, preferred_element_type=jnp.float32).astype(
        jnp.bfloat16
    )
    outbound = outbound.reshape(local_experts, slot_total, column_count)
    arrived = lax.all_to_all(outbound, "expert", split_axis=1, concat_axis=1, tiled=True)
    block_cols = lax.all_gather(arrived, "dp", axis=2, tiled=True)
    table_cols = weight_table
    hidden_acc = jnp.einsum(
        "esd,efd->efs", block_cols, table_cols, preferred_element_type=jnp.float32
    )
    weight_piece = jnp.einsum(
        "efs,esd->efd", hidden, block_cols, preferred_element_type=jnp.float32
    )
    hidden_acc, weight_grad = (hidden_acc, weight_piece)
    hidden_grad = hidden_acc.astype(jnp.bfloat16)
    products = weight_grad * weight_codes.astype(jnp.float32)
    scale_grad = jnp.sum(products.reshape(local_experts, -1, GROUP, feature_width), axis=2)
    return (combined, gate_grad, hidden_grad, weight_grad, scale_grad)


def solution(mesh):
    return jax.shard_map(
        on_device,
        mesh=mesh,
        in_specs=(
            P("expert", "dp", None),
            P("expert", "dp", None),
            P("expert", "dp", None),
            P("expert", None),
            P("expert", None),
            P("expert", "dp"),
        ),
        out_specs=(
            P("expert", "dp"),
            P("expert", None),
            P("expert", "dp", None),
            P("expert", "dp", None),
            P("expert", "dp", None),
        ),
        check_vma=False,
    )
```

profile of v0, /device:TPU:8, one launch (start us, length us, event | category | flops | bytes accessed | tf_op | source)
XLA Modules:
  0.0 422.4 jit_solution(741626494181359657)
XLA Ops:
  7.2 0.9 copy.63
  8.5 2.3 reduce-window.6
  11.7 0.7 broadcast_select_fusion.1
  12.8 1.0 copy.77
  14.0 1.2 fusion.29
  16.1 2.3 reduce.3
  18.6 9.4 %all_to_all.10 = bf16[8,2,4096]{2,1,0:T(2,128)(2,1)S(1)} all-to-all(bf16[8,2,4096]{2,1,0:T(2,128)(2,1)S(1)} %reshape.142), channel_id=1, replica_groups=mesh['expert'=8,'dp'=32] {'expert'}, dimensions={0} | all-to-all | bytes 262144 | tf_op jit(solution)/shard_map/all_to_all | solution.py:76
  28.4 0.9 copy.74
  29.3 0.6 convert_element_type.45
  30.4 82.7 %all-gather.2.cloned.1.call-done = bf16[1,1024,2048]{1,2,0:T(8,128)(2,1)} async-done(((bf16[1,1024,64]{1,2,0:T(8,128)(2,1)}), bf16[1,1024,2048]{1,2,0:T(8,128)(2,1)}) %all-gather.2.cloned.1.call-update) | async-done | bytes 4194320 | tf_op jit(solution)/shard_map/all_gather | solution.py:77
  113.1 4.3 %fusion.12 = f32[1,448,2048]{2,1,0:T(8,128)S(1)} fusion(bf16[1,1024,2048]{1,2,0:T(8,128)(2,1)} %all-gather.2.cloned.1.call-done, bf16[1,448,1024]{2,1,0:T(8,128)(2,1)S(1)} %copy-done), kind=kOutput, calls=%fused_computation.14 | convolution fusion | flops 1879048192 | bytes 8781824 | tf_op jit(solution)/shard_map/efs,esd->efd/dot_general | solution.py:82
  117.8 2.9 copy-done.1
  120.7 3.1 convert_multiply_fusion
  123.9 5.6 %fusion.33 = f32[2048,1024]{1,0:T(8,128)} fusion(bf16[448,2048]{1,0:T(8,128)(2,1)S(1)} %get-tuple-element.13, bf16[1,448,1024]{2,1,0:T(8,128)(2,1)S(1)} %copy-done), kind=kOutput, calls=%fused_computation.25 | convolution fusion | flops 1879048192 | bytes 11141120 | tf_op jit(solution)/shard_map/efs,efd->des/dot_general | solution.py:40
  129.5 192.6 %all-reduce.1 = bf16[2048,1024]{1,0:T(8,128)(2,1)} all-reduce(f32[2048,1024]{1,0:T(8,128)} %fusion.33), channel_id=1, replica_groups=mesh['expert'=8,'dp'=32] {'dp'}, use_global_device_ids=true, to_apply=%region_3.4 | all-reduce | flops 2097152 | bytes 12582912 | tf_op jit(solution)/shard_map/psum | solution.py:43
  322.1 0.9 fusion.36
  323.4 2.4 reduce.4
  325.8 0.9 reshape.140
  326.7 4.8 %all-to-all-start = ((bf16[8,2,4096]{2,1,0:T(2,128)(2,1)}), bf16[8,2,4096]{2,1,0:T(2,128)(2,1)S(1)}, u32[]{:S(2)}, u32[]{:S(2)}) async-start(bf16[8,2,4096]{2,1,0:T(2,128)(2,1)} %reshape.140), calls=%async_computation | async-start | bytes 262144 | tf_op jit(solution)/shard_map/all_to_all | solution.py:48
  331.5 5.2 %fusion.23 = bf16[1,448,1024]{2,1,0:T(8,128)(2,1)} fusion(bf16[448,2048]{1,0:T(8,128)(2,1)S(1)} %get-tuple-element.13, bf16[1,1024,2048]{1,2,0:T(8,128)(2,1)} %all-gather.2.cloned.1.call-done), kind=kOutput, calls=%fused_computation.21 | convolution fusion | flops 1879506944 | bytes 6946816 | tf_op jit(solution)/shard_map/esd,efd->efs/dot_general | solution.py:79
  336.7 2.6 reduce_sum.41
  339.3 0.7 reduce_sum.42
  340.7 2.0 multiply_reduce_fusion
  342.7 72.9 %psum.15 = f32[512,2]{0,1:T(2,128)} all-reduce(f32[512,2]{0,1:T(2,128)S(1)} %broadcast_select_fusion), channel_id=1, replica_groups=mesh['expert'=8,'dp'=32] {'dp'}, use_global_device_ids=true, to_apply=%region_6.7 | all-reduce | flops 1024 | bytes 8192 | tf_op jit(solution)/shard_map/psum | solution.py:66
  (43 shorter events, 5.1 us)
Async XLA Ops:
  7.2 105.9 %copy-start = (bf16[1,448,1024]{2,1,0:T(8,128)(2,1)S(1)}, bf16[1,448,1024]{2,1,0:T(8,128)(2,1)}, u32[]{:S(2)}) copy-start(bf16[1,448,1024]{2,1,0:T(8,128)(2,1)} %param.6) | copy-start | bytes 2752516
  7.2 105.9 %all-gather.2.cloned.1.call-start = ((), (), s32[]{:S(2)}) async-start(), calls=%async_computation.2 | async-start | bytes 4325376 | tf_op jit(solution)/shard_map/all_gather | solution.py:77
  12.8 16.6 %copy-start.3 = (bf16[512,64]{0,1:T(8,128)(2,1)S(1)}, bf16[512,64]{0,1:T(8,128)(2,1)}, u32[]{:S(2)}) copy-start(bf16[512,64]{0,1:T(8,128)(2,1)} %param.11) | copy-start | bytes 196612
  13.8 16.2 %copy-start.5 = (f32[1,14,2048]{2,0,1:T(1,128)S(1)}, f32[1,14,2048]{2,0,1:T(1,128)}, u32[]{:S(2)}) copy-start(f32[1,14,2048]{2,0,1:T(1,128)} %param.8) | copy-start | bytes 344068
  14.0 16.4 %copy-start.6 = (s32[512,2]{0,1:T(2,128)S(1)}, s32[512,2]{0,1:T(2,128)}, u32[]{:S(2)}) copy-start(s32[512,2]{0,1:T(2,128)} %param.9) | copy-start | bytes 12292
  117.3 6.5 %copy-start.2 = (f32[1,448,2048]{2,1,0:T(8,128)}, f32[1,448,2048]{2,1,0:T(8,128)S(1)}, u32[]{:S(2)}) copy-start(f32[1,448,2048]{2,1,0:T(8,128)S(1)} %fusion.12) | copy-start | bytes 11010052
  117.4 3.4 copy-start.1
  326.7 13.3 %all-to-all-start = ((bf16[8,2,4096]{2,1,0:T(2,128)(2,1)}), bf16[8,2,4096]{2,1,0:T(2,128)(2,1)S(1)}, u32[]{:S(2)}, u32[]{:S(2)}) async-start(bf16[8,2,4096]{2,1,0:T(2,128)(2,1)} %reshape.140), calls=%async_computation | async-start | bytes 262144 | tf_op jit(solution)/shard_map/all_to_all | solution.py:48
  336.7 4.0 copy-start.4
Sparse Core Ops, SparseCore 0:
  29.4 83.5 all-gather.1
where the time goes:
time: 423 us; the launch traced here: 422 us
  blocking collectives  275 us (65%)
  waiting for transfers between devices  82.7 us (20%)
  matrix products  18.3 us (4%)
  other arithmetic  14.3 us (3%)
  between operations  14.3 us (3%)
  local copies, waits for them, and re-layouts  13.1 us (3%)
  starting transfers between devices  4.84 us (1%)
    psum x1, blocking collectives, on_device(): lax.psum(partial_value.reshape(feature_width, local_experts * slot_total)...  193 us
    all_gather x1, waiting for transfers between devices, on_device(): block_cols = lax.all_gather(arrived, 'dp', axis=2, tiled=True)  82.7 us
    psum x1, blocking collectives, on_device(): gate_grad = lax.psum(gate_partial, 'dp')  72.9 us
    all_to_all x1, blocking collectives, on_device(): lax.all_to_all(outbound, 'expert', split_axis=1, concat_axis=1, tiled=True)  9.39 us
  transfers between devices with their start and end apart: 2, of which 1 were waited for; matrix products, arithmetic and copies ran while one was open for 2% of the time, Pallas kernels for 0%

commit v1 on v0

v1 whole, which is shorter than its diff:
```python
import jax
import jax.numpy as jnp
from jax import lax
from jax.experimental import pallas as pl
from jax.experimental.pallas import tpu as pltpu
from jax.sharding import Mesh, PartitionSpec as P

EXPERTS = 8
GROUP = 32
CAP = 128
NY, NC, NX, NZ = 4, 2, 4, 8
COLS = 64
SLOTS = EXPERTS * CAP
PARAMS = pltpu.CompilerParams(vmem_limit_bytes=56 * 1024 * 1024)
F32, BF16, I32 = jnp.float32, jnp.bfloat16, jnp.int32


def sds(shape, dtype):
    return jax.ShapeDtypeStruct(shape, dtype)


def whole(shape):
    return pl.BlockSpec(shape, lambda *_: (0,) * len(shape))


def dequant(codes, scales):
    rows, width = codes.shape
    grouped = codes.astype(F32).reshape(rows // GROUP, GROUP, width)
    return (grouped * scales[:, None, :]).reshape(rows, width).astype(BF16)


def pickers(place_ref):
    lanes = lax.broadcasted_iota(I32, (place_ref.shape[0], SLOTS), 1)
    return [(place_ref[:, k : k + 1] == lanes).astype(BF16) for k in range(2)]


def slot_body(index_ref, gate_ref, grad_ref, place_ref, out_ref):
    tokens = index_ref.shape[0]
    first, second = index_ref[:, 0:1], index_ref[:, 1:2]
    experts = lax.broadcasted_iota(I32, (tokens, 128), 1)
    one_first = (first == experts).astype(F32)
    one_second = (second == experts).astype(F32)
    row = lax.broadcasted_iota(I32, (tokens, tokens), 0)
    col = lax.broadcasted_iota(I32, (tokens, tokens), 1)
    before = (col < row).astype(BF16)
    counts = jnp.dot(before, (one_first + one_second).astype(BF16), preferred_element_type=F32)
    rank_first = jnp.sum(counts * one_first, axis=1, keepdims=True).astype(I32)
    rank_second = jnp.sum(counts * one_second, axis=1, keepdims=True).astype(I32)
    place_ref[:, 0:1] = jnp.where(rank_first < CAP, first * CAP + rank_first, -1)
    place_ref[:, 1:2] = jnp.where(rank_second < CAP, second * CAP + rank_second, -1)
    grad = grad_ref[...].astype(F32)
    total = None
    for k, pick in enumerate(pickers(place_ref)):
        value = (gate_ref[:, k : k + 1] * grad).astype(BF16)
        piece = lax.dot_general(value, pick, (((0,), (0,)), ((), ())), preferred_element_type=F32)
        total = piece if total is None else total + piece
    total = total.astype(BF16)
    for e in range(EXPERTS):
        out_ref[e] = total[:, e * CAP : (e + 1) * CAP]


def slot_grads(index, gate, grad):
    return pl.pallas_call(
        slot_body,
        out_shape=(sds(index.shape, I32), sds((EXPERTS, COLS, CAP), BF16)),
        compiler_params=PARAMS,
        name="slot_grads",
    )(index, gate, grad)


def forward_block(where, k, hidden, codes, scales, types):
    units, slots = hidden.shape
    half = codes.shape[1] // NX // 2
    groups = units // GROUP

    def body(where_ref, hidden_ref, codes_ref, scales_ref, *outs):
        table = dequant(codes_ref[...], scales_ref[...])
        value = lax.dot_general(table, hidden_ref[...], (((0,), (0,)), ((), ())), preferred_element_type=F32)
        for h in range(2):
            @pl.when(pl.program_id(0) == h)
            def _():
                outs[h][...] = value.astype(types[h])

    return pl.pallas_call(
        body,
        grid_spec=pltpu.PrefetchScalarGridSpec(
            num_scalar_prefetch=1,
            grid=(2,),
            in_specs=[
                pl.BlockSpec((units, slots), lambda h, w: (0, 0)),
                pl.BlockSpec((units, half), lambda h, w: (0, lax.rem(w[0] + k, NX) * 2 + h)),
                pl.BlockSpec((groups, half), lambda h, w: (0, lax.rem(w[0] + k, NX) * 2 + h)),
            ],
            out_specs=[pl.BlockSpec((half, slots), lambda h, w: (0, 0)) for _ in range(2)],
        ),
        out_shape=[sds((half, slots), t) for t in types],
        compiler_params=PARAMS,
        name=f"forward_{k}",
    )(where, hidden, codes, scales)


def x_sum_body(where_ref, top, bottom, top_a, top_b, bottom_a, bottom_b, *outs):
    z = where_ref[1]
    acc_top = top[...] + top_a[...].astype(F32) + top_b[...].astype(F32)
    acc_bottom = bottom[...] + bottom_a[...].astype(F32) + bottom_b[...].astype(F32)
    scratch = outs[-1]
    half = acc_top.shape[0]
    scratch[:half] = acc_top
    scratch[half:] = acc_bottom
    for k in range(NZ):
        start = pl.multiple_of(lax.rem(z + k, NZ) * COLS, COLS)
        outs[k][...] = scratch[pl.ds(start, COLS), :].astype(outs[k].dtype)


def x_sum(where, *arrays):
    half, slots = arrays[0].shape
    kinds = [F32, BF16, F32, BF16, BF16, BF16, F32, BF16]
    return pl.pallas_call(
        x_sum_body,
        grid_spec=pltpu.PrefetchScalarGridSpec(
            num_scalar_prefetch=1,
            grid=(1,),
            in_specs=[whole((half, slots)) for _ in arrays],
            out_specs=[whole((COLS, slots)) for _ in kinds],
            scratch_shapes=[pltpu.VMEM((2 * half, slots), F32)],
        ),
        out_shape=[sds((COLS, slots), t) for t in kinds],
        compiler_params=PARAMS,
        name="x_sum",
    )(where, *arrays)


def z_sum_body(own, *rest):
    total = own[...]
    for piece in rest[:-1]:
        total = total + piece[...].astype(F32)
    total = total.astype(BF16)
    for g in range(EXPERTS):
        rest[-1][g] = total[:, g * CAP : (g + 1) * CAP]


def z_sum(*arrays):
    return pl.pallas_call(
        z_sum_body, out_shape=sds((EXPERTS, COLS, CAP), BF16), compiler_params=PARAMS, name="z_sum"
    )(*arrays)


def combine_body(place_ref, gate_ref, grad_ref, back_ref, out_ref, gate_out_ref):
    back = jnp.concatenate([back_ref[e] for e in range(EXPERTS)], axis=1)
    grad = grad_ref[...].astype(F32)
    total = None
    ones = jnp.ones((8, COLS), F32)
    for k, pick in enumerate(pickers(place_ref)):
        got = lax.dot_general(pick, back, (((1,), (1,)), ((), ())), preferred_element_type=F32)
        piece = gate_ref[:, k : k + 1] * got
        total = piece if total is None else total + piece
        sums = lax.dot_general(
            ones, grad * got, (((1,), (1,)), ((), ())), preferred_element_type=F32, precision=lax.Precision.HIGHEST
        )
        for j in range(4):
            gate_out_ref[k * 4 + j : k * 4 + j + 1, :] = sums[0:1, j * 128 : (j + 1) * 128]
    out_ref[...] = total.astype(BF16)


def combine(place, gate, grad, back):
    return pl.pallas_call(
        combine_body,
        out_shape=(sds(grad.shape, BF16), sds((8, 128), F32)),
        compiler_params=PARAMS,
        name="combine",
    )(place, gate, grad, back)


def gate_sum_body(parts_ref, out_ref):
    total = jnp.sum(parts_ref[...], axis=0)
    turned = total.T
    for j in range(4):
        out_ref[j * 128 : (j + 1) * 128, 0:1] = turned[:, j : j + 1]
        out_ref[j * 128 : (j + 1) * 128, 1:2] = turned[:, 4 + j : 5 + j]


def gate_sum(parts):
    return pl.pallas_call(
        gate_sum_body, out_shape=sds((512, 2), F32), compiler_params=PARAMS, name="gate_sum"
    )(parts)


STEPS = 4


def backward_body(where_ref, hidden_ref, codes_ref, scales_ref, *rest):
    owns, trios = rest[:NZ], rest[NZ : 2 * NZ]
    hidden_out, weight_out, scale_out, grads, acc = rest[2 * NZ :]
    step = pl.program_id(0)
    x, z = where_ref[0], where_ref[1]

    @pl.when(step == 0)
    def _():
        for k in range(NZ):
            for i, dx in enumerate((0, 1, 3, 2)):
                owner = lax.rem(x + dx, NX) * NZ + lax.rem(z + k, NZ)
                start = pl.multiple_of(owner * COLS, COLS)
                for g in range(EXPERTS):
                    piece = owns[k][g] if i == 0 else trios[k][i - 1, g]
                    grads[pl.ds(start, COLS), g * CAP : (g + 1) * CAP] = piece

    width = codes_ref.shape[1]
    codes = codes_ref[...]
    table = dequant(codes, scales_ref[...])
    block = grads[pl.ds(pl.multiple_of(step * width, width), width), :]
    part = jnp.dot(table, block, preferred_element_type=F32)

    @pl.when(step == 0)
    def _():
        acc[...] = part

    @pl.when(jnp.logical_and(step > 0, step < STEPS - 1))
    def _():
        acc[...] = acc[...] + part

    @pl.when(step == STEPS - 1)
    def _():
        hidden_out[...] = (acc[...] + part).astype(BF16)

    weight = lax.dot_general(hidden_ref[...], block, (((1,), (1,)), ((), ())), preferred_element_type=F32)
    weight_out[...] = weight
    products = weight * codes.astype(F32)
    scale_out[...] = jnp.sum(products.reshape(-1, GROUP, width), axis=1)


def backward(where, hidden, codes, scales, owns, trios):
    units, slots = hidden.shape
    features = codes.shape[1]
    width = features // STEPS
    groups = units // GROUP
    return pl.pallas_call(
        backward_body,
        grid_spec=pltpu.PrefetchScalarGridSpec(
            num_scalar_prefetch=1,
            grid=(STEPS,),
            in_specs=[
                whole((units, slots)),
                pl.BlockSpec((units, width), lambda n, w: (0, n)),
                pl.BlockSpec((groups, width), lambda n, w: (0, n)),
            ]
            + [whole(a.shape) for a in owns]
            + [whole(a.shape) for a in trios],
            out_specs=[
                whole((units, slots)),
                pl.BlockSpec((units, width), lambda n, w: (0, n)),
                pl.BlockSpec((groups, width), lambda n, w: (0, n)),
            ],
            scratch_shapes=[pltpu.VMEM((features, slots), BF16), pltpu.VMEM((units, slots), F32)],
        ),
        out_shape=[sds((units, slots), BF16), sds((units, features), F32), sds((groups, features), F32)],
        compiler_params=PARAMS,
        name="backward",
    )(where, hidden, codes, scales, *owns, *trios)


def shift(value, axis, by):
    size = NX if axis == "x" else NZ
    return lax.ppermute(value, axis, [(i, (i + by) % size) for i in range(size)])


def to_experts(value):
    return lax.all_to_all(value, ("y", "c"), 0, 0, tiled=True)


def on_device(hidden, weight_codes, group_scales, expert_index, gate_values, output_grad):
    hidden, codes, scales = hidden[0], weight_codes[0], group_scales[0]
    where = jnp.stack([lax.axis_index("x"), lax.axis_index("z")]).astype(I32)

    far_top, far_bottom = forward_block(where, 2, hidden, codes, scales, (BF16, BF16))
    far_top = shift(far_top, "x", 1)
    far_bottom = shift(far_bottom, "x", -1)
    place, outbound = slot_grads(expert_index, gate_values, output_grad)
    shard = to_experts(outbound)
    up_top, up_bottom = forward_block(where, 1, hidden, codes, scales, (F32, BF16))
    down_top, down_bottom = forward_block(where, 3, hidden, codes, scales, (BF16, F32))
    own_top, own_bottom = forward_block(where, 0, hidden, codes, scales, (F32, F32))
    bottom_a = shift(up_bottom, "x", 1)
    top_a = shift(down_top, "x", -1)
    top_b = shift((up_top + far_top.astype(F32)).astype(BF16), "x", 1)
    bottom_b = shift((down_bottom + far_bottom.astype(F32)).astype(BF16), "x", -1)

    trio = jnp.stack([shift(shard, "x", -1), shift(shard, "x", 1), shift(shard, "x", 2)])
    owns, trios = {0: shard}, {0: trio}
    for hop in range(1, 5):
        owns[NZ - hop] = shift(owns[(NZ - hop + 1) % NZ], "z", 1)
        if hop < 4:
            owns[hop] = shift(owns[hop - 1], "z", -1)
    for hop in range(1, 5):
        trios[hop] = shift(trios[hop - 1], "z", -1)
        if hop < 4:
            trios[NZ - hop] = shift(trios[(NZ - hop + 1) % NZ], "z", 1)

    own, up1, up2, up3, up4, down3, down2, down1 = x_sum(
        where, own_top, own_bottom, top_a, top_b, bottom_a, bottom_b
    )
    got4 = shift(up4, "z", 2)
    got3 = shift(up3, "z", 1)
    gotm3 = shift(down3, "z", -1)
    got1 = shift(up1, "z", 1)
    gotm1 = shift(down1, "z", -1)
    got2 = shift((up2 + got3.astype(F32) + got4.astype(F32)).astype(BF16), "z", 2)
    gotm2 = shift((down2 + gotm3.astype(F32)).astype(BF16), "z", -2)
    outgoing = z_sum(own, got1, got2, gotm1, gotm2)
    returned = to_experts(outgoing)
    combined, gate_part = combine(place, gate_values, output_grad, returned)
    spread = jnp.broadcast_to(gate_part[None], (NX * NZ, 8, 128))
    gate_grad = gate_sum(lax.all_to_all(spread, ("x", "z"), 0, 0, tiled=True))

    hidden_grad, weight_grad, scale_grad = backward(
        where, hidden, codes, scales, [owns[k] for k in range(NZ)], [trios[k] for k in range(NZ)]
    )
    return combined, gate_grad, hidden_grad[None], weight_grad[None], scale_grad[None]


def solution(mesh):
    fine = Mesh(mesh.devices.reshape(NY, NC, NX, NZ), ("y", "c", "x", "z"))
    expert, dp = ("y", "c"), ("x", "z")
    return jax.shard_map(
        on_device,
        mesh=fine,
        in_specs=(
            P(expert, dp, None),
            P(expert, dp, None),
            P(expert, dp, None),
            P(expert, None),
            P(expert, None),
            P(expert, dp),
        ),
        out_specs=(
            P(expert, dp),
            P(expert, None),
            P(expert, dp, None),
            P(expert, dp, None),
            P(expert, dp, None),
        ),
        check_vma=False,
    )
```

time: 423 us -> 167 us (0.39)
  blocking collectives: 275 us -> 9.59 us
  starting transfers between devices: 4.84 us -> 70.7 us
  waiting for transfers between devices: 82.7 us -> 21.8 us
  Pallas kernels: 0 us -> 44.2 us
  matrix products: 18.3 us -> 0 us
  between operations: 14.3 us -> 0.97 us
  other arithmetic: 14.3 us -> 4.1 us
    psum x2 -> x0, blocking collectives: 265 us -> none  [the longest x1 193 us: on_device(): lax.psum(partial_value.reshape(feature_width, local_experts * slot_total)...]
    all_gather x1 -> x0, waiting for transfers between devices: 82.7 us -> none  [on_device(): block_cols = lax.all_gather(arrived, 'dp', axis=2, tiled=True)]
    ppermute x0 -> x30, starting transfers between devices: none -> 56.3 us  [shift(): lax.ppermute(value, axis, [(i, (i + by) % size) for i in range(size)])]
    pallas_call x0 -> x10, Pallas kernels: none -> 44.2 us  [the longest x4 17.2 us: forward_block(): pl.pallas_call(body, grid_spec=pltpu.PrefetchScalarGridSpec(num_scalar_pr...]
    dot_general x5 -> x0, matrix products: 18.3 us -> none  [the longest x1 5.62 us: on_device(): jnp.einsum('efs,efd->des', hidden, table_cols, preferred_element_type=jnp...]
    ppermute x0 -> x30, waiting for transfers between devices: none -> 13.2 us  [shift(): lax.ppermute(value, axis, [(i, (i + by) % size) for i in range(size)])]
    all_to_all x1 -> x2, starting transfers between devices: 4.8 us -> 14.4 us  [the longest x1 9.66 us: on_device(): gate_grad = gate_sum(lax.all_to_all(spread, ('x', 'z'), 0, 0, tiled=True))]
    all_to_all x1 -> x2, waiting for transfers between devices: 0.01 us -> 8.6 us  [the longest x1 6.24 us: on_device(): gate_grad = gate_sum(lax.all_to_all(spread, ('x', 'z'), 0, 0, tiled=True))]
  transfers between devices with their start and end apart: 2 -> 32, of which waited for: 1 -> 8; matrix products, arithmetic and copies ran while one was open for 2% -> 6% of each run, Pallas kernels for 0% -> 17%
where the time goes in v1:
time: 167 us; the launch traced here: 166 us
  starting transfers between devices  70.7 us (42%)
  Pallas kernels  44.2 us (26%)
  waiting for transfers between devices  21.8 us (13%)
  local copies, waits for them, and re-layouts  15.1 us (9%)
  blocking collectives  9.59 us (6%)
  other arithmetic  4.1 us (2%)
    ppermute x30, starting transfers between devices, shift(): lax.ppermute(value, axis, [(i, (i + by) % size) for i in range(size)])  56.3 us
    pallas_call x4, Pallas kernels, forward_block(): pl.pallas_call(body, grid_spec=pltpu.PrefetchScalarGridSpec(num_scalar_pr...  17.2 us
    unnamed x69, local copies, waits for them, and re-layouts  13.8 us
    ppermute x30, waiting for transfers between devices, shift(): lax.ppermute(value, axis, [(i, (i + by) % size) for i in range(size)])  13.2 us
    pallas_call x1, Pallas kernels, backward(): pl.pallas_call(backward_body, grid_spec=pltpu.PrefetchScalarGridSpec(num_...  11.4 us
    all_to_all x1, starting transfers between devices, on_device(): gate_grad = gate_sum(lax.all_to_all(spread, ('x', 'z'), 0, 0, tiled=True))  9.66 us
    all_to_all x1, blocking collectives, to_experts(): return lax.all_to_all(value, ('y', 'c'), 0, 0, tiled=True)  9.59 us
    all_to_all x1, waiting for transfers between devices, on_device(): gate_grad = gate_sum(lax.all_to_all(spread, ('x', 'z'), 0, 0, tiled=True))  6.24 us
  transfers between devices with their start and end apart: 32, of which 8 were waited for; matrix products, arithmetic and copies ran while one was open for 6% of the time, Pallas kernels for 17%

profile of v1, /device:TPU:8, one launch (start us, length us, event | category | flops | bytes accessed | tf_op | source)
XLA Modules:
  0.0 166.5 jit_solution(18382908275410608607)
XLA Ops:
  2.9 4.1 %forward_2.1 = (bf16[256,1024]{1,0:T(8,128)(2,1)}, bf16[256,1024]{1,0:T(8,128)(2,1)}) custom-call(s32[2]{0:T(128)} %pad_add_fusion.where_ref, bf16[448,1024]{1,0:T(8,128)(2,1)} %bitcast.18, s32[448,2048]{1,0:T(8,128)} %bitcast.13, f32[14,2048]{1,0:T(8,128)} %bitcast.23), custom_call_target="tpu_custom_call" | custom-call | tf_op jit(solution)/shard_map/forward_2/pallas_call | solution.py:84
  11.0 3.6 %slot_grads.1 = (s32[512,2]{1,0:T(8,128)}, bf16[8,64,128]{2,1,0:T(8,128)(2,1)}) custom-call(s32[512,2]{1,0:T(8,128)} %copy.11.index_ref, f32[512,2]{1,0:T(8,128)} %copy.12.gate_ref, bf16[512,64]{1,0:T(8,128)(2,1)} %copy.13.grad_ref), custom_call_target="tpu_custom_call" | custom-call | tf_op jit(solution)/shard_map/slot_grads/pallas_call | solution.py:63
  14.6 9.6 %all_to_all.15.rest_0_ = bf16[8,64,128]{2,1,0:T(8,128)(2,1)S(1)} all-to-all(bf16[8,64,128]{2,1,0:T(8,128)(2,1)} %get-tuple-element.47), channel_id=1, replica_groups=mesh['y'=4,'c'=2,'x'=4,'z'=8] {'y','c'}, dimensions={0} | all-to-all | bytes 262144 | tf_op jit(solution)/shard_map/all_to_all | solution.py:267
  24.2 2.7 %collective-permute-start.22 = (bf16[8,64,128]{2,1,0:T(8,128)(2,1)S(1)}, bf16[8,64,128]{2,1,0:T(8,128)(2,1)S(1)}, u32[]{:S(2)}, u32[]{:S(2)}) collective-permute-start(bf16[8,64,128]{2,1,0:T(8,128)(2,1)S(1)} %all_to_all.15.rest_0_), channel_id=1, source_target_pairs={{0,16},{8,24},{16,0},{24,8},{1,17},{9,25},{17,1},{25,9},{2,18},{10... | collective-permute-start | bytes 393224 | tf_op jit(solution)/shard_map/ppermute | solution.py:263
  27.4 2.8 %collective-permute-start.20 = (bf16[8,64,128]{2,1,0:T(8,128)(2,1)S(1)}, bf16[8,64,128]{2,1,0:T(8,128)(2,1)S(1)}, u32[]{:S(2)}, u32[]{:S(2)}) collective-permute-start(bf16[8,64,128]{2,1,0:T(8,128)(2,1)S(1)} %all_to_all.15.rest_0_), channel_id=1, source_target_pairs={{0,24},{8,0},{16,8},{24,16},{1,25},{9,1},{17,9},{25,17},{2,26},{10... | collective-permute-start | bytes 393224 | tf_op jit(solution)/shard_map/ppermute | solution.py:263
  30.4 4.3 %forward_3.1 = (bf16[256,1024]{1,0:T(8,128)(2,1)}, f32[256,1024]{1,0:T(8,128)}) custom-call(s32[2]{0:T(128)} %pad_add_fusion.where_ref, bf16[448,1024]{1,0:T(8,128)(2,1)} %bitcast.19, s32[448,2048]{1,0:T(8,128)} %bitcast.14, f32[14,2048]{1,0:T(8,128)} %bitcast.24), custom_call_target="tpu_custom_call" | custom-call | tf_op jit(solution)/shard_map/forward_3/pallas_call | solution.py:84
  34.7 4.4 %forward_1.1 = (f32[256,1024]{1,0:T(8,128)}, bf16[256,1024]{1,0:T(8,128)(2,1)}) custom-call(s32[2]{0:T(128)} %pad_add_fusion.where_ref, bf16[448,1024]{1,0:T(8,128)(2,1)} %bitcast.20, s32[448,2048]{1,0:T(8,128)} %bitcast.15, f32[14,2048]{1,0:T(8,128)} %bitcast.25), custom_call_target="tpu_custom_call" | custom-call | tf_op jit(solution)/shard_map/forward_1/pallas_call | solution.py:84
  41.2 5.9 %collective-permute-start.23 = (bf16[3,8,64,128]{3,2,1,0:T(8,128)(2,1)S(1)}, bf16[3,8,64,128]{3,2,1,0:T(8,128)(2,1)S(1)}, u32[]{:S(2)}, u32[]{:S(2)}) collective-permute-start(bf16[3,8,64,128]{3,2,1,0:T(8,128)(2,1)S(1)} %pad_maximum_fusion.rest_8_), channel_id=1, source_target_pairs={{0,7},{1,0},{2,1},{3,2},{4,3},{5,4},{6,5},{7,6},{8,15},{9,8},{10,9... | collective-permute-start | bytes 1179656 | tf_op jit(solution)/shard_map/ppermute | solution.py:263
  52.1 4.9 %collective-permute-done.top_a = bf16[256,1024]{1,0:T(8,128)(2,1)S(1)} collective-permute-done((bf16[256,1024]{1,0:T(8,128)(2,1)S(1)}, bf16[256,1024]{1,0:T(8,128)(2,1)S(1)}, u32[]{:S(2)}, u32[]{:S(2)}) %collective-permute-start) | collective-permute-done | bytes 524320 | tf_op jit(solution)/shard_map/ppermute | solution.py:263
  58.5 4.2 %collective-permute-start.24 = (bf16[3,8,64,128]{3,2,1,0:T(8,128)(2,1)S(1)}, bf16[3,8,64,128]{3,2,1,0:T(8,128)(2,1)S(1)}, u32[]{:S(2)}, u32[]{:S(2)}) collective-permute-start(bf16[3,8,64,128]{3,2,1,0:T(8,128)(2,1)S(1)} %collective-permute-done.23.rest_9_), channel_id=1, source_target_pairs={{0,7},{1,0},{2,1},{3,2},{4,3},{5,4},{6,5},{7,6},{8,15},{9,8},{10,9... | collective-permute-start | bytes 1179656 | tf_op jit(solution)/shard_map/ppermute | solution.py:263
  62.7 4.5 %forward_0.1 = (f32[256,1024]{1,0:T(8,128)}, f32[256,1024]{1,0:T(8,128)}) custom-call(s32[2]{0:T(128)} %pad_add_fusion.where_ref, bf16[448,1024]{1,0:T(8,128)(2,1)} %bitcast.21, s32[448,2048]{1,0:T(8,128)} %bitcast.16, f32[14,2048]{1,0:T(8,128)} %bitcast.26), custom_call_target="tpu_custom_call" | custom-call | tf_op jit(solution)/shard_map/forward_0/pallas_call | solution.py:84
  68.4 4.4 %x_sum.1 = (f32[64,1024]{1,0:T(8,128)}, bf16[64,1024]{1,0:T(8,128)(2,1)}, f32[64,1024]{1,0:T(8,128)}, bf16[64,1024]{1,0:T(8,128)(2,1)}, bf16[64,1024]{1,0:T(8,12...) custom-call(s32[2]{0:T(128)} %pad_add_fusion.where_ref, ...), custom_call_target="tpu_custom_call" | custom-call | tf_op jit(solution)/shard_map/x_sum/pallas_call | solution.py:118
  76.8 3.1 %collective-permute-start.16 = (bf16[8,64,128]{2,1,0:T(8,128)(2,1)S(1)}, bf16[8,64,128]{2,1,0:T(8,128)(2,1)S(1)}, u32[]{:S(2)}, u32[]{:S(2)}) collective-permute-start(bf16[8,64,128]{2,1,0:T(8,128)(2,1)S(1)} %all_to_all.15.rest_0_), channel_id=1, source_target_pairs={{0,1},{1,2},{2,3},{3,4},{4,5},{5,6},{6,7},{7,0},{8,9},{9,10},{10,1... | collective-permute-start | bytes 393224 | tf_op jit(solution)/shard_map/ppermute | solution.py:263
  91.3 2.5 %collective-permute-done.11 = bf16[64,1024]{1,0:T(8,128)(2,1)S(1)} collective-permute-done((bf16[64,1024]{1,0:T(8,128)(2,1)}, bf16[64,1024]{1,0:T(8,128)(2,1)S(1)}, u32[]{:S(2)}, u32[]{:S(2)}) %collective-permute-start.11) | collective-permute-done | bytes 131104 | tf_op jit(solution)/shard_map/ppermute | solution.py:263
  97.5 3.0 %collective-permute-start.12 = (bf16[64,1024]{1,0:T(8,128)(2,1)S(1)}, bf16[64,1024]{1,0:T(8,128)(2,1)S(1)}, u32[]{:S(2)}, u32[]{:S(2)}) collective-permute-start(bf16[64,1024]{1,0:T(8,128)(2,1)S(1)} %add_convert_fusion.2), channel_id=1, source_target_pairs={{0,6},{1,7},{2,0},{3,1},{4,2},{5,3},{6,4},{7,5},{8,14},{9,15},{10,... | collective-permute-start | bytes 393224 | tf_op jit(solution)/shard_map/ppermute | solution.py:263
  103.8 3.6 %collective-permute-start.29 = (bf16[3,8,64,128]{3,2,1,0:T(8,128)(2,1)S(1)}, bf16[3,8,64,128]{3,2,1,0:T(8,128)(2,1)S(1)}, u32[]{:S(2)}, u32[]{:S(2)}) collective-permute-start(bf16[3,8,64,128]{3,2,1,0:T(8,128)(2,1)S(1)} %collective-permute-done.28.rest_14_), channel_id=1, source_target_pairs={{0,1},{1,2},{2,3},{3,4},{4,5},{5,6},{6,7},{7,0},{8,9},{9,10},{10,1... | collective-permute-start | bytes 1179656 | tf_op jit(solution)/shard_map/ppermute | solution.py:263
  111.6 4.7 %all-to-all-start = ((bf16[8,64,128]{2,1,0:T(8,128)(2,1)}), bf16[8,64,128]{2,1,0:T(8,128)(2,1)S(1)}, u32[]{:S(2)}, u32[]{:S(2)}) async-start(bf16[8,64,128]{2,1,0:T(8,128)(2,1)} %z_sum.1), calls=%async_computation | async-start | bytes 262144 | tf_op jit(solution)/shard_map/all_to_all | solution.py:267
  116.4 2.2 %collective-permute-start.14 = (bf16[8,64,128]{2,1,0:T(8,128)(2,1)S(1)}, bf16[8,64,128]{2,1,0:T(8,128)(2,1)S(1)}, u32[]{:S(2)}, u32[]{:S(2)}) collective-permute-start(bf16[8,64,128]{2,1,0:T(8,128)(2,1)S(1)} %collective-permute-done.13.rest_1_), channel_id=1, source_target_pairs={{0,7},{1,0},{2,1},{3,2},{4,3},{5,4},{6,5},{7,6},{8,15},{9,8},{10,9... | collective-permute-start | bytes 393224 | tf_op jit(solution)/shard_map/ppermute | solution.py:263
  118.7 2.4 %all-to-all-done.back_ref = bf16[8,64,128]{2,1,0:T(8,128)(2,1)S(1)} async-done(((bf16[8,64,128]{2,1,0:T(8,128)(2,1)}), bf16[8,64,128]{2,1,0:T(8,128)(2,1)S(1)}, u32[]{:S(2)}, u32[]{:S(2)}) %all-to-all-start) | async-done | bytes 131104 | tf_op jit(solution)/shard_map/all_to_all | solution.py:267
  121.7 3.8 %combine.1 = (bf16[512,64]{1,0:T(8,128)(2,1)}, f32[8,128]{1,0:T(8,128)}) custom-call(s32[512,2]{1,0:T(8,128)} %get-tuple-element.28.place_ref, f32[512,2]{1,0:T(8,128)} %copy.12.gate_ref, bf16[512,64]{1,0:T(8,128)(2,1)} %copy.13.grad_ref, bf16[8,64,128]{2,1,0:T(8,128)(2,1)} %copy-done.8), custom_call_target="tpu_custom_call" | custom-call | tf_op jit(solution)/shard_map/combine/pallas_call | solution.py:166
  126.9 9.7 %all-to-all-start.1 = ((f32[32,8,128]{2,1,0:T(8,128)}), f32[32,8,128]{2,1,0:T(8,128)S(1)}, u32[]{:S(2)}, u32[]{:S(2)}) async-start(f32[32,8,128]{2,1,0:T(8,128)} %broadcast_in_dim.15), calls=%async_computation.1 | async-start | bytes 262144 | tf_op jit(solution)/shard_map/all_to_all | solution.py:312
  136.6 3.1 %collective-permute-start.15 = (bf16[8,64,128]{2,1,0:T(8,128)(2,1)S(1)}, bf16[8,64,128]{2,1,0:T(8,128)(2,1)S(1)}, u32[]{:S(2)}, u32[]{:S(2)}) collective-permute-start(bf16[8,64,128]{2,1,0:T(8,128)(2,1)S(1)} %collective-permute-done.14.rest_2_), channel_id=1, source_target_pairs={{0,7},{1,0},{2,1},{3,2},{4,3},{5,4},{6,5},{7,6},{8,15},{9,8},{10,9... | collective-permute-start | bytes 393224 | tf_op jit(solution)/shard_map/ppermute | solution.py:263
  141.4 6.2 %all-to-all-done.1.parts_ref = f32[32,8,128]{2,1,0:T(8,128)S(1)} async-done(((f32[32,8,128]{2,1,0:T(8,128)}), f32[32,8,128]{2,1,0:T(8,128)S(1)}, u32[]{:S(2)}, u32[]{:S(2)}) %all-to-all-start.1) | async-done | bytes 131104 | tf_op jit(solution)/shard_map/all_to_all | solution.py:312
  153.5 11.4 %backward.1 = (bf16[448,1024]{1,0:T(8,128)(2,1)}, f32[448,2048]{1,0:T(8,128)}, f32[14,2048]{1,0:T(8,128)}) custom-call(s32[2]{0:T(128)} %pad_add_fusion.where_ref, bf16[448,1024]{1,0:T(8,128)(2,1)} %bitcast.22, s32[448,2048]{1,0:T(8,128)} %bitcast.17, f32[14,2048]{1,0:T(8,128)} %bitcast.27, bf16[8,64,128]{2,1,0:T(8,128)(2,1)} %copy-done.2, ...), custom_call_target="tpu_custom_call" | custom-call | tf_op jit(solution)/shard_map/backward/pallas_call | solution.py:236
  (127 shorter events, 54.3 us)
Async XLA Ops:
  7.0 40.2 %collective-permute-start.1 = (bf16[256,1024]{1,0:T(8,128)(2,1)}, bf16[256,1024]{1,0:T(8,128)(2,1)S(1)}, u32[]{:S(2)}, u32[]{:S(2)}) collective-permute-start(bf16[256,1024]{1,0:T(8,128)(2,1)} %get-tuple-element.33), channel_id=1, source_target_pairs={{0,8},{8,16},{16,24},{24,0},{1,9},{9,17},{17,25},{25,1},{2,10},{10... | collective-permute-start | bytes 1572872 | tf_op jit(solution)/shard_map/ppermute | solution.py:263
  24.2 14.8 %collective-permute-start.22 = (bf16[8,64,128]{2,1,0:T(8,128)(2,1)S(1)}, bf16[8,64,128]{2,1,0:T(8,128)(2,1)S(1)}, u32[]{:S(2)}, u32[]{:S(2)}) collective-permute-start(bf16[8,64,128]{2,1,0:T(8,128)(2,1)S(1)} %all_to_all.15.rest_0_), channel_id=1, source_target_pairs={{0,16},{8,24},{16,0},{24,8},{1,17},{9,25},{17,1},{25,9},{2,18},{10... | collective-permute-start | bytes 393224 | tf_op jit(solution)/shard_map/ppermute | solution.py:263
  27.4 13.8 %collective-permute-start.20 = (bf16[8,64,128]{2,1,0:T(8,128)(2,1)S(1)}, bf16[8,64,128]{2,1,0:T(8,128)(2,1)S(1)}, u32[]{:S(2)}, u32[]{:S(2)}) collective-permute-start(bf16[8,64,128]{2,1,0:T(8,128)(2,1)S(1)} %all_to_all.15.rest_0_), channel_id=1, source_target_pairs={{0,24},{8,0},{16,8},{24,16},{1,25},{9,1},{17,9},{25,17},{2,26},{10... | collective-permute-start | bytes 393224 | tf_op jit(solution)/shard_map/ppermute | solution.py:263
  30.2 20.2 %collective-permute-start.4 = (bf16[256,1024]{1,0:T(8,128)(2,1)}, bf16[256,1024]{1,0:T(8,128)(2,1)S(1)}, u32[]{:S(2)}, u32[]{:S(2)}) collective-permute-start(bf16[256,1024]{1,0:T(8,128)(2,1)} %get-tuple-element.36), channel_id=1, source_target_pairs={{0,24},{8,0},{16,8},{24,16},{1,25},{9,1},{17,9},{25,17},{2,26},{10... | collective-permute-start | bytes 1572872 | tf_op jit(solution)/shard_map/ppermute | solution.py:263
  39.0 18.0 %collective-permute-start = (bf16[256,1024]{1,0:T(8,128)(2,1)S(1)}, bf16[256,1024]{1,0:T(8,128)(2,1)S(1)}, u32[]{:S(2)}, u32[]{:S(2)}) collective-permute-start(bf16[256,1024]{1,0:T(8,128)(2,1)S(1)} %copy-done.30), channel_id=1, source_target_pairs={{0,24},{8,0},{16,8},{24,16},{1,25},{9,1},{17,9},{25,17},{2,26},{10... | collective-permute-start | bytes 1572872 | tf_op jit(solution)/shard_map/ppermute | solution.py:263
  39.1 28.1 %collective-permute-start.3 = (bf16[256,1024]{1,0:T(8,128)(2,1)}, bf16[256,1024]{1,0:T(8,128)(2,1)S(1)}, u32[]{:S(2)}, u32[]{:S(2)}) collective-permute-start(bf16[256,1024]{1,0:T(8,128)(2,1)} %get-tuple-element.34), channel_id=1, source_target_pairs={{0,8},{8,16},{16,24},{24,0},{1,9},{9,17},{17,25},{25,1},{2,10},{10... | collective-permute-start | bytes 1572872 | tf_op jit(solution)/shard_map/ppermute | solution.py:263
  41.2 17.3 %collective-permute-start.23 = (bf16[3,8,64,128]{3,2,1,0:T(8,128)(2,1)S(1)}, bf16[3,8,64,128]{3,2,1,0:T(8,128)(2,1)S(1)}, u32[]{:S(2)}, u32[]{:S(2)}) collective-permute-start(bf16[3,8,64,128]{3,2,1,0:T(8,128)(2,1)S(1)} %pad_maximum_fusion.rest_8_), channel_id=1, source_target_pairs={{0,7},{1,0},{2,1},{3,2},{4,3},{5,4},{6,5},{7,6},{8,15},{9,8},{10,9... | collective-permute-start | bytes 1179656 | tf_op jit(solution)/shard_map/ppermute | solution.py:263
  48.5 18.7 %collective-permute-start.2 = (bf16[256,1024]{1,0:T(8,128)(2,1)S(1)}, bf16[256,1024]{1,0:T(8,128)(2,1)S(1)}, u32[]{:S(2)}, u32[]{:S(2)}) collective-permute-start(bf16[256,1024]{1,0:T(8,128)(2,1)S(1)} %add_convert_fusion.1), channel_id=1, source_target_pairs={{0,8},{8,16},{16,24},{24,0},{1,9},{9,17},{17,25},{25,1},{2,10},{10... | collective-permute-start | bytes 1572872 | tf_op jit(solution)/shard_map/ppermute | solution.py:263
  50.6 16.7 %collective-permute-start.5 = (bf16[256,1024]{1,0:T(8,128)(2,1)S(1)}, bf16[256,1024]{1,0:T(8,128)(2,1)S(1)}, u32[]{:S(2)}, u32[]{:S(2)}) collective-permute-start(bf16[256,1024]{1,0:T(8,128)(2,1)S(1)} %add_convert_fusion), channel_id=1, source_target_pairs={{0,24},{8,0},{16,8},{24,16},{1,25},{9,1},{17,9},{25,17},{2,26},{10... | collective-permute-start | bytes 1572872 | tf_op jit(solution)/shard_map/ppermute | solution.py:263
  57.0 22.9 %collective-permute-start.27 = (bf16[3,8,64,128]{3,2,1,0:T(8,128)(2,1)S(1)}, bf16[3,8,64,128]{3,2,1,0:T(8,128)(2,1)S(1)}, u32[]{:S(2)}, u32[]{:S(2)}) collective-permute-start(bf16[3,8,64,128]{3,2,1,0:T(8,128)(2,1)S(1)} %pad_maximum_fusion.rest_8_), channel_id=1, source_target_pairs={{0,1},{1,2},{2,3},{3,4},{4,5},{5,6},{6,7},{7,0},{8,9},{9,10},{10,1... | collective-permute-start | bytes 1179656 | tf_op jit(solution)/shard_map/ppermute | solution.py:263
  58.5 22.4 %collective-permute-start.24 = (bf16[3,8,64,128]{3,2,1,0:T(8,128)(2,1)S(1)}, bf16[3,8,64,128]{3,2,1,0:T(8,128)(2,1)S(1)}, u32[]{:S(2)}, u32[]{:S(2)}) collective-permute-start(bf16[3,8,64,128]{3,2,1,0:T(8,128)(2,1)S(1)} %collective-permute-done.23.rest_9_), channel_id=1, source_target_pairs={{0,7},{1,0},{2,1},{3,2},{4,3},{5,4},{6,5},{7,6},{8,15},{9,8},{10,9... | collective-permute-start | bytes 1179656 | tf_op jit(solution)/shard_map/ppermute | solution.py:263
  76.8 12.7 %collective-permute-start.16 = (bf16[8,64,128]{2,1,0:T(8,128)(2,1)S(1)}, bf16[8,64,128]{2,1,0:T(8,128)(2,1)S(1)}, u32[]{:S(2)}, u32[]{:S(2)}) collective-permute-start(bf16[8,64,128]{2,1,0:T(8,128)(2,1)S(1)} %all_to_all.15.rest_0_), channel_id=1, source_target_pairs={{0,1},{1,2},{2,3},{3,4},{4,5},{5,6},{6,7},{7,0},{8,9},{9,10},{10,1... | collective-permute-start | bytes 393224 | tf_op jit(solution)/shard_map/ppermute | solution.py:263
  79.9 17.6 %collective-permute-start.28 = (bf16[3,8,64,128]{3,2,1,0:T(8,128)(2,1)S(1)}, bf16[3,8,64,128]{3,2,1,0:T(8,128)(2,1)S(1)}, u32[]{:S(2)}, u32[]{:S(2)}) collective-permute-start(bf16[3,8,64,128]{3,2,1,0:T(8,128)(2,1)S(1)} %collective-permute-done.27.rest_15_), channel_id=1, source_target_pairs={{0,1},{1,2},{2,3},{3,4},{4,5},{5,6},{6,7},{7,0},{8,9},{9,10},{10,1... | collective-permute-start | bytes 1179656 | tf_op jit(solution)/shard_map/ppermute | solution.py:263
  81.0 26.5 %collective-permute-start.25 = (bf16[3,8,64,128]{3,2,1,0:T(8,128)(2,1)S(1)}, bf16[3,8,64,128]{3,2,1,0:T(8,128)(2,1)S(1)}, u32[]{:S(2)}, u32[]{:S(2)}) collective-permute-start(bf16[3,8,64,128]{3,2,1,0:T(8,128)(2,1)S(1)} %collective-permute-done.24.rest_10_), channel_id=1, source_target_pairs={{0,7},{1,0},{2,1},{3,2},{4,3},{5,4},{6,5},{7,6},{8,15},{9,8},{10,9... | collective-permute-start | bytes 1179656 | tf_op jit(solution)/shard_map/ppermute | solution.py:263
  84.9 16.9 %collective-permute-start.6 = (bf16[64,1024]{1,0:T(8,128)(2,1)}, bf16[64,1024]{1,0:T(8,128)(2,1)S(1)}, u32[]{:S(2)}, u32[]{:S(2)}) collective-permute-start(bf16[64,1024]{1,0:T(8,128)(2,1)} %get-tuple-element.38), channel_id=1, source_target_pairs={{0,1},{1,2},{2,3},{3,4},{4,5},{5,6},{6,7},{7,0},{8,9},{9,10},{10,1... | collective-permute-start | bytes 393224 | tf_op jit(solution)/shard_map/ppermute | solution.py:263
  89.5 13.0 %collective-permute-start.10 = (bf16[64,1024]{1,0:T(8,128)(2,1)}, bf16[64,1024]{1,0:T(8,128)(2,1)S(1)}, u32[]{:S(2)}, u32[]{:S(2)}) collective-permute-start(bf16[64,1024]{1,0:T(8,128)(2,1)} %get-tuple-element.42), channel_id=1, source_target_pairs={{0,7},{1,0},{2,1},{3,2},{4,3},{5,4},{6,5},{7,6},{8,15},{9,8},{10,9... | collective-permute-start | bytes 393224 | tf_op jit(solution)/shard_map/ppermute | solution.py:263
  101.8 14.6 %collective-permute-start.13 = (bf16[8,64,128]{2,1,0:T(8,128)(2,1)S(1)}, bf16[8,64,128]{2,1,0:T(8,128)(2,1)S(1)}, u32[]{:S(2)}, u32[]{:S(2)}) collective-permute-start(bf16[8,64,128]{2,1,0:T(8,128)(2,1)S(1)} %all_to_all.15.rest_0_), channel_id=1, source_target_pairs={{0,7},{1,0},{2,1},{3,2},{4,3},{5,4},{6,5},{7,6},{8,15},{9,8},{10,9... | collective-permute-start | bytes 393224 | tf_op jit(solution)/shard_map/ppermute | solution.py:263
  102.5 16.1 %collective-permute-start.17 = (bf16[8,64,128]{2,1,0:T(8,128)(2,1)S(1)}, bf16[8,64,128]{2,1,0:T(8,128)(2,1)S(1)}, u32[]{:S(2)}, u32[]{:S(2)}) collective-permute-start(bf16[8,64,128]{2,1,0:T(8,128)(2,1)S(1)} %collective-permute-done.16.rest_7_), channel_id=1, source_target_pairs={{0,1},{1,2},{2,3},{3,4},{4,5},{5,6},{6,7},{7,0},{8,9},{9,10},{10,1... | collective-permute-start | bytes 393224 | tf_op jit(solution)/shard_map/ppermute | solution.py:263
  103.8 48.0 %collective-permute-start.29 = (bf16[3,8,64,128]{3,2,1,0:T(8,128)(2,1)S(1)}, bf16[3,8,64,128]{3,2,1,0:T(8,128)(2,1)S(1)}, u32[]{:S(2)}, u32[]{:S(2)}) collective-permute-start(bf16[3,8,64,128]{3,2,1,0:T(8,128)(2,1)S(1)} %collective-permute-done.28.rest_14_), channel_id=1, source_target_pairs={{0,1},{1,2},{2,3},{3,4},{4,5},{5,6},{6,7},{7,0},{8,9},{9,10},{10,1... | collective-permute-start | bytes 1179656 | tf_op jit(solution)/shard_map/ppermute | solution.py:263
  107.4 44.4 %collective-permute-start.26 = (bf16[3,8,64,128]{3,2,1,0:T(8,128)(2,1)S(1)}, bf16[3,8,64,128]{3,2,1,0:T(8,128)(2,1)S(1)}, u32[]{:S(2)}, u32[]{:S(2)}) collective-permute-start(bf16[3,8,64,128]{3,2,1,0:T(8,128)(2,1)S(1)} %collective-permute-done.25.rest_11_), channel_id=1, source_target_pairs={{0,7},{1,0},{2,1},{3,2},{4,3},{5,4},{6,5},{7,6},{8,15},{9,8},{10,9... | collective-permute-start | bytes 1179656 | tf_op jit(solution)/shard_map/ppermute | solution.py:263
  116.4 20.2 %collective-permute-start.14 = (bf16[8,64,128]{2,1,0:T(8,128)(2,1)S(1)}, bf16[8,64,128]{2,1,0:T(8,128)(2,1)S(1)}, u32[]{:S(2)}, u32[]{:S(2)}) collective-permute-start(bf16[8,64,128]{2,1,0:T(8,128)(2,1)S(1)} %collective-permute-done.13.rest_1_), channel_id=1, source_target_pairs={{0,7},{1,0},{2,1},{3,2},{4,3},{5,4},{6,5},{7,6},{8,15},{9,8},{10,9... | collective-permute-start | bytes 393224 | tf_op jit(solution)/shard_map/ppermute | solution.py:263
  118.6 21.1 %collective-permute-start.18 = (bf16[8,64,128]{2,1,0:T(8,128)(2,1)S(1)}, bf16[8,64,128]{2,1,0:T(8,128)(2,1)S(1)}, u32[]{:S(2)}, u32[]{:S(2)}) collective-permute-start(bf16[8,64,128]{2,1,0:T(8,128)(2,1)S(1)} %collective-permute-done.17.rest_6_), channel_id=1, source_target_pairs={{0,1},{1,2},{2,3},{3,4},{4,5},{5,6},{6,7},{7,0},{8,9},{9,10},{10,1... | collective-permute-start | bytes 393224 | tf_op jit(solution)/shard_map/ppermute | solution.py:263
  126.9 20.7 %all-to-all-start.1 = ((f32[32,8,128]{2,1,0:T(8,128)}), f32[32,8,128]{2,1,0:T(8,128)S(1)}, u32[]{:S(2)}, u32[]{:S(2)}) async-start(f32[32,8,128]{2,1,0:T(8,128)} %broadcast_in_dim.15), calls=%async_computation.1 | async-start | bytes 262144 | tf_op jit(solution)/shard_map/all_to_all | solution.py:312
  136.6 15.2 %collective-permute-start.15 = (bf16[8,64,128]{2,1,0:T(8,128)(2,1)S(1)}, bf16[8,64,128]{2,1,0:T(8,128)(2,1)S(1)}, u32[]{:S(2)}, u32[]{:S(2)}) collective-permute-start(bf16[8,64,128]{2,1,0:T(8,128)(2,1)S(1)} %collective-permute-done.14.rest_2_), channel_id=1, source_target_pairs={{0,7},{1,0},{2,1},{3,2},{4,3},{5,4},{6,5},{7,6},{8,15},{9,8},{10,9... | collective-permute-start | bytes 393224 | tf_op jit(solution)/shard_map/ppermute | solution.py:263
  (39 other events, 688.1 us)

commit v2 on v1

v2 whole, which is shorter than its diff:
```python
import jax
import jax.numpy as jnp
from jax import lax
from jax.experimental import pallas as pl
from jax.experimental.pallas import tpu as pltpu
from jax.sharding import Mesh, PartitionSpec as P

EXPERTS = 8
GROUP = 32
CAP = 128
NY, NC, NX, NZ = 4, 2, 4, 8
COLS = 64
SLOTS = EXPERTS * CAP
BLOCK = NZ * COLS
PARAMS = pltpu.CompilerParams(vmem_limit_bytes=56 * 1024 * 1024)
F32, BF16, I32 = jnp.float32, jnp.bfloat16, jnp.int32


def sds(shape, dtype):
    return jax.ShapeDtypeStruct(shape, dtype)


def whole(shape):
    return pl.BlockSpec(shape, lambda *_: (0,) * len(shape))


def dequant(codes, scales):
    rows, width = codes.shape
    grouped = codes.astype(F32).reshape(rows // GROUP, GROUP, width)
    return (grouped * scales[:, None, :]).reshape(rows, width).astype(BF16)


def picker(place_ref, k):
    slots = lax.broadcasted_iota(I32, (SLOTS, place_ref.shape[1]), 0)
    return (place_ref[k : k + 1, :] == slots).astype(BF16)


def slot_body(index_ref, gate_ref, grad_ref, place_ref, out_ref):
    tokens = index_ref.shape[1]
    experts = lax.broadcasted_iota(I32, (EXPERTS, tokens), 0)
    hot = [(index_ref[k : k + 1, :] == experts).astype(F32) for k in range(2)]
    row = lax.broadcasted_iota(I32, (tokens, tokens), 0)
    col = lax.broadcasted_iota(I32, (tokens, tokens), 1)
    before = (row < col).astype(BF16)
    counts = jnp.dot((hot[0] + hot[1]).astype(BF16), before, preferred_element_type=F32)
    for k in range(2):
        rank = jnp.sum(counts * hot[k], axis=0, keepdims=True).astype(I32)
        place_ref[k : k + 1, :] = jnp.where(rank < CAP, index_ref[k : k + 1, :] * CAP + rank, -1)
    grad = grad_ref[...].astype(F32)
    total = None
    for k in range(2):
        value = (gate_ref[k : k + 1, :] * grad).astype(BF16)
        piece = lax.dot_general(
            value, picker(place_ref, k), (((1,), (1,)), ((), ())), preferred_element_type=F32
        )
        total = piece if total is None else total + piece
    total = total.astype(BF16)
    for e in range(EXPERTS):
        for x in range(NX):
            out_ref[e * NX + x] = total[:, e * CAP : (e + 1) * CAP]


def slot_grads(index, gate, grad):
    return pl.pallas_call(
        slot_body,
        out_shape=(sds(index.shape, I32), sds((EXPERTS * NX, COLS, CAP), BF16)),
        compiler_params=PARAMS,
        name="slot_grads",
    )(index, gate, grad)


def forward_body(where_ref, hidden_ref, codes_ref, scales_ref, out_ref):
    table = dequant(codes_ref[...], scales_ref[...])
    value = lax.dot_general(table, hidden_ref[...], (((0,), (0,)), ((), ())), preferred_element_type=F32)
    out_ref[0] = value.astype(out_ref.dtype)


def forward(where, hidden, codes, scales, far):
    units, slots = hidden.shape
    count = 1 if far else 3
    half = BLOCK // 2

    def block(n, w):
        away = 2 if far else lax.rem(2 * (n // 2) + 1, 5)
        return (0, lax.rem(w[0] + away, NX) * 2 + lax.rem(n, 2))

    return pl.pallas_call(
        forward_body,
        grid_spec=pltpu.PrefetchScalarGridSpec(
            num_scalar_prefetch=1,
            grid=(count * 2,),
            in_specs=[
                pl.BlockSpec((units, slots), lambda n, w: (0, 0)),
                pl.BlockSpec((units, half), block),
                pl.BlockSpec((units // GROUP, half), block),
            ],
            out_specs=pl.BlockSpec((1, half, slots), lambda n, w: (n, 0, 0)),
        ),
        out_shape=sds((count * 2, half, slots), BF16 if far else F32),
        compiler_params=PARAMS,
        name="forward_far" if far else "forward_near",
    )(where, hidden, codes, scales)


def join_body(near_ref, top_ref, bottom_ref, up_ref, down_ref):
    half = BLOCK // 2
    up_ref[:half] = (near_ref[0] + top_ref[...].astype(F32)).astype(BF16)
    up_ref[half:] = near_ref[1].astype(BF16)
    down_ref[:half] = near_ref[2].astype(BF16)
    down_ref[half:] = (near_ref[3] + bottom_ref[...].astype(F32)).astype(BF16)


def join(near, top, bottom):
    half, slots = top.shape
    return pl.pallas_call(
        join_body,
        grid=(1,),
        in_specs=[pl.BlockSpec((4, half, slots), lambda n: (0, 0, 0)), whole(top.shape), whole(top.shape)],
        out_specs=[whole((2 * half, slots))] * 2,
        out_shape=[sds((2 * half, slots), BF16)] * 2,
        compiler_params=PARAMS,
        name="join",
    )(near, top, bottom)


def x_sum_body(near_ref, up_ref, down_ref, out_ref):
    half = BLOCK // 2
    for z in range(NZ):
        rows = slice(z * COLS, (z + 1) * COLS)
        h, r = divmod(z * COLS, half)
        total = near_ref[h, r : r + COLS, :] + up_ref[rows, :].astype(F32) + down_ref[rows, :].astype(F32)
        total = total.astype(BF16)
        for g in range(EXPERTS):
            out_ref[z * EXPERTS + g] = total[:, g * CAP : (g + 1) * CAP]


def x_sum(near, up, down):
    rows, slots = up.shape
    return pl.pallas_call(
        x_sum_body,
        grid=(1,),
        in_specs=[pl.BlockSpec((2, rows // 2, slots), lambda n: (2, 0, 0)), whole(up.shape), whole(up.shape)],
        out_specs=whole((NZ * EXPERTS, COLS, CAP)),
        out_shape=sds((NZ * EXPERTS, COLS, CAP), BF16),
        compiler_params=PARAMS,
        name="x_sum",
    )(near, up, down)


def combine_body(place_ref, gate_ref, grad_ref, back_ref, out_ref, spread_ref):
    sums = []
    for e in range(EXPERTS):
        total = back_ref[e].astype(F32)
        for z in range(1, NZ):
            total = total + back_ref[z * EXPERTS + e].astype(F32)
        sums.append(total.astype(BF16))
    back = jnp.concatenate(sums, axis=1)
    grad = grad_ref[...].astype(F32)
    total = None
    for k in range(2):
        got = jnp.dot(back, picker(place_ref, k), preferred_element_type=F32)
        piece = gate_ref[k : k + 1, :] * got
        total = piece if total is None else total + piece
        part = jnp.sum(grad * got, axis=0, keepdims=True)
        for j in range(4):
            line = part[:, j * 128 : (j + 1) * 128]
            spread_ref[:, k * 4 + j : k * 4 + j + 1, :] = jnp.broadcast_to(line[None], (NX * NZ, 1, 128))
    out_ref[...] = total.astype(BF16)


def combine(place, gate, grad, back):
    return pl.pallas_call(
        combine_body,
        out_shape=(sds(grad.shape, BF16), sds((NX * NZ, 8, 128), F32)),
        compiler_params=PARAMS,
        name="combine",
    )(place, gate, grad, back)


def gate_sum_body(parts_ref, out_ref):
    total = jnp.sum(parts_ref[...], axis=0)
    for k in range(2):
        for j in range(4):
            out_ref[k : k + 1, j * 128 : (j + 1) * 128] = total[k * 4 + j : k * 4 + j + 1, :]


def gate_sum(parts):
    return pl.pallas_call(
        gate_sum_body, out_shape=sds((2, 512), F32), compiler_params=PARAMS, name="gate_sum"
    )(parts)


def backward_body(hidden_ref, codes_ref, scales_ref, grads_ref, hidden_out, weight_out, scale_out, acc):
    step = pl.program_id(0)
    width = codes_ref.shape[1]
    block = jnp.concatenate(
        [jnp.concatenate([grads_ref[z, g, 0] for g in range(EXPERTS)], axis=1) for z in range(NZ)], axis=0
    )
    codes = codes_ref[...]
    part = jnp.dot(dequant(codes, scales_ref[...]), block, preferred_element_type=F32)

    @pl.when(step == 0)
    def _():
        acc[...] = part

    @pl.when(jnp.logical_and(step > 0, step < NX - 1))
    def _():
        acc[...] = acc[...] + part

    @pl.when(step == NX - 1)
    def _():
        hidden_out[...] = (acc[...] + part).astype(BF16)

    weight = lax.dot_general(hidden_ref[...], block, (((1,), (1,)), ((), ())), preferred_element_type=F32)
    weight_out[...] = weight
    products = weight * codes.astype(F32)
    scale_out[...] = jnp.sum(products.reshape(-1, GROUP, width), axis=1)


def backward(hidden, codes, scales, grads):
    units, slots = hidden.shape
    features = codes.shape[1]
    groups = units // GROUP
    return pl.pallas_call(
        backward_body,
        grid=(NX,),
        in_specs=[
            whole((units, slots)),
            pl.BlockSpec((units, BLOCK), lambda n: (0, n)),
            pl.BlockSpec((groups, BLOCK), lambda n: (0, n)),
            pl.BlockSpec((NZ, EXPERTS, 1, COLS, CAP), lambda n: (0, 0, n, 0, 0)),
        ],
        out_specs=[
            whole((units, slots)),
            pl.BlockSpec((units, BLOCK), lambda n: (0, n)),
            pl.BlockSpec((groups, BLOCK), lambda n: (0, n)),
        ],
        out_shape=[sds((units, slots), BF16), sds((units, features), F32), sds((groups, features), F32)],
        scratch_shapes=[pltpu.VMEM((units, slots), F32)],
        compiler_params=PARAMS,
        name="backward",
    )(hidden, codes, scales, grads)


def shift(value, axis, by):
    size = NX if axis == "x" else NZ
    return lax.ppermute(value, axis, [(i, (i + by) % size) for i in range(size)])


def on_device(hidden, weight_codes, group_scales, expert_index, gate_values, output_grad):
    hidden, codes, scales = hidden[0], weight_codes[0], group_scales[0]
    index, gate, grad = expert_index.T, gate_values.T, output_grad.T
    where = lax.axis_index("x").astype(I32).reshape(1)

    far = forward(where, hidden, codes, scales, True)
    far_top = shift(far[0], "x", 1)
    far_bottom = shift(far[1], "x", -1)

    place, outbound = slot_grads(index, gate, grad)
    shard = lax.all_to_all(outbound, ("y", "c", "x"), 0, 0, tiled=True)
    gathered = lax.all_gather(shard.reshape(EXPERTS * NX * COLS, CAP), "z", axis=0, tiled=True)

    near = forward(where, hidden, codes, scales, False)
    up, down = join(near, far_top, far_bottom)
    up = shift(up, "x", 1)
    down = shift(down, "x", -1)

    returned = lax.all_to_all(x_sum(near, up, down), ("z", "y", "c"), 0, 0, tiled=True)
    combined, spread = combine(place, gate, grad, returned)
    gate_grad = gate_sum(lax.all_to_all(spread, ("x", "z"), 0, 0, tiled=True))

    grads = gathered.reshape(NZ, EXPERTS, NX, COLS, CAP)
    hidden_grad, weight_grad, scale_grad = backward(hidden, codes, scales, grads)
    return combined.T, gate_grad.T, hidden_grad[None], weight_grad[None], scale_grad[None]


def solution(mesh):
    fine = Mesh(mesh.devices.reshape(NY, NC, NX, NZ), ("y", "c", "x", "z"))
    expert, dp = ("y", "c"), ("x", "z")
    return jax.shard_map(
        on_device,
        mesh=fine,
        in_specs=(
            P(expert, dp, None),
            P(expert, dp, None),
            P(expert, dp, None),
            P(expert, None),
            P(expert, None),
            P(expert, dp),
        ),
        out_specs=(
            P(expert, dp),
            P(expert, None),
            P(expert, dp, None),
            P(expert, dp, None),
            P(expert, dp, None),
        ),
        check_vma=False,
    )
```

time: 167 us -> 165 us (0.988)
  blocking collectives: 9.59 us -> 74.1 us
  starting transfers between devices: 70.7 us -> 6.58 us
  between operations: 0.97 us -> 14.1 us
  Pallas kernels: 44.2 us -> 33.7 us
  local copies, waits for them, and re-layouts: 15.1 us -> 8.08 us
  waiting for transfers between devices: 21.8 us -> 26.9 us
  other arithmetic: 4.1 us -> 0 us
    all_to_all x1 -> x3, blocking collectives: 9.59 us -> 74.1 us  [the longest x1 40.6 us: on_device(): lax.all_to_all(x_sum(near, up, down), ('z', 'y', 'c'), 0, 0, tiled=True)]
    ppermute x30 -> x4, starting transfers between devices: 56.3 us -> 6.54 us  [shift(): lax.ppermute(value, axis, [(i, (i + by) % size) for i in range(size)])]
    all_to_all x2 -> x0, starting transfers between devices: 14.4 us -> none  [the longest x1 9.66 us: on_device(): gate_grad = gate_sum(lax.all_to_all(spread, ('x', 'z'), 0, 0, tiled=True))]
    ppermute x30 -> x4, waiting for transfers between devices: 13.2 us -> 26.9 us  [shift(): lax.ppermute(value, axis, [(i, (i + by) % size) for i in range(size)])]
    pallas_call x10 -> x8, Pallas kernels: 44.2 us -> 33.7 us  [the longest x2 10.3 us: forward(): pl.pallas_call(forward_body, grid_spec=pltpu.PrefetchScalarGridSpec(num_s...]
    all_to_all x2 -> x0, waiting for transfers between devices: 8.6 us -> none  [the longest x1 6.24 us: on_device(): gate_grad = gate_sum(lax.all_to_all(spread, ('x', 'z'), 0, 0, tiled=True))]
    unnamed x69 -> x10, local copies, waits for them, and re-layouts: 13.8 us -> 6.81 us
    convert_element_type x4 -> x0, other arithmetic: 3.47 us -> none  [the longest x1 1.37 us: on_device(): top_b = shift((up_top + far_top.astype(F32)).astype(BF16), 'x', 1)]
  transfers between devices with their start and end apart: 32 -> 5, of which waited for: 8 -> 2; matrix products, arithmetic and copies ran while one was open for 6% -> 2% of each run, Pallas kernels for 17% -> 13%
where the time goes in v2:
time: 165 us; the launch traced here: 163 us
  blocking collectives  74.1 us (45%)
  Pallas kernels  33.7 us (20%)
  waiting for transfers between devices  26.9 us (16%)
  between operations  14.1 us (9%)
  local copies, waits for them, and re-layouts  8.08 us (5%)
  starting transfers between devices  6.58 us (4%)
    all_to_all x1, blocking collectives, on_device(): lax.all_to_all(x_sum(near, up, down), ('z', 'y', 'c'), 0, 0, tiled=True)  40.6 us
    ppermute x4, waiting for transfers between devices, shift(): lax.ppermute(value, axis, [(i, (i + by) % size) for i in range(size)])  26.9 us
    all_to_all x1, blocking collectives, on_device(): shard = lax.all_to_all(outbound, ('y', 'c', 'x'), 0, 0, tiled=True)  18.3 us
    all_to_all x1, blocking collectives, on_device(): gate_grad = gate_sum(lax.all_to_all(spread, ('x', 'z'), 0, 0, tiled=True))  15.2 us
    pallas_call x2, Pallas kernels, forward(): pl.pallas_call(forward_body, grid_spec=pltpu.PrefetchScalarGridSpec(num_s...  10.3 us
    pallas_call x1, Pallas kernels, backward(): pl.pallas_call(backward_body, grid=(NX,), in_specs=[whole((units, slots))...  9.14 us
    unnamed x10, local copies, waits for them, and re-layouts  6.81 us
    ppermute x4, starting transfers between devices, shift(): lax.ppermute(value, axis, [(i, (i + by) % size) for i in range(size)])  6.54 us
  transfers between devices with their start and end apart: 5, of which 2 were waited for; matrix products, arithmetic and copies ran while one was open for 2% of the time, Pallas kernels for 13%

profile of v2, /device:TPU:8, one launch (start us, length us, event | category | flops | bytes accessed | tf_op | source)
XLA Modules:
  0.0 163.4 jit_solution(16856605942246188229)
XLA Ops:
  7.2 0.0 all-gather.2.cloned.1.call-start
  7.2 2.7 %slot_grads.1 = (s32[2,512]{1,0:T(2,128)}, bf16[32,64,128]{2,1,0:T(8,128)(2,1)}) custom-call(s32[2,512]{1,0:T(2,128)} %bitcast.36, f32[2,512]{1,0:T(2,128)} %bitcast.34, bf16[64,512]{1,0:T(8,128)(2,1)} %bitcast.31), custom_call_target="tpu_custom_call" | custom-call | tf_op jit(solution)/shard_map/slot_grads/pallas_call | solution.py:64
  9.9 18.3 %all_to_all.15 = bf16[32,64,128]{2,1,0:T(8,128)(2,1)} all-to-all(bf16[32,64,128]{2,1,0:T(8,128)(2,1)} %get-tuple-element.19), channel_id=1, replica_groups=mesh['y'=4,'c'=2,'x'=4,'z'=8] {'y','c','x'}, dimensions={0} | all-to-all | bytes 1048576 | tf_op jit(solution)/shard_map/all_to_all | solution.py:260
  28.2 1.6 copy.14
  29.7 3.1 %forward_far.1 = bf16[2,256,1024]{2,1,0:T(8,128)(2,1)} custom-call(s32[1]{0:T(128)} %bitcast.3.where_ref, bf16[448,1024]{1,0:T(8,128)(2,1)} %bitcast.23, s32[448,2048]{1,0:T(8,128)} %bitcast.20, f32[14,2048]{1,0:T(8,128)} %bitcast.27), custom_call_target="tpu_custom_call" | custom-call | tf_op jit(solution)/shard_map/forward_far/pallas_call | solution.py:87
  32.9 1.3 slice_bitcast_fusion
  34.1 0.1 collective-permute-start
  34.2 3.2 %collective-permute-start.1 = (bf16[256,1024]{1,0:T(8,128)(2,1)S(1)}, bf16[256,1024]{1,0:T(8,128)(2,1)S(1)}, u32[]{:S(2)}, u32[]{:S(2)}) collective-permute-start(bf16[256,1024]{1,0:T(8,128)(2,1)S(1)} %get-tuple-element.28), channel_id=1, source_target_pairs={{0,24},{8,0},{16,8},{24,16},{1,25},{9,1},{17,9},{25,17},{2,26},{10... | collective-permute-start | bytes 1572872 | tf_op jit(solution)/shard_map/ppermute | solution.py:247
  37.5 7.2 %forward_near.1.near_ref = f32[6,256,1024]{2,1,0:T(8,128)} custom-call(s32[1]{0:T(128)} %bitcast.3.where_ref, bf16[448,1024]{1,0:T(8,128)(2,1)} %bitcast.24, s32[448,2048]{1,0:T(8,128)} %bitcast.21, f32[14,2048]{1,0:T(8,128)} %bitcast.28), custom_call_target="tpu_custom_call" | custom-call | tf_op jit(solution)/shard_map/forward_near/pallas_call | solution.py:87
  44.7 4.5 %collective-permute-done.top_ref = bf16[256,1024]{1,0:T(8,128)(2,1)S(1)} collective-permute-done((bf16[256,1024]{1,0:T(8,128)(2,1)S(1)}, bf16[256,1024]{1,0:T(8,128)(2,1)S(1)}, u32[]{:S(2)}, u32[]{:S(2)}) %collective-permute-start) | collective-permute-done | bytes 524320 | tf_op jit(solution)/shard_map/ppermute | solution.py:247
  49.2 0.8 copy-done.2
  50.0 0.8 copy-done.3
  50.8 4.0 %join.1 = (bf16[512,1024]{1,0:T(8,128)(2,1)}, bf16[512,1024]{1,0:T(8,128)(2,1)}) custom-call(f32[6,256,1024]{2,1,0:T(8,128)} %forward_near.1.near_ref, bf16[256,1024]{1,0:T(8,128)(2,1)} %copy-done.2, bf16[256,1024]{1,0:T(8,128)(2,1)} %copy-done.3), custom_call_target="tpu_custom_call" | custom-call | tf_op jit(solution)/shard_map/join/pallas_call | solution.py:115
  54.7 3.2 %collective-permute-start.3 = (bf16[512,1024]{1,0:T(8,128)(2,1)}, bf16[512,1024]{1,0:T(8,128)(2,1)S(1)}, u32[]{:S(2)}, u32[]{:S(2)}) collective-permute-start(bf16[512,1024]{1,0:T(8,128)(2,1)} %get-tuple-element.16), channel_id=1, source_target_pairs={{0,24},{8,0},{16,8},{24,16},{1,25},{9,1},{17,9},{25,17},{2,26},{10... | collective-permute-start | bytes 3145736 | tf_op jit(solution)/shard_map/ppermute | solution.py:247
  58.0 22.4 %collective-permute-done.2.up_ref = bf16[512,1024]{1,0:T(8,128)(2,1)S(1)} collective-permute-done((bf16[512,1024]{1,0:T(8,128)(2,1)}, bf16[512,1024]{1,0:T(8,128)(2,1)S(1)}, u32[]{:S(2)}, u32[]{:S(2)}) %collective-permute-start.2) | collective-permute-done | bytes 1048608 | tf_op jit(solution)/shard_map/ppermute | solution.py:247
  80.4 1.0 copy-done
  81.3 1.0 copy-done.1
  82.3 3.5 %x_sum.1 = bf16[64,64,128]{2,1,0:T(8,128)(2,1)} custom-call(f32[6,256,1024]{2,1,0:T(8,128)} %forward_near.1.near_ref, bf16[512,1024]{1,0:T(8,128)(2,1)} %copy-done, bf16[512,1024]{1,0:T(8,128)(2,1)} %copy-done.1), custom_call_target="tpu_custom_call" | custom-call | tf_op jit(solution)/shard_map/x_sum/pallas_call | solution.py:139
  85.8 40.6 %all_to_all.16.back_ref = bf16[64,64,128]{2,1,0:T(8,128)(2,1)} all-to-all(bf16[64,64,128]{2,1,0:T(8,128)(2,1)} %x_sum.1), channel_id=1, replica_groups=mesh['y'=4,'c'=2,'x'=4,'z'=8] {'z','y','c'}, dimensions={0} | all-to-all | bytes 2097152 | tf_op jit(solution)/shard_map/all_to_all | solution.py:268
  126.4 2.6 %combine.1 = (bf16[64,512]{1,0:T(8,128)(2,1)}, f32[32,8,128]{2,1,0:T(8,128)}) custom-call(s32[2,512]{1,0:T(2,128)} %get-tuple-element.14.place_ref, f32[2,512]{1,0:T(2,128)} %bitcast.35, bf16[64,512]{1,0:T(8,128)(2,1)} %bitcast.32, bf16[64,64,128]{2,1,0:T(8,128)(2,1)} %all_to_all.16.back_ref), custom_call_target="tpu_custom_call" | custom-call | tf_op jit(solution)/shard_map/combine/pallas_call | solution.py:172
  129.0 15.2 %all_to_all.17.parts_ref = f32[32,8,128]{2,1,0:T(8,128)} all-to-all(f32[32,8,128]{2,1,0:T(8,128)} %get-tuple-element.18), channel_id=1, replica_groups=mesh['y'=4,'c'=2,'x'=4,'z'=8] {'x','z'}, dimensions={0} | all-to-all | bytes 262144 | tf_op jit(solution)/shard_map/all_to_all | solution.py:270
  144.2 1.5 gate_sum.1
  145.8 9.1 %backward.1 = (bf16[448,1024]{1,0:T(8,128)(2,1)}, f32[448,2048]{1,0:T(8,128)}, f32[14,2048]{1,0:T(8,128)}) custom-call(bf16[448,1024]{1,0:T(8,128)(2,1)} %bitcast.25, s32[448,2048]{1,0:T(8,128)} %bitcast.22, f32[14,2048]{1,0:T(8,128)} %bitcast.29, bf16[8,8,4,64,128]{4,3,2,1,0:T(8,128)(2,1)} %bitcast.26), custom_call_target="tpu_custom_call" | custom-call | tf_op jit(solution)/shard_map/backward/pallas_call | solution.py:224
  154.9 1.7 %copy.11 = f32[1,14,2048]{2,0,1:T(1,128)} copy(f32[1,14,2048]{2,1,0:T(8,128)} %bitcast.33) | data formatting | bytes 229376
  (9 shorter events, 0.0 us)
Async XLA Ops:
  7.2 138.6 %all-gather.2.cloned.1.call-start = ((), (), s32[]{:S(2)}) async-start(), calls=%async_computation.3 | async-start | bytes 4718592 | tf_op jit(solution)/shard_map/all_gather | solution.py:261
  34.1 15.0 %collective-permute-start = (bf16[256,1024]{1,0:T(8,128)(2,1)S(1)}, bf16[256,1024]{1,0:T(8,128)(2,1)S(1)}, u32[]{:S(2)}, u32[]{:S(2)}) collective-permute-start(bf16[256,1024]{1,0:T(8,128)(2,1)S(1)} %get-tuple-element.29), channel_id=1, source_target_pairs={{0,8},{8,16},{16,24},{24,0},{1,9},{9,17},{17,25},{25,1},{2,10},{10... | collective-permute-start | bytes 1572872 | tf_op jit(solution)/shard_map/ppermute | solution.py:247
  34.2 14.9 %collective-permute-start.1 = (bf16[256,1024]{1,0:T(8,128)(2,1)S(1)}, bf16[256,1024]{1,0:T(8,128)(2,1)S(1)}, u32[]{:S(2)}, u32[]{:S(2)}) collective-permute-start(bf16[256,1024]{1,0:T(8,128)(2,1)S(1)} %get-tuple-element.28), channel_id=1, source_target_pairs={{0,24},{8,0},{16,8},{24,16},{1,25},{9,1},{17,9},{25,17},{2,26},{10... | collective-permute-start | bytes 1572872 | tf_op jit(solution)/shard_map/ppermute | solution.py:247
  49.2 0.8 copy-start.2
  50.0 0.8 copy-start.3
  54.7 25.6 %collective-permute-start.2 = (bf16[512,1024]{1,0:T(8,128)(2,1)}, bf16[512,1024]{1,0:T(8,128)(2,1)S(1)}, u32[]{:S(2)}, u32[]{:S(2)}) collective-permute-start(bf16[512,1024]{1,0:T(8,128)(2,1)} %get-tuple-element.15), channel_id=1, source_target_pairs={{0,8},{8,16},{16,24},{24,0},{1,9},{9,17},{17,25},{25,1},{2,10},{10... | collective-permute-start | bytes 3145736 | tf_op jit(solution)/shard_map/ppermute | solution.py:247
  54.7 25.6 %collective-permute-start.3 = (bf16[512,1024]{1,0:T(8,128)(2,1)}, bf16[512,1024]{1,0:T(8,128)(2,1)S(1)}, u32[]{:S(2)}, u32[]{:S(2)}) collective-permute-start(bf16[512,1024]{1,0:T(8,128)(2,1)} %get-tuple-element.16), channel_id=1, source_target_pairs={{0,24},{8,0},{16,8},{24,16},{1,25},{9,1},{17,9},{25,17},{2,26},{10... | collective-permute-start | bytes 3145736 | tf_op jit(solution)/shard_map/ppermute | solution.py:247
  80.4 1.0 copy-start
  81.3 1.0 copy-start.1
Sparse Core Ops, SparseCore 0:
  28.3 55.2 all-gather.1

commit v3 on v2

v3 whole, which is shorter than its diff:
```python
import jax
import jax.numpy as jnp
from jax import lax
from jax.experimental import pallas as pl
from jax.experimental.pallas import tpu as pltpu
from jax.sharding import Mesh, PartitionSpec as P

EXPERTS = 8
GROUP = 32
CAP = 128
NY, NC, NX, NZ = 4, 2, 4, 8
COLS = 64
SLOTS = EXPERTS * CAP
BLOCK = NZ * COLS
SMALL = pltpu.CompilerParams(vmem_limit_bytes=16 * 1024 * 1024)
LARGE = pltpu.CompilerParams(vmem_limit_bytes=32 * 1024 * 1024)
F32, BF16, I32 = jnp.float32, jnp.bfloat16, jnp.int32


sds = jax.ShapeDtypeStruct
HBM, VMEM, SMEM = (pl.BlockSpec(memory_space=m) for m in (pltpu.HBM, pltpu.VMEM, pltpu.SMEM))


def near(array):
    return pltpu.with_memory_space_constraint(array, pltpu.VMEM)


def away(array):
    return pltpu.with_memory_space_constraint(array, pltpu.HBM)


def call(body, name, where, operands, outs, scratch=(), far=()):
    heads = [] if where is None else [where]
    return pl.pallas_call(
        body,
        in_specs=[SMEM] * len(heads) + [HBM] * len(far) + [VMEM] * len(operands),
        out_specs=[VMEM] * len(outs),
        out_shape=[pltpu.VMEM(shape, dtype) for shape, dtype in outs],
        scratch_shapes=list(scratch),
        compiler_params=SMALL,
        name=name,
    )(*heads, *[away(a) for a in far], *[near(a) for a in operands])


def dequant(codes_ref, scales_ref, tile, table_ref):
    units, width = codes_ref.shape
    tiles = scales_ref.shape[0] // (units // GROUP)
    for j in range(width // 128):
        lanes = slice(j * 128, (j + 1) * 128)
        for g in range(units // GROUP):
            rows = slice(g * GROUP, (g + 1) * GROUP)
            scale = scales_ref[pl.ds(g * tiles + tile + j, 1), :]
            table_ref[rows, lanes] = (codes_ref[rows, lanes].astype(F32) * scale).astype(BF16)


def picker(place_ref, k):
    slots = lax.broadcasted_iota(I32, (SLOTS, place_ref.shape[1]), 0)
    return (place_ref[k : k + 1, :] == slots).astype(BF16)


def slot_body(index_ref, gate_ref, grad_ref, place_ref, out_ref):
    tokens = index_ref.shape[1]
    experts = lax.broadcasted_iota(I32, (EXPERTS, tokens), 0)
    hot = [(index_ref[k : k + 1, :] == experts).astype(F32) for k in range(2)]
    row = lax.broadcasted_iota(I32, (tokens, tokens), 0)
    col = lax.broadcasted_iota(I32, (tokens, tokens), 1)
    before = (row < col).astype(BF16)
    counts = jnp.dot((hot[0] + hot[1]).astype(BF16), before, preferred_element_type=F32)
    for k in range(2):
        rank = jnp.sum(counts * hot[k], axis=0, keepdims=True).astype(I32)
        place_ref[k : k + 1, :] = jnp.where(rank < CAP, index_ref[k : k + 1, :] * CAP + rank, -1)
    grad = grad_ref[...].astype(F32)
    total = None
    for k in range(2):
        value = (gate_ref[k : k + 1, :] * grad).astype(BF16)
        piece = lax.dot_general(
            value, picker(place_ref, k), (((1,), (1,)), ((), ())), preferred_element_type=F32
        )
        total = piece if total is None else total + piece
    total = total.astype(BF16)
    for e in range(EXPERTS):
        for x in range(NX):
            out_ref[e * NX + x] = total[:, e * CAP : (e + 1) * CAP]


def slot_grads(index, gate, grad):
    outs = [(index.shape, I32), ((EXPERTS * NX, COLS, CAP), BF16)]
    return call(slot_body, "slot_grads", None, [index, gate, grad], outs)


def loads(where_ref, hops, hidden_hbm, codes_hbm, scales_hbm, hidden, codes, scales, sems):
    copies = [
        pltpu.make_async_copy(scales_hbm, scales, sems.at[0]),
        pltpu.make_async_copy(hidden_hbm, hidden, sems.at[1]),
    ]
    for i, hop in enumerate(hops):
        start = pl.multiple_of(lax.rem(where_ref[0] + hop, NX) * BLOCK, BLOCK)
        copies.append(pltpu.make_async_copy(codes_hbm.at[:, pl.ds(start, BLOCK)], codes.at[i], sems.at[2 + i]))
    for copy in copies:
        copy.start()
    copies[0].wait()
    return copies[1:]


def buffers(units, count):
    return [
        pltpu.VMEM((units, SLOTS), BF16),
        pltpu.VMEM((count, units, BLOCK), I32),
        pltpu.VMEM((units // GROUP * (NX * BLOCK // 128), 128), F32),
        pltpu.VMEM((units, BLOCK), BF16),
        pltpu.SemaphoreType.DMA((2 + count,)),
    ]


def block_value(where_ref, hops, hidden, codes, scales, table, copy, others=()):
    copy.wait()
    dequant(codes, scales, lax.rem(where_ref[0] + hops, NX) * (BLOCK // 128), table)
    for other in others:
        other.wait()
    return lax.dot_general(table[...], hidden[...], (((0,), (0,)), ((), ())), preferred_element_type=F32)


def far_body(where_ref, hidden_hbm, codes_hbm, scales_hbm, top_ref, bottom_ref, hidden, codes, scales, table, sems):
    first, *copies = loads(where_ref, (2,), hidden_hbm, codes_hbm, scales_hbm, hidden, codes, scales, sems)
    value = block_value(where_ref, 2, hidden, codes.at[0], scales, table, copies[0], (first,)).astype(BF16)
    top_ref[...] = value[: BLOCK // 2]
    bottom_ref[...] = value[BLOCK // 2 :]


def forward_far(where, *arrays):
    half = ((BLOCK // 2, SLOTS), BF16)
    return call(far_body, "forward_far", where, [], [half, half], buffers(arrays[0].shape[0], 1), arrays)


def join_body(
    where_ref, hidden_hbm, codes_hbm, scales_hbm, top_ref, bottom_ref, up_ref, down_ref, hidden, codes, scales, table, sems
):
    first, *copies = loads(where_ref, (1, 3), hidden_hbm, codes_hbm, scales_hbm, hidden, codes, scales, sems)
    half = BLOCK // 2
    value = block_value(where_ref, 1, hidden, codes.at[0], scales, table, copies[0], (first,))
    up_ref[:half] = (value[:half] + top_ref[...].astype(F32)).astype(BF16)
    up_ref[half:] = value[half:].astype(BF16)
    value = block_value(where_ref, 3, hidden, codes.at[1], scales, table, copies[1])
    down_ref[:half] = value[:half].astype(BF16)
    down_ref[half:] = (value[half:] + bottom_ref[...].astype(F32)).astype(BF16)


def forward_join(where, hidden, codes, scales, top, bottom):
    outs = [((BLOCK, SLOTS), BF16)] * 2
    far = (hidden, codes, scales)
    return call(join_body, "forward_join", where, [top, bottom], outs, buffers(hidden.shape[0], 2), far)


def own_body(where_ref, hidden_hbm, codes_hbm, scales_hbm, own_ref, hidden, codes, scales, table, sems):
    first, *copies = loads(where_ref, (0,), hidden_hbm, codes_hbm, scales_hbm, hidden, codes, scales, sems)
    own_ref[...] = block_value(where_ref, 0, hidden, codes.at[0], scales, table, copies[0], (first,))


def forward_own(where, *arrays):
    outs = [((BLOCK, SLOTS), F32)]
    return call(own_body, "forward_own", where, [], outs, buffers(arrays[0].shape[0], 1), arrays)[0]


def x_sum_body(own_ref, up_ref, down_ref, out_ref):
    for z in range(NZ):
        rows = slice(z * COLS, (z + 1) * COLS)
        total = own_ref[rows, :] + up_ref[rows, :].astype(F32) + down_ref[rows, :].astype(F32)
        out_ref[z] = total.astype(BF16)


def x_sum(*arrays):
    return call(x_sum_body, "x_sum", None, arrays, [((NZ, COLS, SLOTS), BF16)])[0]


def z_sum_body(parts_ref, out_ref):
    total = parts_ref[0].astype(F32)
    for z in range(1, NZ):
        total = total + parts_ref[z].astype(F32)
    total = total.astype(BF16)
    for g in range(EXPERTS):
        out_ref[g] = total[:, g * CAP : (g + 1) * CAP]


def z_sum(parts):
    return call(z_sum_body, "z_sum", None, [parts], [((EXPERTS, COLS, CAP), BF16)])[0]


def combine_body(place_ref, gate_ref, grad_ref, back_ref, out_ref, spread_ref):
    back = jnp.concatenate([back_ref[e] for e in range(EXPERTS)], axis=1)
    grad = grad_ref[...].astype(F32)
    total = None
    for k in range(2):
        got = jnp.dot(back, picker(place_ref, k), preferred_element_type=F32)
        piece = gate_ref[k : k + 1, :] * got
        total = piece if total is None else total + piece
        part = jnp.sum(grad * got, axis=0, keepdims=True)
        for j in range(4):
            line = part[:, j * 128 : (j + 1) * 128]
            spread_ref[:, k * 4 + j : k * 4 + j + 1, :] = jnp.broadcast_to(line[None], (NX * NZ, 1, 128))
    out_ref[...] = total.astype(BF16)


def combine(place, gate, grad, back):
    outs = [(grad.shape, BF16), ((NX * NZ, 8, 128), F32)]
    return call(combine_body, "combine", None, [place, gate, grad, back], outs)


def gate_sum_body(parts_ref, out_ref):
    total = jnp.sum(parts_ref[...], axis=0)
    for k in range(2):
        for j in range(4):
            out_ref[k : k + 1, j * 128 : (j + 1) * 128] = total[k * 4 + j : k * 4 + j + 1, :]


def gate_sum(parts):
    return call(gate_sum_body, "gate_sum", None, [parts], [((2, 512), F32)])[0]


def backward_body(where_ref, hidden_hbm, codes_hbm, scales_hbm, *rest):
    pieces = rest[:NZ]
    hidden_out, weight_out, scale_out = rest[NZ : NZ + 3]
    hidden, codes, scales, grads, table, weight, sems = rest[NZ + 3 :]
    units = hidden.shape[0]
    tiles = BLOCK // 128
    head = [
        pltpu.make_async_copy(hidden_hbm, hidden, sems.at[0]),
        pltpu.make_async_copy(scales_hbm, scales, sems.at[1]),
    ]
    parts, arrive = [], []
    for n in range(NX):
        lanes = slice(n * BLOCK, (n + 1) * BLOCK)
        parts.append(pltpu.make_async_copy(codes_hbm.at[:, lanes], codes.at[n], sems.at[2 + n]))
        arrive.append([])
        for k in range(NZ):
            z = lax.rem(where_ref[1] + k, NZ)
            rows = pl.ds(pl.multiple_of(n * BLOCK + z * COLS, COLS), COLS)
            arrive[n].append(pltpu.make_async_copy(pieces[k].at[:, n], grads.at[:, rows], sems.at[8 + n * NZ + k]))
    head[0].start()
    for copy in arrive[0]:
        copy.start()
    head[1].start()
    parts[0].start()
    for n in range(1, NX):
        for copy in arrive[n]:
            copy.start()
        parts[n].start()
    head[0].wait()
    head[1].wait()
    copies = []
    for n in range(NX):
        lanes = slice(n * BLOCK, (n + 1) * BLOCK)
        for copy in arrive[n]:
            copy.wait()
        block = jnp.concatenate([grads[g, lanes, :] for g in range(EXPERTS)], axis=1)
        slot = n % 2
        if n >= 2:
            copies[n - 2].wait()
        weight[slot] = lax.dot_general(
            hidden[...], block, (((1,), (1,)), ((), ())), preferred_element_type=F32
        )
        copies.append(pltpu.make_async_copy(weight.at[slot], weight_out.at[:, lanes], sems.at[6 + slot]))
        copies[n].start()
        parts[n].wait()
        dequant(codes.at[n], scales, n * tiles, table.at[:, lanes])
        for g in range(units // GROUP):
            rows = slice(g * GROUP, (g + 1) * GROUP)
            line = jnp.sum(weight[slot, rows, :] * codes[n, rows, :].astype(F32), axis=0, keepdims=True)
            for j in range(tiles):
                row = (g * NX + n) * tiles + j
                scale_out[row : row + 1, :] = line[:, j * 128 : (j + 1) * 128]
    block = jnp.concatenate([grads[g] for g in range(EXPERTS)], axis=1)
    hidden_out[...] = jnp.dot(table[...], block, preferred_element_type=F32).astype(BF16)
    copies[2].wait()
    copies[3].wait()


def backward(where, hidden, codes, scales, pieces):
    units, slots = hidden.shape
    features = codes.shape[1]
    pieces = [a.reshape(EXPERTS, NX, COLS, CAP) for a in pieces]
    return pl.pallas_call(
        backward_body,
        in_specs=[SMEM] + [HBM] * (3 + NZ),
        out_specs=[VMEM, HBM, VMEM],
        out_shape=[sds((units, slots), BF16), sds((units, features), F32), sds(scales.shape, F32)],
        scratch_shapes=[
            pltpu.VMEM((units, slots), BF16),
            pltpu.VMEM((NX, units, BLOCK), I32),
            pltpu.VMEM(scales.shape, F32),
            pltpu.VMEM((EXPERTS, features, CAP), BF16),
            pltpu.VMEM((units, features), BF16),
            pltpu.VMEM((2, units, BLOCK), F32),
            pltpu.SemaphoreType.DMA((8 + NX * NZ,)),
        ],
        compiler_params=LARGE,
        name="backward",
    )(where, *[away(a) for a in (hidden, codes, scales, *pieces)])


def shift(value, axis, by):
    size = NX if axis == "x" else NZ
    return lax.ppermute(value, axis, [(i, (i + by) % size) for i in range(size)])


def on_device(hidden, weight_codes, group_scales, expert_index, gate_values, output_grad):
    weights = (hidden[0], weight_codes[0], group_scales.reshape(-1, 128))
    index, gate, grad = expert_index.T, gate_values.T, output_grad.T
    where = jnp.stack([lax.axis_index("x"), lax.axis_index("z")]).astype(I32)

    far_top, far_bottom = forward_far(where, *weights)
    far_top = shift(far_top, "x", 1)
    far_bottom = shift(far_bottom, "x", -1)

    place, outbound = slot_grads(index, gate, grad)
    pieces = {0: lax.all_to_all(outbound, ("y", "c", "x"), 0, 0, tiled=True)}

    def turn(hop):
        pieces[hop] = shift(pieces[hop - 1], "z", -1)
        if hop < 4:
            pieces[NZ - hop] = shift(pieces[(NZ - hop + 1) % NZ], "z", 1)

    far_top, far_bottom, pieces[0] = lax.optimization_barrier((far_top, far_bottom, pieces[0]))
    up, down = forward_join(where, *weights, far_top, far_bottom)
    where_late, up, down = lax.optimization_barrier((where, up, down))
    up = shift(up, "x", 1)
    down = shift(down, "x", -1)
    own = forward_own(where_late, *weights)
    turn(1)
    up, down, pieces[1], pieces[7] = lax.optimization_barrier((up, down, pieces[1], pieces[7]))
    turn(2)

    parts = lax.all_to_all(x_sum(own, up, down), "z", 0, 0, tiled=True)
    parts, pieces[2], pieces[6] = lax.optimization_barrier((parts, pieces[2], pieces[6]))
    turn(3)
    returned = lax.all_to_all(z_sum(parts), ("y", "c"), 0, 0, tiled=True)
    returned, pieces[3], pieces[5] = lax.optimization_barrier((returned, pieces[3], pieces[5]))
    turn(4)
    combined, spread = combine(place, gate, grad, returned)
    gate_parts = lax.all_to_all(spread, ("x", "z"), 0, 0, tiled=True)
    hidden_grad, weight_grad, scale_grad = backward(where, *weights, [pieces[k] for k in range(NZ)])
    gate_parts, hidden_grad = lax.optimization_barrier((gate_parts, hidden_grad))
    gate_grad = gate_sum(gate_parts)
    return combined.T, gate_grad.T, hidden_grad[None], weight_grad[None], scale_grad.reshape(group_scales.shape)


def solution(mesh):
    fine = Mesh(mesh.devices.reshape(NY, NC, NX, NZ), ("y", "c", "x", "z"))
    expert, dp = ("y", "c"), ("x", "z")
    return jax.shard_map(
        on_device,
        mesh=fine,
        in_specs=(
            P(expert, dp, None),
            P(expert, dp, None),
            P(expert, dp, None),
            P(expert, None),
            P(expert, None),
            P(expert, dp),
        ),
        out_specs=(
            P(expert, dp),
            P(expert, None),
            P(expert, dp, None),
            P(expert, dp, None),
            P(expert, dp, None),
        ),
        check_vma=False,
    )
```

time: 165 us -> 144 us (0.87)
  blocking collectives: 74.1 us -> 25.7 us
  waiting for transfers between devices: 26.9 us -> 56.1 us
  starting transfers between devices: 6.58 us -> 35.3 us
  between operations: 14.1 us -> 0.77 us
  Pallas kernels: 33.7 us -> 22.5 us
  local copies, waits for them, and re-layouts: 8.08 us -> 2.04 us
    all_to_all x3 -> x2, blocking collectives: 74.1 us -> 25.7 us  [the longest x1 17.1 us: on_device(): pieces = {0: lax.all_to_all(outbound, ('y', 'c', 'x'), 0, 0, tiled=True)}]
    ppermute x4 -> x11, waiting for transfers between devices: 26.9 us -> 56.1 us  [shift(): lax.ppermute(value, axis, [(i, (i + by) % size) for i in range(size)])]
    all_to_all x0 -> x2, starting transfers between devices: none -> 16.7 us  [the longest x1 8.46 us: on_device(): parts = lax.all_to_all(x_sum(own, up, down), 'z', 0, 0, tiled=True)]
    ppermute x4 -> x11, starting transfers between devices: 6.54 us -> 18.7 us  [shift(): lax.ppermute(value, axis, [(i, (i + by) % size) for i in range(size)])]
    pallas_call x8 -> x9, Pallas kernels: 33.7 us -> 22.5 us  [the longest x8 13.3 us: call(): pl.pallas_call(body, in_specs=[SMEM] * len(heads) + [HBM] * len(far) + [V...]
    unnamed x10 -> x24, local copies, waits for them, and re-layouts: 6.81 us -> 2.04 us
  transfers between devices with their start and end apart: 5 -> 13, of which waited for: 2 -> 8; matrix products, arithmetic and copies ran while one was open for 2% -> 0% of each run, Pallas kernels for 13% -> 10%
where the time goes in v3:
time: 144 us; the launch traced here: 142 us
  waiting for transfers between devices  56.1 us (39%)
  starting transfers between devices  35.3 us (25%)
  blocking collectives  25.7 us (18%)
  Pallas kernels  22.5 us (16%)
  local copies, waits for them, and re-layouts  2.04 us (1%)
    ppermute x11, waiting for transfers between devices, shift(): lax.ppermute(value, axis, [(i, (i + by) % size) for i in range(size)])  56.1 us
    ppermute x11, starting transfers between devices, shift(): lax.ppermute(value, axis, [(i, (i + by) % size) for i in range(size)])  18.7 us
    all_to_all x1, blocking collectives, on_device(): pieces = {0: lax.all_to_all(outbound, ('y', 'c', 'x'), 0, 0, tiled=True)}  17.1 us
    pallas_call x8, Pallas kernels, call(): pl.pallas_call(body, in_specs=[SMEM] * len(heads) + [HBM] * len(far) + [V...  13.3 us
    pallas_call x1, Pallas kernels, backward(): pl.pallas_call(backward_body, in_specs=[SMEM] + [HBM] * (3 + NZ), out_spe...  9.14 us
    all_to_all x1, blocking collectives, on_device(): returned = lax.all_to_all(z_sum(parts), ('y', 'c'), 0, 0, tiled=True)  8.57 us
    all_to_all x1, starting transfers between devices, on_device(): parts = lax.all_to_all(x_sum(own, up, down), 'z', 0, 0, tiled=True)  8.46 us
    all_to_all x1, starting transfers between devices, on_device(): gate_parts = lax.all_to_all(spread, ('x', 'z'), 0, 0, tiled=True)  8.19 us
  transfers between devices with their start and end apart: 13, of which 8 were waited for; matrix products, arithmetic and copies ran while one was open for 0% of the time, Pallas kernels for 10%

profile of v3, /device:TPU:8, one launch (start us, length us, event | category | flops | bytes accessed | tf_op | source)
XLA Modules:
  0.0 142.5 jit_solution(1835890767695307023)
XLA Ops:
  0.7 2.9 %forward_far.1 = (bf16[256,1024]{1,0:T(8,128)(2,1)S(1)}, bf16[256,1024]{1,0:T(8,128)(2,1)S(1)}) custom-call(s32[2]{0:T(128)S(1)} %pad_add_fusion.where_ref, bf16[448,1024]{1,0:T(8,128)(2,1)} %bitcast.32, s32[448,2048]{1,0:T(8,128)} %bitcast.28, f32[224,128]{1,0:T(8,128)} %bitcast.37), custom_call_target="tpu_custom_call" | custom-call | tf_op jit(solution)/shard_map/forward_far/pallas_call | solution.py:34
  3.7 1.6 %collective-permute-start = (bf16[256,1024]{1,0:T(8,128)(2,1)S(1)}, bf16[256,1024]{1,0:T(8,128)(2,1)S(1)}, u32[]{:S(2)}, u32[]{:S(2)}) collective-permute-start(bf16[256,1024]{1,0:T(8,128)(2,1)S(1)} %get-tuple-element.35), channel_id=1, source_target_pairs={{0,8},{8,16},{16,24},{24,0},{1,9},{9,17},{17,25},{25,1},{2,10},{10... | collective-permute-start | bytes 1572872 | tf_op jit(solution)/shard_map/ppermute | solution.py:302
  5.3 1.7 %collective-permute-start.1 = (bf16[256,1024]{1,0:T(8,128)(2,1)S(1)}, bf16[256,1024]{1,0:T(8,128)(2,1)S(1)}, u32[]{:S(2)}, u32[]{:S(2)}) collective-permute-start(bf16[256,1024]{1,0:T(8,128)(2,1)S(1)} %get-tuple-element.36), channel_id=1, source_target_pairs={{0,24},{8,0},{16,8},{24,16},{1,25},{9,1},{17,9},{25,17},{2,26},{10... | collective-permute-start | bytes 1572872 | tf_op jit(solution)/shard_map/ppermute | solution.py:302
  8.0 17.1 %all_to_all.20 = bf16[32,64,128]{2,1,0:T(8,128)(2,1)S(1)} all-to-all(bf16[32,64,128]{2,1,0:T(8,128)(2,1)S(1)} %get-tuple-element.37), channel_id=1, replica_groups=mesh['y'=4,'c'=2,'x'=4,'z'=8] {'y','c','x'}, dimensions={0} | all-to-all | bytes 1048576 | tf_op jit(solution)/shard_map/all_to_all | solution.py:315
  25.1 3.7 %forward_join.1 = (bf16[512,1024]{1,0:T(8,128)(2,1)S(1)}, bf16[512,1024]{1,0:T(8,128)(2,1)S(1)}) custom-call(s32[2]{0:T(128)S(1)} %pad_add_fusion.where_ref, bf16[448,1024]{1,0:T(8,128)(2,1)} %bitcast.33, s32[448,2048]{1,0:T(8,128)} %bitcast.29, f32[224,128]{1,0:T(8,128)} %bitcast.38, bf16[256,1024]{1,0:T(8,128)(2,1)S(1)} %collective-permute-done.top_ref, ...), custom_call_target="tpu_custom_call" | custom-call | tf_op jit(solution)/shard_map/forward_join/pallas_call | solution.py:34
  29.8 2.3 %collective-permute-start.3 = (bf16[512,1024]{1,0:T(8,128)(2,1)S(1)}, bf16[512,1024]{1,0:T(8,128)(2,1)S(1)}, u32[]{:S(2)}, u32[]{:S(2)}) collective-permute-start(bf16[512,1024]{1,0:T(8,128)(2,1)S(1)} %get-tuple-element.44), channel_id=1, source_target_pairs={{0,24},{8,0},{16,8},{24,16},{1,25},{9,1},{17,9},{25,17},{2,26},{10... | collective-permute-start | bytes 3145736 | tf_op jit(solution)/shard_map/ppermute | solution.py:302
  32.2 5.9 %collective-permute-start.4 = (bf16[32,64,128]{2,1,0:T(8,128)(2,1)S(1)}, bf16[32,64,128]{2,1,0:T(8,128)(2,1)S(1)}, u32[]{:S(2)}, u32[]{:S(2)}) collective-permute-start(bf16[32,64,128]{2,1,0:T(8,128)(2,1)S(1)} %all_to_all.20), channel_id=1, source_target_pairs={{0,7},{1,0},{2,1},{3,2},{4,3},{5,4},{6,5},{7,6},{8,15},{9,8},{10,9... | collective-permute-start | bytes 1572872 | tf_op jit(solution)/shard_map/ppermute | solution.py:302
  38.0 2.9 %forward_own.1.own_ref = f32[512,1024]{1,0:T(8,128)S(1)} custom-call(s32[2]{0:T(128)S(1)} %pad_add_fusion.where_ref, bf16[448,1024]{1,0:T(8,128)(2,1)} %bitcast.34, s32[448,2048]{1,0:T(8,128)} %bitcast.30, f32[224,128]{1,0:T(8,128)} %bitcast.39), custom_call_target="tpu_custom_call" | custom-call | tf_op jit(solution)/shard_map/forward_own/pallas_call | solution.py:34
  41.0 9.0 %collective-permute-done.4 = bf16[32,64,128]{2,1,0:T(8,128)(2,1)S(1)} collective-permute-done((bf16[32,64,128]{2,1,0:T(8,128)(2,1)S(1)}, bf16[32,64,128]{2,1,0:T(8,128)(2,1)S(1)}, u32[]{:S(2)}, u32[]{:S(2)}) %collective-permute-start.4) | collective-permute-done | bytes 524320 | tf_op jit(solution)/shard_map/ppermute | solution.py:302
  50.0 3.4 %collective-permute-done.5 = bf16[32,64,128]{2,1,0:T(8,128)(2,1)S(1)} collective-permute-done((bf16[32,64,128]{2,1,0:T(8,128)(2,1)S(1)}, bf16[32,64,128]{2,1,0:T(8,128)(2,1)S(1)}, u32[]{:S(2)}, u32[]{:S(2)}) %collective-permute-start.5) | collective-permute-done | bytes 524320 | tf_op jit(solution)/shard_map/ppermute | solution.py:302
  53.4 2.6 %collective-permute-done.2.up_ref = bf16[512,1024]{1,0:T(8,128)(2,1)S(1)} collective-permute-done((bf16[512,1024]{1,0:T(8,128)(2,1)S(1)}, bf16[512,1024]{1,0:T(8,128)(2,1)S(1)}, u32[]{:S(2)}, u32[]{:S(2)}) %collective-permute-start.2) | collective-permute-done | bytes 1048608 | tf_op jit(solution)/shard_map/ppermute | solution.py:302
  56.0 1.3 x_sum.1
  57.3 8.5 %all-to-all-start.1 = ((bf16[8,64,1024]{2,1,0:T(8,128)(2,1)}), bf16[8,64,1024]{2,1,0:T(8,128)(2,1)S(1)}, u32[]{:S(2)}, u32[]{:S(2)}) async-start(bf16[8,64,1024]{2,1,0:T(8,128)(2,1)} %x_sum.1), calls=%async_computation.1 | async-start | bytes 2097152 | tf_op jit(solution)/shard_map/all_to_all | solution.py:332
  65.8 3.2 %collective-permute-start.6 = (bf16[32,64,128]{2,1,0:T(8,128)(2,1)S(1)}, bf16[32,64,128]{2,1,0:T(8,128)(2,1)S(1)}, u32[]{:S(2)}, u32[]{:S(2)}) collective-permute-start(bf16[32,64,128]{2,1,0:T(8,128)(2,1)S(1)} %collective-permute-done.4), channel_id=1, source_target_pairs={{0,7},{1,0},{2,1},{3,2},{4,3},{5,4},{6,5},{7,6},{8,15},{9,8},{10,9... | collective-permute-start | bytes 1572872 | tf_op jit(solution)/shard_map/ppermute | solution.py:302
  69.0 33.1 %collective-permute-done.6 = bf16[32,64,128]{2,1,0:T(8,128)(2,1)S(1)} collective-permute-done((bf16[32,64,128]{2,1,0:T(8,128)(2,1)S(1)}, bf16[32,64,128]{2,1,0:T(8,128)(2,1)S(1)}, u32[]{:S(2)}, u32[]{:S(2)}) %collective-permute-start.6) | collective-permute-done | bytes 524320 | tf_op jit(solution)/shard_map/ppermute | solution.py:302
  102.1 1.2 collective-permute-done.7
  103.4 1.5 %collective-permute-start.8 = (bf16[32,64,128]{2,1,0:T(8,128)(2,1)S(1)}, bf16[32,64,128]{2,1,0:T(8,128)(2,1)S(1)}, u32[]{:S(2)}, u32[]{:S(2)}) collective-permute-start(bf16[32,64,128]{2,1,0:T(8,128)(2,1)S(1)} %collective-permute-done.6), channel_id=1, source_target_pairs={{0,7},{1,0},{2,1},{3,2},{4,3},{5,4},{6,5},{7,6},{8,15},{9,8},{10,9... | collective-permute-start | bytes 1572872 | tf_op jit(solution)/shard_map/ppermute | solution.py:302
  105.6 8.6 %all_to_all.21.back_ref = bf16[8,64,128]{2,1,0:T(8,128)(2,1)S(1)} all-to-all(bf16[8,64,128]{2,1,0:T(8,128)(2,1)S(1)} %z_sum.1), channel_id=1, replica_groups=mesh['y'=4,'c'=2,'x'=4,'z'=8] {'y','c'}, dimensions={0} | all-to-all | bytes 262144 | tf_op jit(solution)/shard_map/all_to_all | solution.py:335
  114.1 2.1 %collective-permute-done.8 = bf16[32,64,128]{2,1,0:T(8,128)(2,1)S(1)} collective-permute-done((bf16[32,64,128]{2,1,0:T(8,128)(2,1)S(1)}, bf16[32,64,128]{2,1,0:T(8,128)(2,1)S(1)}, u32[]{:S(2)}, u32[]{:S(2)}) %collective-permute-start.8) | collective-permute-done | bytes 524320 | tf_op jit(solution)/shard_map/ppermute | solution.py:302
  116.3 2.4 %collective-permute-done.9 = bf16[32,64,128]{2,1,0:T(8,128)(2,1)S(1)} collective-permute-done((bf16[32,64,128]{2,1,0:T(8,128)(2,1)S(1)}, bf16[32,64,128]{2,1,0:T(8,128)(2,1)S(1)}, u32[]{:S(2)}, u32[]{:S(2)}) %collective-permute-start.9) | collective-permute-done | bytes 524320 | tf_op jit(solution)/shard_map/ppermute | solution.py:302
  119.7 1.2 combine.1
  120.9 8.2 %all-to-all-start.3 = ((f32[32,8,128]{2,1,0:T(8,128)}), f32[32,8,128]{2,1,0:T(8,128)S(1)}, u32[]{:S(2)}, u32[]{:S(2)}) async-start(f32[32,8,128]{2,1,0:T(8,128)} %get-tuple-element.55), calls=%async_computation.3 | async-start | bytes 262144 | tf_op jit(solution)/shard_map/all_to_all | solution.py:339
  129.7 2.1 %collective-permute-done.10 = bf16[32,64,128]{2,1,0:T(8,128)(2,1)S(1)} collective-permute-done((bf16[32,64,128]{2,1,0:T(8,128)(2,1)S(1)}, bf16[32,64,128]{2,1,0:T(8,128)(2,1)S(1)}, u32[]{:S(2)}, u32[]{:S(2)}) %collective-permute-start.10) | collective-permute-done | bytes 524320 | tf_op jit(solution)/shard_map/ppermute | solution.py:302
  132.7 9.1 %backward.1 = (bf16[448,1024]{1,0:T(8,128)(2,1)}, f32[448,2048]{1,0:T(8,128)}, f32[224,128]{1,0:T(8,128)}) custom-call(s32[2]{0:T(128)S(1)} %pad_add_fusion.where_ref, bf16[448,1024]{1,0:T(8,128)(2,1)} %bitcast.35, s32[448,2048]{1,0:T(8,128)} %bitcast.31, f32[224,128]{1,0:T(8,128)} %bitcast.40, bf16[8,4,64,128]{3,2,1,0:T(8,128)(2,1)} %bitcast.36, ...), custom_call_target="tpu_custom_call" | custom-call | tf_op jit(solution)/shard_map/backward/pallas_call | solution.py:281
  (38 shorter events, 5.7 us)
Async XLA Ops:
  0.6 6.4 %copy-start.1 = (f32[512,2]{0,1:T(2,128)S(1)}, f32[512,2]{0,1:T(2,128)}, u32[]{:S(2)}) copy-start(f32[512,2]{0,1:T(2,128)} %param.10) | copy-start | bytes 12292
  0.6 6.4 %copy-start = (bf16[512,64]{0,1:T(8,128)(2,1)S(1)}, bf16[512,64]{0,1:T(8,128)(2,1)}, u32[]{:S(2)}) copy-start(bf16[512,64]{0,1:T(8,128)(2,1)} %param.11) | copy-start | bytes 196612
  0.7 6.4 %copy-start.2 = (s32[512,2]{0,1:T(2,128)S(1)}, s32[512,2]{0,1:T(2,128)}, u32[]{:S(2)}) copy-start(s32[512,2]{0,1:T(2,128)} %param.9) | copy-start | bytes 12292
  3.7 21.4 %collective-permute-start = (bf16[256,1024]{1,0:T(8,128)(2,1)S(1)}, bf16[256,1024]{1,0:T(8,128)(2,1)S(1)}, u32[]{:S(2)}, u32[]{:S(2)}) collective-permute-start(bf16[256,1024]{1,0:T(8,128)(2,1)S(1)} %get-tuple-element.35), channel_id=1, source_target_pairs={{0,8},{8,16},{16,24},{24,0},{1,9},{9,17},{17,25},{25,1},{2,10},{10... | collective-permute-start | bytes 1572872 | tf_op jit(solution)/shard_map/ppermute | solution.py:302
  5.3 19.9 %collective-permute-start.1 = (bf16[256,1024]{1,0:T(8,128)(2,1)S(1)}, bf16[256,1024]{1,0:T(8,128)(2,1)S(1)}, u32[]{:S(2)}, u32[]{:S(2)}) collective-permute-start(bf16[256,1024]{1,0:T(8,128)(2,1)S(1)} %get-tuple-element.36), channel_id=1, source_target_pairs={{0,24},{8,0},{16,8},{24,16},{1,25},{9,1},{17,9},{25,17},{2,26},{10... | collective-permute-start | bytes 1572872 | tf_op jit(solution)/shard_map/ppermute | solution.py:302
  25.1 15.9 %copy-start.3 = (bf16[32,64,128]{2,1,0:T(8,128)(2,1)}, bf16[32,64,128]{2,1,0:T(8,128)(2,1)S(1)}, u32[]{:S(2)}) copy-start(bf16[32,64,128]{2,1,0:T(8,128)(2,1)S(1)} %all_to_all.20) | copy-start | bytes 1572868
  28.9 27.1 %collective-permute-start.2 = (bf16[512,1024]{1,0:T(8,128)(2,1)S(1)}, bf16[512,1024]{1,0:T(8,128)(2,1)S(1)}, u32[]{:S(2)}, u32[]{:S(2)}) collective-permute-start(bf16[512,1024]{1,0:T(8,128)(2,1)S(1)} %get-tuple-element.43), channel_id=1, source_target_pairs={{0,8},{8,16},{16,24},{24,0},{1,9},{9,17},{17,25},{25,1},{2,10},{10... | collective-permute-start | bytes 3145736 | tf_op jit(solution)/shard_map/ppermute | solution.py:302
  29.8 26.2 %collective-permute-start.3 = (bf16[512,1024]{1,0:T(8,128)(2,1)S(1)}, bf16[512,1024]{1,0:T(8,128)(2,1)S(1)}, u32[]{:S(2)}, u32[]{:S(2)}) collective-permute-start(bf16[512,1024]{1,0:T(8,128)(2,1)S(1)} %get-tuple-element.44), channel_id=1, source_target_pairs={{0,24},{8,0},{16,8},{24,16},{1,25},{9,1},{17,9},{25,17},{2,26},{10... | collective-permute-start | bytes 3145736 | tf_op jit(solution)/shard_map/ppermute | solution.py:302
  32.2 17.8 %collective-permute-start.4 = (bf16[32,64,128]{2,1,0:T(8,128)(2,1)S(1)}, bf16[32,64,128]{2,1,0:T(8,128)(2,1)S(1)}, u32[]{:S(2)}, u32[]{:S(2)}) collective-permute-start(bf16[32,64,128]{2,1,0:T(8,128)(2,1)S(1)} %all_to_all.20), channel_id=1, source_target_pairs={{0,7},{1,0},{2,1},{3,2},{4,3},{5,4},{6,5},{7,6},{8,15},{9,8},{10,9... | collective-permute-start | bytes 1572872 | tf_op jit(solution)/shard_map/ppermute | solution.py:302
  38.0 15.3 %collective-permute-start.5 = (bf16[32,64,128]{2,1,0:T(8,128)(2,1)S(1)}, bf16[32,64,128]{2,1,0:T(8,128)(2,1)S(1)}, u32[]{:S(2)}, u32[]{:S(2)}) collective-permute-start(bf16[32,64,128]{2,1,0:T(8,128)(2,1)S(1)} %all_to_all.20), channel_id=1, source_target_pairs={{0,1},{1,2},{2,3},{3,4},{4,5},{5,6},{6,7},{7,0},{8,9},{9,10},{10,1... | collective-permute-start | bytes 1572872 | tf_op jit(solution)/shard_map/ppermute | solution.py:302
  50.0 15.8 %copy-start.4 = (bf16[32,64,128]{2,1,0:T(8,128)(2,1)}, bf16[32,64,128]{2,1,0:T(8,128)(2,1)S(1)}, u32[]{:S(2)}) copy-start(bf16[32,64,128]{2,1,0:T(8,128)(2,1)S(1)} %collective-permute-done.4) | copy-start | bytes 1572868
  53.4 15.6 %copy-start.5 = (bf16[32,64,128]{2,1,0:T(8,128)(2,1)}, bf16[32,64,128]{2,1,0:T(8,128)(2,1)S(1)}, u32[]{:S(2)}) copy-start(bf16[32,64,128]{2,1,0:T(8,128)(2,1)S(1)} %collective-permute-done.5) | copy-start | bytes 1572868
  57.3 46.0 %all-to-all-start.1 = ((bf16[8,64,1024]{2,1,0:T(8,128)(2,1)}), bf16[8,64,1024]{2,1,0:T(8,128)(2,1)S(1)}, u32[]{:S(2)}, u32[]{:S(2)}) async-start(bf16[8,64,1024]{2,1,0:T(8,128)(2,1)} %x_sum.1), calls=%async_computation.1 | async-start | bytes 2097152 | tf_op jit(solution)/shard_map/all_to_all | solution.py:332
  65.8 36.3 %collective-permute-start.6 = (bf16[32,64,128]{2,1,0:T(8,128)(2,1)S(1)}, bf16[32,64,128]{2,1,0:T(8,128)(2,1)S(1)}, u32[]{:S(2)}, u32[]{:S(2)}) collective-permute-start(bf16[32,64,128]{2,1,0:T(8,128)(2,1)S(1)} %collective-permute-done.4), channel_id=1, source_target_pairs={{0,7},{1,0},{2,1},{3,2},{4,3},{5,4},{6,5},{7,6},{8,15},{9,8},{10,9... | collective-permute-start | bytes 1572872 | tf_op jit(solution)/shard_map/ppermute | solution.py:302
  69.0 34.3 %collective-permute-start.7 = (bf16[32,64,128]{2,1,0:T(8,128)(2,1)S(1)}, bf16[32,64,128]{2,1,0:T(8,128)(2,1)S(1)}, u32[]{:S(2)}, u32[]{:S(2)}) collective-permute-start(bf16[32,64,128]{2,1,0:T(8,128)(2,1)S(1)} %collective-permute-done.5), channel_id=1, source_target_pairs={{0,1},{1,2},{2,3},{3,4},{4,5},{5,6},{6,7},{7,0},{8,9},{9,10},{10,1... | collective-permute-start | bytes 1572872 | tf_op jit(solution)/shard_map/ppermute | solution.py:302
  102.1 29.7 %copy-start.6 = (bf16[32,64,128]{2,1,0:T(8,128)(2,1)}, bf16[32,64,128]{2,1,0:T(8,128)(2,1)S(1)}, u32[]{:S(2)}) copy-start(bf16[32,64,128]{2,1,0:T(8,128)(2,1)S(1)} %collective-permute-done.6) | copy-start | bytes 1572868
  103.3 28.5 %copy-start.7 = (bf16[32,64,128]{2,1,0:T(8,128)(2,1)}, bf16[32,64,128]{2,1,0:T(8,128)(2,1)S(1)}, u32[]{:S(2)}) copy-start(bf16[32,64,128]{2,1,0:T(8,128)(2,1)S(1)} %collective-permute-done.7) | copy-start | bytes 1572868
  103.4 12.9 %collective-permute-start.8 = (bf16[32,64,128]{2,1,0:T(8,128)(2,1)S(1)}, bf16[32,64,128]{2,1,0:T(8,128)(2,1)S(1)}, u32[]{:S(2)}, u32[]{:S(2)}) collective-permute-start(bf16[32,64,128]{2,1,0:T(8,128)(2,1)S(1)} %collective-permute-done.6), channel_id=1, source_target_pairs={{0,7},{1,0},{2,1},{3,2},{4,3},{5,4},{6,5},{7,6},{8,15},{9,8},{10,9... | collective-permute-start | bytes 1572872 | tf_op jit(solution)/shard_map/ppermute | solution.py:302
  104.9 13.9 %collective-permute-start.9 = (bf16[32,64,128]{2,1,0:T(8,128)(2,1)S(1)}, bf16[32,64,128]{2,1,0:T(8,128)(2,1)S(1)}, u32[]{:S(2)}, u32[]{:S(2)}) collective-permute-start(bf16[32,64,128]{2,1,0:T(8,128)(2,1)S(1)} %collective-permute-done.7), channel_id=1, source_target_pairs={{0,1},{1,2},{2,3},{3,4},{4,5},{5,6},{6,7},{7,0},{8,9},{9,10},{10,1... | collective-permute-start | bytes 1572872 | tf_op jit(solution)/shard_map/ppermute | solution.py:302
  116.3 15.6 %copy-start.8 = (bf16[32,64,128]{2,1,0:T(8,128)(2,1)}, bf16[32,64,128]{2,1,0:T(8,128)(2,1)S(1)}, u32[]{:S(2)}) copy-start(bf16[32,64,128]{2,1,0:T(8,128)(2,1)S(1)} %collective-permute-done.8) | copy-start | bytes 1572868
  118.7 13.2 %copy-start.9 = (bf16[32,64,128]{2,1,0:T(8,128)(2,1)}, bf16[32,64,128]{2,1,0:T(8,128)(2,1)S(1)}, u32[]{:S(2)}) copy-start(bf16[32,64,128]{2,1,0:T(8,128)(2,1)S(1)} %collective-permute-done.9) | copy-start | bytes 1572868
  118.7 13.1 %collective-permute-start.10 = (bf16[32,64,128]{2,1,0:T(8,128)(2,1)S(1)}, bf16[32,64,128]{2,1,0:T(8,128)(2,1)S(1)}, u32[]{:S(2)}, u32[]{:S(2)}) collective-permute-start(bf16[32,64,128]{2,1,0:T(8,128)(2,1)S(1)} %collective-permute-done.8), channel_id=1, source_target_pairs={{0,7},{1,0},{2,1},{3,2},{4,3},{5,4},{6,5},{7,6},{8,15},{9,8},{10,9... | collective-permute-start | bytes 1572872 | tf_op jit(solution)/shard_map/ppermute | solution.py:302
  120.9 20.9 %all-to-all-start.3 = ((f32[32,8,128]{2,1,0:T(8,128)}), f32[32,8,128]{2,1,0:T(8,128)S(1)}, u32[]{:S(2)}, u32[]{:S(2)}) async-start(f32[32,8,128]{2,1,0:T(8,128)} %get-tuple-element.55), calls=%async_computation.3 | async-start | bytes 262144 | tf_op jit(solution)/shard_map/all_to_all | solution.py:339
  131.9 0.8 copy-start.10

commit v4 on v3

--- a/solution.py
+++ b/solution.py
@@ -161,28 +161,45 @@
     return call(own_body, "forward_own", where, [], outs, buffers(arrays[0].shape[0], 1), arrays)[0]
 
 
-def x_sum_body(own_ref, up_ref, down_ref, out_ref):
-    for z in range(NZ):
-        rows = slice(z * COLS, (z + 1) * COLS)
-        total = own_ref[rows, :] + up_ref[rows, :].astype(F32) + down_ref[rows, :].astype(F32)
-        out_ref[z] = total.astype(BF16)
-
-
-def x_sum(*arrays):
-    return call(x_sum_body, "x_sum", None, arrays, [((NZ, COLS, SLOTS), BF16)])[0]
-
-
-def z_sum_body(parts_ref, out_ref):
-    total = parts_ref[0].astype(F32)
-    for z in range(1, NZ):
-        total = total + parts_ref[z].astype(F32)
-    total = total.astype(BF16)
+def x_sum_body(where_ref, own_ref, up_ref, down_ref, ups_ref, downs_ref, far_ref, up2_ref, down2_ref, rest_ref):
+    def total(hops):
+        rows = pl.ds(pl.multiple_of(lax.rem(where_ref[1] + hops, NZ) * COLS, COLS), COLS)
+        return own_ref[rows, :] + up_ref[rows, :].astype(F32) + down_ref[rows, :].astype(F32)
+
+    ups_ref[0] = total(3).astype(BF16)
+    ups_ref[1] = total(1).astype(BF16)
+    downs_ref[0] = total(5).astype(BF16)
+    downs_ref[1] = total(7).astype(BF16)
+    far_ref[...] = total(4).astype(BF16)
+    up2_ref[...] = total(2)
+    down2_ref[...] = total(6)
+    rest_ref[...] = total(0)
+
+
+def x_sum(where, *arrays):
+    one, two = (COLS, SLOTS), (2, COLS, SLOTS)
+    outs = [(two, BF16), (two, BF16), (one, BF16), (one, F32), (one, F32), (one, F32)]
+    return call(x_sum_body, "x_sum", where, arrays, outs)
+
+
+def mid_sum_body(up2_ref, down2_ref, ups_ref, downs_ref, far_ref, up_out, down_out):
+    up_out[...] = (up2_ref[...] + ups_ref[0].astype(F32) + far_ref[...].astype(F32)).astype(BF16)
+    down_out[...] = (down2_ref[...] + downs_ref[0].astype(F32)).astype(BF16)
+
+
+def mid_sum(*arrays):
+    return call(mid_sum_body, "mid_sum", None, arrays, [((COLS, SLOTS), BF16)] * 2)
+
+
+def z_sum_body(rest_ref, ups_ref, downs_ref, up_ref, down_ref, out_ref):
+    total = rest_ref[...] + ups_ref[1].astype(F32) + downs_ref[1].astype(F32)
+    total = (total + up_ref[...].astype(F32) + down_ref[...].astype(F32)).astype(BF16)
     for g in range(EXPERTS):
         out_ref[g] = total[:, g * CAP : (g + 1) * CAP]
 
 
-def z_sum(parts):
-    return call(z_sum_body, "z_sum", None, [parts], [((EXPERTS, COLS, CAP), BF16)])[0]
+def z_sum(*arrays):
+    return call(z_sum_body, "z_sum", None, arrays, [((EXPERTS, COLS, CAP), BF16)])[0]
 
 
 def combine_body(place_ref, gate_ref, grad_ref, back_ref, out_ref, spread_ref):
@@ -217,9 +234,9 @@
 
 
 def backward_body(where_ref, hidden_hbm, codes_hbm, scales_hbm, *rest):
-    pieces = rest[:NZ]
-    hidden_out, weight_out, scale_out = rest[NZ : NZ + 3]
-    hidden, codes, scales, grads, table, weight, sems = rest[NZ + 3 :]
+    pieces = rest[: NZ + 1]
+    hidden_out, weight_out, scale_out = rest[NZ + 1 : NZ + 4]
+    hidden, codes, scales, grads, table, weight, sems = rest[NZ + 4 :]
     units = hidden.shape[0]
     tiles = BLOCK // 128
     head = [
@@ -231,10 +248,13 @@
         lanes = slice(n * BLOCK, (n + 1) * BLOCK)
         parts.append(pltpu.make_async_copy(codes_hbm.at[:, lanes], codes.at[n], sems.at[2 + n]))
         arrive.append([])
-        for k in range(NZ):
-            z = lax.rem(where_ref[1] + k, NZ)
+        for k in range(NZ + 1):
+            z = lax.rem(where_ref[1] + (k if k < NZ else 4), NZ)
             rows = pl.ds(pl.multiple_of(n * BLOCK + z * COLS, COLS), COLS)
-            arrive[n].append(pltpu.make_async_copy(pieces[k].at[:, n], grads.at[:, rows], sems.at[8 + n * NZ + k]))
+            first = EXPERTS - pieces[k].shape[0] if k == NZ else 0
+            groups = slice(first, first + pieces[k].shape[0])
+            sem = sems.at[8 + n * (NZ + 1) + k]
+            arrive[n].append(pltpu.make_async_copy(pieces[k].at[:, n], grads.at[groups, rows], sem))
     head[0].start()
     for copy in arrive[0]:
         copy.start()
@@ -277,10 +297,10 @@
 def backward(where, hidden, codes, scales, pieces):
     units, slots = hidden.shape
     features = codes.shape[1]
-    pieces = [a.reshape(EXPERTS, NX, COLS, CAP) for a in pieces]
+    pieces = [a.reshape(-1, NX, COLS, CAP) for a in pieces]
     return pl.pallas_call(
         backward_body,
-        in_specs=[SMEM] + [HBM] * (3 + NZ),
+        in_specs=[SMEM] + [HBM] * (4 + NZ),
         out_specs=[VMEM, HBM, VMEM],
         out_shape=[sds((units, slots), BF16), sds((units, features), F32), sds(scales.shape, F32)],
         scratch_shapes=[
@@ -290,7 +310,7 @@
             pltpu.VMEM((EXPERTS, features, CAP), BF16),
             pltpu.VMEM((units, features), BF16),
             pltpu.VMEM((2, units, BLOCK), F32),
-            pltpu.SemaphoreType.DMA((8 + NX * NZ,)),
+            pltpu.SemaphoreType.DMA((8 + NX * (NZ + 1),)),
         ],
         compiler_params=LARGE,
         name="backward",
@@ -316,8 +336,7 @@
 
     def turn(hop):
         pieces[hop] = shift(pieces[hop - 1], "z", -1)
-        if hop < 4:
-            pieces[NZ - hop] = shift(pieces[(NZ - hop + 1) % NZ], "z", 1)
+        pieces[NZ - hop] = shift(pieces[(NZ - hop + 1) % NZ], "z", 1)
 
     far_top, far_bottom, pieces[0] = lax.optimization_barrier((far_top, far_bottom, pieces[0]))
     up, down = forward_join(where, *weights, far_top, far_bottom)
@@ -326,18 +345,22 @@
     down = shift(down, "x", -1)
     own = forward_own(where_late, *weights)
     turn(1)
-    up, down, pieces[1], pieces[7] = lax.optimization_barrier((up, down, pieces[1], pieces[7]))
     turn(2)
-
-    parts = lax.all_to_all(x_sum(own, up, down), "z", 0, 0, tiled=True)
-    parts, pieces[2], pieces[6] = lax.optimization_barrier((parts, pieces[2], pieces[6]))
+    up, down, pieces[2], pieces[6] = lax.optimization_barrier((up, down, pieces[2], pieces[6]))
+
+    ups, downs, far, up2, down2, rest = x_sum(where, own, up, down)
+    ups, downs, far = shift(ups, "z", 1), shift(downs, "z", -1), shift(far, "z", 2)
+    up2, down2 = mid_sum(up2, down2, ups, downs, far)
+    up2, pieces[2], pieces[6] = lax.optimization_barrier((up2, pieces[2], pieces[6]))
     turn(3)
-    returned = lax.all_to_all(z_sum(parts), ("y", "c"), 0, 0, tiled=True)
+    summed = z_sum(rest, ups, downs, shift(up2, "z", 2), shift(down2, "z", -2))
+    returned = lax.all_to_all(summed, ("y", "c"), 0, 0, tiled=True)
     returned, pieces[3], pieces[5] = lax.optimization_barrier((returned, pieces[3], pieces[5]))
-    turn(4)
+    last = [shift(pieces[3][: EXPERTS * NX // 2], "z", -1), shift(pieces[5][EXPERTS * NX // 2 :], "z", 1)]
     combined, spread = combine(place, gate, grad, returned)
     gate_parts = lax.all_to_all(spread, ("x", "z"), 0, 0, tiled=True)
-    hidden_grad, weight_grad, scale_grad = backward(where, *weights, [pieces[k] for k in range(NZ)])
+    ordered = [pieces[k] if k != 4 else last[0] for k in range(NZ)] + [last[1]]
+    hidden_grad, weight_grad, scale_grad = backward(where, *weights, ordered)
     gate_parts, hidden_grad = lax.optimization_barrier((gate_parts, hidden_grad))
     gate_grad = gate_sum(gate_parts)
     return combined.T, gate_grad.T, hidden_grad[None], weight_grad[None], scale_grad.reshape(group_scales.shape)

time: 144 us -> 132 us (0.917)
  waiting for transfers between devices: 56.1 us -> 43.7 us
  blocking collectives: 25.7 us -> 27.7 us
    ppermute x11 -> x17, waiting for transfers between devices: 56.1 us -> 43.7 us  [shift(): lax.ppermute(value, axis, [(i, (i + by) % size) for i in range(size)])]
    ppermute x11 -> x17, starting transfers between devices: 18.7 us -> 28.8 us  [shift(): lax.ppermute(value, axis, [(i, (i + by) % size) for i in range(size)])]
    all_to_all x1 -> x0, starting transfers between devices: 8.46 us -> none  [on_device(): parts = lax.all_to_all(x_sum(own, up, down), 'z', 0, 0, tiled=True)]
    all_to_all x1, starting transfers between devices: 8.19 us -> 5.65 us  [on_device(): gate_parts = lax.all_to_all(spread, ('x', 'z'), 0, 0, tiled=True)]
    all_to_all x1, blocking collectives: 8.57 us -> 10.6 us  [on_device(): returned = lax.all_to_all(summed, ('y', 'c'), 0, 0, tiled=True)]
    pallas_call x8 -> x9, Pallas kernels: 13.3 us -> 12.8 us  [call(): pl.pallas_call(body, in_specs=[SMEM] * len(heads) + [HBM] * len(far) + [V...]
  transfers between devices with their start and end apart: 13 -> 18, of which waited for: 8 -> 9; matrix products, arithmetic and copies ran while one was open for 0% -> 0% of each run, Pallas kernels for 10% -> 11%
where the time goes in v4:
time: 132 us; the launch traced here: 131 us
  waiting for transfers between devices  43.7 us (33%)
  starting transfers between devices  34.5 us (26%)
  blocking collectives  27.7 us (21%)
  Pallas kernels  22 us (17%)
  local copies, waits for them, and re-layouts  2.01 us (2%)
    ppermute x17, waiting for transfers between devices, shift(): lax.ppermute(value, axis, [(i, (i + by) % size) for i in range(size)])  43.7 us
    ppermute x17, starting transfers between devices, shift(): lax.ppermute(value, axis, [(i, (i + by) % size) for i in range(size)])  28.8 us
    all_to_all x1, blocking collectives, on_device(): pieces = {0: lax.all_to_all(outbound, ('y', 'c', 'x'), 0, 0, tiled=True)}  17.1 us
    pallas_call x9, Pallas kernels, call(): pl.pallas_call(body, in_specs=[SMEM] * len(heads) + [HBM] * len(far) + [V...  12.8 us
    all_to_all x1, blocking collectives, on_device(): returned = lax.all_to_all(summed, ('y', 'c'), 0, 0, tiled=True)  10.6 us
    pallas_call x1, Pallas kernels, backward(): pl.pallas_call(backward_body, in_specs=[SMEM] + [HBM] * (4 + NZ), out_spe...  9.17 us
    all_to_all x1, starting transfers between devices, on_device(): gate_parts = lax.all_to_all(spread, ('x', 'z'), 0, 0, tiled=True)  5.65 us
  transfers between devices with their start and end apart: 18, of which 9 were waited for; matrix products, arithmetic and copies ran while one was open for 0% of the time, Pallas kernels for 11%

profile of v4, /device:TPU:8, one launch (start us, length us, event | category | flops | bytes accessed | tf_op | source)
XLA Modules:
  0.0 130.9 jit_solution(10118785748632521777)
XLA Ops:
  0.7 2.9 %forward_far.1 = (bf16[256,1024]{1,0:T(8,128)(2,1)S(1)}, bf16[256,1024]{1,0:T(8,128)(2,1)S(1)}) custom-call(s32[2]{0:T(128)S(1)} %pad_add_fusion.where_ref, bf16[448,1024]{1,0:T(8,128)(2,1)} %bitcast.33, s32[448,2048]{1,0:T(8,128)} %bitcast.29, f32[224,128]{1,0:T(8,128)} %bitcast.38), custom_call_target="tpu_custom_call" | custom-call | tf_op jit(solution)/shard_map/forward_far/pallas_call | solution.py:34
  3.7 1.6 %collective-permute-start = (bf16[256,1024]{1,0:T(8,128)(2,1)S(1)}, bf16[256,1024]{1,0:T(8,128)(2,1)S(1)}, u32[]{:S(2)}, u32[]{:S(2)}) collective-permute-start(bf16[256,1024]{1,0:T(8,128)(2,1)S(1)} %get-tuple-element.43), channel_id=1, source_target_pairs={{0,8},{8,16},{16,24},{24,0},{1,9},{9,17},{17,25},{25,1},{2,10},{10... | collective-permute-start | bytes 1572872 | tf_op jit(solution)/shard_map/ppermute | solution.py:322
  5.3 1.7 %collective-permute-start.1 = (bf16[256,1024]{1,0:T(8,128)(2,1)S(1)}, bf16[256,1024]{1,0:T(8,128)(2,1)S(1)}, u32[]{:S(2)}, u32[]{:S(2)}) collective-permute-start(bf16[256,1024]{1,0:T(8,128)(2,1)S(1)} %get-tuple-element.44), channel_id=1, source_target_pairs={{0,24},{8,0},{16,8},{24,16},{1,25},{9,1},{17,9},{25,17},{2,26},{10... | collective-permute-start | bytes 1572872 | tf_op jit(solution)/shard_map/ppermute | solution.py:322
  8.0 17.1 %all_to_all.15 = bf16[32,64,128]{2,1,0:T(8,128)(2,1)S(1)} all-to-all(bf16[32,64,128]{2,1,0:T(8,128)(2,1)S(1)} %get-tuple-element.45), channel_id=1, replica_groups=mesh['y'=4,'c'=2,'x'=4,'z'=8] {'y','c','x'}, dimensions={0} | all-to-all | bytes 1048576 | tf_op jit(solution)/shard_map/all_to_all | solution.py:335
  25.1 3.7 %forward_join.1 = (bf16[512,1024]{1,0:T(8,128)(2,1)S(1)}, bf16[512,1024]{1,0:T(8,128)(2,1)S(1)}) custom-call(s32[2]{0:T(128)S(1)} %pad_add_fusion.where_ref, bf16[448,1024]{1,0:T(8,128)(2,1)} %bitcast.34, s32[448,2048]{1,0:T(8,128)} %bitcast.30, f32[224,128]{1,0:T(8,128)} %bitcast.39, bf16[256,1024]{1,0:T(8,128)(2,1)S(1)} %collective-permute-done.top_ref, ...), custom_call_target="tpu_custom_call" | custom-call | tf_op jit(solution)/shard_map/forward_join/pallas_call | solution.py:34
  29.8 5.9 %collective-permute-start.4 = (bf16[32,64,128]{2,1,0:T(8,128)(2,1)S(1)}, bf16[32,64,128]{2,1,0:T(8,128)(2,1)S(1)}, u32[]{:S(2)}, u32[]{:S(2)}) collective-permute-start(bf16[32,64,128]{2,1,0:T(8,128)(2,1)S(1)} %all_to_all.15), channel_id=1, source_target_pairs={{0,7},{1,0},{2,1},{3,2},{4,3},{5,4},{6,5},{7,6},{8,15},{9,8},{10,9... | collective-permute-start | bytes 1572872 | tf_op jit(solution)/shard_map/ppermute | solution.py:322
  35.7 2.3 %collective-permute-start.3 = (bf16[512,1024]{1,0:T(8,128)(2,1)S(1)}, bf16[512,1024]{1,0:T(8,128)(2,1)S(1)}, u32[]{:S(2)}, u32[]{:S(2)}) collective-permute-start(bf16[512,1024]{1,0:T(8,128)(2,1)S(1)} %get-tuple-element.52), channel_id=1, source_target_pairs={{0,24},{8,0},{16,8},{24,16},{1,25},{9,1},{17,9},{25,17},{2,26},{10... | collective-permute-start | bytes 3145736 | tf_op jit(solution)/shard_map/ppermute | solution.py:322
  38.0 9.8 %collective-permute-done.4 = bf16[32,64,128]{2,1,0:T(8,128)(2,1)S(1)} collective-permute-done((bf16[32,64,128]{2,1,0:T(8,128)(2,1)S(1)}, bf16[32,64,128]{2,1,0:T(8,128)(2,1)S(1)}, u32[]{:S(2)}, u32[]{:S(2)}) %collective-permute-start.4) | collective-permute-done | bytes 524320 | tf_op jit(solution)/shard_map/ppermute | solution.py:322
  47.9 3.7 %collective-permute-start.5 = (bf16[32,64,128]{2,1,0:T(8,128)(2,1)S(1)}, bf16[32,64,128]{2,1,0:T(8,128)(2,1)S(1)}, u32[]{:S(2)}, u32[]{:S(2)}) collective-permute-start(bf16[32,64,128]{2,1,0:T(8,128)(2,1)S(1)} %collective-permute-done.4), channel_id=1, source_target_pairs={{0,7},{1,0},{2,1},{3,2},{4,3},{5,4},{6,5},{7,6},{8,15},{9,8},{10,9... | collective-permute-start | bytes 1572872 | tf_op jit(solution)/shard_map/ppermute | solution.py:322
  51.6 1.8 %collective-permute-done.6 = bf16[32,64,128]{2,1,0:T(8,128)(2,1)S(1)} collective-permute-done((bf16[32,64,128]{2,1,0:T(8,128)(2,1)S(1)}, bf16[32,64,128]{2,1,0:T(8,128)(2,1)S(1)}, u32[]{:S(2)}, u32[]{:S(2)}) %collective-permute-start.6) | collective-permute-done | bytes 524320 | tf_op jit(solution)/shard_map/ppermute | solution.py:322
  53.4 2.9 %forward_own.1.own_ref = f32[512,1024]{1,0:T(8,128)S(1)} custom-call(s32[2]{0:T(128)S(1)} %pad_add_fusion.where_ref, bf16[448,1024]{1,0:T(8,128)(2,1)} %bitcast.35, s32[448,2048]{1,0:T(8,128)} %bitcast.31, f32[224,128]{1,0:T(8,128)} %bitcast.40), custom_call_target="tpu_custom_call" | custom-call | tf_op jit(solution)/shard_map/forward_own/pallas_call | solution.py:34
  56.4 5.2 %collective-permute-done.3.down_ref = bf16[512,1024]{1,0:T(8,128)(2,1)S(1)} collective-permute-done((bf16[512,1024]{1,0:T(8,128)(2,1)S(1)}, bf16[512,1024]{1,0:T(8,128)(2,1)S(1)}, u32[]{:S(2)}, u32[]{:S(2)}) %collective-permute-start.3) | collective-permute-done | bytes 1048608 | tf_op jit(solution)/shard_map/ppermute | solution.py:322
  61.6 1.6 %collective-permute-done.5 = bf16[32,64,128]{2,1,0:T(8,128)(2,1)S(1)} collective-permute-done((bf16[32,64,128]{2,1,0:T(8,128)(2,1)S(1)}, bf16[32,64,128]{2,1,0:T(8,128)(2,1)S(1)}, u32[]{:S(2)}, u32[]{:S(2)}) %collective-permute-start.5) | collective-permute-done | bytes 524320 | tf_op jit(solution)/shard_map/ppermute | solution.py:322
  63.2 4.8 %collective-permute-done.7 = bf16[32,64,128]{2,1,0:T(8,128)(2,1)S(1)} collective-permute-done((bf16[32,64,128]{2,1,0:T(8,128)(2,1)S(1)}, bf16[32,64,128]{2,1,0:T(8,128)(2,1)S(1)}, u32[]{:S(2)}, u32[]{:S(2)}) %collective-permute-start.7) | collective-permute-done | bytes 524320 | tf_op jit(solution)/shard_map/ppermute | solution.py:322
  68.9 3.2 %collective-permute-start.9 = (bf16[2,64,1024]{2,1,0:T(8,128)(2,1)S(1)}, bf16[2,64,1024]{2,1,0:T(8,128)(2,1)S(1)}, u32[]{:S(2)}, u32[]{:S(2)}) collective-permute-start(bf16[2,64,1024]{2,1,0:T(8,128)(2,1)S(1)} %get-tuple-element.58), channel_id=1, source_target_pairs={{0,7},{1,0},{2,1},{3,2},{4,3},{5,4},{6,5},{7,6},{8,15},{9,8},{10,9... | collective-permute-start | bytes 786440 | tf_op jit(solution)/shard_map/ppermute | solution.py:322
  72.1 8.5 %collective-permute-done.10.far_ref = bf16[64,1024]{1,0:T(8,128)(2,1)S(1)} collective-permute-done((bf16[64,1024]{1,0:T(8,128)(2,1)S(1)}, bf16[64,1024]{1,0:T(8,128)(2,1)S(1)}, u32[]{:S(2)}, u32[]{:S(2)}) %collective-permute-start.10) | collective-permute-done | bytes 131104 | tf_op jit(solution)/shard_map/ppermute | solution.py:322
  82.2 2.0 %collective-permute-start.14 = (bf16[32,64,128]{2,1,0:T(8,128)(2,1)S(1)}, bf16[32,64,128]{2,1,0:T(8,128)(2,1)S(1)}, u32[]{:S(2)}, u32[]{:S(2)}) collective-permute-start(bf16[32,64,128]{2,1,0:T(8,128)(2,1)S(1)} %collective-permute-done.7), channel_id=1, source_target_pairs={{0,1},{1,2},{2,3},{3,4},{4,5},{5,6},{6,7},{7,0},{8,9},{9,10},{10,1... | collective-permute-start | bytes 1572872 | tf_op jit(solution)/shard_map/ppermute | solution.py:322
  84.2 1.4 %collective-permute-start.11 = (bf16[64,1024]{1,0:T(8,128)(2,1)S(1)}, bf16[64,1024]{1,0:T(8,128)(2,1)S(1)}, u32[]{:S(2)}, u32[]{:S(2)}) collective-permute-start(bf16[64,1024]{1,0:T(8,128)(2,1)S(1)} %get-tuple-element.65), channel_id=1, source_target_pairs={{0,2},{1,3},{2,4},{3,5},{4,6},{5,7},{6,0},{7,1},{8,10},{9,11},{10,... | collective-permute-start | bytes 393224 | tf_op jit(solution)/shard_map/ppermute | solution.py:322
  85.6 2.8 %collective-permute-start.12 = (bf16[64,1024]{1,0:T(8,128)(2,1)S(1)}, bf16[64,1024]{1,0:T(8,128)(2,1)S(1)}, u32[]{:S(2)}, u32[]{:S(2)}) collective-permute-start(bf16[64,1024]{1,0:T(8,128)(2,1)S(1)} %get-tuple-element.66), channel_id=1, source_target_pairs={{0,6},{1,7},{2,0},{3,1},{4,2},{5,3},{6,4},{7,5},{8,14},{9,15},{10,... | collective-permute-start | bytes 393224 | tf_op jit(solution)/shard_map/ppermute | solution.py:322
  88.4 10.2 %collective-permute-done.11.up_ref = bf16[64,1024]{1,0:T(8,128)(2,1)S(1)} collective-permute-done((bf16[64,1024]{1,0:T(8,128)(2,1)S(1)}, bf16[64,1024]{1,0:T(8,128)(2,1)S(1)}, u32[]{:S(2)}, u32[]{:S(2)}) %collective-permute-start.11) | collective-permute-done | bytes 131104 | tf_op jit(solution)/shard_map/ppermute | solution.py:322
  98.7 10.6 %all_to_all.16.back_ref = bf16[8,64,128]{2,1,0:T(8,128)(2,1)S(1)} all-to-all(bf16[8,64,128]{2,1,0:T(8,128)(2,1)S(1)} %z_sum.1), channel_id=1, replica_groups=mesh['y'=4,'c'=2,'x'=4,'z'=8] {'y','c'}, dimensions={0} | all-to-all | bytes 262144 | tf_op jit(solution)/shard_map/all_to_all | solution.py:357
  109.3 2.1 %collective-permute-start.15 = (bf16[16,64,128]{2,1,0:T(8,128)(2,1)S(1)}, bf16[16,64,128]{2,1,0:T(8,128)(2,1)S(1)}, u32[]{:S(2)}, u32[]{:S(2)}) collective-permute-start(bf16[16,64,128]{2,1,0:T(8,128)(2,1)S(1)} %slice.6), channel_id=1, source_target_pairs={{0,7},{1,0},{2,1},{3,2},{4,3},{5,4},{6,5},{7,6},{8,15},{9,8},{10,9... | collective-permute-start | bytes 786440 | tf_op jit(solution)/shard_map/ppermute | solution.py:322
  112.8 5.6 %all-to-all-start.2 = ((f32[32,8,128]{2,1,0:T(8,128)}), f32[32,8,128]{2,1,0:T(8,128)S(1)}, u32[]{:S(2)}, u32[]{:S(2)}) async-start(f32[32,8,128]{2,1,0:T(8,128)} %get-tuple-element.71), calls=%async_computation.2 | async-start | bytes 262144 | tf_op jit(solution)/shard_map/all_to_all | solution.py:361
  121.0 9.2 %backward.1 = (bf16[448,1024]{1,0:T(8,128)(2,1)}, f32[448,2048]{1,0:T(8,128)}, f32[224,128]{1,0:T(8,128)}) custom-call(s32[2]{0:T(128)S(1)} %pad_add_fusion.where_ref, bf16[448,1024]{1,0:T(8,128)(2,1)} %bitcast.36, s32[448,2048]{1,0:T(8,128)} %bitcast.32, f32[224,128]{1,0:T(8,128)} %bitcast.41, bf16[8,4,64,128]{3,2,1,0:T(8,128)(2,1)} %bitcast.37, ...), custom_call_target="tpu_custom_call" | custom-call | tf_op jit(solution)/shard_map/backward/pallas_call | solution.py:301
  (53 shorter events, 9.3 us)
Async XLA Ops:
  3.7 21.4 %collective-permute-start = (bf16[256,1024]{1,0:T(8,128)(2,1)S(1)}, bf16[256,1024]{1,0:T(8,128)(2,1)S(1)}, u32[]{:S(2)}, u32[]{:S(2)}) collective-permute-start(bf16[256,1024]{1,0:T(8,128)(2,1)S(1)} %get-tuple-element.43), channel_id=1, source_target_pairs={{0,8},{8,16},{16,24},{24,0},{1,9},{9,17},{17,25},{25,1},{2,10},{10... | collective-permute-start | bytes 1572872 | tf_op jit(solution)/shard_map/ppermute | solution.py:322
  5.3 19.9 %collective-permute-start.1 = (bf16[256,1024]{1,0:T(8,128)(2,1)S(1)}, bf16[256,1024]{1,0:T(8,128)(2,1)S(1)}, u32[]{:S(2)}, u32[]{:S(2)}) collective-permute-start(bf16[256,1024]{1,0:T(8,128)(2,1)S(1)} %get-tuple-element.44), channel_id=1, source_target_pairs={{0,24},{8,0},{16,8},{24,16},{1,25},{9,1},{17,9},{25,17},{2,26},{10... | collective-permute-start | bytes 1572872 | tf_op jit(solution)/shard_map/ppermute | solution.py:322
  25.1 31.2 %copy-start.3 = (bf16[32,64,128]{2,1,0:T(8,128)(2,1)}, bf16[32,64,128]{2,1,0:T(8,128)(2,1)S(1)}, u32[]{:S(2)}) copy-start(bf16[32,64,128]{2,1,0:T(8,128)(2,1)S(1)} %all_to_all.15) | copy-start | bytes 1572868
  28.9 27.5 %collective-permute-start.2 = (bf16[512,1024]{1,0:T(8,128)(2,1)S(1)}, bf16[512,1024]{1,0:T(8,128)(2,1)S(1)}, u32[]{:S(2)}, u32[]{:S(2)}) collective-permute-start(bf16[512,1024]{1,0:T(8,128)(2,1)S(1)} %get-tuple-element.51), channel_id=1, source_target_pairs={{0,8},{8,16},{16,24},{24,0},{1,9},{9,17},{17,25},{25,1},{2,10},{10... | collective-permute-start | bytes 3145736 | tf_op jit(solution)/shard_map/ppermute | solution.py:322
  29.8 18.0 %collective-permute-start.4 = (bf16[32,64,128]{2,1,0:T(8,128)(2,1)S(1)}, bf16[32,64,128]{2,1,0:T(8,128)(2,1)S(1)}, u32[]{:S(2)}, u32[]{:S(2)}) collective-permute-start(bf16[32,64,128]{2,1,0:T(8,128)(2,1)S(1)} %all_to_all.15), channel_id=1, source_target_pairs={{0,7},{1,0},{2,1},{3,2},{4,3},{5,4},{6,5},{7,6},{8,15},{9,8},{10,9... | collective-permute-start | bytes 1572872 | tf_op jit(solution)/shard_map/ppermute | solution.py:322
  35.7 25.9 %collective-permute-start.3 = (bf16[512,1024]{1,0:T(8,128)(2,1)S(1)}, bf16[512,1024]{1,0:T(8,128)(2,1)S(1)}, u32[]{:S(2)}, u32[]{:S(2)}) collective-permute-start(bf16[512,1024]{1,0:T(8,128)(2,1)S(1)} %get-tuple-element.52), channel_id=1, source_target_pairs={{0,24},{8,0},{16,8},{24,16},{1,25},{9,1},{17,9},{25,17},{2,26},{10... | collective-permute-start | bytes 3145736 | tf_op jit(solution)/shard_map/ppermute | solution.py:322
  38.0 15.3 %collective-permute-start.6 = (bf16[32,64,128]{2,1,0:T(8,128)(2,1)S(1)}, bf16[32,64,128]{2,1,0:T(8,128)(2,1)S(1)}, u32[]{:S(2)}, u32[]{:S(2)}) collective-permute-start(bf16[32,64,128]{2,1,0:T(8,128)(2,1)S(1)} %all_to_all.15), channel_id=1, source_target_pairs={{0,1},{1,2},{2,3},{3,4},{4,5},{5,6},{6,7},{7,0},{8,9},{9,10},{10,1... | collective-permute-start | bytes 1572872 | tf_op jit(solution)/shard_map/ppermute | solution.py:322
  47.9 20.9 %copy-start.6 = (bf16[32,64,128]{2,1,0:T(8,128)(2,1)}, bf16[32,64,128]{2,1,0:T(8,128)(2,1)S(1)}, u32[]{:S(2)}) copy-start(bf16[32,64,128]{2,1,0:T(8,128)(2,1)S(1)} %collective-permute-done.4) | copy-start | bytes 1572868
  47.9 15.3 %collective-permute-start.5 = (bf16[32,64,128]{2,1,0:T(8,128)(2,1)S(1)}, bf16[32,64,128]{2,1,0:T(8,128)(2,1)S(1)}, u32[]{:S(2)}, u32[]{:S(2)}) collective-permute-start(bf16[32,64,128]{2,1,0:T(8,128)(2,1)S(1)} %collective-permute-done.4), channel_id=1, source_target_pairs={{0,7},{1,0},{2,1},{3,2},{4,3},{5,4},{6,5},{7,6},{8,15},{9,8},{10,9... | collective-permute-start | bytes 1572872 | tf_op jit(solution)/shard_map/ppermute | solution.py:322
  53.4 15.4 %copy-start.7 = (bf16[32,64,128]{2,1,0:T(8,128)(2,1)}, bf16[32,64,128]{2,1,0:T(8,128)(2,1)S(1)}, u32[]{:S(2)}) copy-start(bf16[32,64,128]{2,1,0:T(8,128)(2,1)S(1)} %collective-permute-done.6) | copy-start | bytes 1572868
  53.4 14.5 %collective-permute-start.7 = (bf16[32,64,128]{2,1,0:T(8,128)(2,1)S(1)}, bf16[32,64,128]{2,1,0:T(8,128)(2,1)S(1)}, u32[]{:S(2)}, u32[]{:S(2)}) collective-permute-start(bf16[32,64,128]{2,1,0:T(8,128)(2,1)S(1)} %collective-permute-done.6), channel_id=1, source_target_pairs={{0,1},{1,2},{2,3},{3,4},{4,5},{5,6},{6,7},{7,0},{8,9},{9,10},{10,1... | collective-permute-start | bytes 1572872 | tf_op jit(solution)/shard_map/ppermute | solution.py:322
  63.2 46.1 %copy-start.8 = (bf16[32,64,128]{2,1,0:T(8,128)(2,1)}, bf16[32,64,128]{2,1,0:T(8,128)(2,1)S(1)}, u32[]{:S(2)}) copy-start(bf16[32,64,128]{2,1,0:T(8,128)(2,1)S(1)} %collective-permute-done.5) | copy-start | bytes 1572868
  67.9 41.4 %copy-start.9 = (bf16[32,64,128]{2,1,0:T(8,128)(2,1)}, bf16[32,64,128]{2,1,0:T(8,128)(2,1)S(1)}, u32[]{:S(2)}) copy-start(bf16[32,64,128]{2,1,0:T(8,128)(2,1)S(1)} %collective-permute-done.7) | copy-start | bytes 1572868
  68.8 12.3 %collective-permute-start.8 = (bf16[2,64,1024]{2,1,0:T(8,128)(2,1)S(1)}, bf16[2,64,1024]{2,1,0:T(8,128)(2,1)S(1)}, u32[]{:S(2)}, u32[]{:S(2)}) collective-permute-start(bf16[2,64,1024]{2,1,0:T(8,128)(2,1)S(1)} %get-tuple-element.57), channel_id=1, source_target_pairs={{0,1},{1,2},{2,3},{3,4},{4,5},{5,6},{6,7},{7,0},{8,9},{9,10},{10,1... | collective-permute-start | bytes 786440 | tf_op jit(solution)/shard_map/ppermute | solution.py:322
  68.9 12.2 %collective-permute-start.9 = (bf16[2,64,1024]{2,1,0:T(8,128)(2,1)S(1)}, bf16[2,64,1024]{2,1,0:T(8,128)(2,1)S(1)}, u32[]{:S(2)}, u32[]{:S(2)}) collective-permute-start(bf16[2,64,1024]{2,1,0:T(8,128)(2,1)S(1)} %get-tuple-element.58), channel_id=1, source_target_pairs={{0,7},{1,0},{2,1},{3,2},{4,3},{5,4},{6,5},{7,6},{8,15},{9,8},{10,9... | collective-permute-start | bytes 786440 | tf_op jit(solution)/shard_map/ppermute | solution.py:322
  72.1 8.5 %collective-permute-start.10 = (bf16[64,1024]{1,0:T(8,128)(2,1)S(1)}, bf16[64,1024]{1,0:T(8,128)(2,1)S(1)}, u32[]{:S(2)}, u32[]{:S(2)}) collective-permute-start(bf16[64,1024]{1,0:T(8,128)(2,1)S(1)} %get-tuple-element.61), channel_id=1, source_target_pairs={{0,2},{1,3},{2,4},{3,5},{4,6},{5,7},{6,0},{7,1},{8,10},{9,11},{10,... | collective-permute-start | bytes 393224 | tf_op jit(solution)/shard_map/ppermute | solution.py:322
  81.2 28.1 %collective-permute-start.13 = (bf16[32,64,128]{2,1,0:T(8,128)(2,1)S(1)}, bf16[32,64,128]{2,1,0:T(8,128)(2,1)S(1)}, u32[]{:S(2)}, u32[]{:S(2)}) collective-permute-start(bf16[32,64,128]{2,1,0:T(8,128)(2,1)S(1)} %collective-permute-done.5), channel_id=1, source_target_pairs={{0,7},{1,0},{2,1},{3,2},{4,3},{5,4},{6,5},{7,6},{8,15},{9,8},{10,9... | collective-permute-start | bytes 1572872 | tf_op jit(solution)/shard_map/ppermute | solution.py:322
  82.2 27.1 %collective-permute-start.14 = (bf16[32,64,128]{2,1,0:T(8,128)(2,1)S(1)}, bf16[32,64,128]{2,1,0:T(8,128)(2,1)S(1)}, u32[]{:S(2)}, u32[]{:S(2)}) collective-permute-start(bf16[32,64,128]{2,1,0:T(8,128)(2,1)S(1)} %collective-permute-done.7), channel_id=1, source_target_pairs={{0,1},{1,2},{2,3},{3,4},{4,5},{5,6},{6,7},{7,0},{8,9},{9,10},{10,1... | collective-permute-start | bytes 1572872 | tf_op jit(solution)/shard_map/ppermute | solution.py:322
  84.2 14.3 %collective-permute-start.11 = (bf16[64,1024]{1,0:T(8,128)(2,1)S(1)}, bf16[64,1024]{1,0:T(8,128)(2,1)S(1)}, u32[]{:S(2)}, u32[]{:S(2)}) collective-permute-start(bf16[64,1024]{1,0:T(8,128)(2,1)S(1)} %get-tuple-element.65), channel_id=1, source_target_pairs={{0,2},{1,3},{2,4},{3,5},{4,6},{5,7},{6,0},{7,1},{8,10},{9,11},{10,... | collective-permute-start | bytes 393224 | tf_op jit(solution)/shard_map/ppermute | solution.py:322
  85.6 13.0 %collective-permute-start.12 = (bf16[64,1024]{1,0:T(8,128)(2,1)S(1)}, bf16[64,1024]{1,0:T(8,128)(2,1)S(1)}, u32[]{:S(2)}, u32[]{:S(2)}) collective-permute-start(bf16[64,1024]{1,0:T(8,128)(2,1)S(1)} %get-tuple-element.66), channel_id=1, source_target_pairs={{0,6},{1,7},{2,0},{3,1},{4,2},{5,3},{6,4},{7,5},{8,14},{9,15},{10,... | collective-permute-start | bytes 393224 | tf_op jit(solution)/shard_map/ppermute | solution.py:322
  109.3 11.1 %copy-start.4 = (bf16[32,64,128]{2,1,0:T(8,128)(2,1)}, bf16[32,64,128]{2,1,0:T(8,128)(2,1)S(1)}, u32[]{:S(2)}) copy-start(bf16[32,64,128]{2,1,0:T(8,128)(2,1)S(1)} %collective-permute-done.13) | copy-start | bytes 1572868
  109.3 9.7 %collective-permute-start.15 = (bf16[16,64,128]{2,1,0:T(8,128)(2,1)S(1)}, bf16[16,64,128]{2,1,0:T(8,128)(2,1)S(1)}, u32[]{:S(2)}, u32[]{:S(2)}) collective-permute-start(bf16[16,64,128]{2,1,0:T(8,128)(2,1)S(1)} %slice.6), channel_id=1, source_target_pairs={{0,7},{1,0},{2,1},{3,2},{4,3},{5,4},{6,5},{7,6},{8,15},{9,8},{10,9... | collective-permute-start | bytes 786440 | tf_op jit(solution)/shard_map/ppermute | solution.py:322
  111.5 8.9 %collective-permute-start.16 = (bf16[16,64,128]{2,1,0:T(8,128)(2,1)S(1)}, bf16[16,64,128]{2,1,0:T(8,128)(2,1)S(1)}, u32[]{:S(2)}, u32[]{:S(2)}) collective-permute-start(bf16[16,64,128]{2,1,0:T(8,128)(2,1)S(1)} %slice.7), channel_id=1, source_target_pairs={{0,1},{1,2},{2,3},{3,4},{4,5},{5,6},{6,7},{7,0},{8,9},{9,10},{10,1... | collective-permute-start | bytes 786440 | tf_op jit(solution)/shard_map/ppermute | solution.py:322
  112.8 17.5 %all-to-all-start.2 = ((f32[32,8,128]{2,1,0:T(8,128)}), f32[32,8,128]{2,1,0:T(8,128)S(1)}, u32[]{:S(2)}, u32[]{:S(2)}) async-start(f32[32,8,128]{2,1,0:T(8,128)} %get-tuple-element.71), calls=%async_computation.2 | async-start | bytes 262144 | tf_op jit(solution)/shard_map/all_to_all | solution.py:361
  (6 other events, 32.2 us)

commit v5 on v4

--- a/solution.py
+++ b/solution.py
@@ -328,34 +328,35 @@
     where = jnp.stack([lax.axis_index("x"), lax.axis_index("z")]).astype(I32)
 
     far_top, far_bottom = forward_far(where, *weights)
+    where_late, index, far_top, far_bottom = lax.optimization_barrier((where, index, far_top, far_bottom))
     far_top = shift(far_top, "x", 1)
     far_bottom = shift(far_bottom, "x", -1)
-
+    own = forward_own(where_late, *weights)
     place, outbound = slot_grads(index, gate, grad)
+    far_top, far_bottom, own, outbound = lax.optimization_barrier((far_top, far_bottom, own, outbound))
+    up, down = forward_join(where, *weights, far_top, far_bottom)
+    up, down, outbound = lax.optimization_barrier((up, down, outbound))
+    up = shift(up, "x", 1)
+    down = shift(down, "x", -1)
+
     pieces = {0: lax.all_to_all(outbound, ("y", "c", "x"), 0, 0, tiled=True)}
 
     def turn(hop):
         pieces[hop] = shift(pieces[hop - 1], "z", -1)
         pieces[NZ - hop] = shift(pieces[(NZ - hop + 1) % NZ], "z", 1)
 
-    far_top, far_bottom, pieces[0] = lax.optimization_barrier((far_top, far_bottom, pieces[0]))
-    up, down = forward_join(where, *weights, far_top, far_bottom)
-    where_late, up, down = lax.optimization_barrier((where, up, down))
-    up = shift(up, "x", 1)
-    down = shift(down, "x", -1)
-    own = forward_own(where_late, *weights)
     turn(1)
-    turn(2)
-    up, down, pieces[2], pieces[6] = lax.optimization_barrier((up, down, pieces[2], pieces[6]))
+    up, down, _ = lax.optimization_barrier((up, down, pieces[0]))
 
     ups, downs, far, up2, down2, rest = x_sum(where, own, up, down)
     ups, downs, far = shift(ups, "z", 1), shift(downs, "z", -1), shift(far, "z", 2)
     up2, down2 = mid_sum(up2, down2, ups, downs, far)
-    up2, pieces[2], pieces[6] = lax.optimization_barrier((up2, pieces[2], pieces[6]))
+    up2, down2, pieces[1], pieces[7] = lax.optimization_barrier((up2, down2, pieces[1], pieces[7]))
+    turn(2)
+    up2, down2 = shift(up2, "z", 2), shift(down2, "z", -2)
+    up2, down2, pieces[2], pieces[6] = lax.optimization_barrier((up2, down2, pieces[2], pieces[6]))
     turn(3)
-    summed = z_sum(rest, ups, downs, shift(up2, "z", 2), shift(down2, "z", -2))
-    returned = lax.all_to_all(summed, ("y", "c"), 0, 0, tiled=True)
-    returned, pieces[3], pieces[5] = lax.optimization_barrier((returned, pieces[3], pieces[5]))
+    returned = lax.all_to_all(z_sum(rest, ups, downs, up2, down2), ("y", "c"), 0, 0, tiled=True)
     last = [shift(pieces[3][: EXPERTS * NX // 2], "z", -1), shift(pieces[5][EXPERTS * NX // 2 :], "z", 1)]
     combined, spread = combine(place, gate, grad, returned)
     gate_parts = lax.all_to_all(spread, ("x", "z"), 0, 0, tiled=True)

time: 132 us -> 143 us (1.083)
  starting transfers between devices: 34.5 us -> 39.4 us
  waiting for transfers between devices: 43.7 us -> 47.7 us
    all_to_all x1, blocking collectives: 17.1 us -> 28.5 us  [on_device(): pieces = {0: lax.all_to_all(outbound, ('y', 'c', 'x'), 0, 0, tiled=True)}]
    all_to_all x1 -> x0, blocking collectives: 10.6 us -> none  [on_device(): returned = lax.all_to_all(summed, ('y', 'c'), 0, 0, tiled=True)]
    all_to_all x0 -> x1, starting transfers between devices: none -> 4.55 us  [on_device(): lax.all_to_all(z_sum(rest, ups, downs, up2, down2), ('y', 'c'), 0, 0, til...]
    ppermute x17, waiting for transfers between devices: 43.7 us -> 47.7 us  [shift(): lax.ppermute(value, axis, [(i, (i + by) % size) for i in range(size)])]
  transfers between devices with their start and end apart: 18 -> 19, of which waited for: 9 -> 6; matrix products, arithmetic and copies ran while one was open for 0% -> 1% of each run, Pallas kernels for 11% -> 11%
where the time goes in v5:
time: 143 us; the launch traced here: 142 us
  waiting for transfers between devices  47.7 us (33%)
  starting transfers between devices  39.4 us (28%)
  blocking collectives  28.5 us (20%)
  Pallas kernels  22.7 us (16%)
  local copies, waits for them, and re-layouts  2.75 us (2%)
    ppermute x17, waiting for transfers between devices, shift(): lax.ppermute(value, axis, [(i, (i + by) % size) for i in range(size)])  47.7 us
    ppermute x17, starting transfers between devices, shift(): lax.ppermute(value, axis, [(i, (i + by) % size) for i in range(size)])  29.5 us
    all_to_all x1, blocking collectives, on_device(): pieces = {0: lax.all_to_all(outbound, ('y', 'c', 'x'), 0, 0, tiled=True)}  28.5 us
    pallas_call x9, Pallas kernels, call(): pl.pallas_call(body, in_specs=[SMEM] * len(heads) + [HBM] * len(far) + [V...  13.5 us
    pallas_call x1, Pallas kernels, backward(): pl.pallas_call(backward_body, in_specs=[SMEM] + [HBM] * (4 + NZ), out_spe...  9.17 us
    all_to_all x1, starting transfers between devices, on_device(): gate_parts = lax.all_to_all(spread, ('x', 'z'), 0, 0, tiled=True)  5.37 us
    all_to_all x1, starting transfers between devices, on_device(): lax.all_to_all(z_sum(rest, ups, downs, up2, down2), ('y', 'c'), 0, 0, til...  4.55 us
  transfers between devices with their start and end apart: 19, of which 6 were waited for; matrix products, arithmetic and copies ran while one was open for 1% of the time, Pallas kernels for 11%

profile of v5, /device:TPU:8, one launch (start us, length us, event | category | flops | bytes accessed | tf_op | source)
XLA Modules:
  0.0 141.9 jit_solution(6283112086328422446)
XLA Ops:
  0.7 2.9 %forward_far.1 = (bf16[256,1024]{1,0:T(8,128)(2,1)S(1)}, bf16[256,1024]{1,0:T(8,128)(2,1)S(1)}) custom-call(s32[2]{0:T(128)S(1)} %pad_add_fusion.where_ref, bf16[448,1024]{1,0:T(8,128)(2,1)} %bitcast.33, s32[448,2048]{1,0:T(8,128)} %bitcast.29, f32[224,128]{1,0:T(8,128)} %bitcast.38), custom_call_target="tpu_custom_call" | custom-call | tf_op jit(solution)/shard_map/forward_far/pallas_call | solution.py:34
  3.7 1.6 %collective-permute-start = (bf16[256,1024]{1,0:T(8,128)(2,1)S(1)}, bf16[256,1024]{1,0:T(8,128)(2,1)S(1)}, u32[]{:S(2)}, u32[]{:S(2)}) collective-permute-start(bf16[256,1024]{1,0:T(8,128)(2,1)S(1)} %get-tuple-element.51), channel_id=1, source_target_pairs={{0,8},{8,16},{16,24},{24,0},{1,9},{9,17},{17,25},{25,1},{2,10},{10... | collective-permute-start | bytes 1572872 | tf_op jit(solution)/shard_map/ppermute | solution.py:322
  5.3 1.7 %collective-permute-start.1 = (bf16[256,1024]{1,0:T(8,128)(2,1)S(1)}, bf16[256,1024]{1,0:T(8,128)(2,1)S(1)}, u32[]{:S(2)}, u32[]{:S(2)}) collective-permute-start(bf16[256,1024]{1,0:T(8,128)(2,1)S(1)} %get-tuple-element.52), channel_id=1, source_target_pairs={{0,24},{8,0},{16,8},{24,16},{1,25},{9,1},{17,9},{25,17},{2,26},{10... | collective-permute-start | bytes 1572872 | tf_op jit(solution)/shard_map/ppermute | solution.py:322
  7.0 2.9 %forward_own.1.own_ref = f32[512,1024]{1,0:T(8,128)S(1)} custom-call(s32[2]{0:T(128)S(1)} %pad_add_fusion.where_ref, bf16[448,1024]{1,0:T(8,128)(2,1)} %bitcast.34, s32[448,2048]{1,0:T(8,128)} %bitcast.30, f32[224,128]{1,0:T(8,128)} %bitcast.39), custom_call_target="tpu_custom_call" | custom-call | tf_op jit(solution)/shard_map/forward_own/pallas_call | solution.py:34
  10.0 1.0 slot_grads.1
  11.0 7.7 %collective-permute-done.top_ref = bf16[256,1024]{1,0:T(8,128)(2,1)S(1)} collective-permute-done((bf16[256,1024]{1,0:T(8,128)(2,1)S(1)}, bf16[256,1024]{1,0:T(8,128)(2,1)S(1)}, u32[]{:S(2)}, u32[]{:S(2)}) %collective-permute-start) | collective-permute-done | bytes 524320 | tf_op jit(solution)/shard_map/ppermute | solution.py:322
  18.7 3.7 %forward_join.1 = (bf16[512,1024]{1,0:T(8,128)(2,1)S(1)}, bf16[512,1024]{1,0:T(8,128)(2,1)S(1)}) custom-call(s32[2]{0:T(128)S(1)} %pad_add_fusion.where_ref, bf16[448,1024]{1,0:T(8,128)(2,1)} %bitcast.35, s32[448,2048]{1,0:T(8,128)} %bitcast.31, f32[224,128]{1,0:T(8,128)} %bitcast.40, bf16[256,1024]{1,0:T(8,128)(2,1)S(1)} %collective-permute-done.top_ref, ...), custom_call_target="tpu_custom_call" | custom-call | tf_op jit(solution)/shard_map/forward_join/pallas_call | solution.py:34
  22.4 1.6 %collective-permute-start.2 = (bf16[512,1024]{1,0:T(8,128)(2,1)S(1)}, bf16[512,1024]{1,0:T(8,128)(2,1)S(1)}, u32[]{:S(2)}, u32[]{:S(2)}) collective-permute-start(bf16[512,1024]{1,0:T(8,128)(2,1)S(1)} %get-tuple-element.61), channel_id=1, source_target_pairs={{0,8},{8,16},{16,24},{24,0},{1,9},{9,17},{17,25},{25,1},{2,10},{10... | collective-permute-start | bytes 3145736 | tf_op jit(solution)/shard_map/ppermute | solution.py:322
  24.0 1.7 %collective-permute-start.3 = (bf16[512,1024]{1,0:T(8,128)(2,1)S(1)}, bf16[512,1024]{1,0:T(8,128)(2,1)S(1)}, u32[]{:S(2)}, u32[]{:S(2)}) collective-permute-start(bf16[512,1024]{1,0:T(8,128)(2,1)S(1)} %get-tuple-element.62), channel_id=1, source_target_pairs={{0,24},{8,0},{16,8},{24,16},{1,25},{9,1},{17,9},{25,17},{2,26},{10... | collective-permute-start | bytes 3145736 | tf_op jit(solution)/shard_map/ppermute | solution.py:322
  25.7 28.5 %all_to_all.15 = bf16[32,64,128]{2,1,0:T(8,128)(2,1)S(1)} all-to-all(bf16[32,64,128]{2,1,0:T(8,128)(2,1)S(1)} %get-tuple-element.63), channel_id=1, replica_groups=mesh['y'=4,'c'=2,'x'=4,'z'=8] {'y','c','x'}, dimensions={0} | all-to-all | bytes 1048576 | tf_op jit(solution)/shard_map/all_to_all | solution.py:342
  54.2 1.9 %collective-permute-start.8 = (bf16[32,64,128]{2,1,0:T(8,128)(2,1)S(1)}, bf16[32,64,128]{2,1,0:T(8,128)(2,1)S(1)}, u32[]{:S(2)}, u32[]{:S(2)}) collective-permute-start(bf16[32,64,128]{2,1,0:T(8,128)(2,1)S(1)} %all_to_all.15), channel_id=1, source_target_pairs={{0,1},{1,2},{2,3},{3,4},{4,5},{5,6},{6,7},{7,0},{8,9},{9,10},{10,1... | collective-permute-start | bytes 1572872 | tf_op jit(solution)/shard_map/ppermute | solution.py:322
  56.1 3.9 %collective-permute-start.7 = (bf16[32,64,128]{2,1,0:T(8,128)(2,1)S(1)}, bf16[32,64,128]{2,1,0:T(8,128)(2,1)S(1)}, u32[]{:S(2)}, u32[]{:S(2)}) collective-permute-start(bf16[32,64,128]{2,1,0:T(8,128)(2,1)S(1)} %all_to_all.15), channel_id=1, source_target_pairs={{0,7},{1,0},{2,1},{3,2},{4,3},{5,4},{6,5},{7,6},{8,15},{9,8},{10,9... | collective-permute-start | bytes 1572872 | tf_op jit(solution)/shard_map/ppermute | solution.py:322
  61.0 3.2 %collective-permute-start.5 = (bf16[2,64,1024]{2,1,0:T(8,128)(2,1)S(1)}, bf16[2,64,1024]{2,1,0:T(8,128)(2,1)S(1)}, u32[]{:S(2)}, u32[]{:S(2)}) collective-permute-start(bf16[2,64,1024]{2,1,0:T(8,128)(2,1)S(1)} %get-tuple-element.68), channel_id=1, source_target_pairs={{0,7},{1,0},{2,1},{3,2},{4,3},{5,4},{6,5},{7,6},{8,15},{9,8},{10,9... | collective-permute-start | bytes 786440 | tf_op jit(solution)/shard_map/ppermute | solution.py:322
  64.2 19.0 %collective-permute-done.6.far_ref = bf16[64,1024]{1,0:T(8,128)(2,1)S(1)} collective-permute-done((bf16[64,1024]{1,0:T(8,128)(2,1)S(1)}, bf16[64,1024]{1,0:T(8,128)(2,1)S(1)}, u32[]{:S(2)}, u32[]{:S(2)}) %collective-permute-start.6) | collective-permute-done | bytes 131104 | tf_op jit(solution)/shard_map/ppermute | solution.py:322
  83.3 3.3 %collective-permute-start.11 = (bf16[32,64,128]{2,1,0:T(8,128)(2,1)S(1)}, bf16[32,64,128]{2,1,0:T(8,128)(2,1)S(1)}, u32[]{:S(2)}, u32[]{:S(2)}) collective-permute-start(bf16[32,64,128]{2,1,0:T(8,128)(2,1)S(1)} %collective-permute-done.7), channel_id=1, source_target_pairs={{0,7},{1,0},{2,1},{3,2},{4,3},{5,4},{6,5},{7,6},{8,15},{9,8},{10,9... | collective-permute-start | bytes 1572872 | tf_op jit(solution)/shard_map/ppermute | solution.py:322
  86.9 3.9 %collective-permute-start.10 = (bf16[64,1024]{1,0:T(8,128)(2,1)S(1)}, bf16[64,1024]{1,0:T(8,128)(2,1)S(1)}, u32[]{:S(2)}, u32[]{:S(2)}) collective-permute-start(bf16[64,1024]{1,0:T(8,128)(2,1)S(1)} %get-tuple-element.75), channel_id=1, source_target_pairs={{0,6},{1,7},{2,0},{3,1},{4,2},{5,3},{6,4},{7,5},{8,14},{9,15},{10,... | collective-permute-start | bytes 393224 | tf_op jit(solution)/shard_map/ppermute | solution.py:322
  90.8 14.1 %collective-permute-done.9.up_ref = bf16[64,1024]{1,0:T(8,128)(2,1)S(1)} collective-permute-done((bf16[64,1024]{1,0:T(8,128)(2,1)S(1)}, bf16[64,1024]{1,0:T(8,128)(2,1)S(1)}, u32[]{:S(2)}, u32[]{:S(2)}) %collective-permute-start.9) | collective-permute-done | bytes 131104 | tf_op jit(solution)/shard_map/ppermute | solution.py:322
  105.6 3.1 %collective-permute-start.13 = (bf16[32,64,128]{2,1,0:T(8,128)(2,1)S(1)}, bf16[32,64,128]{2,1,0:T(8,128)(2,1)S(1)}, u32[]{:S(2)}, u32[]{:S(2)}) collective-permute-start(bf16[32,64,128]{2,1,0:T(8,128)(2,1)S(1)} %collective-permute-done.11), channel_id=1, source_target_pairs={{0,7},{1,0},{2,1},{3,2},{4,3},{5,4},{6,5},{7,6},{8,15},{9,8},{10,9... | collective-permute-start | bytes 1572872 | tf_op jit(solution)/shard_map/ppermute | solution.py:322
  109.5 4.6 %all-to-all-start.1 = ((bf16[8,64,128]{2,1,0:T(8,128)(2,1)}), bf16[8,64,128]{2,1,0:T(8,128)(2,1)S(1)}, u32[]{:S(2)}, u32[]{:S(2)}) async-start(bf16[8,64,128]{2,1,0:T(8,128)(2,1)} %z_sum.1), calls=%async_computation.1 | async-start | bytes 262144 | tf_op jit(solution)/shard_map/all_to_all | solution.py:359
  114.1 5.7 %collective-permute-done.13 = bf16[32,64,128]{2,1,0:T(8,128)(2,1)S(1)} collective-permute-done((bf16[32,64,128]{2,1,0:T(8,128)(2,1)S(1)}, bf16[32,64,128]{2,1,0:T(8,128)(2,1)S(1)}, u32[]{:S(2)}, u32[]{:S(2)}) %collective-permute-start.13) | collective-permute-done | bytes 524320 | tf_op jit(solution)/shard_map/ppermute | solution.py:322
  120.5 2.9 %collective-permute-start.14 = (bf16[16,64,128]{2,1,0:T(8,128)(2,1)}, bf16[16,64,128]{2,1,0:T(8,128)(2,1)}, u32[]{:S(2)}, u32[]{:S(2)}) collective-permute-start(bf16[16,64,128]{2,1,0:T(8,128)(2,1)} %slice.8), channel_id=1, source_target_pairs={{0,7},{1,0},{2,1},{3,2},{4,3},{5,4},{6,5},{7,6},{8,15},{9,8},{10,9... | collective-permute-start | bytes 786440 | tf_op jit(solution)/shard_map/ppermute | solution.py:322
  123.6 1.2 combine.1
  124.8 5.4 %all-to-all-start.2 = ((f32[32,8,128]{2,1,0:T(8,128)}), f32[32,8,128]{2,1,0:T(8,128)S(1)}, u32[]{:S(2)}, u32[]{:S(2)}) async-start(f32[32,8,128]{2,1,0:T(8,128)} %get-tuple-element.81), calls=%async_computation.2 | async-start | bytes 262144 | tf_op jit(solution)/shard_map/all_to_all | solution.py:362
  132.1 9.2 %backward.1 = (bf16[448,1024]{1,0:T(8,128)(2,1)}, f32[448,2048]{1,0:T(8,128)}, f32[224,128]{1,0:T(8,128)}) custom-call(s32[2]{0:T(128)S(1)} %pad_add_fusion.where_ref, bf16[448,1024]{1,0:T(8,128)(2,1)} %bitcast.36, s32[448,2048]{1,0:T(8,128)} %bitcast.32, f32[224,128]{1,0:T(8,128)} %bitcast.41, bf16[8,4,64,128]{3,2,1,0:T(8,128)(2,1)} %bitcast.37, ...), custom_call_target="tpu_custom_call" | custom-call | tf_op jit(solution)/shard_map/backward/pallas_call | solution.py:301
  (50 shorter events, 6.4 us)
Async XLA Ops:
  3.7 15.0 %collective-permute-start = (bf16[256,1024]{1,0:T(8,128)(2,1)S(1)}, bf16[256,1024]{1,0:T(8,128)(2,1)S(1)}, u32[]{:S(2)}, u32[]{:S(2)}) collective-permute-start(bf16[256,1024]{1,0:T(8,128)(2,1)S(1)} %get-tuple-element.51), channel_id=1, source_target_pairs={{0,8},{8,16},{16,24},{24,0},{1,9},{9,17},{17,25},{25,1},{2,10},{10... | collective-permute-start | bytes 1572872 | tf_op jit(solution)/shard_map/ppermute | solution.py:322
  5.3 13.4 %collective-permute-start.1 = (bf16[256,1024]{1,0:T(8,128)(2,1)S(1)}, bf16[256,1024]{1,0:T(8,128)(2,1)S(1)}, u32[]{:S(2)}, u32[]{:S(2)}) collective-permute-start(bf16[256,1024]{1,0:T(8,128)(2,1)S(1)} %get-tuple-element.52), channel_id=1, source_target_pairs={{0,24},{8,0},{16,8},{24,16},{1,25},{9,1},{17,9},{25,17},{2,26},{10... | collective-permute-start | bytes 1572872 | tf_op jit(solution)/shard_map/ppermute | solution.py:322
  22.4 37.6 %collective-permute-start.2 = (bf16[512,1024]{1,0:T(8,128)(2,1)S(1)}, bf16[512,1024]{1,0:T(8,128)(2,1)S(1)}, u32[]{:S(2)}, u32[]{:S(2)}) collective-permute-start(bf16[512,1024]{1,0:T(8,128)(2,1)S(1)} %get-tuple-element.61), channel_id=1, source_target_pairs={{0,8},{8,16},{16,24},{24,0},{1,9},{9,17},{17,25},{25,1},{2,10},{10... | collective-permute-start | bytes 3145736 | tf_op jit(solution)/shard_map/ppermute | solution.py:322
  24.0 36.1 %collective-permute-start.3 = (bf16[512,1024]{1,0:T(8,128)(2,1)S(1)}, bf16[512,1024]{1,0:T(8,128)(2,1)S(1)}, u32[]{:S(2)}, u32[]{:S(2)}) collective-permute-start(bf16[512,1024]{1,0:T(8,128)(2,1)S(1)} %get-tuple-element.62), channel_id=1, source_target_pairs={{0,24},{8,0},{16,8},{24,16},{1,25},{9,1},{17,9},{25,17},{2,26},{10... | collective-permute-start | bytes 3145736 | tf_op jit(solution)/shard_map/ppermute | solution.py:322
  54.2 66.4 %copy-start.3 = (bf16[32,64,128]{2,1,0:T(8,128)(2,1)}, bf16[32,64,128]{2,1,0:T(8,128)(2,1)S(1)}, u32[]{:S(2)}) copy-start(bf16[32,64,128]{2,1,0:T(8,128)(2,1)S(1)} %all_to_all.15) | copy-start | bytes 1572868
  54.2 29.1 %collective-permute-start.8 = (bf16[32,64,128]{2,1,0:T(8,128)(2,1)S(1)}, bf16[32,64,128]{2,1,0:T(8,128)(2,1)S(1)}, u32[]{:S(2)}, u32[]{:S(2)}) collective-permute-start(bf16[32,64,128]{2,1,0:T(8,128)(2,1)S(1)} %all_to_all.15), channel_id=1, source_target_pairs={{0,1},{1,2},{2,3},{3,4},{4,5},{5,6},{6,7},{7,0},{8,9},{9,10},{10,1... | collective-permute-start | bytes 1572872 | tf_op jit(solution)/shard_map/ppermute | solution.py:322
  56.1 27.2 %collective-permute-start.7 = (bf16[32,64,128]{2,1,0:T(8,128)(2,1)S(1)}, bf16[32,64,128]{2,1,0:T(8,128)(2,1)S(1)}, u32[]{:S(2)}, u32[]{:S(2)}) collective-permute-start(bf16[32,64,128]{2,1,0:T(8,128)(2,1)S(1)} %all_to_all.15), channel_id=1, source_target_pairs={{0,7},{1,0},{2,1},{3,2},{4,3},{5,4},{6,5},{7,6},{8,15},{9,8},{10,9... | collective-permute-start | bytes 1572872 | tf_op jit(solution)/shard_map/ppermute | solution.py:322
  60.9 22.3 %collective-permute-start.4 = (bf16[2,64,1024]{2,1,0:T(8,128)(2,1)S(1)}, bf16[2,64,1024]{2,1,0:T(8,128)(2,1)S(1)}, u32[]{:S(2)}, u32[]{:S(2)}) collective-permute-start(bf16[2,64,1024]{2,1,0:T(8,128)(2,1)S(1)} %get-tuple-element.67), channel_id=1, source_target_pairs={{0,1},{1,2},{2,3},{3,4},{4,5},{5,6},{6,7},{7,0},{8,9},{9,10},{10,1... | collective-permute-start | bytes 786440 | tf_op jit(solution)/shard_map/ppermute | solution.py:322
  61.0 22.2 %collective-permute-start.5 = (bf16[2,64,1024]{2,1,0:T(8,128)(2,1)S(1)}, bf16[2,64,1024]{2,1,0:T(8,128)(2,1)S(1)}, u32[]{:S(2)}, u32[]{:S(2)}) collective-permute-start(bf16[2,64,1024]{2,1,0:T(8,128)(2,1)S(1)} %get-tuple-element.68), channel_id=1, source_target_pairs={{0,7},{1,0},{2,1},{3,2},{4,3},{5,4},{6,5},{7,6},{8,15},{9,8},{10,9... | collective-permute-start | bytes 786440 | tf_op jit(solution)/shard_map/ppermute | solution.py:322
  64.2 19.0 %collective-permute-start.6 = (bf16[64,1024]{1,0:T(8,128)(2,1)S(1)}, bf16[64,1024]{1,0:T(8,128)(2,1)S(1)}, u32[]{:S(2)}, u32[]{:S(2)}) collective-permute-start(bf16[64,1024]{1,0:T(8,128)(2,1)S(1)} %get-tuple-element.71), channel_id=1, source_target_pairs={{0,2},{1,3},{2,4},{3,5},{4,6},{5,7},{6,0},{7,1},{8,10},{9,11},{10,... | collective-permute-start | bytes 393224 | tf_op jit(solution)/shard_map/ppermute | solution.py:322
  83.3 48.1 %copy-start.6 = (bf16[32,64,128]{2,1,0:T(8,128)(2,1)}, bf16[32,64,128]{2,1,0:T(8,128)(2,1)S(1)}, u32[]{:S(2)}) copy-start(bf16[32,64,128]{2,1,0:T(8,128)(2,1)S(1)} %collective-permute-done.8) | copy-start | bytes 1572868
  83.3 48.1 %copy-start.7 = (bf16[32,64,128]{2,1,0:T(8,128)(2,1)}, bf16[32,64,128]{2,1,0:T(8,128)(2,1)S(1)}, u32[]{:S(2)}) copy-start(bf16[32,64,128]{2,1,0:T(8,128)(2,1)S(1)} %collective-permute-done.7) | copy-start | bytes 1572868
  83.3 21.6 %collective-permute-start.11 = (bf16[32,64,128]{2,1,0:T(8,128)(2,1)S(1)}, bf16[32,64,128]{2,1,0:T(8,128)(2,1)S(1)}, u32[]{:S(2)}, u32[]{:S(2)}) collective-permute-start(bf16[32,64,128]{2,1,0:T(8,128)(2,1)S(1)} %collective-permute-done.7), channel_id=1, source_target_pairs={{0,7},{1,0},{2,1},{3,2},{4,3},{5,4},{6,5},{7,6},{8,15},{9,8},{10,9... | collective-permute-start | bytes 1572872 | tf_op jit(solution)/shard_map/ppermute | solution.py:322
  86.6 18.9 %collective-permute-start.12 = (bf16[32,64,128]{2,1,0:T(8,128)(2,1)S(1)}, bf16[32,64,128]{2,1,0:T(8,128)(2,1)}, u32[]{:S(2)}, u32[]{:S(2)}) collective-permute-start(bf16[32,64,128]{2,1,0:T(8,128)(2,1)S(1)} %collective-permute-done.8), channel_id=1, source_target_pairs={{0,1},{1,2},{2,3},{3,4},{4,5},{5,6},{6,7},{7,0},{8,9},{9,10},{10,1... | collective-permute-start | bytes 1572872 | tf_op jit(solution)/shard_map/ppermute | solution.py:322
  86.6 18.2 %collective-permute-start.9 = (bf16[64,1024]{1,0:T(8,128)(2,1)S(1)}, bf16[64,1024]{1,0:T(8,128)(2,1)S(1)}, u32[]{:S(2)}, u32[]{:S(2)}) collective-permute-start(bf16[64,1024]{1,0:T(8,128)(2,1)S(1)} %get-tuple-element.74), channel_id=1, source_target_pairs={{0,2},{1,3},{2,4},{3,5},{4,6},{5,7},{6,0},{7,1},{8,10},{9,11},{10,... | collective-permute-start | bytes 393224 | tf_op jit(solution)/shard_map/ppermute | solution.py:322
  86.9 18.0 %collective-permute-start.10 = (bf16[64,1024]{1,0:T(8,128)(2,1)S(1)}, bf16[64,1024]{1,0:T(8,128)(2,1)S(1)}, u32[]{:S(2)}, u32[]{:S(2)}) collective-permute-start(bf16[64,1024]{1,0:T(8,128)(2,1)S(1)} %get-tuple-element.75), channel_id=1, source_target_pairs={{0,6},{1,7},{2,0},{3,1},{4,2},{5,3},{6,4},{7,5},{8,14},{9,15},{10,... | collective-permute-start | bytes 393224 | tf_op jit(solution)/shard_map/ppermute | solution.py:322
  104.9 26.5 %copy-start.8 = (bf16[32,64,128]{2,1,0:T(8,128)(2,1)}, bf16[32,64,128]{2,1,0:T(8,128)(2,1)S(1)}, u32[]{:S(2)}) copy-start(bf16[32,64,128]{2,1,0:T(8,128)(2,1)S(1)} %collective-permute-done.11) | copy-start | bytes 1572868
  105.6 14.2 %collective-permute-start.13 = (bf16[32,64,128]{2,1,0:T(8,128)(2,1)S(1)}, bf16[32,64,128]{2,1,0:T(8,128)(2,1)S(1)}, u32[]{:S(2)}, u32[]{:S(2)}) collective-permute-start(bf16[32,64,128]{2,1,0:T(8,128)(2,1)S(1)} %collective-permute-done.11), channel_id=1, source_target_pairs={{0,7},{1,0},{2,1},{3,2},{4,3},{5,4},{6,5},{7,6},{8,15},{9,8},{10,9... | collective-permute-start | bytes 1572872 | tf_op jit(solution)/shard_map/ppermute | solution.py:322
  108.7 14.8 %collective-permute-start.15 = (bf16[32,64,128]{2,1,0:T(8,128)(2,1)}, bf16[32,64,128]{2,1,0:T(8,128)(2,1)S(1)}, u32[]{:S(2)}, u32[]{:S(2)}) collective-permute-start(bf16[32,64,128]{2,1,0:T(8,128)(2,1)} %collective-permute-done.12), channel_id=1, source_target_pairs={{0,1},{1,2},{2,3},{3,4},{4,5},{5,6},{6,7},{7,0},{8,9},{9,10},{10,1... | collective-permute-start | bytes 1572872 | tf_op jit(solution)/shard_map/ppermute | solution.py:322
  109.5 14.1 %all-to-all-start.1 = ((bf16[8,64,128]{2,1,0:T(8,128)(2,1)}), bf16[8,64,128]{2,1,0:T(8,128)(2,1)S(1)}, u32[]{:S(2)}, u32[]{:S(2)}) async-start(bf16[8,64,128]{2,1,0:T(8,128)(2,1)} %z_sum.1), calls=%async_computation.1 | async-start | bytes 262144 | tf_op jit(solution)/shard_map/all_to_all | solution.py:359
  119.7 11.7 %copy-start.4 = (bf16[32,64,128]{2,1,0:T(8,128)(2,1)}, bf16[32,64,128]{2,1,0:T(8,128)(2,1)S(1)}, u32[]{:S(2)}) copy-start(bf16[32,64,128]{2,1,0:T(8,128)(2,1)S(1)} %collective-permute-done.13) | copy-start | bytes 1572868
  120.5 10.3 %collective-permute-start.14 = (bf16[16,64,128]{2,1,0:T(8,128)(2,1)}, bf16[16,64,128]{2,1,0:T(8,128)(2,1)}, u32[]{:S(2)}, u32[]{:S(2)}) collective-permute-start(bf16[16,64,128]{2,1,0:T(8,128)(2,1)} %slice.8), channel_id=1, source_target_pairs={{0,7},{1,0},{2,1},{3,2},{4,3},{5,4},{6,5},{7,6},{8,15},{9,8},{10,9... | collective-permute-start | bytes 786440 | tf_op jit(solution)/shard_map/ppermute | solution.py:322
  123.5 7.9 %collective-permute-start.16 = (bf16[16,64,128]{2,1,0:T(8,128)(2,1)S(1)}, bf16[16,64,128]{2,1,0:T(8,128)(2,1)S(1)}, u32[]{:S(2)}, u32[]{:S(2)}) collective-permute-start(bf16[16,64,128]{2,1,0:T(8,128)(2,1)S(1)} %slice.9), channel_id=1, source_target_pairs={{0,1},{1,2},{2,3},{3,4},{4,5},{5,6},{6,7},{7,0},{8,9},{9,10},{10,1... | collective-permute-start | bytes 786440 | tf_op jit(solution)/shard_map/ppermute | solution.py:322
  124.8 16.5 %all-to-all-start.2 = ((f32[32,8,128]{2,1,0:T(8,128)}), f32[32,8,128]{2,1,0:T(8,128)S(1)}, u32[]{:S(2)}, u32[]{:S(2)}) async-start(f32[32,8,128]{2,1,0:T(8,128)} %get-tuple-element.81), calls=%async_computation.2 | async-start | bytes 262144 | tf_op jit(solution)/shard_map/all_to_all | solution.py:362
  (5 other events, 27.5 us)

commit v6 on v5

--- a/solution.py
+++ b/solution.py
@@ -79,12 +79,11 @@
         total = piece if total is None else total + piece
     total = total.astype(BF16)
     for e in range(EXPERTS):
-        for x in range(NX):
-            out_ref[e * NX + x] = total[:, e * CAP : (e + 1) * CAP]
+        out_ref[e] = total[:, e * CAP : (e + 1) * CAP]
 
 
 def slot_grads(index, gate, grad):
-    outs = [(index.shape, I32), ((EXPERTS * NX, COLS, CAP), BF16)]
+    outs = [(index.shape, I32), ((EXPERTS, COLS, CAP), BF16)]
     return call(slot_body, "slot_grads", None, [index, gate, grad], outs)
 
 
@@ -233,28 +232,42 @@
     return call(gate_sum_body, "gate_sum", None, [parts], [((2, 512), F32)])[0]
 
 
+NEAREST = (0, 1, 7, 2, 6, 3, 5, 4)
+
+
+def pack_body(*refs):
+    for i, k in enumerate(NEAREST):
+        refs[-1][k] = refs[i][...]
+
+
+def pack(*pieces):
+    return call(pack_body, "pack", None, pieces, [((NZ, EXPERTS, COLS, CAP), BF16)])[0]
+
+
+SIDES = (0, 1, 3, 2)
+
+
 def backward_body(where_ref, hidden_hbm, codes_hbm, scales_hbm, *rest):
-    pieces = rest[: NZ + 1]
-    hidden_out, weight_out, scale_out = rest[NZ + 1 : NZ + 4]
-    hidden, codes, scales, grads, table, weight, sems = rest[NZ + 4 :]
+    packs = rest[: NX + 1]
+    hidden_out, weight_out, scale_out = rest[NX + 1 : NX + 4]
+    hidden, codes, scales, grads, table, weight, sems = rest[NX + 4 :]
     units = hidden.shape[0]
     tiles = BLOCK // 128
+    x_of = [lax.rem(where_ref[0] + side, NX) for side in SIDES]
+    lanes_of = [pl.ds(pl.multiple_of(x * BLOCK, BLOCK), BLOCK) for x in x_of]
     head = [
         pltpu.make_async_copy(hidden_hbm, hidden, sems.at[0]),
         pltpu.make_async_copy(scales_hbm, scales, sems.at[1]),
     ]
     parts, arrive = [], []
     for n in range(NX):
-        lanes = slice(n * BLOCK, (n + 1) * BLOCK)
-        parts.append(pltpu.make_async_copy(codes_hbm.at[:, lanes], codes.at[n], sems.at[2 + n]))
+        parts.append(pltpu.make_async_copy(codes_hbm.at[:, lanes_of[n]], codes.at[n], sems.at[2 + n]))
         arrive.append([])
-        for k in range(NZ + 1):
-            z = lax.rem(where_ref[1] + (k if k < NZ else 4), NZ)
+        for k in range(NZ):
+            z = lax.rem(where_ref[1] + k, NZ)
             rows = pl.ds(pl.multiple_of(n * BLOCK + z * COLS, COLS), COLS)
-            first = EXPERTS - pieces[k].shape[0] if k == NZ else 0
-            groups = slice(first, first + pieces[k].shape[0])
-            sem = sems.at[8 + n * (NZ + 1) + k]
-            arrive[n].append(pltpu.make_async_copy(pieces[k].at[:, n], grads.at[groups, rows], sem))
+            source = packs[n].at[k] if n < NX - 1 else packs[n + k // 4].at[k % 4]
+            arrive[n].append(pltpu.make_async_copy(source, grads.at[:, rows], sems.at[8 + n * NZ + k]))
     head[0].start()
     for copy in arrive[0]:
         copy.start()
@@ -268,39 +281,38 @@
     head[1].wait()
     copies = []
     for n in range(NX):
-        lanes = slice(n * BLOCK, (n + 1) * BLOCK)
+        rows_here = slice(n * BLOCK, (n + 1) * BLOCK)
         for copy in arrive[n]:
             copy.wait()
-        block = jnp.concatenate([grads[g, lanes, :] for g in range(EXPERTS)], axis=1)
+        block = jnp.concatenate([grads[g, rows_here, :] for g in range(EXPERTS)], axis=1)
         slot = n % 2
         if n >= 2:
             copies[n - 2].wait()
         weight[slot] = lax.dot_general(
             hidden[...], block, (((1,), (1,)), ((), ())), preferred_element_type=F32
         )
-        copies.append(pltpu.make_async_copy(weight.at[slot], weight_out.at[:, lanes], sems.at[6 + slot]))
+        copies.append(pltpu.make_async_copy(weight.at[slot], weight_out.at[:, lanes_of[n]], sems.at[6 + slot]))
         copies[n].start()
         parts[n].wait()
-        dequant(codes.at[n], scales, n * tiles, table.at[:, lanes])
+        dequant(codes.at[n], scales, x_of[n] * tiles, table.at[:, rows_here])
         for g in range(units // GROUP):
             rows = slice(g * GROUP, (g + 1) * GROUP)
             line = jnp.sum(weight[slot, rows, :] * codes[n, rows, :].astype(F32), axis=0, keepdims=True)
             for j in range(tiles):
-                row = (g * NX + n) * tiles + j
-                scale_out[row : row + 1, :] = line[:, j * 128 : (j + 1) * 128]
+                row = (g * NX + x_of[n]) * tiles + j
+                scale_out[pl.ds(row, 1), :] = line[:, j * 128 : (j + 1) * 128]
     block = jnp.concatenate([grads[g] for g in range(EXPERTS)], axis=1)
     hidden_out[...] = jnp.dot(table[...], block, preferred_element_type=F32).astype(BF16)
     copies[2].wait()
     copies[3].wait()
 
 
-def backward(where, hidden, codes, scales, pieces):
+def backward(where, hidden, codes, scales, packs):
     units, slots = hidden.shape
     features = codes.shape[1]
-    pieces = [a.reshape(-1, NX, COLS, CAP) for a in pieces]
     return pl.pallas_call(
         backward_body,
-        in_specs=[SMEM] + [HBM] * (4 + NZ),
+        in_specs=[SMEM] + [HBM] * (4 + NX),
         out_specs=[VMEM, HBM, VMEM],
         out_shape=[sds((units, slots), BF16), sds((units, features), F32), sds(scales.shape, F32)],
         scratch_shapes=[
@@ -310,11 +322,11 @@
             pltpu.VMEM((EXPERTS, features, CAP), BF16),
             pltpu.VMEM((units, features), BF16),
             pltpu.VMEM((2, units, BLOCK), F32),
-            pltpu.SemaphoreType.DMA((8 + NX * (NZ + 1),)),
+            pltpu.SemaphoreType.DMA((8 + NX * NZ,)),
         ],
         compiler_params=LARGE,
         name="backward",
-    )(where, *[away(a) for a in (hidden, codes, scales, *pieces)])
+    )(where, *[away(a) for a in (hidden, codes, scales, *packs)])
 
 
 def shift(value, axis, by):
@@ -328,40 +340,32 @@
     where = jnp.stack([lax.axis_index("x"), lax.axis_index("z")]).astype(I32)
 
     far_top, far_bottom = forward_far(where, *weights)
-    where_late, index, far_top, far_bottom = lax.optimization_barrier((where, index, far_top, far_bottom))
     far_top = shift(far_top, "x", 1)
     far_bottom = shift(far_bottom, "x", -1)
-    own = forward_own(where_late, *weights)
+
     place, outbound = slot_grads(index, gate, grad)
-    far_top, far_bottom, own, outbound = lax.optimization_barrier((far_top, far_bottom, own, outbound))
+    shard = lax.all_to_all(outbound, ("y", "c"), 0, 0, tiled=True)
+    far_top, far_bottom, shard = lax.optimization_barrier((far_top, far_bottom, shard))
     up, down = forward_join(where, *weights, far_top, far_bottom)
-    up, down, outbound = lax.optimization_barrier((up, down, outbound))
+    where_late, up, down, shard = lax.optimization_barrier((where, up, down, shard))
     up = shift(up, "x", 1)
     down = shift(down, "x", -1)
-
-    pieces = {0: lax.all_to_all(outbound, ("y", "c", "x"), 0, 0, tiled=True)}
-
-    def turn(hop):
-        pieces[hop] = shift(pieces[hop - 1], "z", -1)
-        pieces[NZ - hop] = shift(pieces[(NZ - hop + 1) % NZ], "z", 1)
-
-    turn(1)
-    up, down, _ = lax.optimization_barrier((up, down, pieces[0]))
+    own = forward_own(where_late, *weights)
+    along = [shift(shard, "z", -k) for k in NEAREST[1:]]
 
     ups, downs, far, up2, down2, rest = x_sum(where, own, up, down)
+    rest, *along = lax.optimization_barrier((rest, *along))
+    mine = pack(shard, *along)
+    packs = [mine, shift(mine, "x", -1), shift(mine, "x", 1)]
     ups, downs, far = shift(ups, "z", 1), shift(downs, "z", -1), shift(far, "z", 2)
     up2, down2 = mid_sum(up2, down2, ups, downs, far)
-    up2, down2, pieces[1], pieces[7] = lax.optimization_barrier((up2, down2, pieces[1], pieces[7]))
-    turn(2)
     up2, down2 = shift(up2, "z", 2), shift(down2, "z", -2)
-    up2, down2, pieces[2], pieces[6] = lax.optimization_barrier((up2, down2, pieces[2], pieces[6]))
-    turn(3)
+    up2, down2, packs[1], packs[2] = lax.optimization_barrier((up2, down2, packs[1], packs[2]))
+    packs += [shift(packs[1][: NZ // 2], "x", -1), shift(packs[2][NZ // 2 :], "x", 1)]
     returned = lax.all_to_all(z_sum(rest, ups, downs, up2, down2), ("y", "c"), 0, 0, tiled=True)
-    last = [shift(pieces[3][: EXPERTS * NX // 2], "z", -1), shift(pieces[5][EXPERTS * NX // 2 :], "z", 1)]
     combined, spread = combine(place, gate, grad, returned)
     gate_parts = lax.all_to_all(spread, ("x", "z"), 0, 0, tiled=True)
-    ordered = [pieces[k] if k != 4 else last[0] for k in range(NZ)] + [last[1]]
-    hidden_grad, weight_grad, scale_grad = backward(where, *weights, ordered)
+    hidden_grad, weight_grad, scale_grad = backward(where, *weights, packs)
     gate_parts, hidden_grad = lax.optimization_barrier((gate_parts, hidden_grad))
     gate_grad = gate_sum(gate_parts)
     return combined.T, gate_grad.T, hidden_grad[None], weight_grad[None], scale_grad.reshape(group_scales.shape)

time: 143 us -> 119 us (0.83)
  waiting for transfers between devices: 47.7 us -> 26.2 us
  blocking collectives: 28.5 us -> 18.6 us
  starting transfers between devices: 39.4 us -> 46.6 us
    ppermute x17 -> x20, waiting for transfers between devices: 47.7 us -> 25.7 us  [shift(): lax.ppermute(value, axis, [(i, (i + by) % size) for i in range(size)])]
    ppermute x17 -> x20, starting transfers between devices: 29.5 us -> 40.8 us  [shift(): lax.ppermute(value, axis, [(i, (i + by) % size) for i in range(size)])]
    all_to_all x1 -> x2, blocking collectives: 28.5 us -> 18.6 us  [the longest x1 9.39 us: on_device(): shard = lax.all_to_all(outbound, ('y', 'c'), 0, 0, tiled=True)]
    all_to_all x1 -> x0, starting transfers between devices: 4.55 us -> none  [on_device(): lax.all_to_all(z_sum(rest, ups, downs, up2, down2), ('y', 'c'), 0, 0, til...]
    pallas_call x9 -> x10, Pallas kernels: 13.5 us -> 12.9 us  [call(): pl.pallas_call(body, in_specs=[SMEM] * len(heads) + [HBM] * len(far) + [V...]
  transfers between devices with their start and end apart: 19 -> 21, of which waited for: 6 -> 6; matrix products, arithmetic and copies ran while one was open for 1% -> 1% of each run, Pallas kernels for 11% -> 13%
where the time goes in v6:
time: 119 us; the launch traced here: 117 us
  starting transfers between devices  46.6 us (39%)
  waiting for transfers between devices  26.2 us (22%)
  Pallas kernels  22 us (18%)
  blocking collectives  18.6 us (16%)
  local copies, waits for them, and re-layouts  2.99 us (3%)
    ppermute x20, starting transfers between devices, shift(): lax.ppermute(value, axis, [(i, (i + by) % size) for i in range(size)])  40.8 us
    ppermute x20, waiting for transfers between devices, shift(): lax.ppermute(value, axis, [(i, (i + by) % size) for i in range(size)])  25.7 us
    pallas_call x10, Pallas kernels, call(): pl.pallas_call(body, in_specs=[SMEM] * len(heads) + [HBM] * len(far) + [V...  12.9 us
    all_to_all x1, blocking collectives, on_device(): shard = lax.all_to_all(outbound, ('y', 'c'), 0, 0, tiled=True)  9.39 us
    all_to_all x1, blocking collectives, on_device(): lax.all_to_all(z_sum(rest, ups, downs, up2, down2), ('y', 'c'), 0, 0, til...  9.19 us
    pallas_call x1, Pallas kernels, backward(): pl.pallas_call(backward_body, in_specs=[SMEM] + [HBM] * (4 + NX), out_spe...  9.14 us
    all_to_all x1, starting transfers between devices, on_device(): gate_parts = lax.all_to_all(spread, ('x', 'z'), 0, 0, tiled=True)  5.82 us
  transfers between devices with their start and end apart: 21, of which 6 were waited for; matrix products, arithmetic and copies ran while one was open for 1% of the time, Pallas kernels for 13%

profile of v6, /device:TPU:8, one launch (start us, length us, event | category | flops | bytes accessed | tf_op | source)
XLA Modules:
  0.0 117.3 jit_solution(15882375756905242471)
XLA Ops:
  0.7 2.9 %forward_far.1 = (bf16[256,1024]{1,0:T(8,128)(2,1)S(1)}, bf16[256,1024]{1,0:T(8,128)(2,1)S(1)}) custom-call(s32[2]{0:T(128)S(1)} %pad_add_fusion.where_ref, bf16[448,1024]{1,0:T(8,128)(2,1)} %bitcast.24, s32[448,2048]{1,0:T(8,128)} %bitcast.20, f32[224,128]{1,0:T(8,128)} %bitcast.28), custom_call_target="tpu_custom_call" | custom-call | tf_op jit(solution)/shard_map/forward_far/pallas_call | solution.py:34
  3.7 1.6 %collective-permute-start = (bf16[256,1024]{1,0:T(8,128)(2,1)S(1)}, bf16[256,1024]{1,0:T(8,128)(2,1)S(1)}, u32[]{:S(2)}, u32[]{:S(2)}) collective-permute-start(bf16[256,1024]{1,0:T(8,128)(2,1)S(1)} %get-tuple-element.46), channel_id=1, source_target_pairs={{0,8},{8,16},{16,24},{24,0},{1,9},{9,17},{17,25},{25,1},{2,10},{10... | collective-permute-start | bytes 1572872 | tf_op jit(solution)/shard_map/ppermute | solution.py:334
  5.3 1.7 %collective-permute-start.1 = (bf16[256,1024]{1,0:T(8,128)(2,1)S(1)}, bf16[256,1024]{1,0:T(8,128)(2,1)S(1)}, u32[]{:S(2)}, u32[]{:S(2)}) collective-permute-start(bf16[256,1024]{1,0:T(8,128)(2,1)S(1)} %get-tuple-element.47), channel_id=1, source_target_pairs={{0,24},{8,0},{16,8},{24,16},{1,25},{9,1},{17,9},{25,17},{2,26},{10... | collective-permute-start | bytes 1572872 | tf_op jit(solution)/shard_map/ppermute | solution.py:334
  8.0 9.4 %all_to_all.15.refs_0_ = bf16[8,64,128]{2,1,0:T(8,128)(2,1)S(1)} all-to-all(bf16[8,64,128]{2,1,0:T(8,128)(2,1)S(1)} %get-tuple-element.48), channel_id=1, replica_groups=mesh['y'=4,'c'=2,'x'=4,'z'=8] {'y','c'}, dimensions={0} | all-to-all | bytes 262144 | tf_op jit(solution)/shard_map/all_to_all | solution.py:347
  18.7 3.7 %forward_join.1 = (bf16[512,1024]{1,0:T(8,128)(2,1)S(1)}, bf16[512,1024]{1,0:T(8,128)(2,1)S(1)}) custom-call(s32[2]{0:T(128)S(1)} %pad_add_fusion.where_ref, bf16[448,1024]{1,0:T(8,128)(2,1)} %bitcast.25, s32[448,2048]{1,0:T(8,128)} %bitcast.21, f32[224,128]{1,0:T(8,128)} %bitcast.29, bf16[256,1024]{1,0:T(8,128)(2,1)S(1)} %collective-permute-done.top_ref, ...), custom_call_target="tpu_custom_call" | custom-call | tf_op jit(solution)/shard_map/forward_join/pallas_call | solution.py:34
  22.4 1.6 %collective-permute-start.2 = (bf16[512,1024]{1,0:T(8,128)(2,1)S(1)}, bf16[512,1024]{1,0:T(8,128)(2,1)S(1)}, u32[]{:S(2)}, u32[]{:S(2)}) collective-permute-start(bf16[512,1024]{1,0:T(8,128)(2,1)S(1)} %get-tuple-element.55), channel_id=1, source_target_pairs={{0,8},{8,16},{16,24},{24,0},{1,9},{9,17},{17,25},{25,1},{2,10},{10... | collective-permute-start | bytes 3145736 | tf_op jit(solution)/shard_map/ppermute | solution.py:334
  24.0 1.7 %collective-permute-start.3 = (bf16[512,1024]{1,0:T(8,128)(2,1)S(1)}, bf16[512,1024]{1,0:T(8,128)(2,1)S(1)}, u32[]{:S(2)}, u32[]{:S(2)}) collective-permute-start(bf16[512,1024]{1,0:T(8,128)(2,1)S(1)} %get-tuple-element.56), channel_id=1, source_target_pairs={{0,24},{8,0},{16,8},{24,16},{1,25},{9,1},{17,9},{25,17},{2,26},{10... | collective-permute-start | bytes 3145736 | tf_op jit(solution)/shard_map/ppermute | solution.py:334
  25.7 7.2 %collective-permute-start.10 = (bf16[8,64,128]{2,1,0:T(8,128)(2,1)S(1)}, bf16[8,64,128]{2,1,0:T(8,128)(2,1)S(1)}, u32[]{:S(2)}, u32[]{:S(2)}) collective-permute-start(bf16[8,64,128]{2,1,0:T(8,128)(2,1)S(1)} %all_to_all.15.refs_0_), channel_id=1, source_target_pairs={{0,4},{1,5},{2,6},{3,7},{4,0},{5,1},{6,2},{7,3},{8,12},{9,13},{10,... | collective-permute-start | bytes 393224 | tf_op jit(solution)/shard_map/ppermute | solution.py:334
  32.9 1.9 %collective-permute-start.9 = (bf16[8,64,128]{2,1,0:T(8,128)(2,1)S(1)}, bf16[8,64,128]{2,1,0:T(8,128)(2,1)S(1)}, u32[]{:S(2)}, u32[]{:S(2)}) collective-permute-start(bf16[8,64,128]{2,1,0:T(8,128)(2,1)S(1)} %all_to_all.15.refs_0_), channel_id=1, source_target_pairs={{0,3},{1,4},{2,5},{3,6},{4,7},{5,0},{6,1},{7,2},{8,11},{9,12},{10,... | collective-permute-start | bytes 393224 | tf_op jit(solution)/shard_map/ppermute | solution.py:334
  34.8 3.1 %collective-permute-start.8 = (bf16[8,64,128]{2,1,0:T(8,128)(2,1)S(1)}, bf16[8,64,128]{2,1,0:T(8,128)(2,1)S(1)}, u32[]{:S(2)}, u32[]{:S(2)}) collective-permute-start(bf16[8,64,128]{2,1,0:T(8,128)(2,1)S(1)} %all_to_all.15.refs_0_), channel_id=1, source_target_pairs={{0,5},{1,6},{2,7},{3,0},{4,1},{5,2},{6,3},{7,4},{8,13},{9,14},{10,... | collective-permute-start | bytes 393224 | tf_op jit(solution)/shard_map/ppermute | solution.py:334
  37.9 4.6 %collective-permute-done.10.refs_7_ = bf16[8,64,128]{2,1,0:T(8,128)(2,1)S(1)} collective-permute-done((bf16[8,64,128]{2,1,0:T(8,128)(2,1)S(1)}, bf16[8,64,128]{2,1,0:T(8,128)(2,1)S(1)}, u32[]{:S(2)}, u32[]{:S(2)}) %collective-permute-start.10) | collective-permute-done | bytes 131104 | tf_op jit(solution)/shard_map/ppermute | solution.py:334
  42.6 5.1 %collective-permute-done.9.refs_6_ = bf16[8,64,128]{2,1,0:T(8,128)(2,1)S(1)} collective-permute-done((bf16[8,64,128]{2,1,0:T(8,128)(2,1)S(1)}, bf16[8,64,128]{2,1,0:T(8,128)(2,1)S(1)}, u32[]{:S(2)}, u32[]{:S(2)}) %collective-permute-start.9) | collective-permute-done | bytes 131104 | tf_op jit(solution)/shard_map/ppermute | solution.py:334
  47.7 4.3 %collective-permute-start.6 = (bf16[8,64,128]{2,1,0:T(8,128)(2,1)S(1)}, bf16[8,64,128]{2,1,0:T(8,128)(2,1)S(1)}, u32[]{:S(2)}, u32[]{:S(2)}) collective-permute-start(bf16[8,64,128]{2,1,0:T(8,128)(2,1)S(1)} %all_to_all.15.refs_0_), channel_id=1, source_target_pairs={{0,6},{1,7},{2,0},{3,1},{4,2},{5,3},{6,4},{7,5},{8,14},{9,15},{10,... | collective-permute-start | bytes 393224 | tf_op jit(solution)/shard_map/ppermute | solution.py:334
  52.0 3.2 %collective-permute-start.4 = (bf16[8,64,128]{2,1,0:T(8,128)(2,1)S(1)}, bf16[8,64,128]{2,1,0:T(8,128)(2,1)S(1)}, u32[]{:S(2)}, u32[]{:S(2)}) collective-permute-start(bf16[8,64,128]{2,1,0:T(8,128)(2,1)S(1)} %all_to_all.15.refs_0_), channel_id=1, source_target_pairs={{0,7},{1,0},{2,1},{3,2},{4,3},{5,4},{6,5},{7,6},{8,15},{9,8},{10,9... | collective-permute-start | bytes 393224 | tf_op jit(solution)/shard_map/ppermute | solution.py:334
  55.2 2.9 %forward_own.1.own_ref = f32[512,1024]{1,0:T(8,128)S(1)} custom-call(s32[2]{0:T(128)S(1)} %pad_add_fusion.where_ref, bf16[448,1024]{1,0:T(8,128)(2,1)} %bitcast.26, s32[448,2048]{1,0:T(8,128)} %bitcast.22, f32[224,128]{1,0:T(8,128)} %bitcast.30), custom_call_target="tpu_custom_call" | custom-call | tf_op jit(solution)/shard_map/forward_own/pallas_call | solution.py:34
  59.4 3.2 %collective-permute-start.16 = (bf16[8,8,64,128]{3,2,1,0:T(8,128)(2,1)S(1)}, bf16[8,8,64,128]{3,2,1,0:T(8,128)(2,1)S(1)}, u32[]{:S(2)}, u32[]{:S(2)}) collective-permute-start(bf16[8,8,64,128]{3,2,1,0:T(8,128)(2,1)S(1)} %pack.1.rest_0_), channel_id=1, source_target_pairs={{0,24},{8,0},{16,8},{24,16},{1,25},{9,1},{17,9},{25,17},{2,26},{10... | collective-permute-start | bytes 3145736 | tf_op jit(solution)/shard_map/ppermute | solution.py:334
  62.6 3.2 %collective-permute-start.12 = (bf16[2,64,1024]{2,1,0:T(8,128)(2,1)S(1)}, bf16[2,64,1024]{2,1,0:T(8,128)(2,1)S(1)}, u32[]{:S(2)}, u32[]{:S(2)}) collective-permute-start(bf16[2,64,1024]{2,1,0:T(8,128)(2,1)S(1)} %get-tuple-element.61), channel_id=1, source_target_pairs={{0,7},{1,0},{2,1},{3,2},{4,3},{5,4},{6,5},{7,6},{8,15},{9,8},{10,9... | collective-permute-start | bytes 786440 | tf_op jit(solution)/shard_map/ppermute | solution.py:334
  66.1 11.5 %collective-permute-done.13.far_ref = bf16[64,1024]{1,0:T(8,128)(2,1)S(1)} collective-permute-done((bf16[64,1024]{1,0:T(8,128)(2,1)S(1)}, bf16[64,1024]{1,0:T(8,128)(2,1)S(1)}, u32[]{:S(2)}, u32[]{:S(2)}) %collective-permute-start.13) | collective-permute-done | bytes 131104 | tf_op jit(solution)/shard_map/ppermute | solution.py:334
  77.8 4.1 %collective-permute-start.15 = (bf16[64,1024]{1,0:T(8,128)(2,1)S(1)}, bf16[64,1024]{1,0:T(8,128)(2,1)S(1)}, u32[]{:S(2)}, u32[]{:S(2)}) collective-permute-start(bf16[64,1024]{1,0:T(8,128)(2,1)S(1)} %get-tuple-element.66), channel_id=1, source_target_pairs={{0,6},{1,7},{2,0},{3,1},{4,2},{5,3},{6,4},{7,5},{8,14},{9,15},{10,... | collective-permute-start | bytes 393224 | tf_op jit(solution)/shard_map/ppermute | solution.py:334
  81.9 3.2 %collective-permute-done.14.up_ref = bf16[64,1024]{1,0:T(8,128)(2,1)S(1)} collective-permute-done((bf16[64,1024]{1,0:T(8,128)(2,1)S(1)}, bf16[64,1024]{1,0:T(8,128)(2,1)S(1)}, u32[]{:S(2)}, u32[]{:S(2)}) %collective-permute-start.14) | collective-permute-done | bytes 131104 | tf_op jit(solution)/shard_map/ppermute | solution.py:334
  86.9 3.2 %collective-permute-start.18 = (bf16[4,8,64,128]{3,2,1,0:T(8,128)(2,1)}, bf16[4,8,64,128]{3,2,1,0:T(8,128)(2,1)}, u32[]{:S(2)}, u32[]{:S(2)}) collective-permute-start(bf16[4,8,64,128]{3,2,1,0:T(8,128)(2,1)} %slice.6), channel_id=1, source_target_pairs={{0,24},{8,0},{16,8},{24,16},{1,25},{9,1},{17,9},{25,17},{2,26},{10... | collective-permute-start | bytes 1572872 | tf_op jit(solution)/shard_map/ppermute | solution.py:334
  90.2 9.2 %all_to_all.16.back_ref = bf16[8,64,128]{2,1,0:T(8,128)(2,1)S(1)} all-to-all(bf16[8,64,128]{2,1,0:T(8,128)(2,1)S(1)} %z_sum.1), channel_id=1, replica_groups=mesh['y'=4,'c'=2,'x'=4,'z'=8] {'y','c'}, dimensions={0} | all-to-all | bytes 262144 | tf_op jit(solution)/shard_map/all_to_all | solution.py:365
  100.6 5.8 %all-to-all-start.2 = ((f32[32,8,128]{2,1,0:T(8,128)}), f32[32,8,128]{2,1,0:T(8,128)S(1)}, u32[]{:S(2)}, u32[]{:S(2)}) async-start(f32[32,8,128]{2,1,0:T(8,128)} %get-tuple-element.77), calls=%async_computation.2 | async-start | bytes 262144 | tf_op jit(solution)/shard_map/all_to_all | solution.py:367
  107.1 9.1 %backward.1 = (bf16[448,1024]{1,0:T(8,128)(2,1)}, f32[448,2048]{1,0:T(8,128)}, f32[224,128]{1,0:T(8,128)}) custom-call(s32[2]{0:T(128)S(1)} %pad_add_fusion.where_ref, bf16[448,1024]{1,0:T(8,128)(2,1)} %bitcast.27, s32[448,2048]{1,0:T(8,128)} %bitcast.23, f32[224,128]{1,0:T(8,128)} %bitcast.31, bf16[8,8,64,128]{3,2,1,0:T(8,128)(2,1)} %copy-done, ...), custom_call_target="tpu_custom_call" | custom-call | tf_op jit(solution)/shard_map/backward/pallas_call | solution.py:313
  (48 shorter events, 8.8 us)
Async XLA Ops:
  3.7 15.0 %collective-permute-start = (bf16[256,1024]{1,0:T(8,128)(2,1)S(1)}, bf16[256,1024]{1,0:T(8,128)(2,1)S(1)}, u32[]{:S(2)}, u32[]{:S(2)}) collective-permute-start(bf16[256,1024]{1,0:T(8,128)(2,1)S(1)} %get-tuple-element.46), channel_id=1, source_target_pairs={{0,8},{8,16},{16,24},{24,0},{1,9},{9,17},{17,25},{25,1},{2,10},{10... | collective-permute-start | bytes 1572872 | tf_op jit(solution)/shard_map/ppermute | solution.py:334
  5.3 13.4 %collective-permute-start.1 = (bf16[256,1024]{1,0:T(8,128)(2,1)S(1)}, bf16[256,1024]{1,0:T(8,128)(2,1)S(1)}, u32[]{:S(2)}, u32[]{:S(2)}) collective-permute-start(bf16[256,1024]{1,0:T(8,128)(2,1)S(1)} %get-tuple-element.47), channel_id=1, source_target_pairs={{0,24},{8,0},{16,8},{24,16},{1,25},{9,1},{17,9},{25,17},{2,26},{10... | collective-permute-start | bytes 1572872 | tf_op jit(solution)/shard_map/ppermute | solution.py:334
  22.4 29.6 %collective-permute-start.2 = (bf16[512,1024]{1,0:T(8,128)(2,1)S(1)}, bf16[512,1024]{1,0:T(8,128)(2,1)S(1)}, u32[]{:S(2)}, u32[]{:S(2)}) collective-permute-start(bf16[512,1024]{1,0:T(8,128)(2,1)S(1)} %get-tuple-element.55), channel_id=1, source_target_pairs={{0,8},{8,16},{16,24},{24,0},{1,9},{9,17},{17,25},{25,1},{2,10},{10... | collective-permute-start | bytes 3145736 | tf_op jit(solution)/shard_map/ppermute | solution.py:334
  24.0 28.0 %collective-permute-start.3 = (bf16[512,1024]{1,0:T(8,128)(2,1)S(1)}, bf16[512,1024]{1,0:T(8,128)(2,1)S(1)}, u32[]{:S(2)}, u32[]{:S(2)}) collective-permute-start(bf16[512,1024]{1,0:T(8,128)(2,1)S(1)} %get-tuple-element.56), channel_id=1, source_target_pairs={{0,24},{8,0},{16,8},{24,16},{1,25},{9,1},{17,9},{25,17},{2,26},{10... | collective-permute-start | bytes 3145736 | tf_op jit(solution)/shard_map/ppermute | solution.py:334
  25.7 16.9 %collective-permute-start.10 = (bf16[8,64,128]{2,1,0:T(8,128)(2,1)S(1)}, bf16[8,64,128]{2,1,0:T(8,128)(2,1)S(1)}, u32[]{:S(2)}, u32[]{:S(2)}) collective-permute-start(bf16[8,64,128]{2,1,0:T(8,128)(2,1)S(1)} %all_to_all.15.refs_0_), channel_id=1, source_target_pairs={{0,4},{1,5},{2,6},{3,7},{4,0},{5,1},{6,2},{7,3},{8,12},{9,13},{10,... | collective-permute-start | bytes 393224 | tf_op jit(solution)/shard_map/ppermute | solution.py:334
  32.9 14.8 %collective-permute-start.9 = (bf16[8,64,128]{2,1,0:T(8,128)(2,1)S(1)}, bf16[8,64,128]{2,1,0:T(8,128)(2,1)S(1)}, u32[]{:S(2)}, u32[]{:S(2)}) collective-permute-start(bf16[8,64,128]{2,1,0:T(8,128)(2,1)S(1)} %all_to_all.15.refs_0_), channel_id=1, source_target_pairs={{0,3},{1,4},{2,5},{3,6},{4,7},{5,0},{6,1},{7,2},{8,11},{9,12},{10,... | collective-permute-start | bytes 393224 | tf_op jit(solution)/shard_map/ppermute | solution.py:334
  34.8 24.2 %collective-permute-start.8 = (bf16[8,64,128]{2,1,0:T(8,128)(2,1)S(1)}, bf16[8,64,128]{2,1,0:T(8,128)(2,1)S(1)}, u32[]{:S(2)}, u32[]{:S(2)}) collective-permute-start(bf16[8,64,128]{2,1,0:T(8,128)(2,1)S(1)} %all_to_all.15.refs_0_), channel_id=1, source_target_pairs={{0,5},{1,6},{2,7},{3,0},{4,1},{5,2},{6,3},{7,4},{8,13},{9,14},{10,... | collective-permute-start | bytes 393224 | tf_op jit(solution)/shard_map/ppermute | solution.py:334
  42.6 16.4 %collective-permute-start.7 = (bf16[8,64,128]{2,1,0:T(8,128)(2,1)S(1)}, bf16[8,64,128]{2,1,0:T(8,128)(2,1)S(1)}, u32[]{:S(2)}, u32[]{:S(2)}) collective-permute-start(bf16[8,64,128]{2,1,0:T(8,128)(2,1)S(1)} %all_to_all.15.refs_0_), channel_id=1, source_target_pairs={{0,2},{1,3},{2,4},{3,5},{4,6},{5,7},{6,0},{7,1},{8,10},{9,11},{10,... | collective-permute-start | bytes 393224 | tf_op jit(solution)/shard_map/ppermute | solution.py:334
  47.7 11.3 %collective-permute-start.6 = (bf16[8,64,128]{2,1,0:T(8,128)(2,1)S(1)}, bf16[8,64,128]{2,1,0:T(8,128)(2,1)S(1)}, u32[]{:S(2)}, u32[]{:S(2)}) collective-permute-start(bf16[8,64,128]{2,1,0:T(8,128)(2,1)S(1)} %all_to_all.15.refs_0_), channel_id=1, source_target_pairs={{0,6},{1,7},{2,0},{3,1},{4,2},{5,3},{6,4},{7,5},{8,14},{9,15},{10,... | collective-permute-start | bytes 393224 | tf_op jit(solution)/shard_map/ppermute | solution.py:334
  51.9 7.1 %collective-permute-start.5 = (bf16[8,64,128]{2,1,0:T(8,128)(2,1)S(1)}, bf16[8,64,128]{2,1,0:T(8,128)(2,1)S(1)}, u32[]{:S(2)}, u32[]{:S(2)}) collective-permute-start(bf16[8,64,128]{2,1,0:T(8,128)(2,1)S(1)} %all_to_all.15.refs_0_), channel_id=1, source_target_pairs={{0,1},{1,2},{2,3},{3,4},{4,5},{5,6},{6,7},{7,0},{8,9},{9,10},{10,1... | collective-permute-start | bytes 393224 | tf_op jit(solution)/shard_map/ppermute | solution.py:334
  52.0 7.1 %collective-permute-start.4 = (bf16[8,64,128]{2,1,0:T(8,128)(2,1)S(1)}, bf16[8,64,128]{2,1,0:T(8,128)(2,1)S(1)}, u32[]{:S(2)}, u32[]{:S(2)}) collective-permute-start(bf16[8,64,128]{2,1,0:T(8,128)(2,1)S(1)} %all_to_all.15.refs_0_), channel_id=1, source_target_pairs={{0,7},{1,0},{2,1},{3,2},{4,3},{5,4},{6,5},{7,6},{8,15},{9,8},{10,9... | collective-permute-start | bytes 393224 | tf_op jit(solution)/shard_map/ppermute | solution.py:334
  59.1 48.0 %copy-start = (bf16[8,8,64,128]{3,2,1,0:T(8,128)(2,1)}, bf16[8,8,64,128]{3,2,1,0:T(8,128)(2,1)S(1)}, u32[]{:S(2)}) copy-start(bf16[8,8,64,128]{3,2,1,0:T(8,128)(2,1)S(1)} %pack.1.rest_0_) | copy-start | bytes 3145732
  59.1 26.0 %collective-permute-start.17 = (bf16[8,8,64,128]{3,2,1,0:T(8,128)(2,1)S(1)}, bf16[8,8,64,128]{3,2,1,0:T(8,128)(2,1)S(1)}, u32[]{:S(2)}, u32[]{:S(2)}) collective-permute-start(bf16[8,8,64,128]{3,2,1,0:T(8,128)(2,1)S(1)} %pack.1.rest_0_), channel_id=1, source_target_pairs={{0,8},{8,16},{16,24},{24,0},{1,9},{9,17},{17,25},{25,1},{2,10},{10... | collective-permute-start | bytes 3145736 | tf_op jit(solution)/shard_map/ppermute | solution.py:334
  59.4 25.7 %collective-permute-start.16 = (bf16[8,8,64,128]{3,2,1,0:T(8,128)(2,1)S(1)}, bf16[8,8,64,128]{3,2,1,0:T(8,128)(2,1)S(1)}, u32[]{:S(2)}, u32[]{:S(2)}) collective-permute-start(bf16[8,8,64,128]{3,2,1,0:T(8,128)(2,1)S(1)} %pack.1.rest_0_), channel_id=1, source_target_pairs={{0,24},{8,0},{16,8},{24,16},{1,25},{9,1},{17,9},{25,17},{2,26},{10... | collective-permute-start | bytes 3145736 | tf_op jit(solution)/shard_map/ppermute | solution.py:334
  62.6 15.0 %collective-permute-start.11 = (bf16[2,64,1024]{2,1,0:T(8,128)(2,1)S(1)}, bf16[2,64,1024]{2,1,0:T(8,128)(2,1)S(1)}, u32[]{:S(2)}, u32[]{:S(2)}) collective-permute-start(bf16[2,64,1024]{2,1,0:T(8,128)(2,1)S(1)} %get-tuple-element.60), channel_id=1, source_target_pairs={{0,1},{1,2},{2,3},{3,4},{4,5},{5,6},{6,7},{7,0},{8,9},{9,10},{10,1... | collective-permute-start | bytes 786440 | tf_op jit(solution)/shard_map/ppermute | solution.py:334
  62.6 15.0 %collective-permute-start.12 = (bf16[2,64,1024]{2,1,0:T(8,128)(2,1)S(1)}, bf16[2,64,1024]{2,1,0:T(8,128)(2,1)S(1)}, u32[]{:S(2)}, u32[]{:S(2)}) collective-permute-start(bf16[2,64,1024]{2,1,0:T(8,128)(2,1)S(1)} %get-tuple-element.61), channel_id=1, source_target_pairs={{0,7},{1,0},{2,1},{3,2},{4,3},{5,4},{6,5},{7,6},{8,15},{9,8},{10,9... | collective-permute-start | bytes 786440 | tf_op jit(solution)/shard_map/ppermute | solution.py:334
  65.9 11.7 %collective-permute-start.13 = (bf16[64,1024]{1,0:T(8,128)(2,1)S(1)}, bf16[64,1024]{1,0:T(8,128)(2,1)S(1)}, u32[]{:S(2)}, u32[]{:S(2)}) collective-permute-start(bf16[64,1024]{1,0:T(8,128)(2,1)S(1)} %get-tuple-element.64), channel_id=1, source_target_pairs={{0,2},{1,3},{2,4},{3,5},{4,6},{5,7},{6,0},{7,1},{8,10},{9,11},{10,... | collective-permute-start | bytes 393224 | tf_op jit(solution)/shard_map/ppermute | solution.py:334
  77.7 7.4 %collective-permute-start.14 = (bf16[64,1024]{1,0:T(8,128)(2,1)S(1)}, bf16[64,1024]{1,0:T(8,128)(2,1)S(1)}, u32[]{:S(2)}, u32[]{:S(2)}) collective-permute-start(bf16[64,1024]{1,0:T(8,128)(2,1)S(1)} %get-tuple-element.65), channel_id=1, source_target_pairs={{0,2},{1,3},{2,4},{3,5},{4,6},{5,7},{6,0},{7,1},{8,10},{9,11},{10,... | collective-permute-start | bytes 393224 | tf_op jit(solution)/shard_map/ppermute | solution.py:334
  77.8 7.3 %collective-permute-start.15 = (bf16[64,1024]{1,0:T(8,128)(2,1)S(1)}, bf16[64,1024]{1,0:T(8,128)(2,1)S(1)}, u32[]{:S(2)}, u32[]{:S(2)}) collective-permute-start(bf16[64,1024]{1,0:T(8,128)(2,1)S(1)} %get-tuple-element.66), channel_id=1, source_target_pairs={{0,6},{1,7},{2,0},{3,1},{4,2},{5,3},{6,4},{7,5},{8,14},{9,15},{10,... | collective-permute-start | bytes 393224 | tf_op jit(solution)/shard_map/ppermute | solution.py:334
  85.1 22.0 %copy-start.4 = (bf16[8,8,64,128]{3,2,1,0:T(8,128)(2,1)}, bf16[8,8,64,128]{3,2,1,0:T(8,128)(2,1)S(1)}, u32[]{:S(2)}) copy-start(bf16[8,8,64,128]{3,2,1,0:T(8,128)(2,1)S(1)} %collective-permute-done.17.rest_2_) | copy-start | bytes 3145732
  85.1 22.0 %copy-start.5 = (bf16[8,8,64,128]{3,2,1,0:T(8,128)(2,1)}, bf16[8,8,64,128]{3,2,1,0:T(8,128)(2,1)S(1)}, u32[]{:S(2)}) copy-start(bf16[8,8,64,128]{3,2,1,0:T(8,128)(2,1)S(1)} %collective-permute-done.16.rest_1_) | copy-start | bytes 3145732
  86.9 20.2 %collective-permute-start.19 = (bf16[4,8,64,128]{3,2,1,0:T(8,128)(2,1)}, bf16[4,8,64,128]{3,2,1,0:T(8,128)(2,1)}, u32[]{:S(2)}, u32[]{:S(2)}) collective-permute-start(bf16[4,8,64,128]{3,2,1,0:T(8,128)(2,1)} %slice.7), channel_id=1, source_target_pairs={{0,8},{8,16},{16,24},{24,0},{1,9},{9,17},{17,25},{25,1},{2,10},{10... | collective-permute-start | bytes 1572872 | tf_op jit(solution)/shard_map/ppermute | solution.py:334
  86.9 20.2 %collective-permute-start.18 = (bf16[4,8,64,128]{3,2,1,0:T(8,128)(2,1)}, bf16[4,8,64,128]{3,2,1,0:T(8,128)(2,1)}, u32[]{:S(2)}, u32[]{:S(2)}) collective-permute-start(bf16[4,8,64,128]{3,2,1,0:T(8,128)(2,1)} %slice.6), channel_id=1, source_target_pairs={{0,24},{8,0},{16,8},{24,16},{1,25},{9,1},{17,9},{25,17},{2,26},{10... | collective-permute-start | bytes 1572872 | tf_op jit(solution)/shard_map/ppermute | solution.py:334
  100.6 16.1 %all-to-all-start.2 = ((f32[32,8,128]{2,1,0:T(8,128)}), f32[32,8,128]{2,1,0:T(8,128)S(1)}, u32[]{:S(2)}, u32[]{:S(2)}) async-start(f32[32,8,128]{2,1,0:T(8,128)} %get-tuple-element.77), calls=%async_computation.2 | async-start | bytes 262144 | tf_op jit(solution)/shard_map/all_to_all | solution.py:367
  (3 other events, 19.1 us)

commit v7 on v6

--- a/solution.py
+++ b/solution.py
@@ -244,89 +244,95 @@
     return call(pack_body, "pack", None, pieces, [((NZ, EXPERTS, COLS, CAP), BF16)])[0]
 
 
-SIDES = (0, 1, 3, 2)
-
-
-def backward_body(where_ref, hidden_hbm, codes_hbm, scales_hbm, *rest):
-    packs = rest[: NX + 1]
-    hidden_out, weight_out, scale_out = rest[NX + 1 : NX + 4]
-    hidden, codes, scales, grads, table, weight, sems = rest[NX + 4 :]
-    units = hidden.shape[0]
-    tiles = BLOCK // 128
-    x_of = [lax.rem(where_ref[0] + side, NX) for side in SIDES]
-    lanes_of = [pl.ds(pl.multiple_of(x * BLOCK, BLOCK), BLOCK) for x in x_of]
-    head = [
-        pltpu.make_async_copy(hidden_hbm, hidden, sems.at[0]),
-        pltpu.make_async_copy(scales_hbm, scales, sems.at[1]),
-    ]
-    parts, arrive = [], []
-    for n in range(NX):
-        parts.append(pltpu.make_async_copy(codes_hbm.at[:, lanes_of[n]], codes.at[n], sems.at[2 + n]))
-        arrive.append([])
-        for k in range(NZ):
-            z = lax.rem(where_ref[1] + k, NZ)
-            rows = pl.ds(pl.multiple_of(n * BLOCK + z * COLS, COLS), COLS)
-            source = packs[n].at[k] if n < NX - 1 else packs[n + k // 4].at[k % 4]
-            arrive[n].append(pltpu.make_async_copy(source, grads.at[:, rows], sems.at[8 + n * NZ + k]))
-    head[0].start()
-    for copy in arrive[0]:
-        copy.start()
-    head[1].start()
-    parts[0].start()
-    for n in range(1, NX):
-        for copy in arrive[n]:
-            copy.start()
-        parts[n].start()
-    head[0].wait()
-    head[1].wait()
-    copies = []
-    for n in range(NX):
-        rows_here = slice(n * BLOCK, (n + 1) * BLOCK)
-        for copy in arrive[n]:
-            copy.wait()
-        block = jnp.concatenate([grads[g, rows_here, :] for g in range(EXPERTS)], axis=1)
-        slot = n % 2
-        if n >= 2:
-            copies[n - 2].wait()
-        weight[slot] = lax.dot_general(
-            hidden[...], block, (((1,), (1,)), ((), ())), preferred_element_type=F32
-        )
-        copies.append(pltpu.make_async_copy(weight.at[slot], weight_out.at[:, lanes_of[n]], sems.at[6 + slot]))
-        copies[n].start()
-        parts[n].wait()
-        dequant(codes.at[n], scales, x_of[n] * tiles, table.at[:, rows_here])
-        for g in range(units // GROUP):
-            rows = slice(g * GROUP, (g + 1) * GROUP)
-            line = jnp.sum(weight[slot, rows, :] * codes[n, rows, :].astype(F32), axis=0, keepdims=True)
-            for j in range(tiles):
-                row = (g * NX + x_of[n]) * tiles + j
-                scale_out[pl.ds(row, 1), :] = line[:, j * 128 : (j + 1) * 128]
-    block = jnp.concatenate([grads[g] for g in range(EXPERTS)], axis=1)
-    hidden_out[...] = jnp.dot(table[...], block, preferred_element_type=F32).astype(BF16)
-    copies[2].wait()
-    copies[3].wait()
-
-
-def backward(where, hidden, codes, scales, packs):
+def backward(where, hidden, codes, scales, packs, sides, before=()):
     units, slots = hidden.shape
     features = codes.shape[1]
+    count, tiles = len(sides), BLOCK // 128
+    operands = [hidden, codes, scales, *packs, *before]
+
+    def body(where_ref, hidden_hbm, codes_hbm, scales_hbm, *rest):
+        packs_hbm, rest = rest[: len(packs)], rest[len(packs) :]
+        before_hbm, rest = rest[: len(before)], rest[len(before) :]
+        hidden_out, weight_out, scale_out, hidden_v, codes_v, scales_v, grads, table, weight, acc, sems = rest
+        x_of = [lax.rem(where_ref[0] + side, NX) for side in sides]
+        lanes_of = [pl.ds(pl.multiple_of(x * BLOCK, BLOCK), BLOCK) for x in x_of]
+        head = [
+            pltpu.make_async_copy(hidden_hbm, hidden_v, sems.at[0]),
+            pltpu.make_async_copy(scales_hbm, scales_v, sems.at[1]),
+        ]
+        if before:
+            head.append(pltpu.make_async_copy(before_hbm[0], acc, sems.at[2]))
+            head.append(pltpu.make_async_copy(before_hbm[2], scale_out, sems.at[3]))
+        parts, arrive = [], []
+        for n in range(count):
+            parts.append(pltpu.make_async_copy(codes_hbm.at[:, lanes_of[n]], codes_v.at[n], sems.at[8 + n]))
+            arrive.append([])
+            for k in range(NZ):
+                z = lax.rem(where_ref[1] + k, NZ)
+                rows = pl.ds(pl.multiple_of(n * BLOCK + z * COLS, COLS), COLS)
+                per = NZ * count // len(packs)
+                source = packs_hbm[(n * NZ + k) // per].at[(n * NZ + k) % per]
+                sem = sems.at[8 + count + n * NZ + k]
+                arrive[n].append(pltpu.make_async_copy(source, grads.at[:, rows], sem))
+        head[0].start()
+        for copy in arrive[0]:
+            copy.start()
+        for copy in head[1:]:
+            copy.start()
+        parts[0].start()
+        for n in range(1, count):
+            for copy in arrive[n]:
+                copy.start()
+            parts[n].start()
+        for copy in head:
+            copy.wait()
+        copies = []
+        for n in range(count):
+            rows_here = slice(n * BLOCK, (n + 1) * BLOCK)
+            for copy in arrive[n]:
+                copy.wait()
+            block = jnp.concatenate([grads[g, rows_here, :] for g in range(EXPERTS)], axis=1)
+            weight[n] = lax.dot_general(
+                hidden_v[...], block, (((1,), (1,)), ((), ())), preferred_element_type=F32
+            )
+            copies.append(pltpu.make_async_copy(weight.at[n], weight_out.at[:, lanes_of[n]], sems.at[4 + n]))
+            copies[n].start()
+            parts[n].wait()
+            dequant(codes_v.at[n], scales_v, x_of[n] * tiles, table.at[:, rows_here])
+            for g in range(units // GROUP):
+                rows = slice(g * GROUP, (g + 1) * GROUP)
+                line = jnp.sum(weight[n, rows, :] * codes_v[n, rows, :].astype(F32), axis=0, keepdims=True)
+                for j in range(tiles):
+                    row = (g * NX + x_of[n]) * tiles + j
+                    scale_out[pl.ds(row, 1), :] = line[:, j * 128 : (j + 1) * 128]
+        block = jnp.concatenate([grads[g] for g in range(EXPERTS)], axis=1)
+        value = jnp.dot(table[...], block, preferred_element_type=F32)
+        if before:
+            value = value + acc[...]
+        hidden_out[...] = value.astype(hidden_out.dtype)
+        for copy in copies:
+            copy.wait()
+
+    first = 1 + len(operands) - len(before)
     return pl.pallas_call(
-        backward_body,
-        in_specs=[SMEM] + [HBM] * (4 + NX),
+        body,
+        in_specs=[SMEM] + [HBM] * len(operands),
         out_specs=[VMEM, HBM, VMEM],
-        out_shape=[sds((units, slots), BF16), sds((units, features), F32), sds(scales.shape, F32)],
+        out_shape=[sds((units, slots), BF16 if before else F32), sds((units, features), F32), sds(scales.shape, F32)],
+        input_output_aliases={first + 1: 1} if before else {},
         scratch_shapes=[
             pltpu.VMEM((units, slots), BF16),
-            pltpu.VMEM((NX, units, BLOCK), I32),
+            pltpu.VMEM((count, units, BLOCK), I32),
             pltpu.VMEM(scales.shape, F32),
-            pltpu.VMEM((EXPERTS, features, CAP), BF16),
-            pltpu.VMEM((units, features), BF16),
-            pltpu.VMEM((2, units, BLOCK), F32),
-            pltpu.SemaphoreType.DMA((8 + NX * NZ,)),
+            pltpu.VMEM((EXPERTS, count * BLOCK, CAP), BF16),
+            pltpu.VMEM((units, count * BLOCK), BF16),
+            pltpu.VMEM((count, units, BLOCK), F32),
+            pltpu.VMEM((units, slots), F32),
+            pltpu.SemaphoreType.DMA((8 + count + count * NZ,)),
         ],
         compiler_params=LARGE,
-        name="backward",
-    )(where, *[away(a) for a in (hidden, codes, scales, *packs)])
+        name="backward_last" if before else "backward_first",
+    )(where, *[away(a) for a in operands])
 
 
 def shift(value, axis, by):
@@ -351,7 +357,9 @@
     up = shift(up, "x", 1)
     down = shift(down, "x", -1)
     own = forward_own(where_late, *weights)
-    along = [shift(shard, "z", -k) for k in NEAREST[1:]]
+    along = [shift(shard, "z", -k) for k in NEAREST[4:]]
+    own, shard_late = lax.optimization_barrier((own, shard))
+    along = [shift(shard_late, "z", -k) for k in NEAREST[1:4]] + along
 
     ups, downs, far, up2, down2, rest = x_sum(where, own, up, down)
     rest, *along = lax.optimization_barrier((rest, *along))
@@ -360,12 +368,15 @@
     ups, downs, far = shift(ups, "z", 1), shift(downs, "z", -1), shift(far, "z", 2)
     up2, down2 = mid_sum(up2, down2, ups, downs, far)
     up2, down2 = shift(up2, "z", 2), shift(down2, "z", -2)
-    up2, down2, packs[1], packs[2] = lax.optimization_barrier((up2, down2, packs[1], packs[2]))
-    packs += [shift(packs[1][: NZ // 2], "x", -1), shift(packs[2][NZ // 2 :], "x", 1)]
-    returned = lax.all_to_all(z_sum(rest, ups, downs, up2, down2), ("y", "c"), 0, 0, tiled=True)
+    summed = z_sum(rest, ups, downs, up2, down2)
+    summed, packs[1], packs[2] = lax.optimization_barrier((summed, packs[1], packs[2]))
+    opposite = [shift(packs[1][: NZ // 2], "x", -1), shift(packs[2][NZ // 2 :], "x", 1)]
+    returned = lax.all_to_all(summed, ("y", "c"), 0, 0, tiled=True)
+    begun = backward(where, *weights, packs, (0, 1, 3))
+    returned, *begun = lax.optimization_barrier((returned, *begun))
     combined, spread = combine(place, gate, grad, returned)
     gate_parts = lax.all_to_all(spread, ("x", "z"), 0, 0, tiled=True)
-    hidden_grad, weight_grad, scale_grad = backward(where, *weights, packs)
+    hidden_grad, weight_grad, scale_grad = backward(where, *weights, opposite, (2,), begun)
     gate_parts, hidden_grad = lax.optimization_barrier((gate_parts, hidden_grad))
     gate_grad = gate_sum(gate_parts)
     return combined.T, gate_grad.T, hidden_grad[None], weight_grad[None], scale_grad.reshape(group_scales.shape)

time: 119 us -> 129 us (1.084)
  waiting for transfers between devices: 26.2 us -> 37.3 us
  blocking collectives: 18.6 us -> 9.39 us
  starting transfers between devices: 46.6 us -> 50.4 us
  Pallas kernels: 22 us -> 25.5 us
  local copies, waits for them, and re-layouts: 2.99 us -> 4.85 us
    all_to_all x1 -> x0, blocking collectives: 9.19 us -> none  [on_device(): lax.all_to_all(z_sum(rest, ups, downs, up2, down2), ('y', 'c'), 0, 0, til...]
    ppermute x20, waiting for transfers between devices: 25.7 us -> 32.8 us  [shift(): lax.ppermute(value, axis, [(i, (i + by) % size) for i in range(size)])]
    all_to_all x0 -> x1, starting transfers between devices: none -> 4.98 us  [on_device(): returned = lax.all_to_all(summed, ('y', 'c'), 0, 0, tiled=True)]
    all_to_all x1, waiting for transfers between devices: 0.46 us -> 4.58 us  [on_device(): gate_parts = lax.all_to_all(spread, ('x', 'z'), 0, 0, tiled=True)]
    pallas_call x1 -> x2, Pallas kernels: 9.14 us -> 11.9 us  [backward(): pl.pallas_call(body, in_specs=[SMEM] + [HBM] * len(operands), out_specs=[...]
    ppermute x20, starting transfers between devices: 40.8 us -> 38 us  [shift(): lax.ppermute(value, axis, [(i, (i + by) % size) for i in range(size)])]
    unnamed x14 -> x18, local copies, waits for them, and re-layouts: 1.25 us -> 3.13 us
    all_to_all x1, starting transfers between devices: 5.82 us -> 7.42 us  [on_device(): gate_parts = lax.all_to_all(spread, ('x', 'z'), 0, 0, tiled=True)]
  transfers between devices with their start and end apart: 21 -> 22, of which waited for: 6 -> 12; matrix products, arithmetic and copies ran while one was open for 1% -> 1% of each run, Pallas kernels for 13% -> 15%
where the time goes in v7:
time: 129 us; the launch traced here: 128 us
  starting transfers between devices  50.4 us (39%)
  waiting for transfers between devices  37.3 us (29%)
  Pallas kernels  25.5 us (20%)
  blocking collectives  9.39 us (7%)
  local copies, waits for them, and re-layouts  4.85 us (4%)
    ppermute x20, starting transfers between devices, shift(): lax.ppermute(value, axis, [(i, (i + by) % size) for i in range(size)])  38 us
    ppermute x20, waiting for transfers between devices, shift(): lax.ppermute(value, axis, [(i, (i + by) % size) for i in range(size)])  32.8 us
    pallas_call x10, Pallas kernels, call(): pl.pallas_call(body, in_specs=[SMEM] * len(heads) + [HBM] * len(far) + [V...  13.6 us
    pallas_call x2, Pallas kernels, backward(): pl.pallas_call(body, in_specs=[SMEM] + [HBM] * len(operands), out_specs=[...  11.9 us
    all_to_all x1, blocking collectives, on_device(): shard = lax.all_to_all(outbound, ('y', 'c'), 0, 0, tiled=True)  9.39 us
    all_to_all x1, starting transfers between devices, on_device(): gate_parts = lax.all_to_all(spread, ('x', 'z'), 0, 0, tiled=True)  7.42 us
    all_to_all x1, starting transfers between devices, on_device(): returned = lax.all_to_all(summed, ('y', 'c'), 0, 0, tiled=True)  4.98 us
    all_to_all x1, waiting for transfers between devices, on_device(): gate_parts = lax.all_to_all(spread, ('x', 'z'), 0, 0, tiled=True)  4.58 us
  transfers between devices with their start and end apart: 22, of which 12 were waited for; matrix products, arithmetic and copies ran while one was open for 1% of the time, Pallas kernels for 15%

profile of v7, /device:TPU:8, one launch (start us, length us, event | category | flops | bytes accessed | tf_op | source)
XLA Modules:
  0.0 128.4 jit_solution(1351702044077785600)
XLA Ops:
  0.7 2.9 %forward_far.1 = (bf16[256,1024]{1,0:T(8,128)(2,1)S(1)}, bf16[256,1024]{1,0:T(8,128)(2,1)S(1)}) custom-call(s32[2]{0:T(128)S(1)} %pad_add_fusion.where_ref, bf16[448,1024]{1,0:T(8,128)(2,1)} %bitcast.25, s32[448,2048]{1,0:T(8,128)} %bitcast.20, f32[224,128]{1,0:T(8,128)} %bitcast.31), custom_call_target="tpu_custom_call" | custom-call | tf_op jit(solution)/shard_map/forward_far/pallas_call | solution.py:34
  5.3 1.7 %collective-permute-start.1 = (bf16[256,1024]{1,0:T(8,128)(2,1)S(1)}, bf16[256,1024]{1,0:T(8,128)(2,1)S(1)}, u32[]{:S(2)}, u32[]{:S(2)}) collective-permute-start(bf16[256,1024]{1,0:T(8,128)(2,1)S(1)} %get-tuple-element.55), channel_id=1, source_target_pairs={{0,24},{8,0},{16,8},{24,16},{1,25},{9,1},{17,9},{25,17},{2,26},{10... | collective-permute-start | bytes 1572872 | tf_op jit(solution)/shard_map/ppermute | solution.py:340
  8.0 9.4 %all_to_all.15.refs_0_ = bf16[8,64,128]{2,1,0:T(8,128)(2,1)S(1)} all-to-all(bf16[8,64,128]{2,1,0:T(8,128)(2,1)S(1)} %get-tuple-element.56), channel_id=1, replica_groups=mesh['y'=4,'c'=2,'x'=4,'z'=8] {'y','c'}, dimensions={0} | all-to-all | bytes 262144 | tf_op jit(solution)/shard_map/all_to_all | solution.py:353
  18.7 3.7 %forward_join.1 = (bf16[512,1024]{1,0:T(8,128)(2,1)S(1)}, bf16[512,1024]{1,0:T(8,128)(2,1)S(1)}) custom-call(s32[2]{0:T(128)S(1)} %pad_add_fusion.where_ref, bf16[448,1024]{1,0:T(8,128)(2,1)} %bitcast.26, s32[448,2048]{1,0:T(8,128)} %bitcast.21, f32[224,128]{1,0:T(8,128)} %bitcast.32, bf16[256,1024]{1,0:T(8,128)(2,1)S(1)} %collective-permute-done.top_ref, ...), custom_call_target="tpu_custom_call" | custom-call | tf_op jit(solution)/shard_map/forward_join/pallas_call | solution.py:34
  25.7 2.9 %forward_own.1.own_ref = f32[512,1024]{1,0:T(8,128)S(1)} custom-call(s32[2]{0:T(128)S(1)} %pad_add_fusion.where_ref, bf16[448,1024]{1,0:T(8,128)(2,1)} %bitcast.27, s32[448,2048]{1,0:T(8,128)} %bitcast.22, f32[224,128]{1,0:T(8,128)} %bitcast.33), custom_call_target="tpu_custom_call" | custom-call | tf_op jit(solution)/shard_map/forward_own/pallas_call | solution.py:34
  28.7 5.9 %collective-permute-start.4 = (bf16[8,64,128]{2,1,0:T(8,128)(2,1)S(1)}, bf16[8,64,128]{2,1,0:T(8,128)(2,1)S(1)}, u32[]{:S(2)}, u32[]{:S(2)}) collective-permute-start(bf16[8,64,128]{2,1,0:T(8,128)(2,1)S(1)} %all_to_all.15.refs_0_), channel_id=1, source_target_pairs={{0,7},{1,0},{2,1},{3,2},{4,3},{5,4},{6,5},{7,6},{8,15},{9,8},{10,9... | collective-permute-start | bytes 393224 | tf_op jit(solution)/shard_map/ppermute | solution.py:340
  34.6 2.5 %collective-permute-start.6 = (bf16[8,64,128]{2,1,0:T(8,128)(2,1)S(1)}, bf16[8,64,128]{2,1,0:T(8,128)(2,1)S(1)}, u32[]{:S(2)}, u32[]{:S(2)}) collective-permute-start(bf16[8,64,128]{2,1,0:T(8,128)(2,1)S(1)} %all_to_all.15.refs_0_), channel_id=1, source_target_pairs={{0,6},{1,7},{2,0},{3,1},{4,2},{5,3},{6,4},{7,5},{8,14},{9,15},{10,... | collective-permute-start | bytes 393224 | tf_op jit(solution)/shard_map/ppermute | solution.py:340
  37.1 2.2 %collective-permute-done.4.refs_1_ = bf16[8,64,128]{2,1,0:T(8,128)(2,1)S(1)} collective-permute-done((bf16[8,64,128]{2,1,0:T(8,128)(2,1)S(1)}, bf16[8,64,128]{2,1,0:T(8,128)(2,1)S(1)}, u32[]{:S(2)}, u32[]{:S(2)}) %collective-permute-start.4) | collective-permute-done | bytes 131104 | tf_op jit(solution)/shard_map/ppermute | solution.py:340
  39.3 4.2 %collective-permute-start.10 = (bf16[8,64,128]{2,1,0:T(8,128)(2,1)S(1)}, bf16[8,64,128]{2,1,0:T(8,128)(2,1)S(1)}, u32[]{:S(2)}, u32[]{:S(2)}) collective-permute-start(bf16[8,64,128]{2,1,0:T(8,128)(2,1)S(1)} %all_to_all.15.refs_0_), channel_id=1, source_target_pairs={{0,4},{1,5},{2,6},{3,7},{4,0},{5,1},{6,2},{7,3},{8,12},{9,13},{10,... | collective-permute-start | bytes 393224 | tf_op jit(solution)/shard_map/ppermute | solution.py:340
  43.5 3.3 %collective-permute-done.5.refs_2_ = bf16[8,64,128]{2,1,0:T(8,128)(2,1)S(1)} collective-permute-done((bf16[8,64,128]{2,1,0:T(8,128)(2,1)S(1)}, bf16[8,64,128]{2,1,0:T(8,128)(2,1)S(1)}, u32[]{:S(2)}, u32[]{:S(2)}) %collective-permute-start.5) | collective-permute-done | bytes 131104 | tf_op jit(solution)/shard_map/ppermute | solution.py:340
  47.7 6.7 %collective-permute-start.8 = (bf16[8,64,128]{2,1,0:T(8,128)(2,1)S(1)}, bf16[8,64,128]{2,1,0:T(8,128)(2,1)S(1)}, u32[]{:S(2)}, u32[]{:S(2)}) collective-permute-start(bf16[8,64,128]{2,1,0:T(8,128)(2,1)S(1)} %all_to_all.15.refs_0_), channel_id=1, source_target_pairs={{0,5},{1,6},{2,7},{3,0},{4,1},{5,2},{6,3},{7,4},{8,13},{9,14},{10,... | collective-permute-start | bytes 393224 | tf_op jit(solution)/shard_map/ppermute | solution.py:340
  55.3 5.8 %collective-permute-done.8.refs_5_ = bf16[8,64,128]{2,1,0:T(8,128)(2,1)S(1)} collective-permute-done((bf16[8,64,128]{2,1,0:T(8,128)(2,1)S(1)}, bf16[8,64,128]{2,1,0:T(8,128)(2,1)S(1)}, u32[]{:S(2)}, u32[]{:S(2)}) %collective-permute-start.8) | collective-permute-done | bytes 131104 | tf_op jit(solution)/shard_map/ppermute | solution.py:340
  61.2 3.9 %collective-permute-done.9.refs_6_ = bf16[8,64,128]{2,1,0:T(8,128)(2,1)S(1)} collective-permute-done((bf16[8,64,128]{2,1,0:T(8,128)(2,1)S(1)}, bf16[8,64,128]{2,1,0:T(8,128)(2,1)S(1)}, u32[]{:S(2)}, u32[]{:S(2)}) %collective-permute-start.9) | collective-permute-done | bytes 131104 | tf_op jit(solution)/shard_map/ppermute | solution.py:340
  65.4 2.0 %collective-permute-start.17 = (bf16[8,8,64,128]{3,2,1,0:T(8,128)(2,1)S(1)}, bf16[8,8,64,128]{3,2,1,0:T(8,128)(2,1)S(1)}, u32[]{:S(2)}, u32[]{:S(2)}) collective-permute-start(bf16[8,8,64,128]{3,2,1,0:T(8,128)(2,1)S(1)} %pack.1.rest_0_), channel_id=1, source_target_pairs={{0,8},{8,16},{16,24},{24,0},{1,9},{9,17},{17,25},{25,1},{2,10},{10... | collective-permute-start | bytes 3145736 | tf_op jit(solution)/shard_map/ppermute | solution.py:340
  67.4 2.1 %collective-permute-start.11 = (bf16[2,64,1024]{2,1,0:T(8,128)(2,1)S(1)}, bf16[2,64,1024]{2,1,0:T(8,128)(2,1)S(1)}, u32[]{:S(2)}, u32[]{:S(2)}) collective-permute-start(bf16[2,64,1024]{2,1,0:T(8,128)(2,1)S(1)} %get-tuple-element.70), channel_id=1, source_target_pairs={{0,1},{1,2},{2,3},{3,4},{4,5},{5,6},{6,7},{7,0},{8,9},{9,10},{10,1... | collective-permute-start | bytes 786440 | tf_op jit(solution)/shard_map/ppermute | solution.py:340
  71.0 6.8 %collective-permute-done.13.far_ref = bf16[64,1024]{1,0:T(8,128)(2,1)S(1)} collective-permute-done((bf16[64,1024]{1,0:T(8,128)(2,1)S(1)}, bf16[64,1024]{1,0:T(8,128)(2,1)S(1)}, u32[]{:S(2)}, u32[]{:S(2)}) %collective-permute-start.13) | collective-permute-done | bytes 131104 | tf_op jit(solution)/shard_map/ppermute | solution.py:340
  77.8 2.3 %collective-permute-done.11.ups_ref = bf16[2,64,1024]{2,1,0:T(8,128)(2,1)S(1)} collective-permute-done((bf16[2,64,1024]{2,1,0:T(8,128)(2,1)S(1)}, bf16[2,64,1024]{2,1,0:T(8,128)(2,1)S(1)}, u32[]{:S(2)}, u32[]{:S(2)}) %collective-permute-start.11) | collective-permute-done | bytes 262176 | tf_op jit(solution)/shard_map/ppermute | solution.py:340
  80.2 4.1 %collective-permute-start.15 = (bf16[64,1024]{1,0:T(8,128)(2,1)S(1)}, bf16[64,1024]{1,0:T(8,128)(2,1)S(1)}, u32[]{:S(2)}, u32[]{:S(2)}) collective-permute-start(bf16[64,1024]{1,0:T(8,128)(2,1)S(1)} %get-tuple-element.76), channel_id=1, source_target_pairs={{0,6},{1,7},{2,0},{3,1},{4,2},{5,3},{6,4},{7,5},{8,14},{9,15},{10,... | collective-permute-start | bytes 393224 | tf_op jit(solution)/shard_map/ppermute | solution.py:340
  84.4 4.3 %collective-permute-done.14.up_ref = bf16[64,1024]{1,0:T(8,128)(2,1)S(1)} collective-permute-done((bf16[64,1024]{1,0:T(8,128)(2,1)S(1)}, bf16[64,1024]{1,0:T(8,128)(2,1)S(1)}, u32[]{:S(2)}, u32[]{:S(2)}) %collective-permute-start.14) | collective-permute-done | bytes 131104 | tf_op jit(solution)/shard_map/ppermute | solution.py:340
  95.1 5.0 %all-to-all-start.1 = ((bf16[8,64,128]{2,1,0:T(8,128)(2,1)}), bf16[8,64,128]{2,1,0:T(8,128)(2,1)S(1)}, u32[]{:S(2)}, u32[]{:S(2)}) async-start(bf16[8,64,128]{2,1,0:T(8,128)(2,1)} %z_sum.1), calls=%async_computation.1 | async-start | bytes 262144 | tf_op jit(solution)/shard_map/all_to_all | solution.py:374
  100.1 6.5 %backward_first.1 = (f32[448,1024]{1,0:T(8,128)S(1)}, f32[448,2048]{1,0:T(8,128)}, f32[224,128]{1,0:T(8,128)S(1)}) custom-call(s32[2]{0:T(128)S(1)} %pad_add_fusion.where_ref, bf16[448,1024]{1,0:T(8,128)(2,1)} %bitcast.28, s32[448,2048]{1,0:T(8,128)} %bitcast.23, f32[224,128]{1,0:T(8,128)} %bitcast.34, bf16[8,8,64,128]{3,2,1,0:T(8,128)(2,1)} %copy-done, ...), custom_call_target="tpu_custom_call" | custom-call | tf_op jit(solution)/shard_map/backward_first/pallas_call | solution.py:317
  109.7 7.4 %all-to-all-start.2 = ((f32[32,8,128]{2,1,0:T(8,128)}), f32[32,8,128]{2,1,0:T(8,128)S(1)}, u32[]{:S(2)}, u32[]{:S(2)}) async-start(f32[32,8,128]{2,1,0:T(8,128)} %get-tuple-element.92), calls=%async_computation.2 | async-start | bytes 262144 | tf_op jit(solution)/shard_map/all_to_all | solution.py:378
  117.8 5.4 %backward_last.1 = (bf16[448,1024]{1,0:T(8,128)(2,1)}, f32[448,2048]{1,0:T(8,128)}, f32[224,128]{1,0:T(8,128)}) custom-call(s32[2]{0:T(128)S(1)} %pad_add_fusion.where_ref, bf16[448,1024]{1,0:T(8,128)(2,1)} %bitcast.29, s32[448,2048]{1,0:T(8,128)} %bitcast.24, f32[224,128]{1,0:T(8,128)} %bitcast.35, ...), custom_call_target="tpu_custom_call", output_to_operand_aliasing={{1}: (7, {})} | custom-call | tf_op jit(solution)/shard_map/backward_last/pallas_call | solution.py:317
  123.2 4.6 %all-to-all-done.2.parts_ref = f32[32,8,128]{2,1,0:T(8,128)S(1)} async-done(((f32[32,8,128]{2,1,0:T(8,128)}), f32[32,8,128]{2,1,0:T(8,128)S(1)}, u32[]{:S(2)}, u32[]{:S(2)}) %all-to-all-start.2) | async-done | bytes 131104 | tf_op jit(solution)/shard_map/all_to_all | solution.py:378
  (54 shorter events, 21.6 us)
Async XLA Ops:
  3.7 15.0 %collective-permute-start = (bf16[256,1024]{1,0:T(8,128)(2,1)S(1)}, bf16[256,1024]{1,0:T(8,128)(2,1)S(1)}, u32[]{:S(2)}, u32[]{:S(2)}) collective-permute-start(bf16[256,1024]{1,0:T(8,128)(2,1)S(1)} %get-tuple-element.54), channel_id=1, source_target_pairs={{0,8},{8,16},{16,24},{24,0},{1,9},{9,17},{17,25},{25,1},{2,10},{10... | collective-permute-start | bytes 1572872 | tf_op jit(solution)/shard_map/ppermute | solution.py:340
  5.3 13.4 %collective-permute-start.1 = (bf16[256,1024]{1,0:T(8,128)(2,1)S(1)}, bf16[256,1024]{1,0:T(8,128)(2,1)S(1)}, u32[]{:S(2)}, u32[]{:S(2)}) collective-permute-start(bf16[256,1024]{1,0:T(8,128)(2,1)S(1)} %get-tuple-element.55), channel_id=1, source_target_pairs={{0,24},{8,0},{16,8},{24,16},{1,25},{9,1},{17,9},{25,17},{2,26},{10... | collective-permute-start | bytes 1572872 | tf_op jit(solution)/shard_map/ppermute | solution.py:340
  22.4 25.3 %collective-permute-start.2 = (bf16[512,1024]{1,0:T(8,128)(2,1)S(1)}, bf16[512,1024]{1,0:T(8,128)(2,1)S(1)}, u32[]{:S(2)}, u32[]{:S(2)}) collective-permute-start(bf16[512,1024]{1,0:T(8,128)(2,1)S(1)} %get-tuple-element.65), channel_id=1, source_target_pairs={{0,8},{8,16},{16,24},{24,0},{1,9},{9,17},{17,25},{25,1},{2,10},{10... | collective-permute-start | bytes 3145736 | tf_op jit(solution)/shard_map/ppermute | solution.py:340
  24.0 30.5 %collective-permute-start.3 = (bf16[512,1024]{1,0:T(8,128)(2,1)S(1)}, bf16[512,1024]{1,0:T(8,128)(2,1)S(1)}, u32[]{:S(2)}, u32[]{:S(2)}) collective-permute-start(bf16[512,1024]{1,0:T(8,128)(2,1)S(1)} %get-tuple-element.66), channel_id=1, source_target_pairs={{0,24},{8,0},{16,8},{24,16},{1,25},{9,1},{17,9},{25,17},{2,26},{10... | collective-permute-start | bytes 3145736 | tf_op jit(solution)/shard_map/ppermute | solution.py:340
  28.7 10.6 %collective-permute-start.4 = (bf16[8,64,128]{2,1,0:T(8,128)(2,1)S(1)}, bf16[8,64,128]{2,1,0:T(8,128)(2,1)S(1)}, u32[]{:S(2)}, u32[]{:S(2)}) collective-permute-start(bf16[8,64,128]{2,1,0:T(8,128)(2,1)S(1)} %all_to_all.15.refs_0_), channel_id=1, source_target_pairs={{0,7},{1,0},{2,1},{3,2},{4,3},{5,4},{6,5},{7,6},{8,15},{9,8},{10,9... | collective-permute-start | bytes 393224 | tf_op jit(solution)/shard_map/ppermute | solution.py:340
  34.6 12.2 %collective-permute-start.5 = (bf16[8,64,128]{2,1,0:T(8,128)(2,1)S(1)}, bf16[8,64,128]{2,1,0:T(8,128)(2,1)S(1)}, u32[]{:S(2)}, u32[]{:S(2)}) collective-permute-start(bf16[8,64,128]{2,1,0:T(8,128)(2,1)S(1)} %all_to_all.15.refs_0_), channel_id=1, source_target_pairs={{0,1},{1,2},{2,3},{3,4},{4,5},{5,6},{6,7},{7,0},{8,9},{9,10},{10,1... | collective-permute-start | bytes 393224 | tf_op jit(solution)/shard_map/ppermute | solution.py:340
  34.6 20.7 %collective-permute-start.6 = (bf16[8,64,128]{2,1,0:T(8,128)(2,1)S(1)}, bf16[8,64,128]{2,1,0:T(8,128)(2,1)S(1)}, u32[]{:S(2)}, u32[]{:S(2)}) collective-permute-start(bf16[8,64,128]{2,1,0:T(8,128)(2,1)S(1)} %all_to_all.15.refs_0_), channel_id=1, source_target_pairs={{0,6},{1,7},{2,0},{3,1},{4,2},{5,3},{6,4},{7,5},{8,14},{9,15},{10,... | collective-permute-start | bytes 393224 | tf_op jit(solution)/shard_map/ppermute | solution.py:340
  39.3 16.0 %collective-permute-start.10 = (bf16[8,64,128]{2,1,0:T(8,128)(2,1)S(1)}, bf16[8,64,128]{2,1,0:T(8,128)(2,1)S(1)}, u32[]{:S(2)}, u32[]{:S(2)}) collective-permute-start(bf16[8,64,128]{2,1,0:T(8,128)(2,1)S(1)} %all_to_all.15.refs_0_), channel_id=1, source_target_pairs={{0,4},{1,5},{2,6},{3,7},{4,0},{5,1},{6,2},{7,3},{8,12},{9,13},{10,... | collective-permute-start | bytes 393224 | tf_op jit(solution)/shard_map/ppermute | solution.py:340
  46.8 8.5 %collective-permute-start.7 = (bf16[8,64,128]{2,1,0:T(8,128)(2,1)S(1)}, bf16[8,64,128]{2,1,0:T(8,128)(2,1)S(1)}, u32[]{:S(2)}, u32[]{:S(2)}) collective-permute-start(bf16[8,64,128]{2,1,0:T(8,128)(2,1)S(1)} %all_to_all.15.refs_0_), channel_id=1, source_target_pairs={{0,2},{1,3},{2,4},{3,5},{4,6},{5,7},{6,0},{7,1},{8,10},{9,11},{10,... | collective-permute-start | bytes 393224 | tf_op jit(solution)/shard_map/ppermute | solution.py:340
  47.7 13.4 %collective-permute-start.8 = (bf16[8,64,128]{2,1,0:T(8,128)(2,1)S(1)}, bf16[8,64,128]{2,1,0:T(8,128)(2,1)S(1)}, u32[]{:S(2)}, u32[]{:S(2)}) collective-permute-start(bf16[8,64,128]{2,1,0:T(8,128)(2,1)S(1)} %all_to_all.15.refs_0_), channel_id=1, source_target_pairs={{0,5},{1,6},{2,7},{3,0},{4,1},{5,2},{6,3},{7,4},{8,13},{9,14},{10,... | collective-permute-start | bytes 393224 | tf_op jit(solution)/shard_map/ppermute | solution.py:340
  54.5 10.6 %collective-permute-start.9 = (bf16[8,64,128]{2,1,0:T(8,128)(2,1)S(1)}, bf16[8,64,128]{2,1,0:T(8,128)(2,1)S(1)}, u32[]{:S(2)}, u32[]{:S(2)}) collective-permute-start(bf16[8,64,128]{2,1,0:T(8,128)(2,1)S(1)} %all_to_all.15.refs_0_), channel_id=1, source_target_pairs={{0,3},{1,4},{2,5},{3,6},{4,7},{5,0},{6,1},{7,2},{8,11},{9,12},{10,... | collective-permute-start | bytes 393224 | tf_op jit(solution)/shard_map/ppermute | solution.py:340
  65.1 34.9 %copy-start = (bf16[8,8,64,128]{3,2,1,0:T(8,128)(2,1)}, bf16[8,8,64,128]{3,2,1,0:T(8,128)(2,1)S(1)}, u32[]{:S(2)}) copy-start(bf16[8,8,64,128]{3,2,1,0:T(8,128)(2,1)S(1)} %pack.1.rest_0_) | copy-start | bytes 3145732
  65.1 24.9 %collective-permute-start.16 = (bf16[8,8,64,128]{3,2,1,0:T(8,128)(2,1)S(1)}, bf16[8,8,64,128]{3,2,1,0:T(8,128)(2,1)S(1)}, u32[]{:S(2)}, u32[]{:S(2)}) collective-permute-start(bf16[8,8,64,128]{3,2,1,0:T(8,128)(2,1)S(1)} %pack.1.rest_0_), channel_id=1, source_target_pairs={{0,24},{8,0},{16,8},{24,16},{1,25},{9,1},{17,9},{25,17},{2,26},{10... | collective-permute-start | bytes 3145736 | tf_op jit(solution)/shard_map/ppermute | solution.py:340
  65.4 25.9 %collective-permute-start.17 = (bf16[8,8,64,128]{3,2,1,0:T(8,128)(2,1)S(1)}, bf16[8,8,64,128]{3,2,1,0:T(8,128)(2,1)S(1)}, u32[]{:S(2)}, u32[]{:S(2)}) collective-permute-start(bf16[8,8,64,128]{3,2,1,0:T(8,128)(2,1)S(1)} %pack.1.rest_0_), channel_id=1, source_target_pairs={{0,8},{8,16},{16,24},{24,0},{1,9},{9,17},{17,25},{25,1},{2,10},{10... | collective-permute-start | bytes 3145736 | tf_op jit(solution)/shard_map/ppermute | solution.py:340
  67.4 12.6 %collective-permute-start.11 = (bf16[2,64,1024]{2,1,0:T(8,128)(2,1)S(1)}, bf16[2,64,1024]{2,1,0:T(8,128)(2,1)S(1)}, u32[]{:S(2)}, u32[]{:S(2)}) collective-permute-start(bf16[2,64,1024]{2,1,0:T(8,128)(2,1)S(1)} %get-tuple-element.70), channel_id=1, source_target_pairs={{0,1},{1,2},{2,3},{3,4},{4,5},{5,6},{6,7},{7,0},{8,9},{9,10},{10,1... | collective-permute-start | bytes 786440 | tf_op jit(solution)/shard_map/ppermute | solution.py:340
  69.5 10.6 %collective-permute-start.12 = (bf16[2,64,1024]{2,1,0:T(8,128)(2,1)S(1)}, bf16[2,64,1024]{2,1,0:T(8,128)(2,1)S(1)}, u32[]{:S(2)}, u32[]{:S(2)}) collective-permute-start(bf16[2,64,1024]{2,1,0:T(8,128)(2,1)S(1)} %get-tuple-element.71), channel_id=1, source_target_pairs={{0,7},{1,0},{2,1},{3,2},{4,3},{5,4},{6,5},{7,6},{8,15},{9,8},{10,9... | collective-permute-start | bytes 786440 | tf_op jit(solution)/shard_map/ppermute | solution.py:340
  70.7 7.1 %collective-permute-start.13 = (bf16[64,1024]{1,0:T(8,128)(2,1)S(1)}, bf16[64,1024]{1,0:T(8,128)(2,1)S(1)}, u32[]{:S(2)}, u32[]{:S(2)}) collective-permute-start(bf16[64,1024]{1,0:T(8,128)(2,1)S(1)} %get-tuple-element.74), channel_id=1, source_target_pairs={{0,2},{1,3},{2,4},{3,5},{4,6},{5,7},{6,0},{7,1},{8,10},{9,11},{10,... | collective-permute-start | bytes 393224 | tf_op jit(solution)/shard_map/ppermute | solution.py:340
  80.2 8.6 %collective-permute-start.14 = (bf16[64,1024]{1,0:T(8,128)(2,1)S(1)}, bf16[64,1024]{1,0:T(8,128)(2,1)S(1)}, u32[]{:S(2)}, u32[]{:S(2)}) collective-permute-start(bf16[64,1024]{1,0:T(8,128)(2,1)S(1)} %get-tuple-element.75), channel_id=1, source_target_pairs={{0,2},{1,3},{2,4},{3,5},{4,6},{5,7},{6,0},{7,1},{8,10},{9,11},{10,... | collective-permute-start | bytes 393224 | tf_op jit(solution)/shard_map/ppermute | solution.py:340
  80.2 8.5 %collective-permute-start.15 = (bf16[64,1024]{1,0:T(8,128)(2,1)S(1)}, bf16[64,1024]{1,0:T(8,128)(2,1)S(1)}, u32[]{:S(2)}, u32[]{:S(2)}) collective-permute-start(bf16[64,1024]{1,0:T(8,128)(2,1)S(1)} %get-tuple-element.76), channel_id=1, source_target_pairs={{0,6},{1,7},{2,0},{3,1},{4,2},{5,3},{6,4},{7,5},{8,14},{9,15},{10,... | collective-permute-start | bytes 393224 | tf_op jit(solution)/shard_map/ppermute | solution.py:340
  90.0 10.0 %copy-start.6 = (bf16[8,8,64,128]{3,2,1,0:T(8,128)(2,1)}, bf16[8,8,64,128]{3,2,1,0:T(8,128)(2,1)S(1)}, u32[]{:S(2)}) copy-start(bf16[8,8,64,128]{3,2,1,0:T(8,128)(2,1)S(1)} %collective-permute-done.16.rest_1_) | copy-start | bytes 3145732
  92.2 25.6 %collective-permute-start.18 = (bf16[4,8,64,128]{3,2,1,0:T(8,128)(2,1)}, bf16[4,8,64,128]{3,2,1,0:T(8,128)(2,1)}, u32[]{:S(2)}, u32[]{:S(2)}) collective-permute-start(bf16[4,8,64,128]{3,2,1,0:T(8,128)(2,1)} %slice.6), channel_id=1, source_target_pairs={{0,24},{8,0},{16,8},{24,16},{1,25},{9,1},{17,9},{25,17},{2,26},{10... | collective-permute-start | bytes 1572872 | tf_op jit(solution)/shard_map/ppermute | solution.py:340
  93.7 24.1 %collective-permute-start.19 = (bf16[4,8,64,128]{3,2,1,0:T(8,128)(2,1)}, bf16[4,8,64,128]{3,2,1,0:T(8,128)(2,1)}, u32[]{:S(2)}, u32[]{:S(2)}) collective-permute-start(bf16[4,8,64,128]{3,2,1,0:T(8,128)(2,1)} %slice.7), channel_id=1, source_target_pairs={{0,8},{8,16},{16,24},{24,0},{1,9},{9,17},{17,25},{25,1},{2,10},{10... | collective-permute-start | bytes 1572872 | tf_op jit(solution)/shard_map/ppermute | solution.py:340
  95.1 13.4 %all-to-all-start.1 = ((bf16[8,64,128]{2,1,0:T(8,128)(2,1)}), bf16[8,64,128]{2,1,0:T(8,128)(2,1)S(1)}, u32[]{:S(2)}, u32[]{:S(2)}) async-start(bf16[8,64,128]{2,1,0:T(8,128)(2,1)} %z_sum.1), calls=%async_computation.1 | async-start | bytes 262144 | tf_op jit(solution)/shard_map/all_to_all | solution.py:374
  109.7 18.0 %all-to-all-start.2 = ((f32[32,8,128]{2,1,0:T(8,128)}), f32[32,8,128]{2,1,0:T(8,128)S(1)}, u32[]{:S(2)}, u32[]{:S(2)}) async-start(f32[32,8,128]{2,1,0:T(8,128)} %get-tuple-element.92), calls=%async_computation.2 | async-start | bytes 262144 | tf_op jit(solution)/shard_map/all_to_all | solution.py:378
  (6 other events, 29.7 us)

commit v8 on v7

--- a/solution.py
+++ b/solution.py
@@ -29,13 +29,14 @@
     return pltpu.with_memory_space_constraint(array, pltpu.HBM)
 
 
-def call(body, name, where, operands, outs, scratch=(), far=()):
+def call(body, name, where, operands, outs, scratch=(), far=(), keep=None):
     heads = [] if where is None else [where]
+    keep = len(outs) if keep is None else keep
     return pl.pallas_call(
         body,
         in_specs=[SMEM] * len(heads) + [HBM] * len(far) + [VMEM] * len(operands),
         out_specs=[VMEM] * len(outs),
-        out_shape=[pltpu.VMEM(shape, dtype) for shape, dtype in outs],
+        out_shape=[(pltpu.VMEM if i < keep else sds)(*out) for i, out in enumerate(outs)],
         scratch_shapes=list(scratch),
         compiler_params=SMALL,
         name=name,
@@ -132,9 +133,9 @@
 
 
 def join_body(
-    where_ref, hidden_hbm, codes_hbm, scales_hbm, top_ref, bottom_ref, up_ref, down_ref, hidden, codes, scales, table, sems
+    where_ref, hidden_hbm, codes_hbm, scales_hbm, top_ref, bottom_ref, up_ref, down_ref, own_ref, hidden, codes, scales, table, sems
 ):
-    first, *copies = loads(where_ref, (1, 3), hidden_hbm, codes_hbm, scales_hbm, hidden, codes, scales, sems)
+    first, *copies = loads(where_ref, (1, 3, 0), hidden_hbm, codes_hbm, scales_hbm, hidden, codes, scales, sems)
     half = BLOCK // 2
     value = block_value(where_ref, 1, hidden, codes.at[0], scales, table, copies[0], (first,))
     up_ref[:half] = (value[:half] + top_ref[...].astype(F32)).astype(BF16)
@@ -142,22 +143,13 @@
     value = block_value(where_ref, 3, hidden, codes.at[1], scales, table, copies[1])
     down_ref[:half] = value[:half].astype(BF16)
     down_ref[half:] = (value[half:] + bottom_ref[...].astype(F32)).astype(BF16)
+    own_ref[...] = block_value(where_ref, 0, hidden, codes.at[2], scales, table, copies[2])
 
 
 def forward_join(where, hidden, codes, scales, top, bottom):
-    outs = [((BLOCK, SLOTS), BF16)] * 2
+    outs = [((BLOCK, SLOTS), BF16)] * 2 + [((BLOCK, SLOTS), F32)]
     far = (hidden, codes, scales)
-    return call(join_body, "forward_join", where, [top, bottom], outs, buffers(hidden.shape[0], 2), far)
-
-
-def own_body(where_ref, hidden_hbm, codes_hbm, scales_hbm, own_ref, hidden, codes, scales, table, sems):
-    first, *copies = loads(where_ref, (0,), hidden_hbm, codes_hbm, scales_hbm, hidden, codes, scales, sems)
-    own_ref[...] = block_value(where_ref, 0, hidden, codes.at[0], scales, table, copies[0], (first,))
-
-
-def forward_own(where, *arrays):
-    outs = [((BLOCK, SLOTS), F32)]
-    return call(own_body, "forward_own", where, [], outs, buffers(arrays[0].shape[0], 1), arrays)[0]
+    return call(join_body, "forward_join", where, [top, bottom], outs, buffers(hidden.shape[0], 3), far)
 
 
 def x_sum_body(where_ref, own_ref, up_ref, down_ref, ups_ref, downs_ref, far_ref, up2_ref, down2_ref, rest_ref):
@@ -201,7 +193,7 @@
     return call(z_sum_body, "z_sum", None, arrays, [((EXPERTS, COLS, CAP), BF16)])[0]
 
 
-def combine_body(place_ref, gate_ref, grad_ref, back_ref, out_ref, spread_ref):
+def combine_body(place_ref, gate_ref, grad_ref, back_ref, spread_ref, out_ref):
     back = jnp.concatenate([back_ref[e] for e in range(EXPERTS)], axis=1)
     grad = grad_ref[...].astype(F32)
     total = None
@@ -217,8 +209,8 @@
 
 
 def combine(place, gate, grad, back):
-    outs = [(grad.shape, BF16), ((NX * NZ, 8, 128), F32)]
-    return call(combine_body, "combine", None, [place, gate, grad, back], outs)
+    outs = [((NX * NZ, 8, 128), F32), (grad.shape, BF16)]
+    return call(combine_body, "combine", None, [place, gate, grad, back], outs, keep=1)
 
 
 def gate_sum_body(parts_ref, out_ref):
@@ -229,7 +221,7 @@
 
 
 def gate_sum(parts):
-    return call(gate_sum_body, "gate_sum", None, [parts], [((2, 512), F32)])[0]
+    return call(gate_sum_body, "gate_sum", None, [parts], [((2, 512), F32)], keep=0)[0]
 
 
 NEAREST = (0, 1, 7, 2, 6, 3, 5, 4)
@@ -244,25 +236,24 @@
     return call(pack_body, "pack", None, pieces, [((NZ, EXPERTS, COLS, CAP), BF16)])[0]
 
 
-def backward(where, hidden, codes, scales, packs, sides, before=()):
+SIDES = (0, 1, 3, 2)
+
+
+def backward(where, hidden, codes, scales, packs):
     units, slots = hidden.shape
     features = codes.shape[1]
-    count, tiles = len(sides), BLOCK // 128
-    operands = [hidden, codes, scales, *packs, *before]
+    count, tiles = NX, BLOCK // 128
+    operands = [hidden, codes, scales, *packs]
 
     def body(where_ref, hidden_hbm, codes_hbm, scales_hbm, *rest):
         packs_hbm, rest = rest[: len(packs)], rest[len(packs) :]
-        before_hbm, rest = rest[: len(before)], rest[len(before) :]
-        hidden_out, weight_out, scale_out, hidden_v, codes_v, scales_v, grads, table, weight, acc, sems = rest
-        x_of = [lax.rem(where_ref[0] + side, NX) for side in sides]
+        hidden_out, weight_out, scale_out, hidden_v, codes_v, scales_v, grads, table, weight, sems = rest
+        x_of = [lax.rem(where_ref[0] + side, NX) for side in SIDES]
         lanes_of = [pl.ds(pl.multiple_of(x * BLOCK, BLOCK), BLOCK) for x in x_of]
         head = [
             pltpu.make_async_copy(hidden_hbm, hidden_v, sems.at[0]),
             pltpu.make_async_copy(scales_hbm, scales_v, sems.at[1]),
         ]
-        if before:
-            head.append(pltpu.make_async_copy(before_hbm[0], acc, sems.at[2]))
-            head.append(pltpu.make_async_copy(before_hbm[2], scale_out, sems.at[3]))
         parts, arrive = [], []
         for n in range(count):
             parts.append(pltpu.make_async_copy(codes_hbm.at[:, lanes_of[n]], codes_v.at[n], sems.at[8 + n]))
@@ -270,8 +261,7 @@
             for k in range(NZ):
                 z = lax.rem(where_ref[1] + k, NZ)
                 rows = pl.ds(pl.multiple_of(n * BLOCK + z * COLS, COLS), COLS)
-                per = NZ * count // len(packs)
-                source = packs_hbm[(n * NZ + k) // per].at[(n * NZ + k) % per]
+                source = packs_hbm[n].at[k]
                 sem = sems.at[8 + count + n * NZ + k]
                 arrive[n].append(pltpu.make_async_copy(source, grads.at[:, rows], sem))
         head[0].start()
@@ -306,20 +296,15 @@
                     row = (g * NX + x_of[n]) * tiles + j
                     scale_out[pl.ds(row, 1), :] = line[:, j * 128 : (j + 1) * 128]
         block = jnp.concatenate([grads[g] for g in range(EXPERTS)], axis=1)
-        value = jnp.dot(table[...], block, preferred_element_type=F32)
-        if before:
-            value = value + acc[...]
-        hidden_out[...] = value.astype(hidden_out.dtype)
+        hidden_out[...] = jnp.dot(table[...], block, preferred_element_type=F32).astype(BF16)
         for copy in copies:
             copy.wait()
 
-    first = 1 + len(operands) - len(before)
     return pl.pallas_call(
         body,
         in_specs=[SMEM] + [HBM] * len(operands),
         out_specs=[VMEM, HBM, VMEM],
-        out_shape=[sds((units, slots), BF16 if before else F32), sds((units, features), F32), sds(scales.shape, F32)],
-        input_output_aliases={first + 1: 1} if before else {},
+        out_shape=[sds((units, slots), BF16), sds((units, features), F32), sds(scales.shape, F32)],
         scratch_shapes=[
             pltpu.VMEM((units, slots), BF16),
             pltpu.VMEM((count, units, BLOCK), I32),
@@ -327,11 +312,10 @@
             pltpu.VMEM((EXPERTS, count * BLOCK, CAP), BF16),
             pltpu.VMEM((units, count * BLOCK), BF16),
             pltpu.VMEM((count, units, BLOCK), F32),
-            pltpu.VMEM((units, slots), F32),
             pltpu.SemaphoreType.DMA((8 + count + count * NZ,)),
         ],
         compiler_params=LARGE,
-        name="backward_last" if before else "backward_first",
+        name="backward",
     )(where, *[away(a) for a in operands])
 
 
@@ -352,14 +336,12 @@
     place, outbound = slot_grads(index, gate, grad)
     shard = lax.all_to_all(outbound, ("y", "c"), 0, 0, tiled=True)
     far_top, far_bottom, shard = lax.optimization_barrier((far_top, far_bottom, shard))
-    up, down = forward_join(where, *weights, far_top, far_bottom)
-    where_late, up, down, shard = lax.optimization_barrier((where, up, down, shard))
+    up, down, own = forward_join(where, *weights, far_top, far_bottom)
+    up, down, shard = lax.optimization_barrier((up, down, shard))
     up = shift(up, "x", 1)
     down = shift(down, "x", -1)
-    own = forward_own(where_late, *weights)
-    along = [shift(shard, "z", -k) for k in NEAREST[4:]]
-    own, shard_late = lax.optimization_barrier((own, shard))
-    along = [shift(shard_late, "z", -k) for k in NEAREST[1:4]] + along
+    along = [shift(shard, "z", -k) for k in NEAREST[1:]]
+    up, down, *along[4:] = lax.optimization_barrier((up, down, *along[4:]))
 
     ups, downs, far, up2, down2, rest = x_sum(where, own, up, down)
     rest, *along = lax.optimization_barrier((rest, *along))
@@ -367,16 +349,13 @@
     packs = [mine, shift(mine, "x", -1), shift(mine, "x", 1)]
     ups, downs, far = shift(ups, "z", 1), shift(downs, "z", -1), shift(far, "z", 2)
     up2, down2 = mid_sum(up2, down2, ups, downs, far)
+    up2, down2, mine = lax.optimization_barrier((up2, down2, mine))
+    packs.append(shift(mine, "x", 2))
     up2, down2 = shift(up2, "z", 2), shift(down2, "z", -2)
-    summed = z_sum(rest, ups, downs, up2, down2)
-    summed, packs[1], packs[2] = lax.optimization_barrier((summed, packs[1], packs[2]))
-    opposite = [shift(packs[1][: NZ // 2], "x", -1), shift(packs[2][NZ // 2 :], "x", 1)]
-    returned = lax.all_to_all(summed, ("y", "c"), 0, 0, tiled=True)
-    begun = backward(where, *weights, packs, (0, 1, 3))
-    returned, *begun = lax.optimization_barrier((returned, *begun))
-    combined, spread = combine(place, gate, grad, returned)
+    returned = lax.all_to_all(z_sum(rest, ups, downs, up2, down2), ("y", "c"), 0, 0, tiled=True)
+    spread, combined = combine(place, gate, grad, returned)
     gate_parts = lax.all_to_all(spread, ("x", "z"), 0, 0, tiled=True)
-    hidden_grad, weight_grad, scale_grad = backward(where, *weights, opposite, (2,), begun)
+    hidden_grad, weight_grad, scale_grad = backward(where, *weights, packs)
     gate_parts, hidden_grad = lax.optimization_barrier((gate_parts, hidden_grad))
     gate_grad = gate_sum(gate_parts)
     return combined.T, gate_grad.T, hidden_grad[None], weight_grad[None], scale_grad.reshape(group_scales.shape)

time: 129 us -> 125 us (0.969)
  blocking collectives: 9.39 us -> 18.8 us
  starting transfers between devices: 50.4 us -> 45.2 us
  Pallas kernels: 25.5 us -> 20.4 us
  local copies, waits for them, and re-layouts: 4.85 us -> 0.05 us
    all_to_all x0 -> x1, blocking collectives: none -> 9.39 us  [on_device(): lax.all_to_all(z_sum(rest, ups, downs, up2, down2), ('y', 'c'), 0, 0, til...]
    ppermute x20 -> x19, waiting for transfers between devices: 32.8 us -> 38.1 us  [shift(): lax.ppermute(value, axis, [(i, (i + by) % size) for i in range(size)])]
    all_to_all x1 -> x0, starting transfers between devices: 4.98 us -> none  [on_device(): returned = lax.all_to_all(summed, ('y', 'c'), 0, 0, tiled=True)]
    all_to_all x1, waiting for transfers between devices: 4.58 us -> 0.01 us  [on_device(): gate_parts = lax.all_to_all(spread, ('x', 'z'), 0, 0, tiled=True)]
    unnamed x18 -> x12, local copies, waits for them, and re-layouts: 3.13 us -> 0.05 us
    pallas_call x2 -> x1, Pallas kernels: 11.9 us -> 9.05 us  [backward(): pl.pallas_call(body, in_specs=[SMEM] + [HBM] * len(operands), out_specs=[...]
    pallas_call x10 -> x9, Pallas kernels: 13.6 us -> 11.4 us  [call(): pl.pallas_call(body, in_specs=[SMEM] * len(heads) + [HBM] * len(far) + [V...]
    slice x2 -> x0, local copies, waits for them, and re-layouts: 1.72 us -> none  [the longest x1 0.89 us: on_device(): packs[1][:NZ // 2]]
  transfers between devices with their start and end apart: 22 -> 20, of which waited for: 12 -> 8; matrix products, arithmetic and copies ran while one was open for 1% -> 0% of each run, Pallas kernels for 15% -> 10%
where the time goes in v8:
time: 125 us; the launch traced here: 123 us
  starting transfers between devices  45.2 us (36%)
  waiting for transfers between devices  38.1 us (30%)
  Pallas kernels  20.4 us (16%)
  blocking collectives  18.8 us (15%)
    ppermute x19, waiting for transfers between devices, shift(): lax.ppermute(value, axis, [(i, (i + by) % size) for i in range(size)])  38.1 us
    ppermute x19, starting transfers between devices, shift(): lax.ppermute(value, axis, [(i, (i + by) % size) for i in range(size)])  38 us
    pallas_call x9, Pallas kernels, call(): pl.pallas_call(body, in_specs=[SMEM] * len(heads) + [HBM] * len(far) + [V...  11.4 us
    all_to_all x1, blocking collectives, on_device(): shard = lax.all_to_all(outbound, ('y', 'c'), 0, 0, tiled=True)  9.39 us
    all_to_all x1, blocking collectives, on_device(): lax.all_to_all(z_sum(rest, ups, downs, up2, down2), ('y', 'c'), 0, 0, til...  9.39 us
    pallas_call x1, Pallas kernels, backward(): pl.pallas_call(body, in_specs=[SMEM] + [HBM] * len(operands), out_specs=[...  9.05 us
    all_to_all x1, starting transfers between devices, on_device(): gate_parts = lax.all_to_all(spread, ('x', 'z'), 0, 0, tiled=True)  7.26 us
  transfers between devices with their start and end apart: 20, of which 8 were waited for; matrix products, arithmetic and copies ran while one was open for 0% of the time, Pallas kernels for 10%

profile of v8, /device:TPU:8, one launch (start us, length us, event | category | flops | bytes accessed | tf_op | source)
XLA Modules:
  0.0 123.4 jit_solution(17173758503881254534)
XLA Ops:
  0.7 2.9 %forward_far.1 = (bf16[256,1024]{1,0:T(8,128)(2,1)S(1)}, bf16[256,1024]{1,0:T(8,128)(2,1)S(1)}) custom-call(s32[2]{0:T(128)S(1)} %pad_add_fusion.where_ref, bf16[448,1024]{1,0:T(8,128)(2,1)} %bitcast.21, s32[448,2048]{1,0:T(8,128)} %bitcast.18, f32[224,128]{1,0:T(8,128)} %bitcast.24), custom_call_target="tpu_custom_call" | custom-call | tf_op jit(solution)/shard_map/forward_far/pallas_call | solution.py:35
  3.7 1.6 %collective-permute-start = (bf16[256,1024]{1,0:T(8,128)(2,1)S(1)}, bf16[256,1024]{1,0:T(8,128)(2,1)S(1)}, u32[]{:S(2)}, u32[]{:S(2)}) collective-permute-start(bf16[256,1024]{1,0:T(8,128)(2,1)S(1)} %get-tuple-element.50), channel_id=1, source_target_pairs={{0,8},{8,16},{16,24},{24,0},{1,9},{9,17},{17,25},{25,1},{2,10},{10... | collective-permute-start | bytes 1572872 | tf_op jit(solution)/shard_map/ppermute | solution.py:324
  5.3 1.7 %collective-permute-start.1 = (bf16[256,1024]{1,0:T(8,128)(2,1)S(1)}, bf16[256,1024]{1,0:T(8,128)(2,1)S(1)}, u32[]{:S(2)}, u32[]{:S(2)}) collective-permute-start(bf16[256,1024]{1,0:T(8,128)(2,1)S(1)} %get-tuple-element.51), channel_id=1, source_target_pairs={{0,24},{8,0},{16,8},{24,16},{1,25},{9,1},{17,9},{25,17},{2,26},{10... | collective-permute-start | bytes 1572872 | tf_op jit(solution)/shard_map/ppermute | solution.py:324
  8.0 9.4 %all_to_all.15.refs_0_ = bf16[8,64,128]{2,1,0:T(8,128)(2,1)S(1)} all-to-all(bf16[8,64,128]{2,1,0:T(8,128)(2,1)S(1)} %get-tuple-element.52), channel_id=1, replica_groups=mesh['y'=4,'c'=2,'x'=4,'z'=8] {'y','c'}, dimensions={0} | all-to-all | bytes 262144 | tf_op jit(solution)/shard_map/all_to_all | solution.py:337
  18.7 4.5 %forward_join.1 = (bf16[512,1024]{1,0:T(8,128)(2,1)S(1)}, bf16[512,1024]{1,0:T(8,128)(2,1)S(1)}, f32[512,1024]{1,0:T(8,128)S(1)}) custom-call(s32[2]{0:T(128)S(1)} %pad_add_fusion.where_ref, bf16[448,1024]{1,0:T(8,128)(2,1)} %bitcast.22, s32[448,2048]{1,0:T(8,128)} %bitcast.19, f32[224,128]{1,0:T(8,128)} %bitcast.25, ...), custom_call_target="tpu_custom_call" | custom-call | tf_op jit(solution)/shard_map/forward_join/pallas_call | solution.py:35
  23.2 1.6 %collective-permute-start.2 = (bf16[512,1024]{1,0:T(8,128)(2,1)S(1)}, bf16[512,1024]{1,0:T(8,128)(2,1)S(1)}, u32[]{:S(2)}, u32[]{:S(2)}) collective-permute-start(bf16[512,1024]{1,0:T(8,128)(2,1)S(1)} %get-tuple-element.59), channel_id=1, source_target_pairs={{0,8},{8,16},{16,24},{24,0},{1,9},{9,17},{17,25},{25,1},{2,10},{10... | collective-permute-start | bytes 3145736 | tf_op jit(solution)/shard_map/ppermute | solution.py:324
  24.8 1.7 %collective-permute-start.3 = (bf16[512,1024]{1,0:T(8,128)(2,1)S(1)}, bf16[512,1024]{1,0:T(8,128)(2,1)S(1)}, u32[]{:S(2)}, u32[]{:S(2)}) collective-permute-start(bf16[512,1024]{1,0:T(8,128)(2,1)S(1)} %get-tuple-element.60), channel_id=1, source_target_pairs={{0,24},{8,0},{16,8},{24,16},{1,25},{9,1},{17,9},{25,17},{2,26},{10... | collective-permute-start | bytes 3145736 | tf_op jit(solution)/shard_map/ppermute | solution.py:324
  26.5 7.2 %collective-permute-start.6 = (bf16[8,64,128]{2,1,0:T(8,128)(2,1)S(1)}, bf16[8,64,128]{2,1,0:T(8,128)(2,1)S(1)}, u32[]{:S(2)}, u32[]{:S(2)}) collective-permute-start(bf16[8,64,128]{2,1,0:T(8,128)(2,1)S(1)} %all_to_all.15.refs_0_), channel_id=1, source_target_pairs={{0,4},{1,5},{2,6},{3,7},{4,0},{5,1},{6,2},{7,3},{8,12},{9,13},{10,... | collective-permute-start | bytes 393224 | tf_op jit(solution)/shard_map/ppermute | solution.py:324
  33.7 1.9 %collective-permute-start.5 = (bf16[8,64,128]{2,1,0:T(8,128)(2,1)S(1)}, bf16[8,64,128]{2,1,0:T(8,128)(2,1)S(1)}, u32[]{:S(2)}, u32[]{:S(2)}) collective-permute-start(bf16[8,64,128]{2,1,0:T(8,128)(2,1)S(1)} %all_to_all.15.refs_0_), channel_id=1, source_target_pairs={{0,3},{1,4},{2,5},{3,6},{4,7},{5,0},{6,1},{7,2},{8,11},{9,12},{10,... | collective-permute-start | bytes 393224 | tf_op jit(solution)/shard_map/ppermute | solution.py:324
  35.6 3.1 %collective-permute-start.4 = (bf16[8,64,128]{2,1,0:T(8,128)(2,1)S(1)}, bf16[8,64,128]{2,1,0:T(8,128)(2,1)S(1)}, u32[]{:S(2)}, u32[]{:S(2)}) collective-permute-start(bf16[8,64,128]{2,1,0:T(8,128)(2,1)S(1)} %all_to_all.15.refs_0_), channel_id=1, source_target_pairs={{0,5},{1,6},{2,7},{3,0},{4,1},{5,2},{6,3},{7,4},{8,13},{9,14},{10,... | collective-permute-start | bytes 393224 | tf_op jit(solution)/shard_map/ppermute | solution.py:324
  38.7 4.6 %collective-permute-done.6.refs_7_ = bf16[8,64,128]{2,1,0:T(8,128)(2,1)S(1)} collective-permute-done((bf16[8,64,128]{2,1,0:T(8,128)(2,1)S(1)}, bf16[8,64,128]{2,1,0:T(8,128)(2,1)S(1)}, u32[]{:S(2)}, u32[]{:S(2)}) %collective-permute-start.6) | collective-permute-done | bytes 131104 | tf_op jit(solution)/shard_map/ppermute | solution.py:324
  43.4 5.1 %collective-permute-done.5.refs_6_ = bf16[8,64,128]{2,1,0:T(8,128)(2,1)S(1)} collective-permute-done((bf16[8,64,128]{2,1,0:T(8,128)(2,1)S(1)}, bf16[8,64,128]{2,1,0:T(8,128)(2,1)S(1)}, u32[]{:S(2)}, u32[]{:S(2)}) %collective-permute-start.5) | collective-permute-done | bytes 131104 | tf_op jit(solution)/shard_map/ppermute | solution.py:324
  48.5 4.3 %collective-permute-start.9 = (bf16[8,64,128]{2,1,0:T(8,128)(2,1)S(1)}, bf16[8,64,128]{2,1,0:T(8,128)(2,1)S(1)}, u32[]{:S(2)}, u32[]{:S(2)}) collective-permute-start(bf16[8,64,128]{2,1,0:T(8,128)(2,1)S(1)} %all_to_all.15.refs_0_), channel_id=1, source_target_pairs={{0,6},{1,7},{2,0},{3,1},{4,2},{5,3},{6,4},{7,5},{8,14},{9,15},{10,... | collective-permute-start | bytes 393224 | tf_op jit(solution)/shard_map/ppermute | solution.py:324
  53.7 3.2 %collective-permute-start.12 = (bf16[2,64,1024]{2,1,0:T(8,128)(2,1)S(1)}, bf16[2,64,1024]{2,1,0:T(8,128)(2,1)S(1)}, u32[]{:S(2)}, u32[]{:S(2)}) collective-permute-start(bf16[2,64,1024]{2,1,0:T(8,128)(2,1)S(1)} %get-tuple-element.70), channel_id=1, source_target_pairs={{0,7},{1,0},{2,1},{3,2},{4,3},{5,4},{6,5},{7,6},{8,15},{9,8},{10,9... | collective-permute-start | bytes 786440 | tf_op jit(solution)/shard_map/ppermute | solution.py:324
  56.9 3.2 %collective-permute-start.7 = (bf16[8,64,128]{2,1,0:T(8,128)(2,1)S(1)}, bf16[8,64,128]{2,1,0:T(8,128)(2,1)S(1)}, u32[]{:S(2)}, u32[]{:S(2)}) collective-permute-start(bf16[8,64,128]{2,1,0:T(8,128)(2,1)S(1)} %all_to_all.15.refs_0_), channel_id=1, source_target_pairs={{0,7},{1,0},{2,1},{3,2},{4,3},{5,4},{6,5},{7,6},{8,15},{9,8},{10,9... | collective-permute-start | bytes 393224 | tf_op jit(solution)/shard_map/ppermute | solution.py:324
  60.2 6.2 %collective-permute-done.8.refs_2_ = bf16[8,64,128]{2,1,0:T(8,128)(2,1)S(1)} collective-permute-done((bf16[8,64,128]{2,1,0:T(8,128)(2,1)S(1)}, bf16[8,64,128]{2,1,0:T(8,128)(2,1)S(1)}, u32[]{:S(2)}, u32[]{:S(2)}) %collective-permute-start.8) | collective-permute-done | bytes 131104 | tf_op jit(solution)/shard_map/ppermute | solution.py:324
  66.5 3.2 %collective-permute-start.16 = (bf16[8,8,64,128]{3,2,1,0:T(8,128)(2,1)S(1)}, bf16[8,8,64,128]{3,2,1,0:T(8,128)(2,1)S(1)}, u32[]{:S(2)}, u32[]{:S(2)}) collective-permute-start(bf16[8,8,64,128]{3,2,1,0:T(8,128)(2,1)S(1)} %pack.1.rest_0_), channel_id=1, source_target_pairs={{0,24},{8,0},{16,8},{24,16},{1,25},{9,1},{17,9},{25,17},{2,26},{10... | collective-permute-start | bytes 3145736 | tf_op jit(solution)/shard_map/ppermute | solution.py:324
  70.7 4.1 %collective-permute-start.15 = (bf16[64,1024]{1,0:T(8,128)(2,1)S(1)}, bf16[64,1024]{1,0:T(8,128)(2,1)S(1)}, u32[]{:S(2)}, u32[]{:S(2)}) collective-permute-start(bf16[64,1024]{1,0:T(8,128)(2,1)S(1)} %get-tuple-element.84), channel_id=1, source_target_pairs={{0,6},{1,7},{2,0},{3,1},{4,2},{5,3},{6,4},{7,5},{8,14},{9,15},{10,... | collective-permute-start | bytes 393224 | tf_op jit(solution)/shard_map/ppermute | solution.py:324
  74.9 3.2 %collective-permute-done.14.up_ref = bf16[64,1024]{1,0:T(8,128)(2,1)S(1)} collective-permute-done((bf16[64,1024]{1,0:T(8,128)(2,1)S(1)}, bf16[64,1024]{1,0:T(8,128)(2,1)S(1)}, u32[]{:S(2)}, u32[]{:S(2)}) %collective-permute-start.14) | collective-permute-done | bytes 131104 | tf_op jit(solution)/shard_map/ppermute | solution.py:324
  78.0 2.0 %collective-permute-done.15.down_ref = bf16[64,1024]{1,0:T(8,128)(2,1)S(1)} collective-permute-done((bf16[64,1024]{1,0:T(8,128)(2,1)S(1)}, bf16[64,1024]{1,0:T(8,128)(2,1)S(1)}, u32[]{:S(2)}, u32[]{:S(2)}) %collective-permute-start.15) | collective-permute-done | bytes 131104 | tf_op jit(solution)/shard_map/ppermute | solution.py:324
  80.1 9.4 %all_to_all.16.back_ref = bf16[8,64,128]{2,1,0:T(8,128)(2,1)S(1)} all-to-all(bf16[8,64,128]{2,1,0:T(8,128)(2,1)S(1)} %z_sum.1), channel_id=1, replica_groups=mesh['y'=4,'c'=2,'x'=4,'z'=8] {'y','c'}, dimensions={0} | all-to-all | bytes 262144 | tf_op jit(solution)/shard_map/all_to_all | solution.py:355
  90.7 7.3 %all-to-all-start.2 = ((f32[32,8,128]{2,1,0:T(8,128)}), f32[32,8,128]{2,1,0:T(8,128)S(1)}, u32[]{:S(2)}, u32[]{:S(2)}) async-start(f32[32,8,128]{2,1,0:T(8,128)} %get-tuple-element.86), calls=%async_computation.2 | async-start | bytes 262144 | tf_op jit(solution)/shard_map/all_to_all | solution.py:357
  98.0 14.8 %collective-permute-done.16.rest_1_ = bf16[8,8,64,128]{3,2,1,0:T(8,128)(2,1)S(1)} collective-permute-done((bf16[8,8,64,128]{3,2,1,0:T(8,128)(2,1)S(1)}, bf16[8,8,64,128]{3,2,1,0:T(8,128)(2,1)S(1)}, u32[]{:S(2)}, u32[]{:S(2)}) %collective-permute-start.16) | collective-permute-done | bytes 1048608 | tf_op jit(solution)/shard_map/ppermute | solution.py:324
  113.7 9.0 %backward.1 = (bf16[448,1024]{1,0:T(8,128)(2,1)}, f32[448,2048]{1,0:T(8,128)}, f32[224,128]{1,0:T(8,128)}) custom-call(s32[2]{0:T(128)S(1)} %pad_add_fusion.where_ref, bf16[448,1024]{1,0:T(8,128)(2,1)} %bitcast.23, s32[448,2048]{1,0:T(8,128)} %bitcast.20, f32[224,128]{1,0:T(8,128)} %bitcast.26, bf16[8,8,64,128]{3,2,1,0:T(8,128)(2,1)} %copy-done, ...), custom_call_target="tpu_custom_call" | custom-call | tf_op jit(solution)/shard_map/backward/pallas_call | solution.py:303
  (41 shorter events, 7.3 us)
Async XLA Ops:
  0.6 6.4 %copy-start.1 = (bf16[512,64]{0,1:T(8,128)(2,1)S(1)}, bf16[512,64]{0,1:T(8,128)(2,1)}, u32[]{:S(2)}) copy-start(bf16[512,64]{0,1:T(8,128)(2,1)} %param.11) | copy-start | bytes 196612
  0.6 6.4 %copy-start.2 = (f32[512,2]{0,1:T(2,128)S(1)}, f32[512,2]{0,1:T(2,128)}, u32[]{:S(2)}) copy-start(f32[512,2]{0,1:T(2,128)} %param.10) | copy-start | bytes 12292
  3.7 15.0 %collective-permute-start = (bf16[256,1024]{1,0:T(8,128)(2,1)S(1)}, bf16[256,1024]{1,0:T(8,128)(2,1)S(1)}, u32[]{:S(2)}, u32[]{:S(2)}) collective-permute-start(bf16[256,1024]{1,0:T(8,128)(2,1)S(1)} %get-tuple-element.50), channel_id=1, source_target_pairs={{0,8},{8,16},{16,24},{24,0},{1,9},{9,17},{17,25},{25,1},{2,10},{10... | collective-permute-start | bytes 1572872 | tf_op jit(solution)/shard_map/ppermute | solution.py:324
  5.3 13.4 %collective-permute-start.1 = (bf16[256,1024]{1,0:T(8,128)(2,1)S(1)}, bf16[256,1024]{1,0:T(8,128)(2,1)S(1)}, u32[]{:S(2)}, u32[]{:S(2)}) collective-permute-start(bf16[256,1024]{1,0:T(8,128)(2,1)S(1)} %get-tuple-element.51), channel_id=1, source_target_pairs={{0,24},{8,0},{16,8},{24,16},{1,25},{9,1},{17,9},{25,17},{2,26},{10... | collective-permute-start | bytes 1572872 | tf_op jit(solution)/shard_map/ppermute | solution.py:324
  23.2 29.6 %collective-permute-start.2 = (bf16[512,1024]{1,0:T(8,128)(2,1)S(1)}, bf16[512,1024]{1,0:T(8,128)(2,1)S(1)}, u32[]{:S(2)}, u32[]{:S(2)}) collective-permute-start(bf16[512,1024]{1,0:T(8,128)(2,1)S(1)} %get-tuple-element.59), channel_id=1, source_target_pairs={{0,8},{8,16},{16,24},{24,0},{1,9},{9,17},{17,25},{25,1},{2,10},{10... | collective-permute-start | bytes 3145736 | tf_op jit(solution)/shard_map/ppermute | solution.py:324
  24.8 28.0 %collective-permute-start.3 = (bf16[512,1024]{1,0:T(8,128)(2,1)S(1)}, bf16[512,1024]{1,0:T(8,128)(2,1)S(1)}, u32[]{:S(2)}, u32[]{:S(2)}) collective-permute-start(bf16[512,1024]{1,0:T(8,128)(2,1)S(1)} %get-tuple-element.60), channel_id=1, source_target_pairs={{0,24},{8,0},{16,8},{24,16},{1,25},{9,1},{17,9},{25,17},{2,26},{10... | collective-permute-start | bytes 3145736 | tf_op jit(solution)/shard_map/ppermute | solution.py:324
  26.5 16.9 %collective-permute-start.6 = (bf16[8,64,128]{2,1,0:T(8,128)(2,1)S(1)}, bf16[8,64,128]{2,1,0:T(8,128)(2,1)S(1)}, u32[]{:S(2)}, u32[]{:S(2)}) collective-permute-start(bf16[8,64,128]{2,1,0:T(8,128)(2,1)S(1)} %all_to_all.15.refs_0_), channel_id=1, source_target_pairs={{0,4},{1,5},{2,6},{3,7},{4,0},{5,1},{6,2},{7,3},{8,12},{9,13},{10,... | collective-permute-start | bytes 393224 | tf_op jit(solution)/shard_map/ppermute | solution.py:324
  33.7 14.8 %collective-permute-start.5 = (bf16[8,64,128]{2,1,0:T(8,128)(2,1)S(1)}, bf16[8,64,128]{2,1,0:T(8,128)(2,1)S(1)}, u32[]{:S(2)}, u32[]{:S(2)}) collective-permute-start(bf16[8,64,128]{2,1,0:T(8,128)(2,1)S(1)} %all_to_all.15.refs_0_), channel_id=1, source_target_pairs={{0,3},{1,4},{2,5},{3,6},{4,7},{5,0},{6,1},{7,2},{8,11},{9,12},{10,... | collective-permute-start | bytes 393224 | tf_op jit(solution)/shard_map/ppermute | solution.py:324
  35.6 17.1 %collective-permute-start.4 = (bf16[8,64,128]{2,1,0:T(8,128)(2,1)S(1)}, bf16[8,64,128]{2,1,0:T(8,128)(2,1)S(1)}, u32[]{:S(2)}, u32[]{:S(2)}) collective-permute-start(bf16[8,64,128]{2,1,0:T(8,128)(2,1)S(1)} %all_to_all.15.refs_0_), channel_id=1, source_target_pairs={{0,5},{1,6},{2,7},{3,0},{4,1},{5,2},{6,3},{7,4},{8,13},{9,14},{10,... | collective-permute-start | bytes 393224 | tf_op jit(solution)/shard_map/ppermute | solution.py:324
  43.4 13.6 %collective-permute-start.10 = (bf16[8,64,128]{2,1,0:T(8,128)(2,1)S(1)}, bf16[8,64,128]{2,1,0:T(8,128)(2,1)S(1)}, u32[]{:S(2)}, u32[]{:S(2)}) collective-permute-start(bf16[8,64,128]{2,1,0:T(8,128)(2,1)S(1)} %all_to_all.15.refs_0_), channel_id=1, source_target_pairs={{0,2},{1,3},{2,4},{3,5},{4,6},{5,7},{6,0},{7,1},{8,10},{9,11},{10,... | collective-permute-start | bytes 393224 | tf_op jit(solution)/shard_map/ppermute | solution.py:324
  48.5 11.7 %collective-permute-start.9 = (bf16[8,64,128]{2,1,0:T(8,128)(2,1)S(1)}, bf16[8,64,128]{2,1,0:T(8,128)(2,1)S(1)}, u32[]{:S(2)}, u32[]{:S(2)}) collective-permute-start(bf16[8,64,128]{2,1,0:T(8,128)(2,1)S(1)} %all_to_all.15.refs_0_), channel_id=1, source_target_pairs={{0,6},{1,7},{2,0},{3,1},{4,2},{5,3},{6,4},{7,5},{8,14},{9,15},{10,... | collective-permute-start | bytes 393224 | tf_op jit(solution)/shard_map/ppermute | solution.py:324
  53.6 16.2 %collective-permute-start.11 = (bf16[2,64,1024]{2,1,0:T(8,128)(2,1)S(1)}, bf16[2,64,1024]{2,1,0:T(8,128)(2,1)S(1)}, u32[]{:S(2)}, u32[]{:S(2)}) collective-permute-start(bf16[2,64,1024]{2,1,0:T(8,128)(2,1)S(1)} %get-tuple-element.69), channel_id=1, source_target_pairs={{0,1},{1,2},{2,3},{3,4},{4,5},{5,6},{6,7},{7,0},{8,9},{9,10},{10,1... | collective-permute-start | bytes 786440 | tf_op jit(solution)/shard_map/ppermute | solution.py:324
  53.7 16.1 %collective-permute-start.12 = (bf16[2,64,1024]{2,1,0:T(8,128)(2,1)S(1)}, bf16[2,64,1024]{2,1,0:T(8,128)(2,1)S(1)}, u32[]{:S(2)}, u32[]{:S(2)}) collective-permute-start(bf16[2,64,1024]{2,1,0:T(8,128)(2,1)S(1)} %get-tuple-element.70), channel_id=1, source_target_pairs={{0,7},{1,0},{2,1},{3,2},{4,3},{5,4},{6,5},{7,6},{8,15},{9,8},{10,9... | collective-permute-start | bytes 786440 | tf_op jit(solution)/shard_map/ppermute | solution.py:324
  56.9 9.4 %collective-permute-start.8 = (bf16[8,64,128]{2,1,0:T(8,128)(2,1)S(1)}, bf16[8,64,128]{2,1,0:T(8,128)(2,1)S(1)}, u32[]{:S(2)}, u32[]{:S(2)}) collective-permute-start(bf16[8,64,128]{2,1,0:T(8,128)(2,1)S(1)} %all_to_all.15.refs_0_), channel_id=1, source_target_pairs={{0,1},{1,2},{2,3},{3,4},{4,5},{5,6},{6,7},{7,0},{8,9},{9,10},{10,1... | collective-permute-start | bytes 393224 | tf_op jit(solution)/shard_map/ppermute | solution.py:324
  56.9 9.4 %collective-permute-start.7 = (bf16[8,64,128]{2,1,0:T(8,128)(2,1)S(1)}, bf16[8,64,128]{2,1,0:T(8,128)(2,1)S(1)}, u32[]{:S(2)}, u32[]{:S(2)}) collective-permute-start(bf16[8,64,128]{2,1,0:T(8,128)(2,1)S(1)} %all_to_all.15.refs_0_), channel_id=1, source_target_pairs={{0,7},{1,0},{2,1},{3,2},{4,3},{5,4},{6,5},{7,6},{8,15},{9,8},{10,9... | collective-permute-start | bytes 393224 | tf_op jit(solution)/shard_map/ppermute | solution.py:324
  60.2 9.6 %collective-permute-start.13 = (bf16[64,1024]{1,0:T(8,128)(2,1)S(1)}, bf16[64,1024]{1,0:T(8,128)(2,1)S(1)}, u32[]{:S(2)}, u32[]{:S(2)}) collective-permute-start(bf16[64,1024]{1,0:T(8,128)(2,1)S(1)} %get-tuple-element.73), channel_id=1, source_target_pairs={{0,2},{1,3},{2,4},{3,5},{4,6},{5,7},{6,0},{7,1},{8,10},{9,11},{10,... | collective-permute-start | bytes 393224 | tf_op jit(solution)/shard_map/ppermute | solution.py:324
  66.4 47.3 %copy-start = (bf16[8,8,64,128]{3,2,1,0:T(8,128)(2,1)}, bf16[8,8,64,128]{3,2,1,0:T(8,128)(2,1)S(1)}, u32[]{:S(2)}) copy-start(bf16[8,8,64,128]{3,2,1,0:T(8,128)(2,1)S(1)} %pack.1.rest_0_) | copy-start | bytes 3145732
  66.5 31.5 %collective-permute-start.17 = (bf16[8,8,64,128]{3,2,1,0:T(8,128)(2,1)S(1)}, bf16[8,8,64,128]{3,2,1,0:T(8,128)(2,1)S(1)}, u32[]{:S(2)}, u32[]{:S(2)}) collective-permute-start(bf16[8,8,64,128]{3,2,1,0:T(8,128)(2,1)S(1)} %pack.1.rest_0_), channel_id=1, source_target_pairs={{0,8},{8,16},{16,24},{24,0},{1,9},{9,17},{17,25},{25,1},{2,10},{10... | collective-permute-start | bytes 3145736 | tf_op jit(solution)/shard_map/ppermute | solution.py:324
  66.5 46.2 %collective-permute-start.16 = (bf16[8,8,64,128]{3,2,1,0:T(8,128)(2,1)S(1)}, bf16[8,8,64,128]{3,2,1,0:T(8,128)(2,1)S(1)}, u32[]{:S(2)}, u32[]{:S(2)}) collective-permute-start(bf16[8,8,64,128]{3,2,1,0:T(8,128)(2,1)S(1)} %pack.1.rest_0_), channel_id=1, source_target_pairs={{0,24},{8,0},{16,8},{24,16},{1,25},{9,1},{17,9},{25,17},{2,26},{10... | collective-permute-start | bytes 3145736 | tf_op jit(solution)/shard_map/ppermute | solution.py:324
  69.9 43.8 %collective-permute-start.18 = (bf16[8,8,64,128]{3,2,1,0:T(8,128)(2,1)S(1)}, bf16[8,8,64,128]{3,2,1,0:T(8,128)(2,1)}, u32[]{:S(2)}, u32[]{:S(2)}) collective-permute-start(bf16[8,8,64,128]{3,2,1,0:T(8,128)(2,1)S(1)} %pack.1.rest_0_), channel_id=1, source_target_pairs={{0,16},{8,24},{16,0},{24,8},{1,17},{9,25},{17,1},{25,9},{2,18},{10... | collective-permute-start | bytes 3145736 | tf_op jit(solution)/shard_map/ppermute | solution.py:324
  70.7 7.3 %collective-permute-start.14 = (bf16[64,1024]{1,0:T(8,128)(2,1)S(1)}, bf16[64,1024]{1,0:T(8,128)(2,1)S(1)}, u32[]{:S(2)}, u32[]{:S(2)}) collective-permute-start(bf16[64,1024]{1,0:T(8,128)(2,1)S(1)} %get-tuple-element.83), channel_id=1, source_target_pairs={{0,2},{1,3},{2,4},{3,5},{4,6},{5,7},{6,0},{7,1},{8,10},{9,11},{10,... | collective-permute-start | bytes 393224 | tf_op jit(solution)/shard_map/ppermute | solution.py:324
  70.7 9.3 %collective-permute-start.15 = (bf16[64,1024]{1,0:T(8,128)(2,1)S(1)}, bf16[64,1024]{1,0:T(8,128)(2,1)S(1)}, u32[]{:S(2)}, u32[]{:S(2)}) collective-permute-start(bf16[64,1024]{1,0:T(8,128)(2,1)S(1)} %get-tuple-element.84), channel_id=1, source_target_pairs={{0,6},{1,7},{2,0},{3,1},{4,2},{5,3},{6,4},{7,5},{8,14},{9,15},{10,... | collective-permute-start | bytes 393224 | tf_op jit(solution)/shard_map/ppermute | solution.py:324
  90.7 32.1 %all-to-all-start.2 = ((f32[32,8,128]{2,1,0:T(8,128)}), f32[32,8,128]{2,1,0:T(8,128)S(1)}, u32[]{:S(2)}, u32[]{:S(2)}) async-start(f32[32,8,128]{2,1,0:T(8,128)} %get-tuple-element.86), calls=%async_computation.2 | async-start | bytes 262144 | tf_op jit(solution)/shard_map/all_to_all | solution.py:357
  98.0 15.7 %copy-start.4 = (bf16[8,8,64,128]{3,2,1,0:T(8,128)(2,1)}, bf16[8,8,64,128]{3,2,1,0:T(8,128)(2,1)S(1)}, u32[]{:S(2)}) copy-start(bf16[8,8,64,128]{3,2,1,0:T(8,128)(2,1)S(1)} %collective-permute-done.17.rest_2_) | copy-start | bytes 3145732
  (2 other events, 7.3 us)

commit v9 on v8

--- a/solution.py
+++ b/solution.py
@@ -224,16 +224,30 @@
     return call(gate_sum_body, "gate_sum", None, [parts], [((2, 512), F32)], keep=0)[0]
 
 
-NEAREST = (0, 1, 7, 2, 6, 3, 5, 4)
+ORDER = (0, 3, 5, 4, 1, 7, 2, 6)
+EARLY = 6
 
 
 def pack_body(*refs):
-    for i, k in enumerate(NEAREST):
-        refs[-1][k] = refs[i][...]
+    for i in range(EARLY):
+        refs[-1][i] = refs[i][...]
 
 
 def pack(*pieces):
-    return call(pack_body, "pack", None, pieces, [((NZ, EXPERTS, COLS, CAP), BF16)])[0]
+    return call(pack_body, "pack", None, pieces, [((EARLY, EXPERTS, COLS, CAP), BF16)])[0]
+
+
+def pack_all_body(first_ref, *refs):
+    second_ref, all_ref = refs[-2:]
+    all_ref[:EARLY] = first_ref[...]
+    for i in range(NZ - EARLY):
+        second_ref[i] = refs[i][...]
+        all_ref[EARLY + i] = refs[i][...]
+
+
+def pack_all(*pieces):
+    outs = [((count, EXPERTS, COLS, CAP), BF16) for count in (NZ - EARLY, NZ)]
+    return call(pack_all_body, "pack_all", None, pieces, outs)
 
 
 SIDES = (0, 1, 3, 2)
@@ -259,9 +273,10 @@
             parts.append(pltpu.make_async_copy(codes_hbm.at[:, lanes_of[n]], codes_v.at[n], sems.at[8 + n]))
             arrive.append([])
             for k in range(NZ):
-                z = lax.rem(where_ref[1] + k, NZ)
+                z = lax.rem(where_ref[1] + ORDER[k], NZ)
                 rows = pl.ds(pl.multiple_of(n * BLOCK + z * COLS, COLS), COLS)
-                source = packs_hbm[n].at[k]
+                half, place = (0, k) if k < EARLY else (1, k - EARLY)
+                source = packs_hbm[(0, 1 + half, 3 + half, 5)[n]].at[k if n in (0, NX - 1) else place]
                 sem = sems.at[8 + count + n * NZ + k]
                 arrive[n].append(pltpu.make_async_copy(source, grads.at[:, rows], sem))
         head[0].start()
@@ -340,19 +355,23 @@
     up, down, shard = lax.optimization_barrier((up, down, shard))
     up = shift(up, "x", 1)
     down = shift(down, "x", -1)
-    along = [shift(shard, "z", -k) for k in NEAREST[1:]]
-    up, down, *along[4:] = lax.optimization_barrier((up, down, *along[4:]))
+    along = {k: shift(shard, "z", -k) for k in ORDER[1:]}
+    up, down, *early = lax.optimization_barrier((up, down, *[along[k] for k in ORDER[1:EARLY]]))
+    half = pack(shard, *early)
+    packs = [shift(half, "x", -1), shift(half, "x", 1)]
 
     ups, downs, far, up2, down2, rest = x_sum(where, own, up, down)
-    rest, *along = lax.optimization_barrier((rest, *along))
-    mine = pack(shard, *along)
-    packs = [mine, shift(mine, "x", -1), shift(mine, "x", 1)]
+    rest, *late = lax.optimization_barrier((rest, *[along[k] for k in ORDER[EARLY:]]))
+    other, mine = pack_all(half, *late)
     ups, downs, far = shift(ups, "z", 1), shift(downs, "z", -1), shift(far, "z", 2)
     up2, down2 = mid_sum(up2, down2, ups, downs, far)
     up2, down2, mine = lax.optimization_barrier((up2, down2, mine))
-    packs.append(shift(mine, "x", 2))
+    opposite = shift(mine, "x", 2)
     up2, down2 = shift(up2, "z", 2), shift(down2, "z", -2)
+    up2, down2, other, *packs = lax.optimization_barrier((up2, down2, other, *packs))
+    packs = [mine, packs[0], shift(other, "x", -1), packs[1], shift(other, "x", 1), opposite]
     returned = lax.all_to_all(z_sum(rest, ups, downs, up2, down2), ("y", "c"), 0, 0, tiled=True)
+    returned, packs[2], packs[4] = lax.optimization_barrier((returned, packs[2], packs[4]))
     spread, combined = combine(place, gate, grad, returned)
     gate_parts = lax.all_to_all(spread, ("x", "z"), 0, 0, tiled=True)
     hidden_grad, weight_grad, scale_grad = backward(where, *weights, packs)

time: 125 us -> 134 us (1.072)
  waiting for transfers between devices: 38.1 us -> 46.2 us
  local copies, waits for them, and re-layouts: 0.05 us -> 1.88 us
    ppermute x19 -> x21, waiting for transfers between devices: 38.1 us -> 46 us  [shift(): lax.ppermute(value, axis, [(i, (i + by) % size) for i in range(size)])]
    unnamed x12 -> x18, local copies, waits for them, and re-layouts: 0.05 us -> 1.88 us
    ppermute x19 -> x21, starting transfers between devices: 38 us -> 37.7 us  [shift(): lax.ppermute(value, axis, [(i, (i + by) % size) for i in range(size)])]
    pallas_call x9 -> x10, Pallas kernels: 11.4 us -> 11.5 us  [call(): pl.pallas_call(body, in_specs=[SMEM] * len(heads) + [HBM] * len(far) + [V...]
  transfers between devices with their start and end apart: 20 -> 22, of which waited for: 8 -> 10; matrix products, arithmetic and copies ran while one was open for 0% -> 0% of each run, Pallas kernels for 10% -> 9%
where the time goes in v9:
time: 134 us; the launch traced here: 132 us
  waiting for transfers between devices  46.2 us (34%)
  starting transfers between devices  44 us (33%)
  Pallas kernels  20.5 us (15%)
  blocking collectives  18.8 us (14%)
  local copies, waits for them, and re-layouts  1.88 us (1%)
    ppermute x21, waiting for transfers between devices, shift(): lax.ppermute(value, axis, [(i, (i + by) % size) for i in range(size)])  46 us
    ppermute x21, starting transfers between devices, shift(): lax.ppermute(value, axis, [(i, (i + by) % size) for i in range(size)])  37.7 us
    pallas_call x10, Pallas kernels, call(): pl.pallas_call(body, in_specs=[SMEM] * len(heads) + [HBM] * len(far) + [V...  11.5 us
    all_to_all x1, blocking collectives, on_device(): lax.all_to_all(z_sum(rest, ups, downs, up2, down2), ('y', 'c'), 0, 0, til...  9.43 us
    all_to_all x1, blocking collectives, on_device(): shard = lax.all_to_all(outbound, ('y', 'c'), 0, 0, tiled=True)  9.39 us
    pallas_call x1, Pallas kernels, backward(): pl.pallas_call(body, in_specs=[SMEM] + [HBM] * len(operands), out_specs=[...  9.04 us
    all_to_all x1, starting transfers between devices, on_device(): gate_parts = lax.all_to_all(spread, ('x', 'z'), 0, 0, tiled=True)  6.26 us
  transfers between devices with their start and end apart: 22, of which 10 were waited for; matrix products, arithmetic and copies ran while one was open for 0% of the time, Pallas kernels for 9%

profile of v9, /device:TPU:8, one launch (start us, length us, event | category | flops | bytes accessed | tf_op | source)
XLA Modules:
  0.0 132.3 jit_solution(5786531659666050346)
XLA Ops:
  0.7 2.9 %forward_far.1 = (bf16[256,1024]{1,0:T(8,128)(2,1)S(1)}, bf16[256,1024]{1,0:T(8,128)(2,1)S(1)}) custom-call(s32[2]{0:T(128)S(1)} %pad_add_fusion.where_ref, bf16[448,1024]{1,0:T(8,128)(2,1)} %bitcast.21, s32[448,2048]{1,0:T(8,128)} %bitcast.18, f32[224,128]{1,0:T(8,128)} %bitcast.24), custom_call_target="tpu_custom_call" | custom-call | tf_op jit(solution)/shard_map/forward_far/pallas_call | solution.py:35
  3.7 1.6 %collective-permute-start = (bf16[256,1024]{1,0:T(8,128)(2,1)S(1)}, bf16[256,1024]{1,0:T(8,128)(2,1)S(1)}, u32[]{:S(2)}, u32[]{:S(2)}) collective-permute-start(bf16[256,1024]{1,0:T(8,128)(2,1)S(1)} %get-tuple-element.57), channel_id=1, source_target_pairs={{0,8},{8,16},{16,24},{24,0},{1,9},{9,17},{17,25},{25,1},{2,10},{10... | collective-permute-start | bytes 1572872 | tf_op jit(solution)/shard_map/ppermute | solution.py:339
  5.3 1.7 %collective-permute-start.1 = (bf16[256,1024]{1,0:T(8,128)(2,1)S(1)}, bf16[256,1024]{1,0:T(8,128)(2,1)S(1)}, u32[]{:S(2)}, u32[]{:S(2)}) collective-permute-start(bf16[256,1024]{1,0:T(8,128)(2,1)S(1)} %get-tuple-element.58), channel_id=1, source_target_pairs={{0,24},{8,0},{16,8},{24,16},{1,25},{9,1},{17,9},{25,17},{2,26},{10... | collective-permute-start | bytes 1572872 | tf_op jit(solution)/shard_map/ppermute | solution.py:339
  8.0 9.4 %all_to_all.15.refs_0_ = bf16[8,64,128]{2,1,0:T(8,128)(2,1)S(1)} all-to-all(bf16[8,64,128]{2,1,0:T(8,128)(2,1)S(1)} %get-tuple-element.59), channel_id=1, replica_groups=mesh['y'=4,'c'=2,'x'=4,'z'=8] {'y','c'}, dimensions={0} | all-to-all | bytes 262144 | tf_op jit(solution)/shard_map/all_to_all | solution.py:352
  18.7 4.5 %forward_join.1 = (bf16[512,1024]{1,0:T(8,128)(2,1)S(1)}, bf16[512,1024]{1,0:T(8,128)(2,1)S(1)}, f32[512,1024]{1,0:T(8,128)S(1)}) custom-call(s32[2]{0:T(128)S(1)} %pad_add_fusion.where_ref, bf16[448,1024]{1,0:T(8,128)(2,1)} %bitcast.22, s32[448,2048]{1,0:T(8,128)} %bitcast.19, f32[224,128]{1,0:T(8,128)} %bitcast.25, ...), custom_call_target="tpu_custom_call" | custom-call | tf_op jit(solution)/shard_map/forward_join/pallas_call | solution.py:35
  23.2 1.6 %collective-permute-start.2 = (bf16[512,1024]{1,0:T(8,128)(2,1)S(1)}, bf16[512,1024]{1,0:T(8,128)(2,1)S(1)}, u32[]{:S(2)}, u32[]{:S(2)}) collective-permute-start(bf16[512,1024]{1,0:T(8,128)(2,1)S(1)} %get-tuple-element.66), channel_id=1, source_target_pairs={{0,8},{8,16},{16,24},{24,0},{1,9},{9,17},{17,25},{25,1},{2,10},{10... | collective-permute-start | bytes 3145736 | tf_op jit(solution)/shard_map/ppermute | solution.py:339
  24.8 1.7 %collective-permute-start.3 = (bf16[512,1024]{1,0:T(8,128)(2,1)S(1)}, bf16[512,1024]{1,0:T(8,128)(2,1)S(1)}, u32[]{:S(2)}, u32[]{:S(2)}) collective-permute-start(bf16[512,1024]{1,0:T(8,128)(2,1)S(1)} %get-tuple-element.67), channel_id=1, source_target_pairs={{0,24},{8,0},{16,8},{24,16},{1,25},{9,1},{17,9},{25,17},{2,26},{10... | collective-permute-start | bytes 3145736 | tf_op jit(solution)/shard_map/ppermute | solution.py:339
  26.5 6.7 %collective-permute-start.4 = (bf16[8,64,128]{2,1,0:T(8,128)(2,1)S(1)}, bf16[8,64,128]{2,1,0:T(8,128)(2,1)S(1)}, u32[]{:S(2)}, u32[]{:S(2)}) collective-permute-start(bf16[8,64,128]{2,1,0:T(8,128)(2,1)S(1)} %all_to_all.15.refs_0_), channel_id=1, source_target_pairs={{0,5},{1,6},{2,7},{3,0},{4,1},{5,2},{6,3},{7,4},{8,13},{9,14},{10,... | collective-permute-start | bytes 393224 | tf_op jit(solution)/shard_map/ppermute | solution.py:339
  33.2 4.3 %collective-permute-start.6 = (bf16[8,64,128]{2,1,0:T(8,128)(2,1)S(1)}, bf16[8,64,128]{2,1,0:T(8,128)(2,1)S(1)}, u32[]{:S(2)}, u32[]{:S(2)}) collective-permute-start(bf16[8,64,128]{2,1,0:T(8,128)(2,1)S(1)} %all_to_all.15.refs_0_), channel_id=1, source_target_pairs={{0,4},{1,5},{2,6},{3,7},{4,0},{5,1},{6,2},{7,3},{8,12},{9,13},{10,... | collective-permute-start | bytes 393224 | tf_op jit(solution)/shard_map/ppermute | solution.py:339
  37.5 8.5 %collective-permute-done.4.refs_1_ = bf16[8,64,128]{2,1,0:T(8,128)(2,1)S(1)} collective-permute-done((bf16[8,64,128]{2,1,0:T(8,128)(2,1)S(1)}, bf16[8,64,128]{2,1,0:T(8,128)(2,1)S(1)}, u32[]{:S(2)}, u32[]{:S(2)}) %collective-permute-start.4) | collective-permute-done | bytes 131104 | tf_op jit(solution)/shard_map/ppermute | solution.py:339
  46.0 3.3 %collective-permute-done.5.refs_2_ = bf16[8,64,128]{2,1,0:T(8,128)(2,1)S(1)} collective-permute-done((bf16[8,64,128]{2,1,0:T(8,128)(2,1)S(1)}, bf16[8,64,128]{2,1,0:T(8,128)(2,1)S(1)}, u32[]{:S(2)}, u32[]{:S(2)}) %collective-permute-start.5) | collective-permute-done | bytes 131104 | tf_op jit(solution)/shard_map/ppermute | solution.py:339
  49.3 3.4 %collective-permute-start.10 = (bf16[8,64,128]{2,1,0:T(8,128)(2,1)S(1)}, bf16[8,64,128]{2,1,0:T(8,128)(2,1)S(1)}, u32[]{:S(2)}, u32[]{:S(2)}) collective-permute-start(bf16[8,64,128]{2,1,0:T(8,128)(2,1)S(1)} %all_to_all.15.refs_0_), channel_id=1, source_target_pairs={{0,2},{1,3},{2,4},{3,5},{4,6},{5,7},{6,0},{7,1},{8,10},{9,11},{10,... | collective-permute-start | bytes 393224 | tf_op jit(solution)/shard_map/ppermute | solution.py:339
  52.8 2.2 %collective-permute-start.9 = (bf16[8,64,128]{2,1,0:T(8,128)(2,1)S(1)}, bf16[8,64,128]{2,1,0:T(8,128)(2,1)S(1)}, u32[]{:S(2)}, u32[]{:S(2)}) collective-permute-start(bf16[8,64,128]{2,1,0:T(8,128)(2,1)S(1)} %all_to_all.15.refs_0_), channel_id=1, source_target_pairs={{0,6},{1,7},{2,0},{3,1},{4,2},{5,3},{6,4},{7,5},{8,14},{9,15},{10,... | collective-permute-start | bytes 393224 | tf_op jit(solution)/shard_map/ppermute | solution.py:339
  57.7 2.5 %collective-permute-start.12 = (bf16[2,64,1024]{2,1,0:T(8,128)(2,1)S(1)}, bf16[2,64,1024]{2,1,0:T(8,128)(2,1)S(1)}, u32[]{:S(2)}, u32[]{:S(2)}) collective-permute-start(bf16[2,64,1024]{2,1,0:T(8,128)(2,1)S(1)} %get-tuple-element.74), channel_id=1, source_target_pairs={{0,7},{1,0},{2,1},{3,2},{4,3},{5,4},{6,5},{7,6},{8,15},{9,8},{10,9... | collective-permute-start | bytes 786440 | tf_op jit(solution)/shard_map/ppermute | solution.py:339
  60.3 2.5 %collective-permute-start.16 = (bf16[6,8,64,128]{3,2,1,0:T(8,128)(2,1)S(1)}, bf16[6,8,64,128]{3,2,1,0:T(8,128)(2,1)S(1)}, u32[]{:S(2)}, u32[]{:S(2)}) collective-permute-start(bf16[6,8,64,128]{3,2,1,0:T(8,128)(2,1)S(1)} %pack.1.first_ref), channel_id=1, source_target_pairs={{0,24},{8,0},{16,8},{24,16},{1,25},{9,1},{17,9},{25,17},{2,26},{10... | collective-permute-start | bytes 2359304 | tf_op jit(solution)/shard_map/ppermute | solution.py:339
  63.6 6.3 %collective-permute-done.13.far_ref = bf16[64,1024]{1,0:T(8,128)(2,1)S(1)} collective-permute-done((bf16[64,1024]{1,0:T(8,128)(2,1)S(1)}, bf16[64,1024]{1,0:T(8,128)(2,1)S(1)}, u32[]{:S(2)}, u32[]{:S(2)}) %collective-permute-start.13) | collective-permute-done | bytes 131104 | tf_op jit(solution)/shard_map/ppermute | solution.py:339
  70.0 2.5 %collective-permute-start.20 = (bf16[8,8,64,128]{3,2,1,0:T(8,128)(2,1)S(1)}, bf16[8,8,64,128]{3,2,1,0:T(8,128)(2,1)S(1)}, u32[]{:S(2)}, u32[]{:S(2)}) collective-permute-start(bf16[8,8,64,128]{3,2,1,0:T(8,128)(2,1)S(1)} %get-tuple-element.97.rest_0_), channel_id=1, source_target_pairs={{0,16},{8,24},{16,0},{24,8},{1,17},{9,25},{17,1},{25,9},{2,18},{10... | collective-permute-start | bytes 3145736 | tf_op jit(solution)/shard_map/ppermute | solution.py:339
  73.2 3.4 %collective-permute-start.15 = (bf16[64,1024]{1,0:T(8,128)(2,1)S(1)}, bf16[64,1024]{1,0:T(8,128)(2,1)S(1)}, u32[]{:S(2)}, u32[]{:S(2)}) collective-permute-start(bf16[64,1024]{1,0:T(8,128)(2,1)S(1)} %get-tuple-element.89), channel_id=1, source_target_pairs={{0,6},{1,7},{2,0},{3,1},{4,2},{5,3},{6,4},{7,5},{8,14},{9,15},{10,... | collective-permute-start | bytes 393224 | tf_op jit(solution)/shard_map/ppermute | solution.py:339
  76.6 3.5 %collective-permute-done.14.up_ref = bf16[64,1024]{1,0:T(8,128)(2,1)S(1)} collective-permute-done((bf16[64,1024]{1,0:T(8,128)(2,1)S(1)}, bf16[64,1024]{1,0:T(8,128)(2,1)S(1)}, u32[]{:S(2)}, u32[]{:S(2)}) %collective-permute-start.14) | collective-permute-done | bytes 131104 | tf_op jit(solution)/shard_map/ppermute | solution.py:339
  80.5 12.8 %collective-permute-done.16.rest_1_ = bf16[6,8,64,128]{3,2,1,0:T(8,128)(2,1)S(1)} collective-permute-done((bf16[6,8,64,128]{3,2,1,0:T(8,128)(2,1)S(1)}, bf16[6,8,64,128]{3,2,1,0:T(8,128)(2,1)S(1)}, u32[]{:S(2)}, u32[]{:S(2)}) %collective-permute-start.16) | collective-permute-done | bytes 786464 | tf_op jit(solution)/shard_map/ppermute | solution.py:339
  93.3 9.0 %collective-permute-done.17.rest_3_ = bf16[6,8,64,128]{3,2,1,0:T(8,128)(2,1)S(1)} collective-permute-done((bf16[6,8,64,128]{3,2,1,0:T(8,128)(2,1)S(1)}, bf16[6,8,64,128]{3,2,1,0:T(8,128)(2,1)S(1)}, u32[]{:S(2)}, u32[]{:S(2)}) %collective-permute-start.17) | collective-permute-done | bytes 786464 | tf_op jit(solution)/shard_map/ppermute | solution.py:339
  104.4 9.4 %all_to_all.16.back_ref = bf16[8,64,128]{2,1,0:T(8,128)(2,1)S(1)} all-to-all(bf16[8,64,128]{2,1,0:T(8,128)(2,1)S(1)} %z_sum.1), channel_id=1, replica_groups=mesh['y'=4,'c'=2,'x'=4,'z'=8] {'y','c'}, dimensions={0} | all-to-all | bytes 262144 | tf_op jit(solution)/shard_map/all_to_all | solution.py:373
  115.1 6.3 %all-to-all-start.2 = ((f32[32,8,128]{2,1,0:T(8,128)}), f32[32,8,128]{2,1,0:T(8,128)S(1)}, u32[]{:S(2)}, u32[]{:S(2)}) async-start(f32[32,8,128]{2,1,0:T(8,128)} %get-tuple-element.96), calls=%async_computation.2 | async-start | bytes 262144 | tf_op jit(solution)/shard_map/all_to_all | solution.py:376
  122.4 9.0 %backward.1 = (bf16[448,1024]{1,0:T(8,128)(2,1)}, f32[448,2048]{1,0:T(8,128)}, f32[224,128]{1,0:T(8,128)}) custom-call(s32[2]{0:T(128)S(1)} %pad_add_fusion.where_ref, bf16[448,1024]{1,0:T(8,128)(2,1)} %bitcast.23, s32[448,2048]{1,0:T(8,128)} %bitcast.20, f32[224,128]{1,0:T(8,128)} %bitcast.26, bf16[8,8,64,128]{3,2,1,0:T(8,128)(2,1)} %copy-done, ...), custom_call_target="tpu_custom_call" | custom-call | tf_op jit(solution)/shard_map/backward/pallas_call | solution.py:318
  (52 shorter events, 12.4 us)
Async XLA Ops:
  3.7 15.0 %collective-permute-start = (bf16[256,1024]{1,0:T(8,128)(2,1)S(1)}, bf16[256,1024]{1,0:T(8,128)(2,1)S(1)}, u32[]{:S(2)}, u32[]{:S(2)}) collective-permute-start(bf16[256,1024]{1,0:T(8,128)(2,1)S(1)} %get-tuple-element.57), channel_id=1, source_target_pairs={{0,8},{8,16},{16,24},{24,0},{1,9},{9,17},{17,25},{25,1},{2,10},{10... | collective-permute-start | bytes 1572872 | tf_op jit(solution)/shard_map/ppermute | solution.py:339
  5.3 13.4 %collective-permute-start.1 = (bf16[256,1024]{1,0:T(8,128)(2,1)S(1)}, bf16[256,1024]{1,0:T(8,128)(2,1)S(1)}, u32[]{:S(2)}, u32[]{:S(2)}) collective-permute-start(bf16[256,1024]{1,0:T(8,128)(2,1)S(1)} %get-tuple-element.58), channel_id=1, source_target_pairs={{0,24},{8,0},{16,8},{24,16},{1,25},{9,1},{17,9},{25,17},{2,26},{10... | collective-permute-start | bytes 1572872 | tf_op jit(solution)/shard_map/ppermute | solution.py:339
  23.2 32.7 %collective-permute-start.2 = (bf16[512,1024]{1,0:T(8,128)(2,1)S(1)}, bf16[512,1024]{1,0:T(8,128)(2,1)S(1)}, u32[]{:S(2)}, u32[]{:S(2)}) collective-permute-start(bf16[512,1024]{1,0:T(8,128)(2,1)S(1)} %get-tuple-element.66), channel_id=1, source_target_pairs={{0,8},{8,16},{16,24},{24,0},{1,9},{9,17},{17,25},{25,1},{2,10},{10... | collective-permute-start | bytes 3145736 | tf_op jit(solution)/shard_map/ppermute | solution.py:339
  24.8 31.1 %collective-permute-start.3 = (bf16[512,1024]{1,0:T(8,128)(2,1)S(1)}, bf16[512,1024]{1,0:T(8,128)(2,1)S(1)}, u32[]{:S(2)}, u32[]{:S(2)}) collective-permute-start(bf16[512,1024]{1,0:T(8,128)(2,1)S(1)} %get-tuple-element.67), channel_id=1, source_target_pairs={{0,24},{8,0},{16,8},{24,16},{1,25},{9,1},{17,9},{25,17},{2,26},{10... | collective-permute-start | bytes 3145736 | tf_op jit(solution)/shard_map/ppermute | solution.py:339
  26.5 19.5 %collective-permute-start.4 = (bf16[8,64,128]{2,1,0:T(8,128)(2,1)S(1)}, bf16[8,64,128]{2,1,0:T(8,128)(2,1)S(1)}, u32[]{:S(2)}, u32[]{:S(2)}) collective-permute-start(bf16[8,64,128]{2,1,0:T(8,128)(2,1)S(1)} %all_to_all.15.refs_0_), channel_id=1, source_target_pairs={{0,5},{1,6},{2,7},{3,0},{4,1},{5,2},{6,3},{7,4},{8,13},{9,14},{10,... | collective-permute-start | bytes 393224 | tf_op jit(solution)/shard_map/ppermute | solution.py:339
  33.2 16.1 %collective-permute-start.5 = (bf16[8,64,128]{2,1,0:T(8,128)(2,1)S(1)}, bf16[8,64,128]{2,1,0:T(8,128)(2,1)S(1)}, u32[]{:S(2)}, u32[]{:S(2)}) collective-permute-start(bf16[8,64,128]{2,1,0:T(8,128)(2,1)S(1)} %all_to_all.15.refs_0_), channel_id=1, source_target_pairs={{0,3},{1,4},{2,5},{3,6},{4,7},{5,0},{6,1},{7,2},{8,11},{9,12},{10,... | collective-permute-start | bytes 393224 | tf_op jit(solution)/shard_map/ppermute | solution.py:339
  33.2 16.1 %collective-permute-start.6 = (bf16[8,64,128]{2,1,0:T(8,128)(2,1)S(1)}, bf16[8,64,128]{2,1,0:T(8,128)(2,1)S(1)}, u32[]{:S(2)}, u32[]{:S(2)}) collective-permute-start(bf16[8,64,128]{2,1,0:T(8,128)(2,1)S(1)} %all_to_all.15.refs_0_), channel_id=1, source_target_pairs={{0,4},{1,5},{2,6},{3,7},{4,0},{5,1},{6,2},{7,3},{8,12},{9,13},{10,... | collective-permute-start | bytes 393224 | tf_op jit(solution)/shard_map/ppermute | solution.py:339
  46.0 6.7 %collective-permute-start.7 = (bf16[8,64,128]{2,1,0:T(8,128)(2,1)S(1)}, bf16[8,64,128]{2,1,0:T(8,128)(2,1)S(1)}, u32[]{:S(2)}, u32[]{:S(2)}) collective-permute-start(bf16[8,64,128]{2,1,0:T(8,128)(2,1)S(1)} %all_to_all.15.refs_0_), channel_id=1, source_target_pairs={{0,7},{1,0},{2,1},{3,2},{4,3},{5,4},{6,5},{7,6},{8,15},{9,8},{10,9... | collective-permute-start | bytes 393224 | tf_op jit(solution)/shard_map/ppermute | solution.py:339
  49.3 6.5 %collective-permute-start.8 = (bf16[8,64,128]{2,1,0:T(8,128)(2,1)S(1)}, bf16[8,64,128]{2,1,0:T(8,128)(2,1)S(1)}, u32[]{:S(2)}, u32[]{:S(2)}) collective-permute-start(bf16[8,64,128]{2,1,0:T(8,128)(2,1)S(1)} %all_to_all.15.refs_0_), channel_id=1, source_target_pairs={{0,1},{1,2},{2,3},{3,4},{4,5},{5,6},{6,7},{7,0},{8,9},{9,10},{10,1... | collective-permute-start | bytes 393224 | tf_op jit(solution)/shard_map/ppermute | solution.py:339
  49.3 13.4 %collective-permute-start.10 = (bf16[8,64,128]{2,1,0:T(8,128)(2,1)S(1)}, bf16[8,64,128]{2,1,0:T(8,128)(2,1)S(1)}, u32[]{:S(2)}, u32[]{:S(2)}) collective-permute-start(bf16[8,64,128]{2,1,0:T(8,128)(2,1)S(1)} %all_to_all.15.refs_0_), channel_id=1, source_target_pairs={{0,2},{1,3},{2,4},{3,5},{4,6},{5,7},{6,0},{7,1},{8,10},{9,11},{10,... | collective-permute-start | bytes 393224 | tf_op jit(solution)/shard_map/ppermute | solution.py:339
  52.8 10.0 %collective-permute-start.9 = (bf16[8,64,128]{2,1,0:T(8,128)(2,1)S(1)}, bf16[8,64,128]{2,1,0:T(8,128)(2,1)S(1)}, u32[]{:S(2)}, u32[]{:S(2)}) collective-permute-start(bf16[8,64,128]{2,1,0:T(8,128)(2,1)S(1)} %all_to_all.15.refs_0_), channel_id=1, source_target_pairs={{0,6},{1,7},{2,0},{3,1},{4,2},{5,3},{6,4},{7,5},{8,14},{9,15},{10,... | collective-permute-start | bytes 393224 | tf_op jit(solution)/shard_map/ppermute | solution.py:339
  56.7 13.2 %collective-permute-start.11 = (bf16[2,64,1024]{2,1,0:T(8,128)(2,1)S(1)}, bf16[2,64,1024]{2,1,0:T(8,128)(2,1)S(1)}, u32[]{:S(2)}, u32[]{:S(2)}) collective-permute-start(bf16[2,64,1024]{2,1,0:T(8,128)(2,1)S(1)} %get-tuple-element.73), channel_id=1, source_target_pairs={{0,1},{1,2},{2,3},{3,4},{4,5},{5,6},{6,7},{7,0},{8,9},{9,10},{10,1... | collective-permute-start | bytes 786440 | tf_op jit(solution)/shard_map/ppermute | solution.py:339
  57.7 12.2 %collective-permute-start.12 = (bf16[2,64,1024]{2,1,0:T(8,128)(2,1)S(1)}, bf16[2,64,1024]{2,1,0:T(8,128)(2,1)S(1)}, u32[]{:S(2)}, u32[]{:S(2)}) collective-permute-start(bf16[2,64,1024]{2,1,0:T(8,128)(2,1)S(1)} %get-tuple-element.74), channel_id=1, source_target_pairs={{0,7},{1,0},{2,1},{3,2},{4,3},{5,4},{6,5},{7,6},{8,15},{9,8},{10,9... | collective-permute-start | bytes 786440 | tf_op jit(solution)/shard_map/ppermute | solution.py:339
  60.3 33.0 %collective-permute-start.16 = (bf16[6,8,64,128]{3,2,1,0:T(8,128)(2,1)S(1)}, bf16[6,8,64,128]{3,2,1,0:T(8,128)(2,1)S(1)}, u32[]{:S(2)}, u32[]{:S(2)}) collective-permute-start(bf16[6,8,64,128]{3,2,1,0:T(8,128)(2,1)S(1)} %pack.1.first_ref), channel_id=1, source_target_pairs={{0,24},{8,0},{16,8},{24,16},{1,25},{9,1},{17,9},{25,17},{2,26},{10... | collective-permute-start | bytes 2359304 | tf_op jit(solution)/shard_map/ppermute | solution.py:339
  62.7 39.6 %collective-permute-start.17 = (bf16[6,8,64,128]{3,2,1,0:T(8,128)(2,1)S(1)}, bf16[6,8,64,128]{3,2,1,0:T(8,128)(2,1)S(1)}, u32[]{:S(2)}, u32[]{:S(2)}) collective-permute-start(bf16[6,8,64,128]{3,2,1,0:T(8,128)(2,1)S(1)} %pack.1.first_ref), channel_id=1, source_target_pairs={{0,8},{8,16},{16,24},{24,0},{1,9},{9,17},{17,25},{25,1},{2,10},{10... | collective-permute-start | bytes 2359304 | tf_op jit(solution)/shard_map/ppermute | solution.py:339
  62.7 7.2 %collective-permute-start.13 = (bf16[64,1024]{1,0:T(8,128)(2,1)S(1)}, bf16[64,1024]{1,0:T(8,128)(2,1)S(1)}, u32[]{:S(2)}, u32[]{:S(2)}) collective-permute-start(bf16[64,1024]{1,0:T(8,128)(2,1)S(1)} %get-tuple-element.77), channel_id=1, source_target_pairs={{0,2},{1,3},{2,4},{3,5},{4,6},{5,7},{6,0},{7,1},{8,10},{9,11},{10,... | collective-permute-start | bytes 393224 | tf_op jit(solution)/shard_map/ppermute | solution.py:339
  63.6 57.7 %copy-start = (bf16[8,8,64,128]{3,2,1,0:T(8,128)(2,1)}, bf16[8,8,64,128]{3,2,1,0:T(8,128)(2,1)S(1)}, u32[]{:S(2)}) copy-start(bf16[8,8,64,128]{3,2,1,0:T(8,128)(2,1)S(1)} %get-tuple-element.97.rest_0_) | copy-start | bytes 3145732
  70.0 51.3 %collective-permute-start.20 = (bf16[8,8,64,128]{3,2,1,0:T(8,128)(2,1)S(1)}, bf16[8,8,64,128]{3,2,1,0:T(8,128)(2,1)S(1)}, u32[]{:S(2)}, u32[]{:S(2)}) collective-permute-start(bf16[8,8,64,128]{3,2,1,0:T(8,128)(2,1)S(1)} %get-tuple-element.97.rest_0_), channel_id=1, source_target_pairs={{0,16},{8,24},{16,0},{24,8},{1,17},{9,25},{17,1},{25,9},{2,18},{10... | collective-permute-start | bytes 3145736 | tf_op jit(solution)/shard_map/ppermute | solution.py:339
  72.5 7.6 %collective-permute-start.14 = (bf16[64,1024]{1,0:T(8,128)(2,1)S(1)}, bf16[64,1024]{1,0:T(8,128)(2,1)S(1)}, u32[]{:S(2)}, u32[]{:S(2)}) collective-permute-start(bf16[64,1024]{1,0:T(8,128)(2,1)S(1)} %get-tuple-element.88), channel_id=1, source_target_pairs={{0,2},{1,3},{2,4},{3,5},{4,6},{5,7},{6,0},{7,1},{8,10},{9,11},{10,... | collective-permute-start | bytes 393224 | tf_op jit(solution)/shard_map/ppermute | solution.py:339
  73.2 7.3 %collective-permute-start.15 = (bf16[64,1024]{1,0:T(8,128)(2,1)S(1)}, bf16[64,1024]{1,0:T(8,128)(2,1)S(1)}, u32[]{:S(2)}, u32[]{:S(2)}) collective-permute-start(bf16[64,1024]{1,0:T(8,128)(2,1)S(1)} %get-tuple-element.89), channel_id=1, source_target_pairs={{0,6},{1,7},{2,0},{3,1},{4,2},{5,3},{6,4},{7,5},{8,14},{9,15},{10,... | collective-permute-start | bytes 393224 | tf_op jit(solution)/shard_map/ppermute | solution.py:339
  93.3 28.1 %copy-start.5 = (bf16[6,8,64,128]{3,2,1,0:T(8,128)(2,1)}, bf16[6,8,64,128]{3,2,1,0:T(8,128)(2,1)S(1)}, u32[]{:S(2)}) copy-start(bf16[6,8,64,128]{3,2,1,0:T(8,128)(2,1)S(1)} %collective-permute-done.16.rest_1_) | copy-start | bytes 2359300
  102.3 11.6 %collective-permute-start.18 = (bf16[2,8,64,128]{3,2,1,0:T(8,128)(2,1)S(1)}, bf16[2,8,64,128]{3,2,1,0:T(8,128)(2,1)S(1)}, u32[]{:S(2)}, u32[]{:S(2)}) collective-permute-start(bf16[2,8,64,128]{3,2,1,0:T(8,128)(2,1)S(1)} %get-tuple-element.93), channel_id=1, source_target_pairs={{0,24},{8,0},{16,8},{24,16},{1,25},{9,1},{17,9},{25,17},{2,26},{10... | collective-permute-start | bytes 786440 | tf_op jit(solution)/shard_map/ppermute | solution.py:339
  103.2 10.7 %collective-permute-start.19 = (bf16[2,8,64,128]{3,2,1,0:T(8,128)(2,1)S(1)}, bf16[2,8,64,128]{3,2,1,0:T(8,128)(2,1)S(1)}, u32[]{:S(2)}, u32[]{:S(2)}) collective-permute-start(bf16[2,8,64,128]{3,2,1,0:T(8,128)(2,1)S(1)} %get-tuple-element.93), channel_id=1, source_target_pairs={{0,8},{8,16},{16,24},{24,0},{1,9},{9,17},{17,25},{25,1},{2,10},{10... | collective-permute-start | bytes 786440 | tf_op jit(solution)/shard_map/ppermute | solution.py:339
  115.1 16.5 %all-to-all-start.2 = ((f32[32,8,128]{2,1,0:T(8,128)}), f32[32,8,128]{2,1,0:T(8,128)S(1)}, u32[]{:S(2)}, u32[]{:S(2)}) async-start(f32[32,8,128]{2,1,0:T(8,128)} %get-tuple-element.96), calls=%async_computation.2 | async-start | bytes 262144 | tf_op jit(solution)/shard_map/all_to_all | solution.py:376
  (7 other events, 36.0 us)

commit v10 on v6

--- a/solution.py
+++ b/solution.py
@@ -29,13 +29,14 @@
     return pltpu.with_memory_space_constraint(array, pltpu.HBM)
 
 
-def call(body, name, where, operands, outs, scratch=(), far=()):
+def call(body, name, where, operands, outs, scratch=(), far=(), keep=None):
     heads = [] if where is None else [where]
+    keep = len(outs) if keep is None else keep
     return pl.pallas_call(
         body,
         in_specs=[SMEM] * len(heads) + [HBM] * len(far) + [VMEM] * len(operands),
         out_specs=[VMEM] * len(outs),
-        out_shape=[pltpu.VMEM(shape, dtype) for shape, dtype in outs],
+        out_shape=[(pltpu.VMEM if i < keep else sds)(*out) for i, out in enumerate(outs)],
         scratch_shapes=list(scratch),
         compiler_params=SMALL,
         name=name,
@@ -132,9 +133,9 @@
 
 
 def join_body(
-    where_ref, hidden_hbm, codes_hbm, scales_hbm, top_ref, bottom_ref, up_ref, down_ref, hidden, codes, scales, table, sems
+    where_ref, hidden_hbm, codes_hbm, scales_hbm, top_ref, bottom_ref, up_ref, down_ref, own_ref, hidden, codes, scales, table, sems
 ):
-    first, *copies = loads(where_ref, (1, 3), hidden_hbm, codes_hbm, scales_hbm, hidden, codes, scales, sems)
+    first, *copies = loads(where_ref, (1, 3, 0), hidden_hbm, codes_hbm, scales_hbm, hidden, codes, scales, sems)
     half = BLOCK // 2
     value = block_value(where_ref, 1, hidden, codes.at[0], scales, table, copies[0], (first,))
     up_ref[:half] = (value[:half] + top_ref[...].astype(F32)).astype(BF16)
@@ -142,22 +143,13 @@
     value = block_value(where_ref, 3, hidden, codes.at[1], scales, table, copies[1])
     down_ref[:half] = value[:half].astype(BF16)
     down_ref[half:] = (value[half:] + bottom_ref[...].astype(F32)).astype(BF16)
+    own_ref[...] = block_value(where_ref, 0, hidden, codes.at[2], scales, table, copies[2])
 
 
 def forward_join(where, hidden, codes, scales, top, bottom):
-    outs = [((BLOCK, SLOTS), BF16)] * 2
+    outs = [((BLOCK, SLOTS), BF16)] * 2 + [((BLOCK, SLOTS), F32)]
     far = (hidden, codes, scales)
-    return call(join_body, "forward_join", where, [top, bottom], outs, buffers(hidden.shape[0], 2), far)
-
-
-def own_body(where_ref, hidden_hbm, codes_hbm, scales_hbm, own_ref, hidden, codes, scales, table, sems):
-    first, *copies = loads(where_ref, (0,), hidden_hbm, codes_hbm, scales_hbm, hidden, codes, scales, sems)
-    own_ref[...] = block_value(where_ref, 0, hidden, codes.at[0], scales, table, copies[0], (first,))
-
-
-def forward_own(where, *arrays):
-    outs = [((BLOCK, SLOTS), F32)]
-    return call(own_body, "forward_own", where, [], outs, buffers(arrays[0].shape[0], 1), arrays)[0]
+    return call(join_body, "forward_join", where, [top, bottom], outs, buffers(hidden.shape[0], 3), far)
 
 
 def x_sum_body(where_ref, own_ref, up_ref, down_ref, ups_ref, downs_ref, far_ref, up2_ref, down2_ref, rest_ref):
@@ -201,7 +193,7 @@
     return call(z_sum_body, "z_sum", None, arrays, [((EXPERTS, COLS, CAP), BF16)])[0]
 
 
-def combine_body(place_ref, gate_ref, grad_ref, back_ref, out_ref, spread_ref):
+def combine_body(place_ref, gate_ref, grad_ref, back_ref, spread_ref, out_ref):
     back = jnp.concatenate([back_ref[e] for e in range(EXPERTS)], axis=1)
     grad = grad_ref[...].astype(F32)
     total = None
@@ -217,8 +209,8 @@
 
 
 def combine(place, gate, grad, back):
-    outs = [(grad.shape, BF16), ((NX * NZ, 8, 128), F32)]
-    return call(combine_body, "combine", None, [place, gate, grad, back], outs)
+    outs = [((NX * NZ, 8, 128), F32), (grad.shape, BF16)]
+    return call(combine_body, "combine", None, [place, gate, grad, back], outs, keep=1)
 
 
 def gate_sum_body(parts_ref, out_ref):
@@ -229,7 +221,7 @@
 
 
 def gate_sum(parts):
-    return call(gate_sum_body, "gate_sum", None, [parts], [((2, 512), F32)])[0]
+    return call(gate_sum_body, "gate_sum", None, [parts], [((2, 512), F32)], keep=0)[0]
 
 
 NEAREST = (0, 1, 7, 2, 6, 3, 5, 4)
@@ -346,24 +338,25 @@
     place, outbound = slot_grads(index, gate, grad)
     shard = lax.all_to_all(outbound, ("y", "c"), 0, 0, tiled=True)
     far_top, far_bottom, shard = lax.optimization_barrier((far_top, far_bottom, shard))
-    up, down = forward_join(where, *weights, far_top, far_bottom)
-    where_late, up, down, shard = lax.optimization_barrier((where, up, down, shard))
+    up, down, own = forward_join(where, *weights, far_top, far_bottom)
+    up, down, shard = lax.optimization_barrier((up, down, shard))
     up = shift(up, "x", 1)
     down = shift(down, "x", -1)
-    own = forward_own(where_late, *weights)
     along = [shift(shard, "z", -k) for k in NEAREST[1:]]
+    up, down, *along[3:] = lax.optimization_barrier((up, down, *along[3:]))
 
     ups, downs, far, up2, down2, rest = x_sum(where, own, up, down)
     rest, *along = lax.optimization_barrier((rest, *along))
     mine = pack(shard, *along)
     packs = [mine, shift(mine, "x", -1), shift(mine, "x", 1)]
+    ups, downs, far, _ = lax.optimization_barrier((ups, downs, far, mine))
     ups, downs, far = shift(ups, "z", 1), shift(downs, "z", -1), shift(far, "z", 2)
     up2, down2 = mid_sum(up2, down2, ups, downs, far)
     up2, down2 = shift(up2, "z", 2), shift(down2, "z", -2)
     up2, down2, packs[1], packs[2] = lax.optimization_barrier((up2, down2, packs[1], packs[2]))
     packs += [shift(packs[1][: NZ // 2], "x", -1), shift(packs[2][NZ // 2 :], "x", 1)]
     returned = lax.all_to_all(z_sum(rest, ups, downs, up2, down2), ("y", "c"), 0, 0, tiled=True)
-    combined, spread = combine(place, gate, grad, returned)
+    spread, combined = combine(place, gate, grad, returned)
     gate_parts = lax.all_to_all(spread, ("x", "z"), 0, 0, tiled=True)
     hidden_grad, weight_grad, scale_grad = backward(where, *weights, packs)
     gate_parts, hidden_grad = lax.optimization_barrier((gate_parts, hidden_grad))

time: 119 us -> 119 us (level); the launches traced: 117 us -> 119 us
  waiting for transfers between devices: 26.2 us -> 28.4 us
  starting transfers between devices: 46.6 us -> 48.5 us
  Pallas kernels: 22 us -> 20.5 us
  local copies, waits for them, and re-layouts: 2.99 us -> 1.77 us
    ppermute x20, starting transfers between devices: 40.8 us -> 42.4 us  [shift(): lax.ppermute(value, axis, [(i, (i + by) % size) for i in range(size)])]
    ppermute x20, waiting for transfers between devices: 25.7 us -> 27.3 us  [shift(): lax.ppermute(value, axis, [(i, (i + by) % size) for i in range(size)])]
    pallas_call x10 -> x9, Pallas kernels: 12.9 us -> 11.4 us  [call(): pl.pallas_call(body, in_specs=[SMEM] * len(heads) + [HBM] * len(far) + [V...]
    unnamed x14 -> x12, local copies, waits for them, and re-layouts: 1.25 us -> 0.02 us
  transfers between devices with their start and end apart: 21 -> 21, of which waited for: 6 -> 8; matrix products, arithmetic and copies ran while one was open for 1% -> 0% of each run, Pallas kernels for 13% -> 10%
where the time goes in v10:
time: 119 us
  starting transfers between devices  48.5 us (41%)
  waiting for transfers between devices  28.4 us (24%)
  Pallas kernels  20.5 us (17%)
  blocking collectives  18.8 us (16%)
  local copies, waits for them, and re-layouts  1.77 us (1%)
    ppermute x20, starting transfers between devices, shift(): lax.ppermute(value, axis, [(i, (i + by) % size) for i in range(size)])  42.4 us
    ppermute x20, waiting for transfers between devices, shift(): lax.ppermute(value, axis, [(i, (i + by) % size) for i in range(size)])  27.3 us
    pallas_call x9, Pallas kernels, call(): pl.pallas_call(body, in_specs=[SMEM] * len(heads) + [HBM] * len(far) + [V...  11.4 us
    all_to_all x1, blocking collectives, on_device(): shard = lax.all_to_all(outbound, ('y', 'c'), 0, 0, tiled=True)  9.39 us
    all_to_all x1, blocking collectives, on_device(): lax.all_to_all(z_sum(rest, ups, downs, up2, down2), ('y', 'c'), 0, 0, til...  9.37 us
    pallas_call x1, Pallas kernels, backward(): pl.pallas_call(backward_body, in_specs=[SMEM] + [HBM] * (4 + NX), out_spe...  9.12 us
    all_to_all x1, starting transfers between devices, on_device(): gate_parts = lax.all_to_all(spread, ('x', 'z'), 0, 0, tiled=True)  6.06 us
  transfers between devices with their start and end apart: 21, of which 8 were waited for; matrix products, arithmetic and copies ran while one was open for 0% of the time, Pallas kernels for 10%

profile of v10, /device:TPU:8, one launch (start us, length us, event | category | flops | bytes accessed | tf_op | source)
XLA Modules:
  0.0 118.7 jit_solution(14101862884598701687)
XLA Ops:
  0.7 2.9 %forward_far.1 = (bf16[256,1024]{1,0:T(8,128)(2,1)S(1)}, bf16[256,1024]{1,0:T(8,128)(2,1)S(1)}) custom-call(s32[2]{0:T(128)S(1)} %pad_add_fusion.where_ref, bf16[448,1024]{1,0:T(8,128)(2,1)} %bitcast.21, s32[448,2048]{1,0:T(8,128)} %bitcast.18, f32[224,128]{1,0:T(8,128)} %bitcast.24), custom_call_target="tpu_custom_call" | custom-call | tf_op jit(solution)/shard_map/forward_far/pallas_call | solution.py:35
  3.7 1.6 %collective-permute-start = (bf16[256,1024]{1,0:T(8,128)(2,1)S(1)}, bf16[256,1024]{1,0:T(8,128)(2,1)S(1)}, u32[]{:S(2)}, u32[]{:S(2)}) collective-permute-start(bf16[256,1024]{1,0:T(8,128)(2,1)S(1)} %get-tuple-element.55), channel_id=1, source_target_pairs={{0,8},{8,16},{16,24},{24,0},{1,9},{9,17},{17,25},{25,1},{2,10},{10... | collective-permute-start | bytes 1572872 | tf_op jit(solution)/shard_map/ppermute | solution.py:326
  5.3 1.7 %collective-permute-start.1 = (bf16[256,1024]{1,0:T(8,128)(2,1)S(1)}, bf16[256,1024]{1,0:T(8,128)(2,1)S(1)}, u32[]{:S(2)}, u32[]{:S(2)}) collective-permute-start(bf16[256,1024]{1,0:T(8,128)(2,1)S(1)} %get-tuple-element.56), channel_id=1, source_target_pairs={{0,24},{8,0},{16,8},{24,16},{1,25},{9,1},{17,9},{25,17},{2,26},{10... | collective-permute-start | bytes 1572872 | tf_op jit(solution)/shard_map/ppermute | solution.py:326
  8.0 9.4 %all_to_all.15.refs_0_ = bf16[8,64,128]{2,1,0:T(8,128)(2,1)S(1)} all-to-all(bf16[8,64,128]{2,1,0:T(8,128)(2,1)S(1)} %get-tuple-element.57), channel_id=1, replica_groups=mesh['y'=4,'c'=2,'x'=4,'z'=8] {'y','c'}, dimensions={0} | all-to-all | bytes 262144 | tf_op jit(solution)/shard_map/all_to_all | solution.py:339
  17.4 1.3 %collective-permute-done.top_ref = bf16[256,1024]{1,0:T(8,128)(2,1)S(1)} collective-permute-done((bf16[256,1024]{1,0:T(8,128)(2,1)S(1)}, bf16[256,1024]{1,0:T(8,128)(2,1)S(1)}, u32[]{:S(2)}, u32[]{:S(2)}) %collective-permute-start) | collective-permute-done | bytes 524320 | tf_op jit(solution)/shard_map/ppermute | solution.py:326
  18.7 4.5 %forward_join.1 = (bf16[512,1024]{1,0:T(8,128)(2,1)S(1)}, bf16[512,1024]{1,0:T(8,128)(2,1)S(1)}, f32[512,1024]{1,0:T(8,128)S(1)}) custom-call(s32[2]{0:T(128)S(1)} %pad_add_fusion.where_ref, bf16[448,1024]{1,0:T(8,128)(2,1)} %bitcast.22, s32[448,2048]{1,0:T(8,128)} %bitcast.19, f32[224,128]{1,0:T(8,128)} %bitcast.25, ...), custom_call_target="tpu_custom_call" | custom-call | tf_op jit(solution)/shard_map/forward_join/pallas_call | solution.py:35
  23.2 1.6 %collective-permute-start.2 = (bf16[512,1024]{1,0:T(8,128)(2,1)S(1)}, bf16[512,1024]{1,0:T(8,128)(2,1)S(1)}, u32[]{:S(2)}, u32[]{:S(2)}) collective-permute-start(bf16[512,1024]{1,0:T(8,128)(2,1)S(1)} %get-tuple-element.64), channel_id=1, source_target_pairs={{0,8},{8,16},{16,24},{24,0},{1,9},{9,17},{17,25},{25,1},{2,10},{10... | collective-permute-start | bytes 3145736 | tf_op jit(solution)/shard_map/ppermute | solution.py:326
  24.8 1.7 %collective-permute-start.3 = (bf16[512,1024]{1,0:T(8,128)(2,1)S(1)}, bf16[512,1024]{1,0:T(8,128)(2,1)S(1)}, u32[]{:S(2)}, u32[]{:S(2)}) collective-permute-start(bf16[512,1024]{1,0:T(8,128)(2,1)S(1)} %get-tuple-element.65), channel_id=1, source_target_pairs={{0,24},{8,0},{16,8},{24,16},{1,25},{9,1},{17,9},{25,17},{2,26},{10... | collective-permute-start | bytes 3145736 | tf_op jit(solution)/shard_map/ppermute | solution.py:326
  26.5 7.2 %collective-permute-start.7 = (bf16[8,64,128]{2,1,0:T(8,128)(2,1)S(1)}, bf16[8,64,128]{2,1,0:T(8,128)(2,1)S(1)}, u32[]{:S(2)}, u32[]{:S(2)}) collective-permute-start(bf16[8,64,128]{2,1,0:T(8,128)(2,1)S(1)} %all_to_all.15.refs_0_), channel_id=1, source_target_pairs={{0,4},{1,5},{2,6},{3,7},{4,0},{5,1},{6,2},{7,3},{8,12},{9,13},{10,... | collective-permute-start | bytes 393224 | tf_op jit(solution)/shard_map/ppermute | solution.py:326
  33.7 1.9 %collective-permute-start.6 = (bf16[8,64,128]{2,1,0:T(8,128)(2,1)S(1)}, bf16[8,64,128]{2,1,0:T(8,128)(2,1)S(1)}, u32[]{:S(2)}, u32[]{:S(2)}) collective-permute-start(bf16[8,64,128]{2,1,0:T(8,128)(2,1)S(1)} %all_to_all.15.refs_0_), channel_id=1, source_target_pairs={{0,3},{1,4},{2,5},{3,6},{4,7},{5,0},{6,1},{7,2},{8,11},{9,12},{10,... | collective-permute-start | bytes 393224 | tf_op jit(solution)/shard_map/ppermute | solution.py:326
  35.6 3.1 %collective-permute-start.5 = (bf16[8,64,128]{2,1,0:T(8,128)(2,1)S(1)}, bf16[8,64,128]{2,1,0:T(8,128)(2,1)S(1)}, u32[]{:S(2)}, u32[]{:S(2)}) collective-permute-start(bf16[8,64,128]{2,1,0:T(8,128)(2,1)S(1)} %all_to_all.15.refs_0_), channel_id=1, source_target_pairs={{0,5},{1,6},{2,7},{3,0},{4,1},{5,2},{6,3},{7,4},{8,13},{9,14},{10,... | collective-permute-start | bytes 393224 | tf_op jit(solution)/shard_map/ppermute | solution.py:326
  38.7 4.6 %collective-permute-done.7.refs_7_ = bf16[8,64,128]{2,1,0:T(8,128)(2,1)S(1)} collective-permute-done((bf16[8,64,128]{2,1,0:T(8,128)(2,1)S(1)}, bf16[8,64,128]{2,1,0:T(8,128)(2,1)S(1)}, u32[]{:S(2)}, u32[]{:S(2)}) %collective-permute-start.7) | collective-permute-done | bytes 131104 | tf_op jit(solution)/shard_map/ppermute | solution.py:326
  43.4 5.1 %collective-permute-done.6.refs_6_ = bf16[8,64,128]{2,1,0:T(8,128)(2,1)S(1)} collective-permute-done((bf16[8,64,128]{2,1,0:T(8,128)(2,1)S(1)}, bf16[8,64,128]{2,1,0:T(8,128)(2,1)S(1)}, u32[]{:S(2)}, u32[]{:S(2)}) %collective-permute-start.6) | collective-permute-done | bytes 131104 | tf_op jit(solution)/shard_map/ppermute | solution.py:326
  48.5 4.3 %collective-permute-start.10 = (bf16[8,64,128]{2,1,0:T(8,128)(2,1)S(1)}, bf16[8,64,128]{2,1,0:T(8,128)(2,1)S(1)}, u32[]{:S(2)}, u32[]{:S(2)}) collective-permute-start(bf16[8,64,128]{2,1,0:T(8,128)(2,1)S(1)} %all_to_all.15.refs_0_), channel_id=1, source_target_pairs={{0,6},{1,7},{2,0},{3,1},{4,2},{5,3},{6,4},{7,5},{8,14},{9,15},{10,... | collective-permute-start | bytes 393224 | tf_op jit(solution)/shard_map/ppermute | solution.py:326
  52.8 4.5 %collective-permute-start.8 = (bf16[8,64,128]{2,1,0:T(8,128)(2,1)S(1)}, bf16[8,64,128]{2,1,0:T(8,128)(2,1)S(1)}, u32[]{:S(2)}, u32[]{:S(2)}) collective-permute-start(bf16[8,64,128]{2,1,0:T(8,128)(2,1)S(1)} %all_to_all.15.refs_0_), channel_id=1, source_target_pairs={{0,7},{1,0},{2,1},{3,2},{4,3},{5,4},{6,5},{7,6},{8,15},{9,8},{10,9... | collective-permute-start | bytes 393224 | tf_op jit(solution)/shard_map/ppermute | solution.py:326
  60.4 3.0 %collective-permute-start.16 = (bf16[8,8,64,128]{3,2,1,0:T(8,128)(2,1)S(1)}, bf16[8,8,64,128]{3,2,1,0:T(8,128)(2,1)S(1)}, u32[]{:S(2)}, u32[]{:S(2)}) collective-permute-start(bf16[8,8,64,128]{3,2,1,0:T(8,128)(2,1)S(1)} %pack.1.rest_0_), channel_id=1, source_target_pairs={{0,24},{8,0},{16,8},{24,16},{1,25},{9,1},{17,9},{25,17},{2,26},{10... | collective-permute-start | bytes 3145736 | tf_op jit(solution)/shard_map/ppermute | solution.py:326
  63.4 3.7 %collective-permute-start.12 = (bf16[2,64,1024]{2,1,0:T(8,128)(2,1)S(1)}, bf16[2,64,1024]{2,1,0:T(8,128)(2,1)S(1)}, u32[]{:S(2)}, u32[]{:S(2)}) collective-permute-start(bf16[2,64,1024]{2,1,0:T(8,128)(2,1)S(1)} %get-tuple-element.86), channel_id=1, source_target_pairs={{0,7},{1,0},{2,1},{3,2},{4,3},{5,4},{6,5},{7,6},{8,15},{9,8},{10,9... | collective-permute-start | bytes 786440 | tf_op jit(solution)/shard_map/ppermute | solution.py:326
  67.2 11.6 %collective-permute-done.13.far_ref = bf16[64,1024]{1,0:T(8,128)(2,1)S(1)} collective-permute-done((bf16[64,1024]{1,0:T(8,128)(2,1)S(1)}, bf16[64,1024]{1,0:T(8,128)(2,1)S(1)}, u32[]{:S(2)}, u32[]{:S(2)}) %collective-permute-start.13) | collective-permute-done | bytes 131104 | tf_op jit(solution)/shard_map/ppermute | solution.py:326
  79.0 4.1 %collective-permute-start.15 = (bf16[64,1024]{1,0:T(8,128)(2,1)S(1)}, bf16[64,1024]{1,0:T(8,128)(2,1)S(1)}, u32[]{:S(2)}, u32[]{:S(2)}) collective-permute-start(bf16[64,1024]{1,0:T(8,128)(2,1)S(1)} %get-tuple-element.91), channel_id=1, source_target_pairs={{0,6},{1,7},{2,0},{3,1},{4,2},{5,3},{6,4},{7,5},{8,14},{9,15},{10,... | collective-permute-start | bytes 393224 | tf_op jit(solution)/shard_map/ppermute | solution.py:326
  83.1 2.9 %collective-permute-done.14.up_ref = bf16[64,1024]{1,0:T(8,128)(2,1)S(1)} collective-permute-done((bf16[64,1024]{1,0:T(8,128)(2,1)S(1)}, bf16[64,1024]{1,0:T(8,128)(2,1)S(1)}, u32[]{:S(2)}, u32[]{:S(2)}) %collective-permute-start.14) | collective-permute-done | bytes 131104 | tf_op jit(solution)/shard_map/ppermute | solution.py:326
  87.9 3.2 %collective-permute-start.18 = (bf16[4,8,64,128]{3,2,1,0:T(8,128)(2,1)}, bf16[4,8,64,128]{3,2,1,0:T(8,128)(2,1)}, u32[]{:S(2)}, u32[]{:S(2)}) collective-permute-start(bf16[4,8,64,128]{3,2,1,0:T(8,128)(2,1)} %slice.6), channel_id=1, source_target_pairs={{0,24},{8,0},{16,8},{24,16},{1,25},{9,1},{17,9},{25,17},{2,26},{10... | collective-permute-start | bytes 1572872 | tf_op jit(solution)/shard_map/ppermute | solution.py:326
  91.2 9.4 %all_to_all.16.back_ref = bf16[8,64,128]{2,1,0:T(8,128)(2,1)S(1)} all-to-all(bf16[8,64,128]{2,1,0:T(8,128)(2,1)S(1)} %z_sum.1), channel_id=1, replica_groups=mesh['y'=4,'c'=2,'x'=4,'z'=8] {'y','c'}, dimensions={0} | all-to-all | bytes 262144 | tf_op jit(solution)/shard_map/all_to_all | solution.py:358
  101.8 6.1 %all-to-all-start.2 = ((f32[32,8,128]{2,1,0:T(8,128)}), f32[32,8,128]{2,1,0:T(8,128)S(1)}, u32[]{:S(2)}, u32[]{:S(2)}) async-start(f32[32,8,128]{2,1,0:T(8,128)} %get-tuple-element.95), calls=%async_computation.2 | async-start | bytes 262144 | tf_op jit(solution)/shard_map/all_to_all | solution.py:360
  107.9 9.1 %backward.1 = (bf16[448,1024]{1,0:T(8,128)(2,1)}, f32[448,2048]{1,0:T(8,128)}, f32[224,128]{1,0:T(8,128)}) custom-call(s32[2]{0:T(128)S(1)} %pad_add_fusion.where_ref, bf16[448,1024]{1,0:T(8,128)(2,1)} %bitcast.23, s32[448,2048]{1,0:T(8,128)} %bitcast.20, f32[224,128]{1,0:T(8,128)} %bitcast.26, bf16[8,8,64,128]{3,2,1,0:T(8,128)(2,1)} %copy-done, ...), custom_call_target="tpu_custom_call" | custom-call | tf_op jit(solution)/shard_map/backward/pallas_call | solution.py:305
  (45 shorter events, 9.2 us)
Async XLA Ops:
  3.7 15.0 %collective-permute-start = (bf16[256,1024]{1,0:T(8,128)(2,1)S(1)}, bf16[256,1024]{1,0:T(8,128)(2,1)S(1)}, u32[]{:S(2)}, u32[]{:S(2)}) collective-permute-start(bf16[256,1024]{1,0:T(8,128)(2,1)S(1)} %get-tuple-element.55), channel_id=1, source_target_pairs={{0,8},{8,16},{16,24},{24,0},{1,9},{9,17},{17,25},{25,1},{2,10},{10... | collective-permute-start | bytes 1572872 | tf_op jit(solution)/shard_map/ppermute | solution.py:326
  5.3 13.4 %collective-permute-start.1 = (bf16[256,1024]{1,0:T(8,128)(2,1)S(1)}, bf16[256,1024]{1,0:T(8,128)(2,1)S(1)}, u32[]{:S(2)}, u32[]{:S(2)}) collective-permute-start(bf16[256,1024]{1,0:T(8,128)(2,1)S(1)} %get-tuple-element.56), channel_id=1, source_target_pairs={{0,24},{8,0},{16,8},{24,16},{1,25},{9,1},{17,9},{25,17},{2,26},{10... | collective-permute-start | bytes 1572872 | tf_op jit(solution)/shard_map/ppermute | solution.py:326
  23.2 34.1 %collective-permute-start.2 = (bf16[512,1024]{1,0:T(8,128)(2,1)S(1)}, bf16[512,1024]{1,0:T(8,128)(2,1)S(1)}, u32[]{:S(2)}, u32[]{:S(2)}) collective-permute-start(bf16[512,1024]{1,0:T(8,128)(2,1)S(1)} %get-tuple-element.64), channel_id=1, source_target_pairs={{0,8},{8,16},{16,24},{24,0},{1,9},{9,17},{17,25},{25,1},{2,10},{10... | collective-permute-start | bytes 3145736 | tf_op jit(solution)/shard_map/ppermute | solution.py:326
  24.8 32.5 %collective-permute-start.3 = (bf16[512,1024]{1,0:T(8,128)(2,1)S(1)}, bf16[512,1024]{1,0:T(8,128)(2,1)S(1)}, u32[]{:S(2)}, u32[]{:S(2)}) collective-permute-start(bf16[512,1024]{1,0:T(8,128)(2,1)S(1)} %get-tuple-element.65), channel_id=1, source_target_pairs={{0,24},{8,0},{16,8},{24,16},{1,25},{9,1},{17,9},{25,17},{2,26},{10... | collective-permute-start | bytes 3145736 | tf_op jit(solution)/shard_map/ppermute | solution.py:326
  26.5 16.9 %collective-permute-start.7 = (bf16[8,64,128]{2,1,0:T(8,128)(2,1)S(1)}, bf16[8,64,128]{2,1,0:T(8,128)(2,1)S(1)}, u32[]{:S(2)}, u32[]{:S(2)}) collective-permute-start(bf16[8,64,128]{2,1,0:T(8,128)(2,1)S(1)} %all_to_all.15.refs_0_), channel_id=1, source_target_pairs={{0,4},{1,5},{2,6},{3,7},{4,0},{5,1},{6,2},{7,3},{8,12},{9,13},{10,... | collective-permute-start | bytes 393224 | tf_op jit(solution)/shard_map/ppermute | solution.py:326
  33.7 14.8 %collective-permute-start.6 = (bf16[8,64,128]{2,1,0:T(8,128)(2,1)S(1)}, bf16[8,64,128]{2,1,0:T(8,128)(2,1)S(1)}, u32[]{:S(2)}, u32[]{:S(2)}) collective-permute-start(bf16[8,64,128]{2,1,0:T(8,128)(2,1)S(1)} %all_to_all.15.refs_0_), channel_id=1, source_target_pairs={{0,3},{1,4},{2,5},{3,6},{4,7},{5,0},{6,1},{7,2},{8,11},{9,12},{10,... | collective-permute-start | bytes 393224 | tf_op jit(solution)/shard_map/ppermute | solution.py:326
  35.6 17.1 %collective-permute-start.5 = (bf16[8,64,128]{2,1,0:T(8,128)(2,1)S(1)}, bf16[8,64,128]{2,1,0:T(8,128)(2,1)S(1)}, u32[]{:S(2)}, u32[]{:S(2)}) collective-permute-start(bf16[8,64,128]{2,1,0:T(8,128)(2,1)S(1)} %all_to_all.15.refs_0_), channel_id=1, source_target_pairs={{0,5},{1,6},{2,7},{3,0},{4,1},{5,2},{6,3},{7,4},{8,13},{9,14},{10,... | collective-permute-start | bytes 393224 | tf_op jit(solution)/shard_map/ppermute | solution.py:326
  43.4 9.4 %collective-permute-start.4 = (bf16[8,64,128]{2,1,0:T(8,128)(2,1)S(1)}, bf16[8,64,128]{2,1,0:T(8,128)(2,1)S(1)}, u32[]{:S(2)}, u32[]{:S(2)}) collective-permute-start(bf16[8,64,128]{2,1,0:T(8,128)(2,1)S(1)} %all_to_all.15.refs_0_), channel_id=1, source_target_pairs={{0,2},{1,3},{2,4},{3,5},{4,6},{5,7},{6,0},{7,1},{8,10},{9,11},{10,... | collective-permute-start | bytes 393224 | tf_op jit(solution)/shard_map/ppermute | solution.py:326
  48.5 9.7 %collective-permute-start.10 = (bf16[8,64,128]{2,1,0:T(8,128)(2,1)S(1)}, bf16[8,64,128]{2,1,0:T(8,128)(2,1)S(1)}, u32[]{:S(2)}, u32[]{:S(2)}) collective-permute-start(bf16[8,64,128]{2,1,0:T(8,128)(2,1)S(1)} %all_to_all.15.refs_0_), channel_id=1, source_target_pairs={{0,6},{1,7},{2,0},{3,1},{4,2},{5,3},{6,4},{7,5},{8,14},{9,15},{10,... | collective-permute-start | bytes 393224 | tf_op jit(solution)/shard_map/ppermute | solution.py:326
  52.8 6.2 %collective-permute-start.9 = (bf16[8,64,128]{2,1,0:T(8,128)(2,1)S(1)}, bf16[8,64,128]{2,1,0:T(8,128)(2,1)S(1)}, u32[]{:S(2)}, u32[]{:S(2)}) collective-permute-start(bf16[8,64,128]{2,1,0:T(8,128)(2,1)S(1)} %all_to_all.15.refs_0_), channel_id=1, source_target_pairs={{0,1},{1,2},{2,3},{3,4},{4,5},{5,6},{6,7},{7,0},{8,9},{9,10},{10,1... | collective-permute-start | bytes 393224 | tf_op jit(solution)/shard_map/ppermute | solution.py:326
  52.8 7.1 %collective-permute-start.8 = (bf16[8,64,128]{2,1,0:T(8,128)(2,1)S(1)}, bf16[8,64,128]{2,1,0:T(8,128)(2,1)S(1)}, u32[]{:S(2)}, u32[]{:S(2)}) collective-permute-start(bf16[8,64,128]{2,1,0:T(8,128)(2,1)S(1)} %all_to_all.15.refs_0_), channel_id=1, source_target_pairs={{0,7},{1,0},{2,1},{3,2},{4,3},{5,4},{6,5},{7,6},{8,15},{9,8},{10,9... | collective-permute-start | bytes 393224 | tf_op jit(solution)/shard_map/ppermute | solution.py:326
  59.9 48.0 %copy-start = (bf16[8,8,64,128]{3,2,1,0:T(8,128)(2,1)}, bf16[8,8,64,128]{3,2,1,0:T(8,128)(2,1)S(1)}, u32[]{:S(2)}) copy-start(bf16[8,8,64,128]{3,2,1,0:T(8,128)(2,1)S(1)} %pack.1.rest_0_) | copy-start | bytes 3145732
  59.9 26.2 %collective-permute-start.17 = (bf16[8,8,64,128]{3,2,1,0:T(8,128)(2,1)S(1)}, bf16[8,8,64,128]{3,2,1,0:T(8,128)(2,1)S(1)}, u32[]{:S(2)}, u32[]{:S(2)}) collective-permute-start(bf16[8,8,64,128]{3,2,1,0:T(8,128)(2,1)S(1)} %pack.1.rest_0_), channel_id=1, source_target_pairs={{0,8},{8,16},{16,24},{24,0},{1,9},{9,17},{17,25},{25,1},{2,10},{10... | collective-permute-start | bytes 3145736 | tf_op jit(solution)/shard_map/ppermute | solution.py:326
  60.4 25.7 %collective-permute-start.16 = (bf16[8,8,64,128]{3,2,1,0:T(8,128)(2,1)S(1)}, bf16[8,8,64,128]{3,2,1,0:T(8,128)(2,1)S(1)}, u32[]{:S(2)}, u32[]{:S(2)}) collective-permute-start(bf16[8,8,64,128]{3,2,1,0:T(8,128)(2,1)S(1)} %pack.1.rest_0_), channel_id=1, source_target_pairs={{0,24},{8,0},{16,8},{24,16},{1,25},{9,1},{17,9},{25,17},{2,26},{10... | collective-permute-start | bytes 3145736 | tf_op jit(solution)/shard_map/ppermute | solution.py:326
  63.4 15.4 %collective-permute-start.11 = (bf16[2,64,1024]{2,1,0:T(8,128)(2,1)S(1)}, bf16[2,64,1024]{2,1,0:T(8,128)(2,1)S(1)}, u32[]{:S(2)}, u32[]{:S(2)}) collective-permute-start(bf16[2,64,1024]{2,1,0:T(8,128)(2,1)S(1)} %get-tuple-element.85), channel_id=1, source_target_pairs={{0,1},{1,2},{2,3},{3,4},{4,5},{5,6},{6,7},{7,0},{8,9},{9,10},{10,1... | collective-permute-start | bytes 786440 | tf_op jit(solution)/shard_map/ppermute | solution.py:326
  63.4 15.4 %collective-permute-start.12 = (bf16[2,64,1024]{2,1,0:T(8,128)(2,1)S(1)}, bf16[2,64,1024]{2,1,0:T(8,128)(2,1)S(1)}, u32[]{:S(2)}, u32[]{:S(2)}) collective-permute-start(bf16[2,64,1024]{2,1,0:T(8,128)(2,1)S(1)} %get-tuple-element.86), channel_id=1, source_target_pairs={{0,7},{1,0},{2,1},{3,2},{4,3},{5,4},{6,5},{7,6},{8,15},{9,8},{10,9... | collective-permute-start | bytes 786440 | tf_op jit(solution)/shard_map/ppermute | solution.py:326
  67.1 11.8 %collective-permute-start.13 = (bf16[64,1024]{1,0:T(8,128)(2,1)S(1)}, bf16[64,1024]{1,0:T(8,128)(2,1)S(1)}, u32[]{:S(2)}, u32[]{:S(2)}) collective-permute-start(bf16[64,1024]{1,0:T(8,128)(2,1)S(1)} %get-tuple-element.89), channel_id=1, source_target_pairs={{0,2},{1,3},{2,4},{3,5},{4,6},{5,7},{6,0},{7,1},{8,10},{9,11},{10,... | collective-permute-start | bytes 393224 | tf_op jit(solution)/shard_map/ppermute | solution.py:326
  78.9 7.2 %collective-permute-start.14 = (bf16[64,1024]{1,0:T(8,128)(2,1)S(1)}, bf16[64,1024]{1,0:T(8,128)(2,1)S(1)}, u32[]{:S(2)}, u32[]{:S(2)}) collective-permute-start(bf16[64,1024]{1,0:T(8,128)(2,1)S(1)} %get-tuple-element.90), channel_id=1, source_target_pairs={{0,2},{1,3},{2,4},{3,5},{4,6},{5,7},{6,0},{7,1},{8,10},{9,11},{10,... | collective-permute-start | bytes 393224 | tf_op jit(solution)/shard_map/ppermute | solution.py:326
  79.0 7.1 %collective-permute-start.15 = (bf16[64,1024]{1,0:T(8,128)(2,1)S(1)}, bf16[64,1024]{1,0:T(8,128)(2,1)S(1)}, u32[]{:S(2)}, u32[]{:S(2)}) collective-permute-start(bf16[64,1024]{1,0:T(8,128)(2,1)S(1)} %get-tuple-element.91), channel_id=1, source_target_pairs={{0,6},{1,7},{2,0},{3,1},{4,2},{5,3},{6,4},{7,5},{8,14},{9,15},{10,... | collective-permute-start | bytes 393224 | tf_op jit(solution)/shard_map/ppermute | solution.py:326
  86.1 21.8 %copy-start.4 = (bf16[8,8,64,128]{3,2,1,0:T(8,128)(2,1)}, bf16[8,8,64,128]{3,2,1,0:T(8,128)(2,1)S(1)}, u32[]{:S(2)}) copy-start(bf16[8,8,64,128]{3,2,1,0:T(8,128)(2,1)S(1)} %collective-permute-done.17.rest_2_) | copy-start | bytes 3145732
  86.1 21.8 %copy-start.5 = (bf16[8,8,64,128]{3,2,1,0:T(8,128)(2,1)}, bf16[8,8,64,128]{3,2,1,0:T(8,128)(2,1)S(1)}, u32[]{:S(2)}) copy-start(bf16[8,8,64,128]{3,2,1,0:T(8,128)(2,1)S(1)} %collective-permute-done.16.rest_1_) | copy-start | bytes 3145732
  87.8 20.0 %collective-permute-start.19 = (bf16[4,8,64,128]{3,2,1,0:T(8,128)(2,1)}, bf16[4,8,64,128]{3,2,1,0:T(8,128)(2,1)}, u32[]{:S(2)}, u32[]{:S(2)}) collective-permute-start(bf16[4,8,64,128]{3,2,1,0:T(8,128)(2,1)} %slice.7), channel_id=1, source_target_pairs={{0,8},{8,16},{16,24},{24,0},{1,9},{9,17},{17,25},{25,1},{2,10},{10... | collective-permute-start | bytes 1572872 | tf_op jit(solution)/shard_map/ppermute | solution.py:326
  87.9 20.0 %collective-permute-start.18 = (bf16[4,8,64,128]{3,2,1,0:T(8,128)(2,1)}, bf16[4,8,64,128]{3,2,1,0:T(8,128)(2,1)}, u32[]{:S(2)}, u32[]{:S(2)}) collective-permute-start(bf16[4,8,64,128]{3,2,1,0:T(8,128)(2,1)} %slice.6), channel_id=1, source_target_pairs={{0,24},{8,0},{16,8},{24,16},{1,25},{9,1},{17,9},{25,17},{2,26},{10... | collective-permute-start | bytes 1572872 | tf_op jit(solution)/shard_map/ppermute | solution.py:326
  101.8 16.3 %all-to-all-start.2 = ((f32[32,8,128]{2,1,0:T(8,128)}), f32[32,8,128]{2,1,0:T(8,128)S(1)}, u32[]{:S(2)}, u32[]{:S(2)}) async-start(f32[32,8,128]{2,1,0:T(8,128)} %get-tuple-element.95), calls=%async_computation.2 | async-start | bytes 262144 | tf_op jit(solution)/shard_map/all_to_all | solution.py:360
  (3 other events, 19.1 us)

commit v11 on v6

--- a/solution.py
+++ b/solution.py
@@ -29,13 +29,14 @@
     return pltpu.with_memory_space_constraint(array, pltpu.HBM)
 
 
-def call(body, name, where, operands, outs, scratch=(), far=()):
+def call(body, name, where, operands, outs, scratch=(), far=(), keep=None):
     heads = [] if where is None else [where]
+    keep = len(outs) if keep is None else keep
     return pl.pallas_call(
         body,
         in_specs=[SMEM] * len(heads) + [HBM] * len(far) + [VMEM] * len(operands),
         out_specs=[VMEM] * len(outs),
-        out_shape=[pltpu.VMEM(shape, dtype) for shape, dtype in outs],
+        out_shape=[(pltpu.VMEM if i < keep else sds)(*out) for i, out in enumerate(outs)],
         scratch_shapes=list(scratch),
         compiler_params=SMALL,
         name=name,
@@ -201,7 +202,7 @@
     return call(z_sum_body, "z_sum", None, arrays, [((EXPERTS, COLS, CAP), BF16)])[0]
 
 
-def combine_body(place_ref, gate_ref, grad_ref, back_ref, out_ref, spread_ref):
+def combine_body(place_ref, gate_ref, grad_ref, back_ref, spread_ref, out_ref):
     back = jnp.concatenate([back_ref[e] for e in range(EXPERTS)], axis=1)
     grad = grad_ref[...].astype(F32)
     total = None
@@ -217,8 +218,8 @@
 
 
 def combine(place, gate, grad, back):
-    outs = [(grad.shape, BF16), ((NX * NZ, 8, 128), F32)]
-    return call(combine_body, "combine", None, [place, gate, grad, back], outs)
+    outs = [((NX * NZ, 8, 128), F32), (grad.shape, BF16)]
+    return call(combine_body, "combine", None, [place, gate, grad, back], outs, keep=1)
 
 
 def gate_sum_body(parts_ref, out_ref):
@@ -229,7 +230,7 @@
 
 
 def gate_sum(parts):
-    return call(gate_sum_body, "gate_sum", None, [parts], [((2, 512), F32)])[0]
+    return call(gate_sum_body, "gate_sum", None, [parts], [((2, 512), F32)], keep=0)[0]
 
 
 NEAREST = (0, 1, 7, 2, 6, 3, 5, 4)
@@ -363,7 +364,7 @@
     up2, down2, packs[1], packs[2] = lax.optimization_barrier((up2, down2, packs[1], packs[2]))
     packs += [shift(packs[1][: NZ // 2], "x", -1), shift(packs[2][NZ // 2 :], "x", 1)]
     returned = lax.all_to_all(z_sum(rest, ups, downs, up2, down2), ("y", "c"), 0, 0, tiled=True)
-    combined, spread = combine(place, gate, grad, returned)
+    spread, combined = combine(place, gate, grad, returned)
     gate_parts = lax.all_to_all(spread, ("x", "z"), 0, 0, tiled=True)
     hidden_grad, weight_grad, scale_grad = backward(where, *weights, packs)
     gate_parts, hidden_grad = lax.optimization_barrier((gate_parts, hidden_grad))

time: 119 us -> 118 us (level)
  local copies, waits for them, and re-layouts: 2.99 us -> 1.77 us
    unnamed x14 -> x12, local copies, waits for them, and re-layouts: 1.25 us -> 0.02 us
  transfers between devices with their start and end apart: 21 -> 21, of which waited for: 6 -> 6; matrix products, arithmetic and copies ran while one was open for 1% -> 0% of each run, Pallas kernels for 13% -> 13%
where the time goes in v11:
time: 118 us; the launch traced here: 117 us
  starting transfers between devices  46.6 us (39%)
  waiting for transfers between devices  26.8 us (23%)
  Pallas kernels  22.6 us (19%)
  blocking collectives  18.6 us (16%)
  local copies, waits for them, and re-layouts  1.77 us (2%)
    ppermute x20, starting transfers between devices, shift(): lax.ppermute(value, axis, [(i, (i + by) % size) for i in range(size)])  40.8 us
    ppermute x20, waiting for transfers between devices, shift(): lax.ppermute(value, axis, [(i, (i + by) % size) for i in range(size)])  25.7 us
    pallas_call x10, Pallas kernels, call(): pl.pallas_call(body, in_specs=[SMEM] * len(heads) + [HBM] * len(far) + [V...  13.5 us
    all_to_all x1, blocking collectives, on_device(): shard = lax.all_to_all(outbound, ('y', 'c'), 0, 0, tiled=True)  9.39 us
    all_to_all x1, blocking collectives, on_device(): lax.all_to_all(z_sum(rest, ups, downs, up2, down2), ('y', 'c'), 0, 0, til...  9.19 us
    pallas_call x1, Pallas kernels, backward(): pl.pallas_call(backward_body, in_specs=[SMEM] + [HBM] * (4 + NX), out_spe...  9.13 us
    all_to_all x1, starting transfers between devices, on_device(): gate_parts = lax.all_to_all(spread, ('x', 'z'), 0, 0, tiled=True)  5.82 us
  transfers between devices with their start and end apart: 21, of which 6 were waited for; matrix products, arithmetic and copies ran while one was open for 0% of the time, Pallas kernels for 13%

profile of v11, /device:TPU:8, one launch (start us, length us, event | category | flops | bytes accessed | tf_op | source)
XLA Modules:
  0.0 117.3 jit_solution(8829803202492119474)
XLA Ops:
  0.7 2.9 %forward_far.1 = (bf16[256,1024]{1,0:T(8,128)(2,1)S(1)}, bf16[256,1024]{1,0:T(8,128)(2,1)S(1)}) custom-call(s32[2]{0:T(128)S(1)} %pad_add_fusion.where_ref, bf16[448,1024]{1,0:T(8,128)(2,1)} %bitcast.22, s32[448,2048]{1,0:T(8,128)} %bitcast.18, f32[224,128]{1,0:T(8,128)} %bitcast.26), custom_call_target="tpu_custom_call" | custom-call | tf_op jit(solution)/shard_map/forward_far/pallas_call | solution.py:35
  3.7 1.6 %collective-permute-start = (bf16[256,1024]{1,0:T(8,128)(2,1)S(1)}, bf16[256,1024]{1,0:T(8,128)(2,1)S(1)}, u32[]{:S(2)}, u32[]{:S(2)}) collective-permute-start(bf16[256,1024]{1,0:T(8,128)(2,1)S(1)} %get-tuple-element.46), channel_id=1, source_target_pairs={{0,8},{8,16},{16,24},{24,0},{1,9},{9,17},{17,25},{25,1},{2,10},{10... | collective-permute-start | bytes 1572872 | tf_op jit(solution)/shard_map/ppermute | solution.py:335
  5.3 1.7 %collective-permute-start.1 = (bf16[256,1024]{1,0:T(8,128)(2,1)S(1)}, bf16[256,1024]{1,0:T(8,128)(2,1)S(1)}, u32[]{:S(2)}, u32[]{:S(2)}) collective-permute-start(bf16[256,1024]{1,0:T(8,128)(2,1)S(1)} %get-tuple-element.47), channel_id=1, source_target_pairs={{0,24},{8,0},{16,8},{24,16},{1,25},{9,1},{17,9},{25,17},{2,26},{10... | collective-permute-start | bytes 1572872 | tf_op jit(solution)/shard_map/ppermute | solution.py:335
  8.0 9.4 %all_to_all.15.refs_0_ = bf16[8,64,128]{2,1,0:T(8,128)(2,1)S(1)} all-to-all(bf16[8,64,128]{2,1,0:T(8,128)(2,1)S(1)} %get-tuple-element.48), channel_id=1, replica_groups=mesh['y'=4,'c'=2,'x'=4,'z'=8] {'y','c'}, dimensions={0} | all-to-all | bytes 262144 | tf_op jit(solution)/shard_map/all_to_all | solution.py:348
  18.7 3.7 %forward_join.1 = (bf16[512,1024]{1,0:T(8,128)(2,1)S(1)}, bf16[512,1024]{1,0:T(8,128)(2,1)S(1)}) custom-call(s32[2]{0:T(128)S(1)} %pad_add_fusion.where_ref, bf16[448,1024]{1,0:T(8,128)(2,1)} %bitcast.23, s32[448,2048]{1,0:T(8,128)} %bitcast.19, f32[224,128]{1,0:T(8,128)} %bitcast.27, bf16[256,1024]{1,0:T(8,128)(2,1)S(1)} %collective-permute-done.top_ref, ...), custom_call_target="tpu_custom_call" | custom-call | tf_op jit(solution)/shard_map/forward_join/pallas_call | solution.py:35
  22.4 1.6 %collective-permute-start.2 = (bf16[512,1024]{1,0:T(8,128)(2,1)S(1)}, bf16[512,1024]{1,0:T(8,128)(2,1)S(1)}, u32[]{:S(2)}, u32[]{:S(2)}) collective-permute-start(bf16[512,1024]{1,0:T(8,128)(2,1)S(1)} %get-tuple-element.55), channel_id=1, source_target_pairs={{0,8},{8,16},{16,24},{24,0},{1,9},{9,17},{17,25},{25,1},{2,10},{10... | collective-permute-start | bytes 3145736 | tf_op jit(solution)/shard_map/ppermute | solution.py:335
  24.0 1.7 %collective-permute-start.3 = (bf16[512,1024]{1,0:T(8,128)(2,1)S(1)}, bf16[512,1024]{1,0:T(8,128)(2,1)S(1)}, u32[]{:S(2)}, u32[]{:S(2)}) collective-permute-start(bf16[512,1024]{1,0:T(8,128)(2,1)S(1)} %get-tuple-element.56), channel_id=1, source_target_pairs={{0,24},{8,0},{16,8},{24,16},{1,25},{9,1},{17,9},{25,17},{2,26},{10... | collective-permute-start | bytes 3145736 | tf_op jit(solution)/shard_map/ppermute | solution.py:335
  25.7 7.2 %collective-permute-start.10 = (bf16[8,64,128]{2,1,0:T(8,128)(2,1)S(1)}, bf16[8,64,128]{2,1,0:T(8,128)(2,1)S(1)}, u32[]{:S(2)}, u32[]{:S(2)}) collective-permute-start(bf16[8,64,128]{2,1,0:T(8,128)(2,1)S(1)} %all_to_all.15.refs_0_), channel_id=1, source_target_pairs={{0,4},{1,5},{2,6},{3,7},{4,0},{5,1},{6,2},{7,3},{8,12},{9,13},{10,... | collective-permute-start | bytes 393224 | tf_op jit(solution)/shard_map/ppermute | solution.py:335
  32.9 1.9 %collective-permute-start.9 = (bf16[8,64,128]{2,1,0:T(8,128)(2,1)S(1)}, bf16[8,64,128]{2,1,0:T(8,128)(2,1)S(1)}, u32[]{:S(2)}, u32[]{:S(2)}) collective-permute-start(bf16[8,64,128]{2,1,0:T(8,128)(2,1)S(1)} %all_to_all.15.refs_0_), channel_id=1, source_target_pairs={{0,3},{1,4},{2,5},{3,6},{4,7},{5,0},{6,1},{7,2},{8,11},{9,12},{10,... | collective-permute-start | bytes 393224 | tf_op jit(solution)/shard_map/ppermute | solution.py:335
  34.8 3.1 %collective-permute-start.8 = (bf16[8,64,128]{2,1,0:T(8,128)(2,1)S(1)}, bf16[8,64,128]{2,1,0:T(8,128)(2,1)S(1)}, u32[]{:S(2)}, u32[]{:S(2)}) collective-permute-start(bf16[8,64,128]{2,1,0:T(8,128)(2,1)S(1)} %all_to_all.15.refs_0_), channel_id=1, source_target_pairs={{0,5},{1,6},{2,7},{3,0},{4,1},{5,2},{6,3},{7,4},{8,13},{9,14},{10,... | collective-permute-start | bytes 393224 | tf_op jit(solution)/shard_map/ppermute | solution.py:335
  37.9 4.6 %collective-permute-done.10.refs_7_ = bf16[8,64,128]{2,1,0:T(8,128)(2,1)S(1)} collective-permute-done((bf16[8,64,128]{2,1,0:T(8,128)(2,1)S(1)}, bf16[8,64,128]{2,1,0:T(8,128)(2,1)S(1)}, u32[]{:S(2)}, u32[]{:S(2)}) %collective-permute-start.10) | collective-permute-done | bytes 131104 | tf_op jit(solution)/shard_map/ppermute | solution.py:335
  42.6 5.1 %collective-permute-done.9.refs_6_ = bf16[8,64,128]{2,1,0:T(8,128)(2,1)S(1)} collective-permute-done((bf16[8,64,128]{2,1,0:T(8,128)(2,1)S(1)}, bf16[8,64,128]{2,1,0:T(8,128)(2,1)S(1)}, u32[]{:S(2)}, u32[]{:S(2)}) %collective-permute-start.9) | collective-permute-done | bytes 131104 | tf_op jit(solution)/shard_map/ppermute | solution.py:335
  47.7 4.3 %collective-permute-start.6 = (bf16[8,64,128]{2,1,0:T(8,128)(2,1)S(1)}, bf16[8,64,128]{2,1,0:T(8,128)(2,1)S(1)}, u32[]{:S(2)}, u32[]{:S(2)}) collective-permute-start(bf16[8,64,128]{2,1,0:T(8,128)(2,1)S(1)} %all_to_all.15.refs_0_), channel_id=1, source_target_pairs={{0,6},{1,7},{2,0},{3,1},{4,2},{5,3},{6,4},{7,5},{8,14},{9,15},{10,... | collective-permute-start | bytes 393224 | tf_op jit(solution)/shard_map/ppermute | solution.py:335
  52.0 3.2 %collective-permute-start.4 = (bf16[8,64,128]{2,1,0:T(8,128)(2,1)S(1)}, bf16[8,64,128]{2,1,0:T(8,128)(2,1)S(1)}, u32[]{:S(2)}, u32[]{:S(2)}) collective-permute-start(bf16[8,64,128]{2,1,0:T(8,128)(2,1)S(1)} %all_to_all.15.refs_0_), channel_id=1, source_target_pairs={{0,7},{1,0},{2,1},{3,2},{4,3},{5,4},{6,5},{7,6},{8,15},{9,8},{10,9... | collective-permute-start | bytes 393224 | tf_op jit(solution)/shard_map/ppermute | solution.py:335
  55.2 2.9 %forward_own.1.own_ref = f32[512,1024]{1,0:T(8,128)S(1)} custom-call(s32[2]{0:T(128)S(1)} %pad_add_fusion.where_ref, bf16[448,1024]{1,0:T(8,128)(2,1)} %bitcast.24, s32[448,2048]{1,0:T(8,128)} %bitcast.20, f32[224,128]{1,0:T(8,128)} %bitcast.28), custom_call_target="tpu_custom_call" | custom-call | tf_op jit(solution)/shard_map/forward_own/pallas_call | solution.py:35
  59.4 3.2 %collective-permute-start.16 = (bf16[8,8,64,128]{3,2,1,0:T(8,128)(2,1)S(1)}, bf16[8,8,64,128]{3,2,1,0:T(8,128)(2,1)S(1)}, u32[]{:S(2)}, u32[]{:S(2)}) collective-permute-start(bf16[8,8,64,128]{3,2,1,0:T(8,128)(2,1)S(1)} %pack.1.rest_0_), channel_id=1, source_target_pairs={{0,24},{8,0},{16,8},{24,16},{1,25},{9,1},{17,9},{25,17},{2,26},{10... | collective-permute-start | bytes 3145736 | tf_op jit(solution)/shard_map/ppermute | solution.py:335
  62.6 3.2 %collective-permute-start.12 = (bf16[2,64,1024]{2,1,0:T(8,128)(2,1)S(1)}, bf16[2,64,1024]{2,1,0:T(8,128)(2,1)S(1)}, u32[]{:S(2)}, u32[]{:S(2)}) collective-permute-start(bf16[2,64,1024]{2,1,0:T(8,128)(2,1)S(1)} %get-tuple-element.61), channel_id=1, source_target_pairs={{0,7},{1,0},{2,1},{3,2},{4,3},{5,4},{6,5},{7,6},{8,15},{9,8},{10,9... | collective-permute-start | bytes 786440 | tf_op jit(solution)/shard_map/ppermute | solution.py:335
  66.1 11.5 %collective-permute-done.13.far_ref = bf16[64,1024]{1,0:T(8,128)(2,1)S(1)} collective-permute-done((bf16[64,1024]{1,0:T(8,128)(2,1)S(1)}, bf16[64,1024]{1,0:T(8,128)(2,1)S(1)}, u32[]{:S(2)}, u32[]{:S(2)}) %collective-permute-start.13) | collective-permute-done | bytes 131104 | tf_op jit(solution)/shard_map/ppermute | solution.py:335
  77.8 4.1 %collective-permute-start.15 = (bf16[64,1024]{1,0:T(8,128)(2,1)S(1)}, bf16[64,1024]{1,0:T(8,128)(2,1)S(1)}, u32[]{:S(2)}, u32[]{:S(2)}) collective-permute-start(bf16[64,1024]{1,0:T(8,128)(2,1)S(1)} %get-tuple-element.66), channel_id=1, source_target_pairs={{0,6},{1,7},{2,0},{3,1},{4,2},{5,3},{6,4},{7,5},{8,14},{9,15},{10,... | collective-permute-start | bytes 393224 | tf_op jit(solution)/shard_map/ppermute | solution.py:335
  81.9 3.2 %collective-permute-done.14.up_ref = bf16[64,1024]{1,0:T(8,128)(2,1)S(1)} collective-permute-done((bf16[64,1024]{1,0:T(8,128)(2,1)S(1)}, bf16[64,1024]{1,0:T(8,128)(2,1)S(1)}, u32[]{:S(2)}, u32[]{:S(2)}) %collective-permute-start.14) | collective-permute-done | bytes 131104 | tf_op jit(solution)/shard_map/ppermute | solution.py:335
  86.9 3.2 %collective-permute-start.18 = (bf16[4,8,64,128]{3,2,1,0:T(8,128)(2,1)}, bf16[4,8,64,128]{3,2,1,0:T(8,128)(2,1)}, u32[]{:S(2)}, u32[]{:S(2)}) collective-permute-start(bf16[4,8,64,128]{3,2,1,0:T(8,128)(2,1)} %slice.6), channel_id=1, source_target_pairs={{0,24},{8,0},{16,8},{24,16},{1,25},{9,1},{17,9},{25,17},{2,26},{10... | collective-permute-start | bytes 1572872 | tf_op jit(solution)/shard_map/ppermute | solution.py:335
  90.2 9.2 %all_to_all.16.back_ref = bf16[8,64,128]{2,1,0:T(8,128)(2,1)S(1)} all-to-all(bf16[8,64,128]{2,1,0:T(8,128)(2,1)S(1)} %z_sum.1), channel_id=1, replica_groups=mesh['y'=4,'c'=2,'x'=4,'z'=8] {'y','c'}, dimensions={0} | all-to-all | bytes 262144 | tf_op jit(solution)/shard_map/all_to_all | solution.py:366
  100.6 5.8 %all-to-all-start.2 = ((f32[32,8,128]{2,1,0:T(8,128)}), f32[32,8,128]{2,1,0:T(8,128)S(1)}, u32[]{:S(2)}, u32[]{:S(2)}) async-start(f32[32,8,128]{2,1,0:T(8,128)} %get-tuple-element.77), calls=%async_computation.2 | async-start | bytes 262144 | tf_op jit(solution)/shard_map/all_to_all | solution.py:368
  106.5 9.1 %backward.1 = (bf16[448,1024]{1,0:T(8,128)(2,1)}, f32[448,2048]{1,0:T(8,128)}, f32[224,128]{1,0:T(8,128)}) custom-call(s32[2]{0:T(128)S(1)} %pad_add_fusion.where_ref, bf16[448,1024]{1,0:T(8,128)(2,1)} %bitcast.25, s32[448,2048]{1,0:T(8,128)} %bitcast.21, f32[224,128]{1,0:T(8,128)} %bitcast.29, bf16[8,8,64,128]{3,2,1,0:T(8,128)(2,1)} %copy-done, ...), custom_call_target="tpu_custom_call" | custom-call | tf_op jit(solution)/shard_map/backward/pallas_call | solution.py:314
  (46 shorter events, 8.8 us)
Async XLA Ops:
  3.7 15.0 %collective-permute-start = (bf16[256,1024]{1,0:T(8,128)(2,1)S(1)}, bf16[256,1024]{1,0:T(8,128)(2,1)S(1)}, u32[]{:S(2)}, u32[]{:S(2)}) collective-permute-start(bf16[256,1024]{1,0:T(8,128)(2,1)S(1)} %get-tuple-element.46), channel_id=1, source_target_pairs={{0,8},{8,16},{16,24},{24,0},{1,9},{9,17},{17,25},{25,1},{2,10},{10... | collective-permute-start | bytes 1572872 | tf_op jit(solution)/shard_map/ppermute | solution.py:335
  5.3 13.4 %collective-permute-start.1 = (bf16[256,1024]{1,0:T(8,128)(2,1)S(1)}, bf16[256,1024]{1,0:T(8,128)(2,1)S(1)}, u32[]{:S(2)}, u32[]{:S(2)}) collective-permute-start(bf16[256,1024]{1,0:T(8,128)(2,1)S(1)} %get-tuple-element.47), channel_id=1, source_target_pairs={{0,24},{8,0},{16,8},{24,16},{1,25},{9,1},{17,9},{25,17},{2,26},{10... | collective-permute-start | bytes 1572872 | tf_op jit(solution)/shard_map/ppermute | solution.py:335
  22.4 29.6 %collective-permute-start.2 = (bf16[512,1024]{1,0:T(8,128)(2,1)S(1)}, bf16[512,1024]{1,0:T(8,128)(2,1)S(1)}, u32[]{:S(2)}, u32[]{:S(2)}) collective-permute-start(bf16[512,1024]{1,0:T(8,128)(2,1)S(1)} %get-tuple-element.55), channel_id=1, source_target_pairs={{0,8},{8,16},{16,24},{24,0},{1,9},{9,17},{17,25},{25,1},{2,10},{10... | collective-permute-start | bytes 3145736 | tf_op jit(solution)/shard_map/ppermute | solution.py:335
  24.0 28.0 %collective-permute-start.3 = (bf16[512,1024]{1,0:T(8,128)(2,1)S(1)}, bf16[512,1024]{1,0:T(8,128)(2,1)S(1)}, u32[]{:S(2)}, u32[]{:S(2)}) collective-permute-start(bf16[512,1024]{1,0:T(8,128)(2,1)S(1)} %get-tuple-element.56), channel_id=1, source_target_pairs={{0,24},{8,0},{16,8},{24,16},{1,25},{9,1},{17,9},{25,17},{2,26},{10... | collective-permute-start | bytes 3145736 | tf_op jit(solution)/shard_map/ppermute | solution.py:335
  25.7 16.9 %collective-permute-start.10 = (bf16[8,64,128]{2,1,0:T(8,128)(2,1)S(1)}, bf16[8,64,128]{2,1,0:T(8,128)(2,1)S(1)}, u32[]{:S(2)}, u32[]{:S(2)}) collective-permute-start(bf16[8,64,128]{2,1,0:T(8,128)(2,1)S(1)} %all_to_all.15.refs_0_), channel_id=1, source_target_pairs={{0,4},{1,5},{2,6},{3,7},{4,0},{5,1},{6,2},{7,3},{8,12},{9,13},{10,... | collective-permute-start | bytes 393224 | tf_op jit(solution)/shard_map/ppermute | solution.py:335
  32.9 14.8 %collective-permute-start.9 = (bf16[8,64,128]{2,1,0:T(8,128)(2,1)S(1)}, bf16[8,64,128]{2,1,0:T(8,128)(2,1)S(1)}, u32[]{:S(2)}, u32[]{:S(2)}) collective-permute-start(bf16[8,64,128]{2,1,0:T(8,128)(2,1)S(1)} %all_to_all.15.refs_0_), channel_id=1, source_target_pairs={{0,3},{1,4},{2,5},{3,6},{4,7},{5,0},{6,1},{7,2},{8,11},{9,12},{10,... | collective-permute-start | bytes 393224 | tf_op jit(solution)/shard_map/ppermute | solution.py:335
  34.8 24.2 %collective-permute-start.8 = (bf16[8,64,128]{2,1,0:T(8,128)(2,1)S(1)}, bf16[8,64,128]{2,1,0:T(8,128)(2,1)S(1)}, u32[]{:S(2)}, u32[]{:S(2)}) collective-permute-start(bf16[8,64,128]{2,1,0:T(8,128)(2,1)S(1)} %all_to_all.15.refs_0_), channel_id=1, source_target_pairs={{0,5},{1,6},{2,7},{3,0},{4,1},{5,2},{6,3},{7,4},{8,13},{9,14},{10,... | collective-permute-start | bytes 393224 | tf_op jit(solution)/shard_map/ppermute | solution.py:335
  42.6 16.4 %collective-permute-start.7 = (bf16[8,64,128]{2,1,0:T(8,128)(2,1)S(1)}, bf16[8,64,128]{2,1,0:T(8,128)(2,1)S(1)}, u32[]{:S(2)}, u32[]{:S(2)}) collective-permute-start(bf16[8,64,128]{2,1,0:T(8,128)(2,1)S(1)} %all_to_all.15.refs_0_), channel_id=1, source_target_pairs={{0,2},{1,3},{2,4},{3,5},{4,6},{5,7},{6,0},{7,1},{8,10},{9,11},{10,... | collective-permute-start | bytes 393224 | tf_op jit(solution)/shard_map/ppermute | solution.py:335
  47.7 11.3 %collective-permute-start.6 = (bf16[8,64,128]{2,1,0:T(8,128)(2,1)S(1)}, bf16[8,64,128]{2,1,0:T(8,128)(2,1)S(1)}, u32[]{:S(2)}, u32[]{:S(2)}) collective-permute-start(bf16[8,64,128]{2,1,0:T(8,128)(2,1)S(1)} %all_to_all.15.refs_0_), channel_id=1, source_target_pairs={{0,6},{1,7},{2,0},{3,1},{4,2},{5,3},{6,4},{7,5},{8,14},{9,15},{10,... | collective-permute-start | bytes 393224 | tf_op jit(solution)/shard_map/ppermute | solution.py:335
  51.9 7.1 %collective-permute-start.5 = (bf16[8,64,128]{2,1,0:T(8,128)(2,1)S(1)}, bf16[8,64,128]{2,1,0:T(8,128)(2,1)S(1)}, u32[]{:S(2)}, u32[]{:S(2)}) collective-permute-start(bf16[8,64,128]{2,1,0:T(8,128)(2,1)S(1)} %all_to_all.15.refs_0_), channel_id=1, source_target_pairs={{0,1},{1,2},{2,3},{3,4},{4,5},{5,6},{6,7},{7,0},{8,9},{9,10},{10,1... | collective-permute-start | bytes 393224 | tf_op jit(solution)/shard_map/ppermute | solution.py:335
  52.0 7.1 %collective-permute-start.4 = (bf16[8,64,128]{2,1,0:T(8,128)(2,1)S(1)}, bf16[8,64,128]{2,1,0:T(8,128)(2,1)S(1)}, u32[]{:S(2)}, u32[]{:S(2)}) collective-permute-start(bf16[8,64,128]{2,1,0:T(8,128)(2,1)S(1)} %all_to_all.15.refs_0_), channel_id=1, source_target_pairs={{0,7},{1,0},{2,1},{3,2},{4,3},{5,4},{6,5},{7,6},{8,15},{9,8},{10,9... | collective-permute-start | bytes 393224 | tf_op jit(solution)/shard_map/ppermute | solution.py:335
  59.1 47.3 %copy-start = (bf16[8,8,64,128]{3,2,1,0:T(8,128)(2,1)}, bf16[8,8,64,128]{3,2,1,0:T(8,128)(2,1)S(1)}, u32[]{:S(2)}) copy-start(bf16[8,8,64,128]{3,2,1,0:T(8,128)(2,1)S(1)} %pack.1.rest_0_) | copy-start | bytes 3145732
  59.1 26.0 %collective-permute-start.17 = (bf16[8,8,64,128]{3,2,1,0:T(8,128)(2,1)S(1)}, bf16[8,8,64,128]{3,2,1,0:T(8,128)(2,1)S(1)}, u32[]{:S(2)}, u32[]{:S(2)}) collective-permute-start(bf16[8,8,64,128]{3,2,1,0:T(8,128)(2,1)S(1)} %pack.1.rest_0_), channel_id=1, source_target_pairs={{0,8},{8,16},{16,24},{24,0},{1,9},{9,17},{17,25},{25,1},{2,10},{10... | collective-permute-start | bytes 3145736 | tf_op jit(solution)/shard_map/ppermute | solution.py:335
  59.4 25.7 %collective-permute-start.16 = (bf16[8,8,64,128]{3,2,1,0:T(8,128)(2,1)S(1)}, bf16[8,8,64,128]{3,2,1,0:T(8,128)(2,1)S(1)}, u32[]{:S(2)}, u32[]{:S(2)}) collective-permute-start(bf16[8,8,64,128]{3,2,1,0:T(8,128)(2,1)S(1)} %pack.1.rest_0_), channel_id=1, source_target_pairs={{0,24},{8,0},{16,8},{24,16},{1,25},{9,1},{17,9},{25,17},{2,26},{10... | collective-permute-start | bytes 3145736 | tf_op jit(solution)/shard_map/ppermute | solution.py:335
  62.6 15.0 %collective-permute-start.11 = (bf16[2,64,1024]{2,1,0:T(8,128)(2,1)S(1)}, bf16[2,64,1024]{2,1,0:T(8,128)(2,1)S(1)}, u32[]{:S(2)}, u32[]{:S(2)}) collective-permute-start(bf16[2,64,1024]{2,1,0:T(8,128)(2,1)S(1)} %get-tuple-element.60), channel_id=1, source_target_pairs={{0,1},{1,2},{2,3},{3,4},{4,5},{5,6},{6,7},{7,0},{8,9},{9,10},{10,1... | collective-permute-start | bytes 786440 | tf_op jit(solution)/shard_map/ppermute | solution.py:335
  62.6 15.0 %collective-permute-start.12 = (bf16[2,64,1024]{2,1,0:T(8,128)(2,1)S(1)}, bf16[2,64,1024]{2,1,0:T(8,128)(2,1)S(1)}, u32[]{:S(2)}, u32[]{:S(2)}) collective-permute-start(bf16[2,64,1024]{2,1,0:T(8,128)(2,1)S(1)} %get-tuple-element.61), channel_id=1, source_target_pairs={{0,7},{1,0},{2,1},{3,2},{4,3},{5,4},{6,5},{7,6},{8,15},{9,8},{10,9... | collective-permute-start | bytes 786440 | tf_op jit(solution)/shard_map/ppermute | solution.py:335
  65.9 11.7 %collective-permute-start.13 = (bf16[64,1024]{1,0:T(8,128)(2,1)S(1)}, bf16[64,1024]{1,0:T(8,128)(2,1)S(1)}, u32[]{:S(2)}, u32[]{:S(2)}) collective-permute-start(bf16[64,1024]{1,0:T(8,128)(2,1)S(1)} %get-tuple-element.64), channel_id=1, source_target_pairs={{0,2},{1,3},{2,4},{3,5},{4,6},{5,7},{6,0},{7,1},{8,10},{9,11},{10,... | collective-permute-start | bytes 393224 | tf_op jit(solution)/shard_map/ppermute | solution.py:335
  77.7 7.4 %collective-permute-start.14 = (bf16[64,1024]{1,0:T(8,128)(2,1)S(1)}, bf16[64,1024]{1,0:T(8,128)(2,1)S(1)}, u32[]{:S(2)}, u32[]{:S(2)}) collective-permute-start(bf16[64,1024]{1,0:T(8,128)(2,1)S(1)} %get-tuple-element.65), channel_id=1, source_target_pairs={{0,2},{1,3},{2,4},{3,5},{4,6},{5,7},{6,0},{7,1},{8,10},{9,11},{10,... | collective-permute-start | bytes 393224 | tf_op jit(solution)/shard_map/ppermute | solution.py:335
  77.8 7.3 %collective-permute-start.15 = (bf16[64,1024]{1,0:T(8,128)(2,1)S(1)}, bf16[64,1024]{1,0:T(8,128)(2,1)S(1)}, u32[]{:S(2)}, u32[]{:S(2)}) collective-permute-start(bf16[64,1024]{1,0:T(8,128)(2,1)S(1)} %get-tuple-element.66), channel_id=1, source_target_pairs={{0,6},{1,7},{2,0},{3,1},{4,2},{5,3},{6,4},{7,5},{8,14},{9,15},{10,... | collective-permute-start | bytes 393224 | tf_op jit(solution)/shard_map/ppermute | solution.py:335
  85.1 21.4 %copy-start.4 = (bf16[8,8,64,128]{3,2,1,0:T(8,128)(2,1)}, bf16[8,8,64,128]{3,2,1,0:T(8,128)(2,1)S(1)}, u32[]{:S(2)}) copy-start(bf16[8,8,64,128]{3,2,1,0:T(8,128)(2,1)S(1)} %collective-permute-done.17.rest_2_) | copy-start | bytes 3145732
  85.1 21.4 %copy-start.5 = (bf16[8,8,64,128]{3,2,1,0:T(8,128)(2,1)}, bf16[8,8,64,128]{3,2,1,0:T(8,128)(2,1)S(1)}, u32[]{:S(2)}) copy-start(bf16[8,8,64,128]{3,2,1,0:T(8,128)(2,1)S(1)} %collective-permute-done.16.rest_1_) | copy-start | bytes 3145732
  86.9 19.6 %collective-permute-start.19 = (bf16[4,8,64,128]{3,2,1,0:T(8,128)(2,1)}, bf16[4,8,64,128]{3,2,1,0:T(8,128)(2,1)}, u32[]{:S(2)}, u32[]{:S(2)}) collective-permute-start(bf16[4,8,64,128]{3,2,1,0:T(8,128)(2,1)} %slice.7), channel_id=1, source_target_pairs={{0,8},{8,16},{16,24},{24,0},{1,9},{9,17},{17,25},{25,1},{2,10},{10... | collective-permute-start | bytes 1572872 | tf_op jit(solution)/shard_map/ppermute | solution.py:335
  86.9 19.6 %collective-permute-start.18 = (bf16[4,8,64,128]{3,2,1,0:T(8,128)(2,1)}, bf16[4,8,64,128]{3,2,1,0:T(8,128)(2,1)}, u32[]{:S(2)}, u32[]{:S(2)}) collective-permute-start(bf16[4,8,64,128]{3,2,1,0:T(8,128)(2,1)} %slice.6), channel_id=1, source_target_pairs={{0,24},{8,0},{16,8},{24,16},{1,25},{9,1},{17,9},{25,17},{2,26},{10... | collective-permute-start | bytes 1572872 | tf_op jit(solution)/shard_map/ppermute | solution.py:335
  100.6 16.1 %all-to-all-start.2 = ((f32[32,8,128]{2,1,0:T(8,128)}), f32[32,8,128]{2,1,0:T(8,128)S(1)}, u32[]{:S(2)}, u32[]{:S(2)}) async-start(f32[32,8,128]{2,1,0:T(8,128)} %get-tuple-element.77), calls=%async_computation.2 | async-start | bytes 262144 | tf_op jit(solution)/shard_map/all_to_all | solution.py:368
  (3 other events, 19.1 us)
